TPU v7x, 128 devices: a whole 4x4x4 slice. The times are simulated.
128 devices in a mesh: row: 16 (over z, x), col: 8 (over y, core).
Axes of the slice: x: 4, y: 4, z: 4, core: 2. Of those that a mesh axis runs over, the one named last changes fastest.
Arguments:
- measured: bfloat16 [512, 32, 16, 512], P('col', 'row'), may hold values from 0 to 2
- module_row: int32 [32], replicated, may hold values from 0 to 31, each once
- scan_offsets: int32 [16, 8, 4, 2], P('row', 'col'), may hold values from 0 to 511, as said below
- specimen: float32 [2, 4096, 4096], P(None, 'row', 'col'), may hold values from -9.3 to 9.3
- illumination: float32 [2, 512, 512], replicated, may hold values from -4 to 4
Outputs:
- specimen_step: float32 [2, 4096, 4096], P(None, 'row', 'col')
- illumination_step: float32 [2, 512, 512], replicated
Inputs may be any that keep to these rules, and one draw needn't show every extreme that they name: `scan_offsets`: position s of a device's tile has row offset in [0, 256) and column offset in [s * 128, (s + 1) * 128).
All inputs are finite; a program needn't handle non-finite values.
Results may differ from a plain program's by a relative error of at most 0.002.
The roundings to bfloat16 on the way count: a program that leaves them out, or rounds other values in their place, can miss the bound.
Values may be sent and summed in bfloat16 or wider, within the bound.
No kernel may reach another device: no remote copies, remote signals or barrier semaphores. Data moves between devices by JAX's collectives and lax.ppermute only.
A program may use at most 128 MiB of HBM per device.

v0:
```python
import math

import jax
import jax.numpy as jnp
from jax import lax
from jax.sharding import PartitionSpec as P


def passed_along(value, axis, steps):
    count = lax.axis_size(axis)
    pairs = [(source, (source + steps) % count) for source in range(count)]
    return lax.ppermute(value, axis, pairs)


def dft_tables(size):
    index = jnp.arange(size, dtype=jnp.int32)
    wrapped = index[:, None] * index[None, :] % size
    angle = wrapped.astype(jnp.float32) * (2.0 * math.pi / size)
    norm = 1.0 / math.sqrt(size)
    return (
        (jnp.cos(angle) * norm).astype(jnp.bfloat16),
        (-jnp.sin(angle) * norm).astype(jnp.bfloat16),
    )


def left_apply(stacked, wave, conjugate):
    size = wave.shape[-1]
    product = jnp.einsum("aj,psjk->psak", stacked, wave, preferred_element_type=jnp.float32)
    cos_real = product[0, :, :size]
    sin_real = product[0, :, size:]
    cos_imag = product[1, :, :size]
    sin_imag = product[1, :, size:]
    if conjugate:
        return jnp.stack([cos_real + sin_imag, cos_imag - sin_real])
    return jnp.stack([cos_real - sin_imag, cos_imag + sin_real])


def right_apply(wave, paired, conjugate):
    size = wave.shape[-1]
    product = jnp.einsum("psjk,kb->psjb", wave, paired, preferred_element_type=jnp.float32)
    real_cos = product[0, :, :, :size]
    real_sin = product[0, :, :, size:]
    imag_cos = product[1, :, :, :size]
    imag_sin = product[1, :, :, size:]
    if conjugate:
        return jnp.stack([real_cos + imag_sin, imag_cos - real_sin])
    return jnp.stack([real_cos - imag_sin, real_sin + imag_cos])


def shards(measured, module_row, scan_offsets, specimen, illumination):
    slots = scan_offsets.shape[2]
    size = illumination.shape[-1]
    tile_rows = specimen.shape[1]
    tile_cols = specimen.shape[2]
    arrived = lax.all_to_all(measured, "row", split_axis=0, concat_axis=1, tiled=True)
    modules = arrived.shape[1]
    inverse = (
        jnp.zeros((modules,), jnp.int32).at[module_row].set(jnp.arange(modules, dtype=jnp.int32))
    )
    amplitude = jnp.take(arrived, inverse, axis=1).reshape(slots, size, size)
    right = passed_along(specimen, "col", -1)
    band = jnp.concatenate([specimen, right], axis=2)
    below = passed_along(band, "row", -1)
    farther = passed_along(band, "row", -2)
    region = jnp.concatenate([band, below, farther], axis=1)
    zero = jnp.zeros((), jnp.int32)
    starts = [
        (zero, scan_offsets[0, 0, slot, 0], scan_offsets[0, 0, slot, 1]) for slot in range(slots)
    ]
    patches = jnp.stack(
        [lax.dynamic_slice(region, starts[slot], (2, size, size)) for slot in range(slots)], axis=1
    )
    ill_real = illumination[0][None]
    ill_imag = illumination[1][None]
    spec_real = patches[0]
    spec_imag = patches[1]
    wave = jnp.stack(
        [ill_real * spec_real - ill_imag * spec_imag, ill_real * spec_imag + ill_imag * spec_real]
    ).astype(jnp.bfloat16)
    cos_table, sin_table = dft_tables(size)
    stacked = jnp.concatenate([cos_table, sin_table], axis=0)
    paired = jnp.concatenate([cos_table, sin_table], axis=1)
    half = left_apply(stacked, wave, False).astype(jnp.bfloat16)
    far_field = right_apply(half, paired, False)
    magnitude = jnp.sqrt(far_field[0] * far_field[0] + far_field[1] * far_field[1])
    factor = amplitude.astype(jnp.float32) / jnp.maximum(magnitude, 0.25) - 1.0
    correction = (factor[None] * far_field).astype(jnp.bfloat16)
    back_half = left_apply(stacked, correction, True).astype(jnp.bfloat16)
    exit_change = right_apply(back_half, paired, True)
    chg_real = exit_change[0]
    chg_imag = exit_change[1]
    patch_grads = jnp.stack(
        [ill_real * chg_real + ill_imag * chg_imag, ill_real * chg_imag - ill_imag * chg_real]
    )
    num_real = jnp.sum(spec_real * chg_real + spec_imag * chg_imag, axis=0)
    num_imag = jnp.sum(spec_real * chg_imag - spec_imag * chg_real, axis=0)
    density = jnp.sum(spec_real * spec_real + spec_imag * spec_imag, axis=0)
    accum = jnp.zeros_like(region)
    for slot in range(slots):
        current = lax.dynamic_slice(accum, starts[slot], (2, size, size))
        accum = lax.dynamic_update_slice(accum, current + patch_grads[:, slot], starts[slot])
    upper = accum[:, :tile_rows]
    middle = accum[:, tile_rows : 2 * tile_rows]
    lower = accum[:, 2 * tile_rows :]
    rows_summed = upper + passed_along(middle, "row", 1) + passed_along(lower, "row", 2)
    specimen_step = rows_summed[:, :, :tile_cols] + passed_along(
        rows_summed[:, :, tile_cols:], "col", 1
    )
    totals = lax.psum((num_real, num_imag, density), ("row", "col"))
    root = jnp.sqrt(totals[2] + 1e-06)
    illumination_step = jnp.stack([totals[0] / root, totals[1] / root])
    return (specimen_step, illumination_step)


def solution(mesh):
    return jax.shard_map(
        shards,
        mesh=mesh,
        in_specs=(
            P("col", "row", None, None),
            P(),
            P("row", "col", None, None),
            P(None, "row", "col"),
            P(),
        ),
        out_specs=(P(None, "row", "col"), P()),
        check_vma=False,
    )
```

profile of v0, /device:TPU:1, one launch (start us, length us, event | category | flops | bytes accessed | tf_op | source)
XLA Modules:
  0.0 553.8 jit_solution(13483703911641076793)
XLA Ops:
  7.2 1.4 collective-permute-start
  8.6 2.3 constant_dynamic-update-slice_fusion.1
  10.8 11.7 %collective-permute-done = f32[2,256,512]{2,1,0:T(8,128)S(1)} collective-permute-done((f32[2,256,512]{2,1,0:T(8,128)}, f32[2,256,512]{2,1,0:T(8,128)S(1)}, u32[]{:S(2)}, u32[]{:S(2)}) %collective-permute-start) | collective-permute-done | bytes 1048608 | tf_op jit(solution)/shard_map/ppermute | solution.py:12
  22.6 1.0 constant_dynamic-update-slice_fusion
  23.6 6.0 %collective-permute-start.1 = (f32[2,256,1024]{2,1,0:T(8,128)}, f32[2,256,1024]{2,1,0:T(8,128)}, u32[]{:S(2)}, u32[]{:S(2)}) collective-permute-start(f32[2,256,1024]{2,1,0:T(8,128)} %constant_dynamic-update-slice_fusion), channel_id=1, source_target_pairs={{0,120},{8,0},{16,8},{24,16},{32,24},{40,32},{48,40},{56,48},{64,5... | collective-permute-start | bytes 6291464 | tf_op jit(solution)/shard_map/ppermute | solution.py:12
  29.6 0.5 collective-permute-start.2
  30.1 4.4 all-to-all-start
  34.5 0.0 all-reduce.3.cloned.1.call-start
  34.6 0.7 fusion.43
  45.5 0.0 copy-start.9
  45.5 1.1 slice_bitcast_fusion.1
  46.7 0.3 copy.61
  47.0 1.6 copy.68
  48.6 0.9 scatter_custom_fusion
  49.5 0.1 broadcast_in_dim.27
  49.6 0.1 broadcast_in_dim.28
  54.8 5.3 multiply_convert_fusion
  60.1 87.5 %all-to-all-done = bf16[64,2,16,512]{3,2,1,0:T(8,128)(2,1)} async-done(((bf16[64,2,16,512]{3,2,1,0:T(8,128)(2,1)}), bf16[64,2,16,512]{3,2,1,0:T(8,128)(2,1)}, u32[]{:S(2)}, u32[]{:S(2)}) %all-to-all-start) | async-done | bytes 2097184 | tf_op jit(solution)/shard_map/all_to_all | solution.py:55
  147.6 3.3 copy.62
  150.9 3.6 gather_fusion
  154.5 3.1 copy.63
  157.7 3.4 pad_maximum_fusion.1
  161.1 5.7 %constant_dynamic-slice_fusion.3 = (f32[2,512,512]{2,1,0:T(8,128)}, f32[2,512,512]{2,1,0:T(8,128)}, f32[2,512,512]{2,1,0:T(8,128)}, f32[2,512,512]{2,1,0:T(8,128)}) fusion(f32[2,768,1024]{2,1,0:T(8,128)S(1)} %pad_maximum_fusion.1, s32[]{:T(128)S(6)} %select_n.74, s32[]{:T(128)S(6)} %select_n.75, s32[]{:T(128)S(6)} %select_n.80, s32[]{:T(128)S(6)} %select_n.81, ...), kind=kLoop, calls=%fused_computation.88 | loop fusion | bytes 16777248 | tf_op jit(solution)/shard_map/dynamic_slice | solution.py:71
  166.8 2.9 copy.65
  169.7 2.9 copy.66
  172.6 3.0 copy.67
  175.6 2.9 copy.64
  178.5 4.0 pad_maximum_fusion
  182.4 1.6 subtract_convert_fusion
  184.0 8.1 %convolution_bitcast_fusion.1 = f32[2,4,1024,512]{2,3,1,0:T(8,128)} fusion(bf16[1,4,512,512]{2,3,1,0:T(8,128)(2,1)S(1)} %get-tuple-element.28, bf16[1,4,512,512]{2,3,1,0:T(8,128)(2,1)S(1)} %get-tuple-element.27, bf16[512,512]{1,0:T(8,128)(2,1)S(1)} %get-tuple-element.47, bf16[512,512]{1,0:T(8,128)(2,1)S(1)} %copy-done.4), kind=kOutput, calls=%fused_computation.12 | convolution fusion | flops 4299161600 | bytes 22020096 | tf_op jit(solution)/shard_map/aj,psjk->psak/dot_general | solution.py:28
  192.2 6.6 %fusion.5 = (bf16[1,4,512,512]{2,3,1,0:T(8,128)(2,1)S(1)}, bf16[1,4,512,512]{2,3,1,0:T(8,128)(2,1)S(1)}) fusion(f32[2,4,1024,512]{2,3,1,0:T(8,128)} %convolution_bitcast_fusion.1), kind=kLoop, calls=%fused_computation.25 | loop fusion | flops 4194304 | bytes 20971520 | tf_op jit(solution)/shard_map/convert.2
  198.8 8.2 %fusion.9 = f32[2,4,512,1024]{3,2,1,0:T(8,128)} fusion(bf16[1,4,512,512]{2,3,1,0:T(8,128)(2,1)S(1)} %get-tuple-element.24, bf16[1,4,512,512]{2,3,1,0:T(8,128)(2,1)S(1)} %get-tuple-element.23, bf16[512,512]{1,0:T(8,128)(2,1)S(1)} %get-tuple-element.47, bf16[512,512]{1,0:T(8,128)(2,1)S(1)} %copy-done.4), kind=kOutput, calls=%fused_computation.29 | convolution fusion | flops 4299161600 | bytes 22020096 | tf_op jit(solution)/shard_map/psjk,kb->psjb/dot_general | solution.py:40
  207.0 9.7 %add_bitcast_fusion = (f32[4,512,512]{2,1,0:T(8,128)S(1)}, f32[1,4,512,512]{3,2,1,0:T(8,128)}, f32[1,4,512,512]{3,2,1,0:T(8,128)}) fusion(bf16[1,4,512,512]{3,2,1,0:T(8,128)(2,1)S(1)} %bitcast.64, pred[512]{0:T(512)(128)(4,1)S(1)} %broadcast_in_dim.28, f32[2,4,512,1024]{3,2,1,0:T(8,128)} %fusion.9), kind=kLoop, calls=%fused_computation.43 | loop fusion | flops 10485760 | bytes 31457792 | tf_op jit(solution)/shard_map/mul | solution.py:87
  216.6 14.0 %convolution_bitcast_fusion = f32[2,4,1024,512]{2,3,1,0:T(8,128)} fusion(f32[1,4,512,512]{3,2,1,0:T(8,128)} %get-tuple-element.20, f32[1,4,512,512]{3,2,1,0:T(8,128)} %get-tuple-element.19, f32[4,512,512]{2,1,0:T(8,128)S(1)} %get-tuple-element.18, bf16[512,512]{1,0:T(8,128)(2,1)S(1)} %get-tuple-element.47, bf16[512,512]{1,0:T(8,128)(2,1)} %get-tuple-element.48), kind=kOutput, calls=%fused_computation.11 | convolution fusion | flops 4303355904 | bytes 30408704 | tf_op jit(solution)/shard_map/aj,psjk->psak/dot_general | solution.py:28
  230.6 6.7 %fusion.3 = (bf16[1,4,512,512]{2,3,1,0:T(8,128)(2,1)S(1)}, bf16[1,4,512,512]{2,3,1,0:T(8,128)(2,1)S(1)}) fusion(f32[2,4,1024,512]{2,3,1,0:T(8,128)} %convolution_bitcast_fusion), kind=kLoop, calls=%fused_computation.19 | loop fusion | flops 4194304 | bytes 20971520 | tf_op jit(solution)/shard_map/convert
  237.3 8.3 %fusion.13 = f32[2,4,512,1024]{2,3,1,0:T(8,128)} fusion(bf16[1,4,512,512]{2,3,1,0:T(8,128)(2,1)S(1)} %get-tuple-element.22, bf16[1,4,512,512]{2,3,1,0:T(8,128)(2,1)S(1)} %get-tuple-element.21, bf16[512,512]{1,0:T(8,128)(2,1)S(1)} %get-tuple-element.47, bf16[512,512]{1,0:T(8,128)(2,1)S(1)} %copy-done.5), kind=kOutput, calls=%fused_computation.33 | convolution fusion | flops 4299161600 | bytes 22020096 | tf_op jit(solution)/shard_map/psjk,kb->psjb/dot_general | solution.py:40
  245.6 10.8 %add_reduce_fusion.1 = (f32[512,512]{0,1:T(8,128)}, f32[512,512]{0,1:T(8,128)}, f32[512,512]{0,1:T(8,128)}, f32[1,4,512,512]{2,3,1,0:T(8,128)S(1)}, f32[1,4,512,512]{2,3,1,0:T(8,128)}) fusion(f32[2,4,512,512]{2,3,1,0:T(8,128)S(1)} %pad_maximum_fusion, f32[2,4,512,1024]{2,3,1,0:T(8,128)} %fusion.13), kind=kLoop, calls=%fused_computation.39 | loop fusion | flops 13893632 | bytes 36700160 | tf_op jit(solution)/shard_map/reduce_sum | solution.py:95
  256.5 3.8 multiply_subtract_fusion
  260.3 0.2 fusion.22
  260.5 1.9 copy-done
  262.4 1.2 copy-done.1
  263.6 3.1 broadcast_in_dim.25
  266.7 14.1 %dynamic_update_slice.12 = f32[2,768,1024]{1,2,0:T(8,128)} dynamic-update-slice(f32[2,768,1024]{1,2,0:T(8,128)} %broadcast_in_dim.25, f32[2,512,512]{1,2,0:T(8,128)S(1)} %fusion.22, s32[]{:T(128)} %constant.16.clone.1, s32[]{:T(128)S(6)} %select_n.74, s32[]{:T(128)S(6)} %select_n.75) | dynamic-update-slice | bytes 4194308 | tf_op jit(solution)/shard_map/dynamic_update_slice | solution.py:101
  280.8 3.0 fusion.25
  283.8 14.3 %dynamic_update_slice.13 = f32[2,768,1024]{1,2,0:T(8,128)} dynamic-update-slice(f32[2,768,1024]{1,2,0:T(8,128)} %dynamic_update_slice.12, f32[2,512,512]{1,2,0:T(8,128)S(1)} %fusion.25, s32[]{:T(128)} %constant.16.clone.1, s32[]{:T(128)S(6)} %select_n.76, s32[]{:T(128)S(6)} %select_n.77) | dynamic-update-slice | bytes 4194308 | tf_op jit(solution)/shard_map/dynamic_update_slice | solution.py:101
  298.1 3.0 fusion.20
  301.1 12.6 %dynamic_update_slice.14 = f32[2,768,1024]{1,2,0:T(8,128)} dynamic-update-slice(f32[2,768,1024]{1,2,0:T(8,128)} %dynamic_update_slice.13, f32[2,512,512]{1,2,0:T(8,128)S(1)} %fusion.20, s32[]{:T(128)} %constant.16.clone.1, s32[]{:T(128)S(6)} %select_n.78, s32[]{:T(128)S(6)} %select_n.79) | dynamic-update-slice | bytes 4194308 | tf_op jit(solution)/shard_map/dynamic_update_slice | solution.py:101
  313.7 3.0 fusion.28
  316.7 13.9 %dynamic_update_slice.15 = f32[2,768,1024]{1,2,0:T(8,128)} dynamic-update-slice(f32[2,768,1024]{1,2,0:T(8,128)} %dynamic_update_slice.14, f32[2,512,512]{1,2,0:T(8,128)S(1)} %fusion.28, s32[]{:T(128)} %constant.16.clone.1, s32[]{:T(128)S(6)} %select_n.80, s32[]{:T(128)S(6)} %select_n.81) | dynamic-update-slice | bytes 4194308 | tf_op jit(solution)/shard_map/dynamic_update_slice | solution.py:101
  330.6 4.7 fusion.42
  335.3 0.9 collective-permute-start.4
  336.3 0.0 all-reduce.3.cloned.1.call-update
  336.3 54.6 %collective-permute-done.3 = f32[2,256,1024]{1,2,0:T(8,128)S(1)} collective-permute-done((f32[2,256,1024]{1,2,0:T(8,128)}, f32[2,256,1024]{1,2,0:T(8,128)S(1)}, u32[]{:S(2)}, u32[]{:S(2)}) %collective-permute-start.3) | collective-permute-done | bytes 2097184 | tf_op jit(solution)/shard_map/ppermute | solution.py:12
  390.9 1.3 copy-done.7
  392.2 45.7 %collective-permute-done.4 = f32[2,256,1024]{1,2,0:T(8,128)} collective-permute-done((f32[2,256,1024]{1,2,0:T(8,128)}, f32[2,256,1024]{1,2,0:T(8,128)}, u32[]{:S(2)}, u32[]{:S(2)}) %collective-permute-start.4) | collective-permute-done | bytes 2097184 | tf_op jit(solution)/shard_map/ppermute | solution.py:12
  437.9 3.3 fusion.26
  441.2 0.1 slice.178
  441.2 5.7 %collective-permute-start.5 = (f32[2,256,512]{1,2,0:T(8,128)S(1)}, f32[2,256,512]{1,2,0:T(8,128)}, u32[]{:S(2)}, u32[]{:S(2)}) collective-permute-start(f32[2,256,512]{1,2,0:T(8,128)S(1)} %slice.178), channel_id=1, source_target_pairs={{0,1},{1,2},{2,3},{3,4},{4,5},{5,6},{6,7},{7,0},{8,9},{9,10},{10,1... | collective-permute-start | bytes 3145736 | tf_op jit(solution)/shard_map/ppermute | solution.py:12
  446.9 90.7 %all-reduce.3.cloned.1.call-done = (f32[512,512]{0,1:T(8,128)}, f32[512,512]{0,1:T(8,128)}, f32[512,512]{0,1:T(8,128)}) async-done(((f32[512,512]{0,1:T(8,128)}, f32[512,512]{0,1:T(8,128)}, f32[512,512]{0,1:T(8,128)}), (f32[512,512]{0,1:T(8,128)}, f32[512,512]{0,1:T(8,128)}, f32[512,512]{0,1:T(8,128)})) %all-reduce.3.cloned.1.call-update) | async-done | bytes 3145744 | tf_op jit(solution)/shard_map/psum | solution.py:109
  537.6 2.2 divide_bitcast_fusion.1
  539.9 1.5 pad_maximum_fusion.3
  541.4 2.9 copy.80
  544.3 1.4 slice_add_fusion.5
  545.6 1.3 copy.79
  (25 shorter events, 0.1 us)
Async XLA Ops:
  7.2 27.4 %copy-start.8 = (s32[1,1,4,2]{2,3,1,0:T(2,128)S(1)}, s32[1,1,4,2]{2,3,1,0:T(2,128)}, u32[]{:S(2)}) copy-start(s32[1,1,4,2]{2,3,1,0:T(2,128)} %param.7) | copy-start | bytes 100
  7.2 38.3 %copy-start.6 = (f32[2,512,512]{2,1,0:T(8,128)S(1)}, f32[2,512,512]{2,1,0:T(8,128)}, u32[]{:S(2)}) copy-start(f32[2,512,512]{2,1,0:T(8,128)} %param.9) | copy-start | bytes 6291460
  7.2 15.4 %collective-permute-start = (f32[2,256,512]{2,1,0:T(8,128)}, f32[2,256,512]{2,1,0:T(8,128)S(1)}, u32[]{:S(2)}, u32[]{:S(2)}) collective-permute-start(f32[2,256,512]{2,1,0:T(8,128)} %param.8), channel_id=1, source_target_pairs={{0,7},{1,0},{2,1},{3,2},{4,3},{5,4},{6,5},{7,6},{8,15},{9,8},{10,9... | collective-permute-start | bytes 3145736 | tf_op jit(solution)/shard_map/ppermute | solution.py:12
  23.6 134.1 %collective-permute-start.1 = (f32[2,256,1024]{2,1,0:T(8,128)}, f32[2,256,1024]{2,1,0:T(8,128)}, u32[]{:S(2)}, u32[]{:S(2)}) collective-permute-start(f32[2,256,1024]{2,1,0:T(8,128)} %constant_dynamic-update-slice_fusion), channel_id=1, source_target_pairs={{0,120},{8,0},{16,8},{24,16},{32,24},{40,32},{48,40},{56,48},{64,5... | collective-permute-start | bytes 6291464 | tf_op jit(solution)/shard_map/ppermute | solution.py:12
  29.6 128.1 %collective-permute-start.2 = (f32[2,256,1024]{2,1,0:T(8,128)}, f32[2,256,1024]{2,1,0:T(8,128)}, u32[]{:S(2)}, u32[]{:S(2)}) collective-permute-start(f32[2,256,1024]{2,1,0:T(8,128)} %constant_dynamic-update-slice_fusion), channel_id=1, source_target_pairs={{0,112},{8,120},{16,0},{24,8},{32,16},{40,24},{48,32},{56,40},{64,... | collective-permute-start | bytes 6291464 | tf_op jit(solution)/shard_map/ppermute | solution.py:12
  30.1 117.6 %all-to-all-start = ((bf16[64,2,16,512]{3,2,1,0:T(8,128)(2,1)}), bf16[64,2,16,512]{3,2,1,0:T(8,128)(2,1)}, u32[]{:S(2)}, u32[]{:S(2)}) async-start(bf16[64,2,16,512]{3,2,1,0:T(8,128)(2,1)} %param.5), calls=%async_computation | async-start | bytes 4194304 | tf_op jit(solution)/shard_map/all_to_all | solution.py:55
  34.5 503.1 %all-reduce.3.cloned.1.call-start = ((), (), s32[]{:S(2)}) async-start(), calls=%async_computation.1 | async-start | bytes 6291456 | tf_op jit(solution)/shard_map/psum | solution.py:109
  45.5 3.1 copy-start.9
  48.6 133.8 %copy-start.2 = (f32[512,512]{0,1:T(8,128)}, f32[512,512]{0,1:T(8,128)S(1)}, u32[]{:S(2)}) copy-start(f32[512,512]{0,1:T(8,128)S(1)} %copy.68) | copy-start | bytes 3145732
  182.4 1.6 copy-start.4
  198.8 8.2 %copy-start.3 = (bf16[4,32,16,512]{3,2,1,0:T(8,128)(2,1)S(1)}, bf16[4,32,16,512]{3,2,1,0:T(8,128)(2,1)}, u32[]{:S(2)}) copy-start(bf16[4,32,16,512]{3,2,1,0:T(8,128)(2,1)} %copy.63) | copy-start | bytes 6291460
  230.6 6.7 %copy-start.5 = (bf16[512,512]{1,0:T(8,128)(2,1)S(1)}, bf16[512,512]{1,0:T(8,128)(2,1)}, u32[]{:S(2)}) copy-start(bf16[512,512]{1,0:T(8,128)(2,1)} %get-tuple-element.48) | copy-start | bytes 1572868
  260.3 2.1 copy-start
  260.3 3.3 copy-start.1
  335.3 55.6 %collective-permute-start.3 = (f32[2,256,1024]{1,2,0:T(8,128)}, f32[2,256,1024]{1,2,0:T(8,128)S(1)}, u32[]{:S(2)}, u32[]{:S(2)}) collective-permute-start(f32[2,256,1024]{1,2,0:T(8,128)} %get-tuple-element.29), channel_id=1, source_target_pairs={{0,8},{8,16},{16,24},{24,32},{32,40},{40,48},{48,56},{56,64},{64,7... | collective-permute-start | bytes 6291464 | tf_op jit(solution)/shard_map/ppermute | solution.py:12
  335.3 102.6 %collective-permute-start.4 = (f32[2,256,1024]{1,2,0:T(8,128)}, f32[2,256,1024]{1,2,0:T(8,128)}, u32[]{:S(2)}, u32[]{:S(2)}) collective-permute-start(f32[2,256,1024]{1,2,0:T(8,128)} %get-tuple-element.30), channel_id=1, source_target_pairs={{0,16},{8,24},{16,32},{24,40},{32,48},{40,56},{48,64},{56,72},{64,... | collective-permute-start | bytes 6291464 | tf_op jit(solution)/shard_map/ppermute | solution.py:12
  390.9 1.3 copy-start.7
  441.2 103.0 %collective-permute-start.5 = (f32[2,256,512]{1,2,0:T(8,128)S(1)}, f32[2,256,512]{1,2,0:T(8,128)}, u32[]{:S(2)}, u32[]{:S(2)}) collective-permute-start(f32[2,256,512]{1,2,0:T(8,128)S(1)} %slice.178), channel_id=1, source_target_pairs={{0,1},{1,2},{2,3},{3,4},{4,5},{5,6},{6,7},{7,0},{8,9},{9,10},{10,1... | collective-permute-start | bytes 3145736 | tf_op jit(solution)/shard_map/ppermute | solution.py:12
Sparse Core Ops, SparseCore 0:
  336.4 201.1 all-reduce.2
where the time goes:
time: 556 us; the launch traced here: 554 us
  waiting for transfers between devices  290 us (52%)
  local copies, waits for them, and re-layouts  107 us (19%)
  other arithmetic  69.5 us (12%)
  matrix products  38.6 us (7%)
  between operations  29.7 us (5%)
  starting transfers between devices  19 us (3%)
    ppermute x6, waiting for transfers between devices, passed_along(): return lax.ppermute(value, axis, pairs)  112 us
    psum x1, waiting for transfers between devices, shards(): totals = lax.psum((num_real, num_imag, density), ('row', 'col'))  90.7 us
    all_to_all x1, waiting for transfers between devices, shards(): lax.all_to_all(measured, 'row', split_axis=0, concat_axis=1, tiled=True)  87.5 us
    dynamic_update_slice x4, local copies, waits for them, and re-layouts, shards(): lax.dynamic_update_slice(accum, current + patch_grads[:, slot], starts[sl...  54.9 us
    dot_general x2, matrix products, left_apply(): jnp.einsum('aj,psjk->psak', stacked, wave, preferred_element_type=jnp.flo...  22.1 us
    dynamic_slice x5, local copies, waits for them, and re-layouts, shards(): lax.dynamic_slice(region, starts[slot], (2, size, size))  17.3 us
    dot_general x2, matrix products, right_apply(): jnp.einsum('psjk,kb->psjb', wave, paired, preferred_element_type=jnp.floa...  16.5 us
    another operation x3, other arithmetic  14.9 us
  transfers between devices with their start and end apart: 8, of which 5 were waited for; matrix products, arithmetic and copies ran while one was open for 6% of the time, Pallas kernels for 0%

commit v1 on v0

v1 whole, which is shorter than its diff:
```python
import functools
import math

import jax
import jax.numpy as jnp
from jax import lax
from jax.experimental import pallas as pl
from jax.experimental.pallas import tpu as pltpu
from jax.sharding import PartitionSpec as P

LANES = 128
SUBLANES = 8
CHUNK = 32
BLOCK = 256


def passed_along(value, axis, steps):
    count = lax.axis_size(axis)
    pairs = [(source, (source + steps) % count) for source in range(count)]
    return lax.ppermute(value, axis, pairs)


def passed_both(value, row_steps, col_steps):
    rows, cols = lax.axis_size("row"), lax.axis_size("col")
    pairs = [
        (row * cols + col, (row + row_steps) % rows * cols + (col + col_steps) % cols)
        for row in range(rows)
        for col in range(cols)
    ]
    return lax.ppermute(value, ("row", "col"), pairs)


def dft_tables(size):
    index = jnp.arange(size, dtype=jnp.int32)
    wrapped = index[:, None] * index[None, :] % size
    angle = wrapped.astype(jnp.float32) * (2.0 * math.pi / size)
    norm = 1.0 / math.sqrt(size)
    return (
        (jnp.cos(angle) * norm).astype(jnp.bfloat16),
        (-jnp.sin(angle) * norm).astype(jnp.bfloat16),
    )


def narrowed(value):
    peak = jnp.maximum(jnp.max(jnp.abs(value)), 1e-30)
    scaled = (value * (32768.0 / peak)).astype(jnp.float16)
    return scaled, (peak * (1.0 / 32768.0)).reshape(1, 1)


def widened(value, unit):
    return value.astype(jnp.float32) * unit[0, 0]


def gather_rows(ref, plane, start, rows, col, shift):
    tiles = rows // SUBLANES + 1
    block = ref[plane, pl.ds(start, tiles * SUBLANES), pl.ds(col, LANES)]
    block = block.reshape(tiles, SUBLANES, LANES)
    rolled = pltpu.roll(block, (SUBLANES - shift) % SUBLANES, axis=1)
    sub = lax.broadcasted_iota(jnp.int32, (tiles - 1, SUBLANES, LANES), 1)
    return jnp.where(sub < SUBLANES - shift, rolled[:-1], rolled[1:]).reshape(rows, LANES)


def forward_kernel(offs, region, ill, left, right, far, patch, density, wave, half):
    slot = pl.program_id(0)
    size = ill.shape[-1]
    row = offs[slot, 0]
    base = slot * LANES
    lane_shift = offs[slot, 1] % LANES
    row_shift = row % SUBLANES
    row_base = row - row_shift
    lane = lax.broadcasted_iota(jnp.int32, (CHUNK, LANES), 1)
    blocks = size // LANES

    @pl.when(slot == 0)
    def _():
        density[...] = jnp.zeros_like(density)

    def extract(step, carry):
        at = pl.multiple_of(step * CHUNK, CHUNK)
        start = pl.multiple_of(row_base + at, SUBLANES)
        last = [None, None]
        for block in range(blocks + 1):
            col = pl.multiple_of(base + block * LANES, LANES)
            now = [
                pltpu.roll(
                    gather_rows(region, plane, start, CHUNK, col, row_shift),
                    (LANES - lane_shift) % LANES,
                    axis=1,
                )
                for plane in range(2)
            ]
            if block > 0:
                to = slice((block - 1) * LANES, block * LANES)
                spec_real, spec_imag = (
                    jnp.where(lane < LANES - lane_shift, last[plane], now[plane])
                    for plane in range(2)
                )
                patch[0, 0, pl.ds(at, CHUNK), to] = spec_real
                patch[0, 1, pl.ds(at, CHUNK), to] = spec_imag
                ill_real = ill[0, pl.ds(at, CHUNK), to]
                ill_imag = ill[1, pl.ds(at, CHUNK), to]
                wave[pl.ds(at, CHUNK), to] = (
                    ill_real * spec_real - ill_imag * spec_imag
                ).astype(jnp.bfloat16)
                wave[pl.ds(size + at, CHUNK), to] = (
                    ill_real * spec_imag + ill_imag * spec_real
                ).astype(jnp.bfloat16)
                density[pl.ds(at, CHUNK), to] += spec_real * spec_real + spec_imag * spec_imag
            last = now
        return carry

    lax.fori_loop(0, size // CHUNK, extract, 0)
    for block in range(size // BLOCK):
        to = slice(block * BLOCK, (block + 1) * BLOCK)
        also = slice(size + block * BLOCK, size + (block + 1) * BLOCK)
        product = jnp.dot(left[...], wave[:, to], preferred_element_type=jnp.float32)
        half[:, to] = product[:size].astype(jnp.bfloat16)
        half[:, also] = product[size:].astype(jnp.bfloat16)
    for plane in range(2):
        for block in range(size // BLOCK):
            to = slice(block * BLOCK, (block + 1) * BLOCK)
            of = slice(plane * size + block * BLOCK, plane * size + (block + 1) * BLOCK)
            far[0, plane, :, to] = jnp.dot(
                half[...], right[:, of], preferred_element_type=jnp.float32
            )


def backward_kernel(
    offs, order, far, patch, amp, ill, left, right, accum, numer, corr, back, change, inverse
):
    slot = pl.program_id(0)
    size = ill.shape[-1]
    modules = size // amp.shape[3]
    senders = amp.shape[0]
    row = offs[slot, 0]
    base = slot * LANES
    lane_shift = offs[slot, 1] % LANES
    row_shift = row % SUBLANES
    row_base = row - row_shift
    blocks = size // LANES
    height = amp.shape[3]
    per = amp.shape[2]

    @pl.when(slot == 0)
    def _():
        numer[...] = jnp.zeros_like(numer)

        def clear(step, carry):
            at = pl.multiple_of(step * CHUNK, CHUNK)
            accum[:, pl.ds(at, CHUNK), :] = jnp.zeros((2, CHUNK, accum.shape[2]), jnp.float32)
            return carry

        lax.fori_loop(0, accum.shape[1] // CHUNK, clear, 0)

        def invert(module, carry):
            inverse[order[module]] = module
            return carry

        lax.fori_loop(0, modules, invert, 0)

    def correct(band, carry):
        at = pl.multiple_of(band * height, height)
        module = inverse[band]
        rows = pl.ds(at, height)
        far_real = far[0, 0, rows, :]
        far_imag = far[0, 1, rows, :]
        sender = (module // per + senders - 1) % senders
        level = amp[sender, 0, module % per].astype(jnp.float32)
        magnitude = jnp.sqrt(far_real * far_real + far_imag * far_imag)
        factor = level / jnp.maximum(magnitude, 0.25) - 1.0
        corr[rows, :] = (factor * far_real).astype(jnp.bfloat16)
        corr[pl.ds(size + at, height), :] = (factor * far_imag).astype(jnp.bfloat16)
        return carry

    lax.fori_loop(0, modules, correct, 0)
    for block in range(size // BLOCK):
        to = slice(block * BLOCK, (block + 1) * BLOCK)
        also = slice(size + block * BLOCK, size + (block + 1) * BLOCK)
        product = jnp.dot(right[...], corr[:, to], preferred_element_type=jnp.float32)
        back[:, to] = product[:size].astype(jnp.bfloat16)
        back[:, also] = product[size:].astype(jnp.bfloat16)
    for plane in range(2):
        for block in range(size // BLOCK):
            to = slice(block * BLOCK, (block + 1) * BLOCK)
            of = slice(plane * size + block * BLOCK, plane * size + (block + 1) * BLOCK)
            change[plane, :, to] = jnp.dot(
                back[...], left[:, of], preferred_element_type=jnp.float32
            )

    lane = lax.broadcasted_iota(jnp.int32, (CHUNK, LANES), 1)
    tiles = CHUNK // SUBLANES
    sub = lax.broadcasted_iota(jnp.int32, (tiles + 1, SUBLANES, LANES), 1)
    empty = jnp.zeros((1, SUBLANES, LANES), jnp.float32)

    def spread(step, carry):
        at = pl.multiple_of(step * CHUNK, CHUNK)
        rows = pl.ds(at, CHUNK)
        start = pl.multiple_of(row_base + at, SUBLANES)
        last = [jnp.zeros((CHUNK, LANES), jnp.float32)] * 2
        for block in range(blocks + 1):
            if block < blocks:
                to = slice(block * LANES, (block + 1) * LANES)
                chg_real = change[0, rows, to]
                chg_imag = change[1, rows, to]
                spec_real = patch[0, 0, rows, to]
                spec_imag = patch[0, 1, rows, to]
                ill_real = ill[0, rows, to]
                ill_imag = ill[1, rows, to]
                numer[0, rows, to] += spec_real * chg_real + spec_imag * chg_imag
                numer[1, rows, to] += spec_real * chg_imag - spec_imag * chg_real
                grads = (
                    ill_real * chg_real + ill_imag * chg_imag,
                    ill_real * chg_imag - ill_imag * chg_real,
                )
                now = [pltpu.roll(grad, lane_shift, axis=1) for grad in grads]
            else:
                now = [jnp.zeros((CHUNK, LANES), jnp.float32)] * 2
            col = pl.multiple_of(base + block * LANES, LANES)
            for plane in range(2):
                placed = jnp.where(lane < lane_shift, last[plane], now[plane])
                placed = pltpu.roll(placed.reshape(tiles, SUBLANES, LANES), row_shift, axis=1)
                placed = jnp.where(
                    sub < row_shift,
                    jnp.concatenate([empty, placed], axis=0),
                    jnp.concatenate([placed, empty], axis=0),
                ).reshape(CHUNK + SUBLANES, LANES)
                accum[plane, pl.ds(start, CHUNK + SUBLANES), pl.ds(col, LANES)] += placed
            last = now
        return carry

    lax.fori_loop(0, size // CHUNK, spread, 0)


def whole(shape):
    return pl.BlockSpec(shape, lambda slot, *refs: (0,) * len(shape))


def once(shape):
    return pl.BlockSpec(
        shape, lambda slot, *refs: (0,) * len(shape), pipeline_mode=pl.Buffered(1)
    )


def one_slot(shape):
    return pl.BlockSpec((1,) + shape, lambda slot, *refs: (slot,) + (0,) * len(shape))


def run_forward(offs, region, ill, left, right):
    slots = offs.shape[0]
    size = ill.shape[-1]
    planes = jax.ShapeDtypeStruct((slots, 2, size, size), jnp.float32)
    return pl.pallas_call(
        forward_kernel,
        grid_spec=pltpu.PrefetchScalarGridSpec(
            num_scalar_prefetch=1,
            grid=(slots,),
            in_specs=[once(region.shape), once(ill.shape), once(left.shape), once(right.shape)],
            out_specs=[
                one_slot((2, size, size)),
                one_slot((2, size, size)),
                whole((size, size)),
            ],
            scratch_shapes=[
                pltpu.VMEM((2 * size, size), jnp.bfloat16),
                pltpu.VMEM((size, 2 * size), jnp.bfloat16),
            ],
        ),
        out_shape=[planes, planes, jax.ShapeDtypeStruct((size, size), jnp.float32)],
        cost_estimate=pl.CostEstimate(
            flops=slots * 16 * size**3, bytes_accessed=30_000_000, transcendentals=0
        ),
        compiler_params=pltpu.CompilerParams(vmem_limit_bytes=48 * 1024 * 1024),
        name="forward",
    )(offs, region, ill, left, right)


def run_backward(offs, order, far, patch, amp, ill, left, right, region_shape):
    slots = offs.shape[0]
    size = ill.shape[-1]
    senders, _, per, height, _ = amp.shape
    return pl.pallas_call(
        backward_kernel,
        grid_spec=pltpu.PrefetchScalarGridSpec(
            num_scalar_prefetch=2,
            grid=(slots,),
            in_specs=[
                one_slot((2, size, size)),
                one_slot((2, size, size)),
                pl.BlockSpec(
                    (senders, 1, per, height, size), lambda slot, *refs: (0, slot, 0, 0, 0)
                ),
                once(ill.shape),
                once(left.shape),
                once(right.shape),
            ],
            out_specs=[whole(region_shape), whole((2, size, size))],
            scratch_shapes=[
                pltpu.VMEM((2 * size, size), jnp.bfloat16),
                pltpu.VMEM((size, 2 * size), jnp.bfloat16),
                pltpu.VMEM((2, size, size), jnp.float32),
                pltpu.SMEM((senders * per,), jnp.int32),
            ],
        ),
        out_shape=[
            jax.ShapeDtypeStruct(region_shape, jnp.float32),
            jax.ShapeDtypeStruct((2, size, size), jnp.float32),
        ],
        cost_estimate=pl.CostEstimate(
            flops=slots * 16 * size**3, bytes_accessed=30_000_000, transcendentals=0
        ),
        compiler_params=pltpu.CompilerParams(vmem_limit_bytes=56 * 1024 * 1024),
        name="backward",
    )(offs, order, far, patch, amp, ill, left, right)


def spread_out(value):
    return lax.all_to_all(value, ("row", "col"), split_axis=0, concat_axis=0, tiled=True)


def shards(measured, module_row, scan_offsets, specimen, illumination):
    slots = scan_offsets.shape[2]
    size = illumination.shape[-1]
    tile_rows = specimen.shape[1]
    tile_cols = specimen.shape[2]
    senders = lax.axis_size("row")
    devices = senders * lax.axis_size("col")
    per, height = measured.shape[1], measured.shape[2]
    late = slots // 2
    edge = tile_cols // 2
    grouped = measured.reshape(senders, slots, per, height, size)
    moved = passed_along(grouped[:, late:], "col", 1)
    upper = passed_along(specimen, "row", 1)
    lower = passed_along(specimen, "row", -1)
    west = passed_along(specimen[:, :, edge:], "col", 1)
    east = passed_along(specimen[:, :, :edge], "col", -1)
    early_offs = passed_along(scan_offsets[0, 0, :late], "row", 1)
    late_offs = passed_both(scan_offsets[0, 0, late:], 1, 1)
    offs = jnp.concatenate([late_offs, early_offs], axis=0)
    outer = jnp.concatenate([upper, lower], axis=1)
    outer_west = passed_along(outer[:, :, edge:], "col", 1)
    outer_east = passed_along(outer[:, :, :edge], "col", -1)
    arrived = lax.all_to_all(
        jnp.concatenate([moved, grouped[:, :late]], axis=1),
        "row",
        split_axis=0,
        concat_axis=0,
        tiled=True,
        axis_index_groups=[[(sender + 1) % senders for sender in range(senders)]],
    )
    region = jnp.concatenate(
        [
            jnp.concatenate(
                [outer_west[:, :tile_rows], upper, outer_east[:, :tile_rows]], axis=2
            ),
            jnp.concatenate([west, specimen, east], axis=2),
            jnp.concatenate(
                [outer_west[:, tile_rows:], lower, outer_east[:, tile_rows:]], axis=2
            ),
        ],
        axis=1,
    )
    cos_table, sin_table = dft_tables(size)
    left = jnp.concatenate(
        [
            jnp.concatenate([cos_table, -sin_table], axis=1),
            jnp.concatenate([sin_table, cos_table], axis=1),
        ],
        axis=0,
    )
    right = jnp.concatenate(
        [
            jnp.concatenate([cos_table, sin_table], axis=1),
            jnp.concatenate([-sin_table, cos_table], axis=1),
        ],
        axis=0,
    )
    far, patch, density = run_forward(offs, region, illumination, left, right)
    share = (devices, size * size // devices // LANES, LANES)
    density_parts = spread_out(density.reshape(share))
    root = jnp.sqrt(jnp.sum(density_parts.reshape(share), axis=0) + 1e-06)
    accum, numer = run_backward(
        offs, module_row, far, patch, arrived, illumination, left, right, region.shape
    )
    small, numer_unit = narrowed(numer)
    rows = share[1]
    small = small.reshape(2, devices, rows, LANES).swapaxes(0, 1).reshape(devices, 2 * rows, LANES)
    parts = spread_out(small)
    units = spread_out(jnp.broadcast_to(numer_unit.reshape(1, 1, 1), (devices, 1, LANES)))
    total = jnp.sum(
        parts.astype(jnp.float32).reshape(devices, 2, rows, LANES) * units[:, None, :, :1], axis=0
    )
    mine, mine_unit = narrowed(total / root[None])
    result = spread_out(jnp.broadcast_to(mine.reshape(1, 2 * rows, LANES), small.shape))
    result_units = spread_out(
        jnp.broadcast_to(mine_unit.reshape(1, 1, 1), (devices, 1, LANES))
    )
    result = (
        result.reshape(devices, 2, rows, LANES).astype(jnp.float32) * result_units[:, :, None, :1][:, :1]
    )
    illumination_step = result.swapaxes(0, 1).reshape(2, size, size)
    to_west, to_west_unit = narrowed(accum[:, :, :edge])
    to_east, to_east_unit = narrowed(accum[:, :, edge + tile_cols :])
    from_east = passed_along(to_west, "col", -1)
    from_west = passed_along(to_east, "col", 1)
    from_east_unit = passed_along(to_west_unit, "col", -1)
    from_west_unit = passed_along(to_east_unit, "col", 1)
    column = accum[:, :, edge : edge + tile_cols] + jnp.concatenate(
        [widened(from_west, from_west_unit), widened(from_east, from_east_unit)], axis=2
    )
    to_upper, to_upper_unit = narrowed(column[:, :tile_rows])
    to_lower, to_lower_unit = narrowed(column[:, 2 * tile_rows :])
    from_lower = passed_along(to_upper, "row", -1)
    from_upper = passed_along(to_lower, "row", 1)
    from_lower_unit = passed_along(to_upper_unit, "row", -1)
    from_upper_unit = passed_along(to_lower_unit, "row", 1)
    specimen_step = (
        column[:, tile_rows : 2 * tile_rows]
        + widened(from_lower, from_lower_unit)
        + widened(from_upper, from_upper_unit)
    )
    return (specimen_step, illumination_step)


def solution(mesh):
    return jax.shard_map(
        shards,
        mesh=mesh,
        in_specs=(
            P("col", "row", None, None),
            P(),
            P("row", "col", None, None),
            P(None, "row", "col"),
            P(),
        ),
        out_specs=(P(None, "row", "col"), P()),
        check_vma=False,
    )
```

time: 556 us -> 265 us (0.48)
  waiting for transfers between devices: 290 us -> 50 us
  local copies, waits for them, and re-layouts: 107 us -> 18.6 us
  starting transfers between devices: 19 us -> 86.1 us
  Pallas kernels: 0 us -> 53.4 us
  matrix products: 38.6 us -> 0 us
  between operations: 29.7 us -> 5.05 us
  other arithmetic: 69.5 us -> 49.4 us
    psum x1 -> x0, waiting for transfers between devices: 90.7 us -> none  [shards(): totals = lax.psum((num_real, num_imag, density), ('row', 'col'))]
    ppermute x6 -> x16, waiting for transfers between devices: 112 us -> 22.1 us  [passed_along(): return lax.ppermute(value, axis, pairs)]
    all_to_all x1 -> x6, waiting for transfers between devices: 87.5 us -> 27.9 us  [the longest x5 27.9 us: spread_out(): lax.all_to_all(value, ('row', 'col'), split_axis=0, concat_axis=0, tiled=...]
    dynamic_update_slice x4 -> x0, local copies, waits for them, and re-layouts: 54.9 us -> none  [shards(): lax.dynamic_update_slice(accum, current + patch_grads[:, slot], starts[sl...]
    pallas_call x0 -> x2, Pallas kernels: none -> 53.4 us  [the longest x1 30.9 us: run_backward(): pl.pallas_call(backward_kernel, grid_spec=pltpu.PrefetchScalarGridSpec(nu...]
    dot_general x4 -> x0, matrix products: 38.6 us -> none  [the longest x2 22.1 us: left_apply(): jnp.einsum('aj,psjk->psak', stacked, wave, preferred_element_type=jnp.flo...]
    all_to_all x1 -> x6, starting transfers between devices: 4.44 us -> 40.3 us  [the longest x5 34 us: spread_out(): lax.all_to_all(value, ('row', 'col'), split_axis=0, concat_axis=0, tiled=...]
    ppermute x6 -> x16, starting transfers between devices: 14.5 us -> 45.5 us  [passed_along(): return lax.ppermute(value, axis, pairs)]
  transfers between devices with their start and end apart: 8 -> 23, of which waited for: 5 -> 5; matrix products, arithmetic and copies ran while one was open for 6% -> 22% of each run, Pallas kernels for 0% -> 9%
where the time goes in v1:
time: 265 us; the launch traced here: 263 us
  starting transfers between devices  86.1 us (32%)
  Pallas kernels  53.4 us (20%)
  waiting for transfers between devices  50 us (19%)
  other arithmetic  49.4 us (19%)
  local copies, waits for them, and re-layouts  18.6 us (7%)
  between operations  5.05 us (2%)
    ppermute x16, starting transfers between devices, passed_along(): return lax.ppermute(value, axis, pairs)  45.5 us
    all_to_all x5, starting transfers between devices, spread_out(): lax.all_to_all(value, ('row', 'col'), split_axis=0, concat_axis=0, tiled=...  34 us
    pallas_call x1, Pallas kernels, run_backward(): pl.pallas_call(backward_kernel, grid_spec=pltpu.PrefetchScalarGridSpec(nu...  30.9 us
    all_to_all x5, waiting for transfers between devices, spread_out(): lax.all_to_all(value, ('row', 'col'), split_axis=0, concat_axis=0, tiled=...  27.9 us
    pallas_call x1, Pallas kernels, run_forward(): pl.pallas_call(forward_kernel, grid_spec=pltpu.PrefetchScalarGridSpec(num...  22.6 us
    ppermute x16, waiting for transfers between devices, passed_along(): return lax.ppermute(value, axis, pairs)  22.1 us
    concatenate x1, other arithmetic, shards(): jnp.concatenate([jnp.concatenate([cos_table, sin_table], axis=1), jnp.con...  9.72 us
    reduce_max x4, other arithmetic, narrowed(): peak = jnp.maximum(jnp.max(jnp.abs(value)), 1e-30)  6.49 us
  transfers between devices with their start and end apart: 23, of which 5 were waited for; matrix products, arithmetic and copies ran while one was open for 22% of the time, Pallas kernels for 9%

profile of v1, /device:TPU:1, one launch (start us, length us, event | category | flops | bytes accessed | tf_op | source)
XLA Modules:
  0.0 262.7 jit_solution(6149210321990661840)
XLA Ops:
  0.6 2.1 collective-permute-start.2
  2.7 4.8 %collective-permute-start.3 = (f32[2,256,512]{2,1,0:T(8,128)}, f32[2,256,512]{2,1,0:T(8,128)S(1)}, u32[]{:S(2)}, u32[]{:S(2)}) collective-permute-start(f32[2,256,512]{2,1,0:T(8,128)} %param.8), channel_id=1, source_target_pairs={{0,120},{8,0},{16,8},{24,16},{32,24},{40,32},{48,40},{56,48},{64,5... | collective-permute-start | bytes 3145736 | tf_op jit(solution)/shard_map/ppermute | solution.py:20
  7.6 0.8 fusion.18
  8.4 0.1 copy.21
  8.5 0.1 copy.20
  8.6 0.3 collective-permute-start
  8.8 1.7 fusion.13
  10.5 1.9 collective-permute-start.8
  12.4 18.1 %collective-permute-done.2 = f32[2,256,512]{2,1,0:T(8,128)S(1)} collective-permute-done((f32[2,256,512]{2,1,0:T(8,128)}, f32[2,256,512]{2,1,0:T(8,128)S(1)}, u32[]{:S(2)}, u32[]{:S(2)}) %collective-permute-start.2) | collective-permute-done | bytes 1048608 | tf_op jit(solution)/shard_map/ppermute | solution.py:20
  30.6 0.1 constant_dynamic-update-slice_fusion
  30.7 1.5 fusion.14
  32.2 0.4 copy-done.7
  32.6 2.5 collective-permute-start.4
  35.0 1.1 fusion.17
  36.1 4.0 %fusion.10 = bf16[512,512]{1,0:T(8,128)(2,1)S(1)} fusion(), kind=kLoop, calls=%fused_computation.37 | loop fusion | flops 5242880 | bytes 524288 | tf_op jit(solution)/shard_map/neg | solution.py:365
  40.1 4.4 %multiply_convert_fusion.5 = (bf16[512,512]{1,0:T(8,128)(2,1)S(1)}, bf16[512,512]{1,0:T(8,128)(2,1)S(1)}) fusion(), kind=kLoop, calls=%fused_computation.32 | loop fusion | flops 4980736 | bytes 1048576 | tf_op jit(solution)/shard_map/convert_element_type | solution.py:40
  44.5 9.7 %fusion.1 = (bf16[1024,1024]{1,0:T(8,128)(2,1)}, bf16[1024,1024]{1,0:T(8,128)(2,1)S(1)}) fusion(bf16[512,512]{1,0:T(8,128)(2,1)S(1)} %get-tuple-element.35, bf16[512,512]{1,0:T(8,128)(2,1)S(1)} %fusion.10, bf16[512,512]{1,0:T(8,128)(2,1)S(1)} %get-tuple-element.34), kind=kLoop, calls=%fused_computation.7 | loop fusion | flops 14680064 | bytes 5767168 | tf_op jit(solution)/shard_map/concatenate | solution.py:370
  54.2 1.7 collective-permute-start.6
  56.1 1.5 pad_maximum_fusion.4
  57.6 6.4 %all-to-all-start = ((bf16[16,4,2,16,512]{4,3,2,1,0:T(8,128)(2,1)}), bf16[16,4,2,16,512]{4,3,2,1,0:T(8,128)(2,1)}, u32[]{:S(2)}, u32[]{:S(2)}) async-start(bf16[16,4,2,16,512]{4,3,2,1,0:T(8,128)(2,1)} %pad_maximum_fusion.4), calls=%async_computation | async-start | bytes 4194304 | tf_op jit(solution)/shard_map/all_to_all | solution.py:342
  64.0 1.4 fusion.15
  65.4 1.3 fusion.16
  66.8 4.2 %maximum_maximum_fusion.region = f32[2,768,1024]{2,1,0:T(8,128)} fusion(f32[2,256,256]{2,1,0:T(8,128)S(1)} %get-tuple-element.29, f32[2,256,512]{2,1,0:T(8,128)S(1)} %copy-done.8, f32[2,256,256]{2,1,0:T(8,128)S(1)} %get-tuple-element.27, f32[2,256,256]{2,1,0:T(8,128)} %collective-permute-done.7, f32[2,256,512]{2,1,0:T(8,128)S(1)} %copy-done.4, ...), kind=kLoop, calls=%fused_computation | loop fusion | flops 12582912 | bytes 12582912 | tf_op jit(solution)/shard_map/concatenate | solution.py:350
  71.0 22.6 %forward.1 = (f32[4,2,512,512]{3,2,1,0:T(8,128)}, f32[4,2,512,512]{3,2,1,0:T(8,128)}, f32[512,512]{1,0:T(8,128)S(1)}) custom-call(s32[4,2]{1,0:T(4,128)S(1)} %pad_add_fusion.offs, f32[2,768,1024]{2,1,0:T(8,128)} %maximum_maximum_fusion.region, f32[2,512,512]{2,1,0:T(8,128)S(1)} %copy-done.2, bf16[1024,1024]{1,0:T(8,128)(2,1)S(1)} %get-tuple-element.25.left, ...), custom_call_target="tpu_custom_call" | custom-call | flops 8589934592 | bytes 30000000 | tf_op jit(solution)/shard_map/forward/pallas_call | solution.py:252
  93.5 30.9 %backward.1 = (f32[2,768,1024]{2,1,0:T(8,128)}, f32[2,512,512]{2,1,0:T(8,128)}) custom-call(s32[4,2]{1,0:T(4,128)} %copy-done.1, s32[32]{0:T(128)} %order.1, f32[4,2,512,512]{3,2,1,0:T(8,128)} %get-tuple-element.7.far, f32[4,2,512,512]{3,2,1,0:T(8,128)} %get-tuple-element.8.patch, bf16[16,4,2,16,512]{4,3,2,1,0:T(8,128)(2,1)} %all-to-all-done.amp, ...), custom_call_target="tpu_custom_call" | custom-call | flops 8589934592 | bytes 30000000 | tf_op jit(solution)/shard_map/backward/pallas_call | solution.py:281
  124.4 2.4 abs_reduce_fusion
  127.4 0.7 broadcast_in_dim.6
  128.1 9.6 %all-to-all-start.2 = ((f32[128,1,128]{2,1,0:T(1,128)}), f32[128,1,128]{2,1,0:T(1,128)S(1)}, u32[]{:S(2)}, u32[]{:S(2)}) async-start(f32[128,1,128]{2,1,0:T(1,128)} %broadcast_in_dim.6), calls=%async_computation.2 | async-start | bytes 131072 | tf_op jit(solution)/shard_map/all_to_all | solution.py:317
  137.7 1.0 reshape.72
  138.8 8.5 %all-to-all-done.2 = f32[128,1,128]{2,1,0:T(1,128)S(1)} async-done(((f32[128,1,128]{2,1,0:T(1,128)}), f32[128,1,128]{2,1,0:T(1,128)S(1)}, u32[]{:S(2)}, u32[]{:S(2)}) %all-to-all-start.2) | async-done | bytes 65568 | tf_op jit(solution)/shard_map/all_to_all | solution.py:317
  147.3 4.4 %all-to-all-start.3 = ((f32[128,16,128]{2,1,0:T(8,128)}), f32[128,16,128]{2,1,0:T(8,128)S(1)}, u32[]{:S(2)}, u32[]{:S(2)}) async-start(f32[128,16,128]{2,1,0:T(8,128)} %reshape.72), calls=%async_computation.3 | async-start | bytes 2097152 | tf_op jit(solution)/shard_map/all_to_all | solution.py:317
  151.7 2.7 %abs_reduce_fusion.2 = (f32[]{:T(128)}, f32[]{:T(128)}) fusion(f32[2,768,1024]{2,1,0:T(8,128)} %get-tuple-element.9), kind=kLoop, calls=%fused_computation.19 | loop fusion | flops 1572862 | bytes 3145736 | tf_op jit(solution)/shard_map/reduce_max | solution.py:45
  155.7 3.6 %multiply_convert_fusion.2 = (f16[2,768,256]{2,1,0:T(8,128)(2,1)}, f16[2,768,256]{2,1,0:T(8,128)(2,1)}) fusion(f32[2,768,1024]{2,1,0:T(8,128)} %get-tuple-element.9, f32[]{:T(128)S(6)} %div.38, f32[]{:T(128)S(6)} %div.39), kind=kLoop, calls=%fused_computation.18 | loop fusion | flops 1572864 | bytes 4718600 | tf_op jit(solution)/shard_map/convert_element_type | solution.py:46
  159.4 1.6 collective-permute-start.9
  161.1 1.2 multiply_convert_fusion
  162.3 1.8 reshape.70
  164.1 1.2 copy.22
  165.3 7.0 %collective-permute-start.10 = (f32[1,1]{1,0:T(1,128)}, f32[1,1]{1,0:T(1,128)}, u32[]{:S(2)}, u32[]{:S(2)}) collective-permute-start(f32[1,1]{1,0:T(1,128)} %bitcast.3), channel_id=1, source_target_pairs={{0,1},{1,2},{2,3},{3,4},{4,5},{5,6},{6,7},{7,0},{8,9},{9,10},{10,1... | collective-permute-start | bytes 20 | tf_op jit(solution)/shard_map/ppermute | solution.py:20
  172.3 0.8 collective-permute-start.12
  173.1 1.0 slice_reduce_fusion.1
  174.2 10.0 %all-to-all-start.1 = ((f16[128,32,128]{2,1,0:T(8,128)(2,1)}), f16[128,32,128]{2,1,0:T(8,128)(2,1)}, u32[]{:S(2)}, u32[]{:S(2)}) async-start(f16[128,32,128]{2,1,0:T(8,128)(2,1)} %bitcast.12), calls=%async_computation.1 | async-start | bytes 2097152 | tf_op jit(solution)/shard_map/all_to_all | solution.py:317
  184.2 0.1 reduce_sum.21
  184.3 1.9 convert_multiply_fusion.2
  186.3 1.9 convert_multiply_fusion.1
  188.2 2.5 maximum_add_fusion
  190.6 11.9 %all-to-all-done.1 = f16[128,32,128]{2,1,0:T(8,128)(2,1)} async-done(((f16[128,32,128]{2,1,0:T(8,128)(2,1)}), f16[128,32,128]{2,1,0:T(8,128)(2,1)}, u32[]{:S(2)}, u32[]{:S(2)}) %all-to-all-start.1) | async-done | bytes 1048608 | tf_op jit(solution)/shard_map/all_to_all | solution.py:317
  202.6 1.5 multiply_reduce_fusion
  204.1 0.6 abs_reduce_fusion.5
  205.3 0.7 broadcast_in_dim.8
  206.0 4.7 %all-to-all-start.5 = ((f32[128,1,128]{2,1,0:T(1,128)}), f32[128,1,128]{2,1,0:T(1,128)S(1)}, u32[]{:S(2)}, u32[]{:S(2)}) async-start(f32[128,1,128]{2,1,0:T(1,128)} %broadcast_in_dim.8), calls=%async_computation.5 | async-start | bytes 131072 | tf_op jit(solution)/shard_map/all_to_all | solution.py:317
  210.7 0.8 abs_reduce_fusion.4
  213.0 7.5 %all-to-all-done.5 = f32[128,1,128]{2,1,0:T(1,128)S(1)} async-done(((f32[128,1,128]{2,1,0:T(1,128)}), f32[128,1,128]{2,1,0:T(1,128)S(1)}, u32[]{:S(2)}, u32[]{:S(2)}) %all-to-all-start.5) | async-done | bytes 65568 | tf_op jit(solution)/shard_map/all_to_all | solution.py:317
  220.4 1.1 broadcast_in_dim.7
  221.6 5.3 %all-to-all-start.4 = ((f16[128,32,128]{2,1,0:T(8,128)(2,1)}), f16[128,32,128]{2,1,0:T(8,128)(2,1)}, u32[]{:S(2)}, u32[]{:S(2)}) async-start(f16[128,32,128]{2,1,0:T(8,128)(2,1)} %broadcast_in_dim.7), calls=%async_computation.4 | async-start | bytes 2097152 | tf_op jit(solution)/shard_map/all_to_all | solution.py:317
  226.8 1.2 multiply_convert_fusion.4
  228.1 5.5 %collective-permute-start.13 = (f16[2,256,512]{2,1,0:T(8,128)(2,1)}, f16[2,256,512]{2,1,0:T(8,128)(2,1)}, u32[]{:S(2)}, u32[]{:S(2)}) collective-permute-start(f16[2,256,512]{2,1,0:T(8,128)(2,1)} %get-tuple-element.18), channel_id=1, source_target_pairs={{0,120},{8,0},{16,8},{24,16},{32,24},{40,32},{48,40},{56,48},{64,5... | collective-permute-start | bytes 1572872 | tf_op jit(solution)/shard_map/ppermute | solution.py:20
  233.6 16.7 %collective-permute-start.14 = (f32[1,1]{1,0:T(1,128)}, f32[1,1]{1,0:T(1,128)}, u32[]{:S(2)}, u32[]{:S(2)}) collective-permute-start(f32[1,1]{1,0:T(1,128)} %bitcast.7), channel_id=1, source_target_pairs={{0,120},{8,0},{16,8},{24,16},{32,24},{40,32},{48,40},{56,48},{64,5... | collective-permute-start | bytes 20 | tf_op jit(solution)/shard_map/ppermute | solution.py:20
  250.3 0.7 collective-permute-start.16
  251.0 1.0 slice_reduce_fusion
  252.0 3.9 %collective-permute-done.16 = f32[1,1]{1,0:T(1,128)} collective-permute-done((f32[1,1]{1,0:T(1,128)}, f32[1,1]{1,0:T(1,128)}, u32[]{:S(2)}, u32[]{:S(2)}) %collective-permute-start.16) | collective-permute-done | bytes 36 | tf_op jit(solution)/shard_map/ppermute | solution.py:20
  256.0 3.6 %fusion.6 = f32[2,256,512]{2,1,0:T(8,128)} fusion(f32[2,768,512]{2,1,0:T(8,128)S(1)} %maximum_add_fusion, f16[2,256,512]{2,1,0:T(8,128)(2,1)} %collective-permute-done.15, f16[2,256,512]{2,1,0:T(8,128)(2,1)} %collective-permute-done.13, f32[]{:T(128)} %bitcast.10, f32[]{:T(128)} %bitcast.8), kind=kLoop, calls=%fused_computation.27 | loop fusion | flops 1572864 | bytes 3145736 | tf_op jit(solution)/shard_map/add | solution.py:417
  259.6 1.4 fusion.2
  261.0 0.1 copy.23
  261.2 1.5 reshape.73
  (44 shorter events, 0.3 us)
Async XLA Ops:
  0.6 29.9 %collective-permute-start.2 = (f32[2,256,512]{2,1,0:T(8,128)}, f32[2,256,512]{2,1,0:T(8,128)S(1)}, u32[]{:S(2)}, u32[]{:S(2)}) collective-permute-start(f32[2,256,512]{2,1,0:T(8,128)} %param.8), channel_id=1, source_target_pairs={{0,8},{8,16},{16,24},{24,32},{32,40},{40,48},{48,56},{56,64},{64,7... | collective-permute-start | bytes 3145736 | tf_op jit(solution)/shard_map/ppermute | solution.py:20
  2.7 27.9 %collective-permute-start.3 = (f32[2,256,512]{2,1,0:T(8,128)}, f32[2,256,512]{2,1,0:T(8,128)S(1)}, u32[]{:S(2)}, u32[]{:S(2)}) collective-permute-start(f32[2,256,512]{2,1,0:T(8,128)} %param.8), channel_id=1, source_target_pairs={{0,120},{8,0},{16,8},{24,16},{32,24},{40,32},{48,40},{56,48},{64,5... | collective-permute-start | bytes 3145736 | tf_op jit(solution)/shard_map/ppermute | solution.py:20
  8.5 45.8 %collective-permute-start.1 = (s32[2,2]{1,0:T(2,128)S(1)}, s32[2,2]{1,0:T(2,128)S(1)}, u32[]{:S(2)}, u32[]{:S(2)}) collective-permute-start(s32[2,2]{1,0:T(2,128)S(1)} %bitcast.30), channel_id=1, source_target_pairs={{0,8},{8,16},{16,24},{24,32},{32,40},{40,48},{48,56},{56,64},{64,7... | collective-permute-start | bytes 56 | tf_op jit(solution)/shard_map/ppermute | solution.py:20
  8.6 47.4 %collective-permute-start = (s32[2,2]{1,0:T(2,128)S(1)}, s32[2,2]{1,0:T(2,128)S(1)}, u32[]{:S(2)}, u32[]{:S(2)}) collective-permute-start(s32[2,2]{1,0:T(2,128)S(1)} %bitcast.29), channel_id=1, source_target_pairs={{0,9},{1,10},{2,11},{3,12},{4,13},{5,14},{6,15},{7,8},{8,17},{9,18... | collective-permute-start | bytes 56 | tf_op jit(solution)/shard_map/ppermute | solution.py:30
  10.5 45.5 %collective-permute-start.8 = (bf16[16,2,2,16,512]{4,3,2,1,0:T(8,128)(2,1)S(1)}, bf16[16,2,2,16,512]{4,3,2,1,0:T(8,128)(2,1)S(1)}, u32[]{:S(2)}, u32[]{:S(2)}) collective-permute-start(bf16[16,2,2,16,512]{4,3,2,1,0:T(8,128)(2,1)S(1)} %get-tuple-element.20), channel_id=1, source_target_pairs={{0,1},{1,2},{2,3},{3,4},{4,5},{5,6},{6,7},{7,0},{8,9},{9,10},{10,1... | collective-permute-start | bytes 3145736 | tf_op jit(solution)/shard_map/ppermute | solution.py:20
  30.5 1.7 copy-start.5
  30.6 1.9 copy-start.7
  30.7 4.3 %copy-start.4 = (f32[2,256,512]{2,1,0:T(8,128)S(1)}, f32[2,256,512]{2,1,0:T(8,128)}, u32[]{:S(2)}) copy-start(f32[2,256,512]{2,1,0:T(8,128)} %param.8) | copy-start | bytes 3145732
  32.6 31.4 %collective-permute-start.4 = (f32[2,512,256]{2,1,0:T(8,128)}, f32[2,512,256]{2,1,0:T(8,128)}, u32[]{:S(2)}, u32[]{:S(2)}) collective-permute-start(f32[2,512,256]{2,1,0:T(8,128)} %get-tuple-element.22), channel_id=1, source_target_pairs={{0,1},{1,2},{2,3},{3,4},{4,5},{5,6},{6,7},{7,0},{8,9},{9,10},{10,1... | collective-permute-start | bytes 3145736 | tf_op jit(solution)/shard_map/ppermute | solution.py:20
  36.1 29.3 %collective-permute-start.5 = (f32[2,512,256]{2,1,0:T(8,128)}, f32[2,512,256]{2,1,0:T(8,128)}, u32[]{:S(2)}, u32[]{:S(2)}) collective-permute-start(f32[2,512,256]{2,1,0:T(8,128)} %get-tuple-element.23), channel_id=1, source_target_pairs={{0,7},{1,0},{2,1},{3,2},{4,3},{5,4},{6,5},{7,6},{8,15},{9,8},{10,9... | collective-permute-start | bytes 3145736 | tf_op jit(solution)/shard_map/ppermute | solution.py:20
  54.2 16.7 %copy-start = (bf16[1024,1024]{1,0:T(8,128)(2,1)}, bf16[1024,1024]{1,0:T(8,128)(2,1)S(1)}, u32[]{:S(2)}) copy-start(bf16[1024,1024]{1,0:T(8,128)(2,1)S(1)} %get-tuple-element.25.left) | copy-start | bytes 6291460
  54.2 12.5 %collective-permute-start.6 = (f32[2,256,256]{2,1,0:T(8,128)}, f32[2,256,256]{2,1,0:T(8,128)}, u32[]{:S(2)}, u32[]{:S(2)}) collective-permute-start(f32[2,256,256]{2,1,0:T(8,128)} %get-tuple-element.30), channel_id=1, source_target_pairs={{0,1},{1,2},{2,3},{3,4},{4,5},{5,6},{6,7},{7,0},{8,9},{9,10},{10,1... | collective-permute-start | bytes 1572872 | tf_op jit(solution)/shard_map/ppermute | solution.py:20
  56.0 10.7 %collective-permute-start.7 = (f32[2,256,256]{2,1,0:T(8,128)}, f32[2,256,256]{2,1,0:T(8,128)}, u32[]{:S(2)}, u32[]{:S(2)}) collective-permute-start(f32[2,256,256]{2,1,0:T(8,128)} %get-tuple-element.31), channel_id=1, source_target_pairs={{0,7},{1,0},{2,1},{3,2},{4,3},{5,4},{6,5},{7,6},{8,15},{9,8},{10,9... | collective-permute-start | bytes 1572872 | tf_op jit(solution)/shard_map/ppermute | solution.py:20
  56.0 14.9 %copy-start.1 = (s32[4,2]{1,0:T(4,128)}, s32[4,2]{1,0:T(4,128)S(1)}, u32[]{:S(2)}) copy-start(s32[4,2]{1,0:T(4,128)S(1)} %pad_add_fusion.offs) | copy-start | bytes 100
  57.6 36.0 %all-to-all-start = ((bf16[16,4,2,16,512]{4,3,2,1,0:T(8,128)(2,1)}), bf16[16,4,2,16,512]{4,3,2,1,0:T(8,128)(2,1)}, u32[]{:S(2)}, u32[]{:S(2)}) async-start(bf16[16,4,2,16,512]{4,3,2,1,0:T(8,128)(2,1)} %pad_maximum_fusion.4), calls=%async_computation | async-start | bytes 4194304 | tf_op jit(solution)/shard_map/all_to_all | solution.py:342
  63.9 2.8 %copy-start.6 = (f32[2,256,512]{2,1,0:T(8,128)S(1)}, f32[2,256,512]{2,1,0:T(8,128)}, u32[]{:S(2)}) copy-start(f32[2,256,512]{2,1,0:T(8,128)} %copy-done.5) | copy-start | bytes 3145732
  63.9 2.8 %copy-start.8 = (f32[2,256,512]{2,1,0:T(8,128)S(1)}, f32[2,256,512]{2,1,0:T(8,128)}, u32[]{:S(2)}) copy-start(f32[2,256,512]{2,1,0:T(8,128)} %copy-done.7) | copy-start | bytes 3145732
  66.7 4.2 %copy-start.2 = (f32[2,512,512]{2,1,0:T(8,128)S(1)}, f32[2,512,512]{2,1,0:T(8,128)}, u32[]{:S(2)}) copy-start(f32[2,512,512]{2,1,0:T(8,128)} %ill.3) | copy-start | bytes 6291460
  128.1 19.2 %all-to-all-start.2 = ((f32[128,1,128]{2,1,0:T(1,128)}), f32[128,1,128]{2,1,0:T(1,128)S(1)}, u32[]{:S(2)}, u32[]{:S(2)}) async-start(f32[128,1,128]{2,1,0:T(1,128)} %broadcast_in_dim.6), calls=%async_computation.2 | async-start | bytes 131072 | tf_op jit(solution)/shard_map/all_to_all | solution.py:317
  147.3 26.9 %all-to-all-start.3 = ((f32[128,16,128]{2,1,0:T(8,128)}), f32[128,16,128]{2,1,0:T(8,128)S(1)}, u32[]{:S(2)}, u32[]{:S(2)}) async-start(f32[128,16,128]{2,1,0:T(8,128)} %reshape.72), calls=%async_computation.3 | async-start | bytes 2097152 | tf_op jit(solution)/shard_map/all_to_all | solution.py:317
  155.7 5.4 %copy-start.3 = (f32[2,512,512]{2,1,0:T(8,128)S(1)}, f32[2,512,512]{2,1,0:T(8,128)}, u32[]{:S(2)}) copy-start(f32[2,512,512]{2,1,0:T(8,128)} %get-tuple-element.10) | copy-start | bytes 6291460
  159.4 25.0 %collective-permute-start.9 = (f16[2,768,256]{2,1,0:T(8,128)(2,1)}, f16[2,768,256]{2,1,0:T(8,128)(2,1)}, u32[]{:S(2)}, u32[]{:S(2)}) collective-permute-start(f16[2,768,256]{2,1,0:T(8,128)(2,1)} %get-tuple-element.16), channel_id=1, source_target_pairs={{0,1},{1,2},{2,3},{3,4},{4,5},{5,6},{6,7},{7,0},{8,9},{9,10},{10,1... | collective-permute-start | bytes 2359304 | tf_op jit(solution)/shard_map/ppermute | solution.py:20
  161.0 25.2 %collective-permute-start.11 = (f16[2,768,256]{2,1,0:T(8,128)(2,1)}, f16[2,768,256]{2,1,0:T(8,128)(2,1)}, u32[]{:S(2)}, u32[]{:S(2)}) collective-permute-start(f16[2,768,256]{2,1,0:T(8,128)(2,1)} %get-tuple-element.17), channel_id=1, source_target_pairs={{0,7},{1,0},{2,1},{3,2},{4,3},{5,4},{6,5},{7,6},{8,15},{9,8},{10,9... | collective-permute-start | bytes 2359304 | tf_op jit(solution)/shard_map/ppermute | solution.py:20
  165.3 19.0 %collective-permute-start.10 = (f32[1,1]{1,0:T(1,128)}, f32[1,1]{1,0:T(1,128)}, u32[]{:S(2)}, u32[]{:S(2)}) collective-permute-start(f32[1,1]{1,0:T(1,128)} %bitcast.3), channel_id=1, source_target_pairs={{0,1},{1,2},{2,3},{3,4},{4,5},{5,6},{6,7},{7,0},{8,9},{9,10},{10,1... | collective-permute-start | bytes 20 | tf_op jit(solution)/shard_map/ppermute | solution.py:20
  172.3 13.9 %collective-permute-start.12 = (f32[1,1]{1,0:T(1,128)}, f32[1,1]{1,0:T(1,128)}, u32[]{:S(2)}, u32[]{:S(2)}) collective-permute-start(f32[1,1]{1,0:T(1,128)} %bitcast.5), channel_id=1, source_target_pairs={{0,7},{1,0},{2,1},{3,2},{4,3},{5,4},{6,5},{7,6},{8,15},{9,8},{10,9... | collective-permute-start | bytes 20 | tf_op jit(solution)/shard_map/ppermute | solution.py:20
  174.2 28.4 %all-to-all-start.1 = ((f16[128,32,128]{2,1,0:T(8,128)(2,1)}), f16[128,32,128]{2,1,0:T(8,128)(2,1)}, u32[]{:S(2)}, u32[]{:S(2)}) async-start(f16[128,32,128]{2,1,0:T(8,128)(2,1)} %bitcast.12), calls=%async_computation.1 | async-start | bytes 2097152 | tf_op jit(solution)/shard_map/all_to_all | solution.py:317
  206.0 14.4 %all-to-all-start.5 = ((f32[128,1,128]{2,1,0:T(1,128)}), f32[128,1,128]{2,1,0:T(1,128)S(1)}, u32[]{:S(2)}, u32[]{:S(2)}) async-start(f32[128,1,128]{2,1,0:T(1,128)} %broadcast_in_dim.8), calls=%async_computation.5 | async-start | bytes 131072 | tf_op jit(solution)/shard_map/all_to_all | solution.py:317
  221.6 38.0 %all-to-all-start.4 = ((f16[128,32,128]{2,1,0:T(8,128)(2,1)}), f16[128,32,128]{2,1,0:T(8,128)(2,1)}, u32[]{:S(2)}, u32[]{:S(2)}) async-start(f16[128,32,128]{2,1,0:T(8,128)(2,1)} %broadcast_in_dim.7), calls=%async_computation.4 | async-start | bytes 2097152 | tf_op jit(solution)/shard_map/all_to_all | solution.py:317
  228.1 27.9 %collective-permute-start.13 = (f16[2,256,512]{2,1,0:T(8,128)(2,1)}, f16[2,256,512]{2,1,0:T(8,128)(2,1)}, u32[]{:S(2)}, u32[]{:S(2)}) collective-permute-start(f16[2,256,512]{2,1,0:T(8,128)(2,1)} %get-tuple-element.18), channel_id=1, source_target_pairs={{0,120},{8,0},{16,8},{24,16},{32,24},{40,32},{48,40},{56,48},{64,5... | collective-permute-start | bytes 1572872 | tf_op jit(solution)/shard_map/ppermute | solution.py:20
  233.6 22.4 %collective-permute-start.15 = (f16[2,256,512]{2,1,0:T(8,128)(2,1)}, f16[2,256,512]{2,1,0:T(8,128)(2,1)}, u32[]{:S(2)}, u32[]{:S(2)}) collective-permute-start(f16[2,256,512]{2,1,0:T(8,128)(2,1)} %get-tuple-element.19), channel_id=1, source_target_pairs={{0,8},{8,16},{16,24},{24,32},{32,40},{40,48},{48,56},{56,64},{64,7... | collective-permute-start | bytes 1572872 | tf_op jit(solution)/shard_map/ppermute | solution.py:20
  233.6 18.4 %collective-permute-start.14 = (f32[1,1]{1,0:T(1,128)}, f32[1,1]{1,0:T(1,128)}, u32[]{:S(2)}, u32[]{:S(2)}) collective-permute-start(f32[1,1]{1,0:T(1,128)} %bitcast.7), channel_id=1, source_target_pairs={{0,120},{8,0},{16,8},{24,16},{32,24},{40,32},{48,40},{56,48},{64,5... | collective-permute-start | bytes 20 | tf_op jit(solution)/shard_map/ppermute | solution.py:20
  250.3 5.7 %collective-permute-start.16 = (f32[1,1]{1,0:T(1,128)}, f32[1,1]{1,0:T(1,128)}, u32[]{:S(2)}, u32[]{:S(2)}) collective-permute-start(f32[1,1]{1,0:T(1,128)} %bitcast.9), channel_id=1, source_target_pairs={{0,8},{8,16},{16,24},{24,32},{32,40},{40,48},{48,56},{56,64},{64,7... | collective-permute-start | bytes 20 | tf_op jit(solution)/shard_map/ppermute | solution.py:20

commit v2 on v1

--- a/solution.py
+++ b/solution.py
@@ -1,4 +1,3 @@
-import functools
 import math
 
 import jax
@@ -8,10 +7,13 @@
 from jax.experimental.pallas import tpu as pltpu
 from jax.sharding import PartitionSpec as P
 
+
 LANES = 128
 SUBLANES = 8
 CHUNK = 32
 BLOCK = 256
+PIECE = 16
+HALF_TOP = 65504.0
 
 
 def passed_along(value, axis, steps):
@@ -41,14 +43,12 @@
     )
 
 
-def narrowed(value):
-    peak = jnp.maximum(jnp.max(jnp.abs(value)), 1e-30)
-    scaled = (value * (32768.0 / peak)).astype(jnp.float16)
-    return scaled, (peak * (1.0 / 32768.0)).reshape(1, 1)
-
-
-def widened(value, unit):
-    return value.astype(jnp.float32) * unit[0, 0]
+def narrowed(value, bound):
+    return (value * (HALF_TOP / bound)).astype(jnp.float16)
+
+
+def widened(value, bound):
+    return value.astype(jnp.float32) * (bound / HALF_TOP)
 
 
 def gather_rows(ref, plane, start, rows, col, shift):
@@ -60,7 +60,7 @@
     return jnp.where(sub < SUBLANES - shift, rolled[:-1], rolled[1:]).reshape(rows, LANES)
 
 
-def forward_kernel(offs, region, ill, left, right, far, patch, density, wave, half):
+def forward_kernel(offs, region, ill, left, right, far, patch, wave, half):
     slot = pl.program_id(0)
     size = ill.shape[-1]
     row = offs[slot, 0]
@@ -70,10 +70,6 @@
     row_base = row - row_shift
     lane = lax.broadcasted_iota(jnp.int32, (CHUNK, LANES), 1)
     blocks = size // LANES
-
-    @pl.when(slot == 0)
-    def _():
-        density[...] = jnp.zeros_like(density)
 
     def extract(step, carry):
         at = pl.multiple_of(step * CHUNK, CHUNK)
@@ -105,7 +101,6 @@
                 wave[pl.ds(size + at, CHUNK), to] = (
                     ill_real * spec_imag + ill_imag * spec_real
                 ).astype(jnp.bfloat16)
-                density[pl.ds(at, CHUNK), to] += spec_real * spec_real + spec_imag * spec_imag
             last = now
         return carry
 
@@ -126,7 +121,7 @@
 
 
 def backward_kernel(
-    offs, order, far, patch, amp, ill, left, right, accum, numer, corr, back, change, inverse
+    offs, order, far, patch, amp, ill, left, right, accum, sums, corr, back, change, inverse
 ):
     slot = pl.program_id(0)
     size = ill.shape[-1]
@@ -143,7 +138,7 @@
 
     @pl.when(slot == 0)
     def _():
-        numer[...] = jnp.zeros_like(numer)
+        sums[...] = jnp.zeros_like(sums)
 
         def clear(step, carry):
             at = pl.multiple_of(step * CHUNK, CHUNK)
@@ -206,8 +201,17 @@
                 spec_imag = patch[0, 1, rows, to]
                 ill_real = ill[0, rows, to]
                 ill_imag = ill[1, rows, to]
-                numer[0, rows, to] += spec_real * chg_real + spec_imag * chg_imag
-                numer[1, rows, to] += spec_real * chg_imag - spec_imag * chg_real
+                places = pl.ds(step * (CHUNK // PIECE), CHUNK // PIECE)
+                pieces = (CHUNK // PIECE, PIECE, LANES)
+                sums[block, places, 0] += (spec_real * chg_real + spec_imag * chg_imag).reshape(
+                    pieces
+                )
+                sums[block, places, 1] += (spec_real * chg_imag - spec_imag * chg_real).reshape(
+                    pieces
+                )
+                sums[block, places, 2] += (spec_real * spec_real + spec_imag * spec_imag).reshape(
+                    pieces
+                )
                 grads = (
                     ill_real * chg_real + ill_imag * chg_imag,
                     ill_real * chg_imag - ill_imag * chg_real,
@@ -258,14 +262,13 @@
             out_specs=[
                 one_slot((2, size, size)),
                 one_slot((2, size, size)),
-                whole((size, size)),
             ],
             scratch_shapes=[
                 pltpu.VMEM((2 * size, size), jnp.bfloat16),
                 pltpu.VMEM((size, 2 * size), jnp.bfloat16),
             ],
         ),
-        out_shape=[planes, planes, jax.ShapeDtypeStruct((size, size), jnp.float32)],
+        out_shape=[planes, planes],
         cost_estimate=pl.CostEstimate(
             flops=slots * 16 * size**3, bytes_accessed=30_000_000, transcendentals=0
         ),
@@ -278,6 +281,7 @@
     slots = offs.shape[0]
     size = ill.shape[-1]
     senders, _, per, height, _ = amp.shape
+    sums_shape = (size // LANES, size // PIECE, 3, PIECE, LANES)
     return pl.pallas_call(
         backward_kernel,
         grid_spec=pltpu.PrefetchScalarGridSpec(
@@ -293,7 +297,7 @@
                 once(left.shape),
                 once(right.shape),
             ],
-            out_specs=[whole(region_shape), whole((2, size, size))],
+            out_specs=[whole(region_shape), whole(sums_shape)],
             scratch_shapes=[
                 pltpu.VMEM((2 * size, size), jnp.bfloat16),
                 pltpu.VMEM((size, 2 * size), jnp.bfloat16),
@@ -303,7 +307,7 @@
         ),
         out_shape=[
             jax.ShapeDtypeStruct(region_shape, jnp.float32),
-            jax.ShapeDtypeStruct((2, size, size), jnp.float32),
+            jax.ShapeDtypeStruct(sums_shape, jnp.float32),
         ],
         cost_estimate=pl.CostEstimate(
             flops=slots * 16 * size**3, bytes_accessed=30_000_000, transcendentals=0
@@ -328,17 +332,57 @@
     late = slots // 2
     edge = tile_cols // 2
     grouped = measured.reshape(senders, slots, per, height, size)
-    moved = passed_along(grouped[:, late:], "col", 1)
     upper = passed_along(specimen, "row", 1)
     lower = passed_along(specimen, "row", -1)
+    moved = passed_along(grouped[:, late:], "col", 1)
     west = passed_along(specimen[:, :, edge:], "col", 1)
     east = passed_along(specimen[:, :, :edge], "col", -1)
     early_offs = passed_along(scan_offsets[0, 0, :late], "row", 1)
     late_offs = passed_both(scan_offsets[0, 0, late:], 1, 1)
     offs = jnp.concatenate([late_offs, early_offs], axis=0)
-    outer = jnp.concatenate([upper, lower], axis=1)
-    outer_west = passed_along(outer[:, :, edge:], "col", 1)
-    outer_east = passed_along(outer[:, :, :edge], "col", -1)
+    lane = lax.broadcasted_iota(jnp.int32, (devices, 1, LANES), 2)
+    peak = jnp.max(jnp.abs(specimen))
+    power = jnp.sum(specimen * specimen)
+    peaks = spread_out(jnp.where(lane < LANES // 2, peak, power))
+    peak = jnp.maximum(jnp.max(peaks[:, :, : LANES // 2]), 1e-12)
+    power = jnp.max(peaks[:, :, LANES // 2 :])
+    ill_power = jnp.sum(illumination * illumination)
+    ill_peak = jnp.maximum(jnp.max(jnp.abs(illumination)), 1e-8)
+    modulus = 1.5 * peak
+    energy = jnp.minimum(
+        modulus * jnp.sqrt(ill_power), 1.5 * ill_peak * jnp.sqrt(6.0 * power)
+    )
+    change_bound = 9.0 * jnp.maximum(energy, 1e-20)
+    grad_bound = 24.0 * ill_peak * change_bound
+    sum_bound = slots * modulus * change_bound
+    density_bound = slots * modulus * modulus
+    step_bound = math.sqrt(slots * devices) * change_bound
+    cos_table, sin_table = dft_tables(size)
+    left = jnp.concatenate(
+        [
+            jnp.concatenate([cos_table, -sin_table], axis=1),
+            jnp.concatenate([sin_table, cos_table], axis=1),
+        ],
+        axis=0,
+    )
+    right = jnp.concatenate(
+        [
+            jnp.concatenate([cos_table, sin_table], axis=1),
+            jnp.concatenate([-sin_table, cos_table], axis=1),
+        ],
+        axis=0,
+    )
+    bounds = (change_bound, grad_bound, sum_bound, density_bound, step_bound)
+    upper, lower, moved, west, east, offs, left, right, bounds = lax.optimization_barrier(
+        (upper, lower, moved, west, east, offs, left, right, bounds)
+    )
+    change_bound, grad_bound, sum_bound, density_bound, step_bound = bounds
+    outer_west = passed_along(
+        jnp.concatenate([upper[:, :, edge:], lower[:, :, edge:]], axis=1), "col", 1
+    )
+    outer_east = passed_along(
+        jnp.concatenate([upper[:, :, :edge], lower[:, :, :edge]], axis=1), "col", -1
+    )
     arrived = lax.all_to_all(
         jnp.concatenate([moved, grouped[:, :late]], axis=1),
         "row",
@@ -359,64 +403,39 @@
         ],
         axis=1,
     )
-    cos_table, sin_table = dft_tables(size)
-    left = jnp.concatenate(
-        [
-            jnp.concatenate([cos_table, -sin_table], axis=1),
-            jnp.concatenate([sin_table, cos_table], axis=1),
-        ],
-        axis=0,
-    )
-    right = jnp.concatenate(
-        [
-            jnp.concatenate([cos_table, sin_table], axis=1),
-            jnp.concatenate([-sin_table, cos_table], axis=1),
-        ],
-        axis=0,
-    )
-    far, patch, density = run_forward(offs, region, illumination, left, right)
-    share = (devices, size * size // devices // LANES, LANES)
-    density_parts = spread_out(density.reshape(share))
-    root = jnp.sqrt(jnp.sum(density_parts.reshape(share), axis=0) + 1e-06)
-    accum, numer = run_backward(
+    far, patch = run_forward(offs, region, illumination, left, right)
+    accum, sums = run_backward(
         offs, module_row, far, patch, arrived, illumination, left, right, region.shape
     )
-    small, numer_unit = narrowed(numer)
-    rows = share[1]
-    small = small.reshape(2, devices, rows, LANES).swapaxes(0, 1).reshape(devices, 2 * rows, LANES)
-    parts = spread_out(small)
-    units = spread_out(jnp.broadcast_to(numer_unit.reshape(1, 1, 1), (devices, 1, LANES)))
-    total = jnp.sum(
-        parts.astype(jnp.float32).reshape(devices, 2, rows, LANES) * units[:, None, :, :1], axis=0
-    )
-    mine, mine_unit = narrowed(total / root[None])
-    result = spread_out(jnp.broadcast_to(mine.reshape(1, 2 * rows, LANES), small.shape))
-    result_units = spread_out(
-        jnp.broadcast_to(mine_unit.reshape(1, 1, 1), (devices, 1, LANES))
-    )
-    result = (
-        result.reshape(devices, 2, rows, LANES).astype(jnp.float32) * result_units[:, :, None, :1][:, :1]
-    )
-    illumination_step = result.swapaxes(0, 1).reshape(2, size, size)
-    to_west, to_west_unit = narrowed(accum[:, :, :edge])
-    to_east, to_east_unit = narrowed(accum[:, :, edge + tile_cols :])
+    to_west = narrowed(accum[:, :, :edge], grad_bound)
+    to_east = narrowed(accum[:, :, edge + tile_cols :], grad_bound)
     from_east = passed_along(to_west, "col", -1)
     from_west = passed_along(to_east, "col", 1)
-    from_east_unit = passed_along(to_west_unit, "col", -1)
-    from_west_unit = passed_along(to_east_unit, "col", 1)
+    sums = sums.reshape(devices, 3 * PIECE, LANES)
+    line = lax.broadcasted_iota(jnp.int32, (1, 3 * PIECE, 1), 1)
+    bounds = jnp.where(line < 2 * PIECE, sum_bound, density_bound)
+    packed = narrowed(sums, bounds)
+    parts = spread_out(packed)
     column = accum[:, :, edge : edge + tile_cols] + jnp.concatenate(
-        [widened(from_west, from_west_unit), widened(from_east, from_east_unit)], axis=2
-    )
-    to_upper, to_upper_unit = narrowed(column[:, :tile_rows])
-    to_lower, to_lower_unit = narrowed(column[:, 2 * tile_rows :])
+        [widened(from_west, grad_bound), widened(from_east, grad_bound)], axis=2
+    )
+    to_upper = narrowed(column[:, :tile_rows], grad_bound)
+    to_lower = narrowed(column[:, 2 * tile_rows :], grad_bound)
     from_lower = passed_along(to_upper, "row", -1)
     from_upper = passed_along(to_lower, "row", 1)
-    from_lower_unit = passed_along(to_upper_unit, "row", -1)
-    from_upper_unit = passed_along(to_lower_unit, "row", 1)
+    total = jnp.sum(widened(parts, bounds), axis=0)
+    mine = total[: 2 * PIECE].reshape(2, PIECE, LANES) / jnp.sqrt(total[2 * PIECE :] + 1e-06)
+    mine = narrowed(mine, step_bound).reshape(1, 2 * PIECE, LANES)
+    copies = jnp.broadcast_to(mine, (devices, 2 * PIECE, LANES))
+    result = spread_out(copies)
+    result = widened(result, step_bound).reshape(
+        size // LANES, size // PIECE, 2, PIECE, LANES
+    )
+    illumination_step = result.transpose(2, 1, 3, 0, 4).reshape(2, size, size)
     specimen_step = (
         column[:, tile_rows : 2 * tile_rows]
-        + widened(from_lower, from_lower_unit)
-        + widened(from_upper, from_upper_unit)
+        + widened(from_lower, grad_bound)
+        + widened(from_upper, grad_bound)
     )
     return (specimen_step, illumination_step)
 

time: 265 us -> 226 us (0.85)
  starting transfers between devices: 86.1 us -> 55 us
  local copies, waits for them, and re-layouts: 18.6 us -> 15.6 us
    ppermute x16 -> x12, waiting for transfers between devices: 22.1 us -> 50.1 us  [passed_along(): return lax.ppermute(value, axis, pairs)]
    all_to_all x5 -> x3, waiting for transfers between devices: 27.9 us -> 0.01 us  [spread_out(): lax.all_to_all(value, ('row', 'col'), split_axis=0, concat_axis=0, tiled=...]
    ppermute x16 -> x12, starting transfers between devices: 45.5 us -> 18.3 us  [passed_along(): return lax.ppermute(value, axis, pairs)]
    all_to_all x5 -> x3, starting transfers between devices: 34 us -> 27 us  [spread_out(): lax.all_to_all(value, ('row', 'col'), split_axis=0, concat_axis=0, tiled=...]
    reshape x4 -> x1, local copies, waits for them, and re-layouts: 5.47 us -> 1.84 us  [shards(): illumination_step = result.transpose(2, 1, 3, 0, 4).reshape(2, size, size)]
    reduce_max x4 -> x2, other arithmetic: 6.49 us -> 3.02 us  [the longest x1 2.13 us: shards(): peak = jnp.max(jnp.abs(specimen))]
    slice x5 -> x4, local copies, waits for them, and re-layouts: 6.33 us -> 6.95 us  [the longest x1 3.26 us: shards(): grouped[:, :late]]
  transfers between devices with their start and end apart: 23 -> 17, of which waited for: 5 -> 5; matrix products, arithmetic and copies ran while one was open for 22% -> 22% of each run, Pallas kernels for 9% -> 10%
where the time goes in v2:
time: 226 us; the launch traced here: 225 us
  starting transfers between devices  55 us (24%)
  Pallas kernels  53.7 us (24%)
  waiting for transfers between devices  50.2 us (22%)
  other arithmetic  47.1 us (21%)
  local copies, waits for them, and re-layouts  15.6 us (7%)
  between operations  3.64 us (2%)
    ppermute x12, waiting for transfers between devices, passed_along(): return lax.ppermute(value, axis, pairs)  50.1 us
    pallas_call x1, Pallas kernels, run_backward(): pl.pallas_call(backward_kernel, grid_spec=pltpu.PrefetchScalarGridSpec(nu...  31.2 us
    all_to_all x3, starting transfers between devices, spread_out(): lax.all_to_all(value, ('row', 'col'), split_axis=0, concat_axis=0, tiled=...  27 us
    pallas_call x1, Pallas kernels, run_forward(): pl.pallas_call(forward_kernel, grid_spec=pltpu.PrefetchScalarGridSpec(num...  22.4 us
    ppermute x12, starting transfers between devices, passed_along(): return lax.ppermute(value, axis, pairs)  18.3 us
    concatenate x1, other arithmetic, shards(): jnp.concatenate([jnp.concatenate([cos_table, sin_table], axis=1), jnp.con...  10.1 us
    all_to_all x1, starting transfers between devices, shards(): lax.all_to_all(jnp.concatenate([moved, grouped[:, :late]], axis=1), 'row'...  7.12 us
    convert_element_type x4, other arithmetic, narrowed(): return (value * (HALF_TOP / bound)).astype(jnp.float16)  5.22 us
  transfers between devices with their start and end apart: 17, of which 5 were waited for; matrix products, arithmetic and copies ran while one was open for 22% of the time, Pallas kernels for 10%

profile of v2, /device:TPU:1, one launch (start us, length us, event | category | flops | bytes accessed | tf_op | source)
XLA Modules:
  0.0 225.2 jit_solution(18131060753517942361)
XLA Ops:
  0.6 0.0 copy-start
  0.6 2.1 collective-permute-start
  2.7 4.8 %collective-permute-start.1 = (f32[2,256,512]{2,1,0:T(8,128)}, f32[2,256,512]{2,1,0:T(8,128)}, u32[]{:S(2)}, u32[]{:S(2)}) collective-permute-start(f32[2,256,512]{2,1,0:T(8,128)} %param.8), channel_id=1, source_target_pairs={{0,120},{8,0},{16,8},{24,16},{32,24},{40,32},{48,40},{56,48},{64,5... | collective-permute-start | bytes 3145736 | tf_op jit(solution)/shard_map/ppermute | solution.py:22
  7.6 2.1 abs_reduce_fusion.1
  9.7 1.3 compare_select_fusion.1
  11.0 0.7 iota.21
  11.7 6.7 %all-to-all-start = ((f32[128,1,128]{2,1,0:T(1,128)}), f32[128,1,128]{2,1,0:T(1,128)S(1)}, u32[]{:S(2)}, u32[]{:S(2)}) async-start(f32[128,1,128]{2,1,0:T(1,128)} %iota.21), calls=%async_computation | async-start | bytes 131072 | tf_op jit(solution)/shard_map/all_to_all | solution.py:321
  18.3 0.8 fusion.23
  19.2 0.1 copy.17
  19.3 2.5 %collective-permute-start.5 = (s32[2,2]{1,0:T(2,128)S(1)}, s32[2,2]{1,0:T(2,128)S(1)}, u32[]{:S(2)}, u32[]{:S(2)}) collective-permute-start(s32[2,2]{1,0:T(2,128)S(1)} %bitcast.13), channel_id=1, source_target_pairs={{0,9},{1,10},{2,11},{3,12},{4,13},{5,14},{6,15},{7,8},{8,17},{9,18... | collective-permute-start | bytes 56 | tf_op jit(solution)/shard_map/ppermute | solution.py:32
  21.8 0.1 copy.18
  21.9 1.2 collective-permute-start.6
  23.1 3.3 %fusion.17 = (bf16[16,2,2,16,512]{4,3,2,1,0:T(8,128)(2,1)}, bf16[16,2,2,16,512]{4,3,2,1,0:T(8,128)(2,1)}) fusion(bf16[16,4,2,16,512]{4,3,2,1,0:T(8,128)(2,1)} %bitcast.11), kind=kLoop, calls=%fused_computation.52 | loop fusion | bytes 4194304 | tf_op jit(solution)/shard_map/slice | solution.py:387
  26.3 0.6 collective-permute-start.2
  26.9 1.2 multiply_reduce_fusion.1
  29.4 4.0 %fusion.11 = bf16[512,512]{1,0:T(8,128)(2,1)S(1)} fusion(), kind=kLoop, calls=%fused_computation.39 | loop fusion | flops 5242880 | bytes 524288 | tf_op jit(solution)/shard_map/neg | solution.py:363
  33.4 4.4 %multiply_convert_fusion.3 = (bf16[512,512]{1,0:T(8,128)(2,1)S(1)}, bf16[512,512]{1,0:T(8,128)(2,1)S(1)}) fusion(), kind=kLoop, calls=%fused_computation.34 | loop fusion | flops 4980736 | bytes 1048576 | tf_op jit(solution)/shard_map/convert_element_type | solution.py:42
  37.8 1.1 fusion.22
  38.8 0.0 collective-permute-done.5
  38.8 1.0 collective-permute-start.3
  39.9 0.0 collective-permute-done.6
  39.9 0.0 collective-permute-start.4
  39.9 10.1 %fusion.1 = (bf16[1024,1024]{1,0:T(8,128)(2,1)}, bf16[1024,1024]{1,0:T(8,128)(2,1)}) fusion(bf16[512,512]{1,0:T(8,128)(2,1)S(1)} %get-tuple-element.61, bf16[512,512]{1,0:T(8,128)(2,1)S(1)} %fusion.11, bf16[512,512]{1,0:T(8,128)(2,1)S(1)} %get-tuple-element.60), kind=kLoop, calls=%fused_computation.9 | loop fusion | flops 14680064 | bytes 5767168 | tf_op jit(solution)/shard_map/concatenate | solution.py:368
  50.0 0.9 slice_reduce_fusion
  52.2 0.0 collective-permute-done.2
  52.2 1.3 fusion.20
  53.5 1.4 fusion.21
  54.9 1.1 pad_maximum_fusion.5
  56.0 1.6 collective-permute-start.7
  57.6 1.0 pad_maximum_fusion.6
  58.6 0.1 collective-permute-start.8
  58.8 2.8 %pad_maximum_fusion.4 = bf16[16,4,2,16,512]{4,3,2,1,0:T(8,128)(2,1)} fusion(bf16[16,2,2,16,512]{4,3,2,1,0:T(8,128)(2,1)S(1)} %copy-done.4, bf16[16,2,2,16,512]{4,3,2,1,0:T(8,128)(2,1)} %collective-permute-done.2), kind=kLoop, calls=%fused_computation.10 | loop fusion | flops 1048576 | bytes 4194304 | tf_op jit(solution)/shard_map/concatenate | solution.py:387
  61.6 7.1 %all-to-all-start.1 = ((bf16[16,4,2,16,512]{4,3,2,1,0:T(8,128)(2,1)}), bf16[16,4,2,16,512]{4,3,2,1,0:T(8,128)(2,1)}, u32[]{:S(2)}, u32[]{:S(2)}) async-start(bf16[16,4,2,16,512]{4,3,2,1,0:T(8,128)(2,1)} %pad_maximum_fusion.4), calls=%async_computation.1 | async-start | bytes 4194304 | tf_op jit(solution)/shard_map/all_to_all | solution.py:386
  68.7 0.9 collective-permute-done.7
  69.7 1.3 fusion.18
  70.9 2.2 collective-permute-done.8
  73.2 1.3 fusion.19
  74.5 4.6 %maximum_maximum_fusion.region = f32[2,768,1024]{2,1,0:T(8,128)} fusion(f32[2,256,256]{2,1,0:T(8,128)S(1)} %get-tuple-element.51, f32[2,256,512]{2,1,0:T(8,128)} %collective-permute-done.1, f32[2,256,256]{2,1,0:T(8,128)S(1)} %get-tuple-element.49, f32[2,256,256]{2,1,0:T(8,128)} %collective-permute-done.4, f32[2,256,512]{2,1,0:T(8,128)S(1)} %copy-done.3, ...), kind=kLoop, calls=%fused_computation | loop fusion | flops 12582912 | bytes 12582912 | tf_op jit(solution)/shard_map/concatenate | solution.py:394
  79.1 22.4 %forward.1 = (f32[4,2,512,512]{3,2,1,0:T(8,128)}, f32[4,2,512,512]{3,2,1,0:T(8,128)}) custom-call(s32[4,2]{1,0:T(4,128)S(1)} %pad_add_fusion.offs, f32[2,768,1024]{2,1,0:T(8,128)} %maximum_maximum_fusion.region, f32[2,512,512]{2,1,0:T(8,128)S(1)} %copy-done, bf16[1024,1024]{1,0:T(8,128)(2,1)S(1)} %copy-done.1, bf16[1024,1024]{1,0:T(8,128)(2,1)} %get-tuple-element.24.right), custom_call_target="tpu_custom_call" | custom-call | flops 8589934592 | bytes 30000000 | tf_op jit(solution)/shard_map/forward/pallas_call | solution.py:256
  101.5 0.0 all-to-all-done.1.amp
  101.5 31.2 %backward.1 = (f32[2,768,1024]{2,1,0:T(8,128)}, f32[4,32,3,16,128]{4,3,2,1,0:T(8,128)}) custom-call(s32[4,2]{1,0:T(4,128)} %copy-done.2, s32[32]{0:T(128)} %order.1, f32[4,2,512,512]{3,2,1,0:T(8,128)} %get-tuple-element.25.far, f32[4,2,512,512]{3,2,1,0:T(8,128)} %get-tuple-element.26.patch, bf16[16,4,2,16,512]{4,3,2,1,0:T(8,128)(2,1)} %all-to-all-done.1.amp, ...), custom_call_target="tpu_custom_call" | custom-call | flops 8589934592 | bytes 30000000 | tf_op jit(solution)/shard_map/backward/pallas_call | solution.py:285
  132.7 2.5 %multiply_convert_fusion.2 = (f16[2,768,256]{2,1,0:T(8,128)(2,1)S(1)}, f16[2,768,256]{2,1,0:T(8,128)(2,1)S(1)}) fusion(f32[2,768,1024]{2,1,0:T(8,128)} %get-tuple-element.28, f32[]{:T(128)S(6)} %div.41), kind=kLoop, calls=%fused_computation.17 | loop fusion | flops 1572864 | bytes 4718596 | tf_op jit(solution)/shard_map/convert_element_type | solution.py:47
  135.2 0.3 collective-permute-start.9
  135.5 0.1 copy-done.5
  135.6 1.5 multiply_convert_fusion
  137.1 10.8 %all-to-all-start.2 = ((f16[128,48,128]{2,1,0:T(8,128)(2,1)}), f16[128,48,128]{2,1,0:T(8,128)(2,1)}, u32[]{:S(2)}, u32[]{:S(2)}) async-start(f16[128,48,128]{2,1,0:T(8,128)(2,1)} %multiply_convert_fusion), calls=%async_computation.2 | async-start | bytes 3145728 | tf_op jit(solution)/shard_map/all_to_all | solution.py:321
  147.9 1.1 collective-permute-start.10
  149.2 0.0 collective-permute-done.9
  149.2 0.1 convert_multiply_fusion.2
  149.3 25.2 %collective-permute-done.10 = f16[2,768,256]{2,1,0:T(8,128)(2,1)S(1)} collective-permute-done((f16[2,768,256]{2,1,0:T(8,128)(2,1)S(1)}, f16[2,768,256]{2,1,0:T(8,128)(2,1)S(1)}, u32[]{:S(2)}, u32[]{:S(2)}) %collective-permute-start.10) | collective-permute-done | bytes 786464 | tf_op jit(solution)/shard_map/ppermute | solution.py:22
  174.5 0.1 convert_multiply_fusion.1
  174.6 2.5 %maximum_add_fusion = f32[2,768,512]{2,1,0:T(8,128)S(1)} fusion(f32[2,768,256]{2,1,0:T(8,128)S(1)} %convert_multiply_fusion.1, f32[2,768,256]{2,1,0:T(8,128)S(1)} %convert_multiply_fusion.2, f32[2,768,1024]{2,1,0:T(8,128)} %get-tuple-element.28), kind=kLoop, calls=%fused_computation.1 | loop fusion | flops 1572864 | bytes 9437184 | tf_op jit(solution)/shard_map/add | solution.py:419
  177.0 0.0 all-to-all-done.2
  177.1 1.9 multiply_reduce_fusion
  179.0 1.1 broadcast_in_dim.28
  180.1 9.5 %all-to-all-start.3 = ((f16[128,32,128]{2,1,0:T(8,128)(2,1)}), f16[128,32,128]{2,1,0:T(8,128)(2,1)}, u32[]{:S(2)}, u32[]{:S(2)}) async-start(f16[128,32,128]{2,1,0:T(8,128)(2,1)} %broadcast_in_dim.28), calls=%async_computation.3 | async-start | bytes 2097152 | tf_op jit(solution)/shard_map/all_to_all | solution.py:321
  189.7 1.2 fusion.6
  190.9 5.4 %collective-permute-start.11 = (f16[2,256,512]{2,1,0:T(8,128)(2,1)}, f16[2,256,512]{2,1,0:T(8,128)(2,1)}, u32[]{:S(2)}, u32[]{:S(2)}) collective-permute-start(f16[2,256,512]{2,1,0:T(8,128)(2,1)} %get-tuple-element.42), channel_id=1, source_target_pairs={{0,120},{8,0},{16,8},{24,16},{32,24},{40,32},{48,40},{56,48},{64,5... | collective-permute-start | bytes 1572872 | tf_op jit(solution)/shard_map/ppermute | solution.py:22
  196.3 16.8 %collective-permute-done.11 = f16[2,256,512]{2,1,0:T(8,128)(2,1)} collective-permute-done((f16[2,256,512]{2,1,0:T(8,128)(2,1)}, f16[2,256,512]{2,1,0:T(8,128)(2,1)}, u32[]{:S(2)}, u32[]{:S(2)}) %collective-permute-start.11) | collective-permute-done | bytes 524320 | tf_op jit(solution)/shard_map/ppermute | solution.py:22
  213.1 5.0 %collective-permute-done.12 = f16[2,256,512]{2,1,0:T(8,128)(2,1)} collective-permute-done((f16[2,256,512]{2,1,0:T(8,128)(2,1)}, f16[2,256,512]{2,1,0:T(8,128)(2,1)}, u32[]{:S(2)}, u32[]{:S(2)}) %collective-permute-start.12) | collective-permute-done | bytes 524320 | tf_op jit(solution)/shard_map/ppermute | solution.py:22
  218.1 2.4 %fusion.7 = f32[2,256,512]{2,1,0:T(8,128)} fusion(f32[2,768,512]{2,1,0:T(8,128)S(1)} %maximum_add_fusion, f16[2,256,512]{2,1,0:T(8,128)(2,1)} %collective-permute-done.12, f16[2,256,512]{2,1,0:T(8,128)(2,1)} %collective-permute-done.11, f32[]{:T(128)S(6)} %div.42), kind=kLoop, calls=%fused_computation.29 | loop fusion | flops 1572864 | bytes 3145732 | tf_op jit(solution)/shard_map/add | solution.py:436
  220.5 1.5 convert_multiply_fusion
  222.0 1.4 copy.21
  223.4 1.8 reshape.48
  (22 shorter events, 0.1 us)
Async XLA Ops:
  0.6 26.3 %copy-start = (f32[2,512,512]{2,1,0:T(8,128)S(1)}, f32[2,512,512]{2,1,0:T(8,128)}, u32[]{:S(2)}) copy-start(f32[2,512,512]{2,1,0:T(8,128)} %ill.3) | copy-start | bytes 6291460
  0.6 51.6 %collective-permute-start = (f32[2,256,512]{2,1,0:T(8,128)}, f32[2,256,512]{2,1,0:T(8,128)}, u32[]{:S(2)}, u32[]{:S(2)}) collective-permute-start(f32[2,256,512]{2,1,0:T(8,128)} %param.8), channel_id=1, source_target_pairs={{0,8},{8,16},{16,24},{24,32},{32,40},{40,48},{48,56},{56,64},{64,7... | collective-permute-start | bytes 3145736 | tf_op jit(solution)/shard_map/ppermute | solution.py:22
  2.7 49.5 %collective-permute-start.1 = (f32[2,256,512]{2,1,0:T(8,128)}, f32[2,256,512]{2,1,0:T(8,128)}, u32[]{:S(2)}, u32[]{:S(2)}) collective-permute-start(f32[2,256,512]{2,1,0:T(8,128)} %param.8), channel_id=1, source_target_pairs={{0,120},{8,0},{16,8},{24,16},{32,24},{40,32},{48,40},{56,48},{64,5... | collective-permute-start | bytes 3145736 | tf_op jit(solution)/shard_map/ppermute | solution.py:22
  11.7 38.3 %all-to-all-start = ((f32[128,1,128]{2,1,0:T(1,128)}), f32[128,1,128]{2,1,0:T(1,128)S(1)}, u32[]{:S(2)}, u32[]{:S(2)}) async-start(f32[128,1,128]{2,1,0:T(1,128)} %iota.21), calls=%async_computation | async-start | bytes 131072 | tf_op jit(solution)/shard_map/all_to_all | solution.py:321
  19.3 19.6 %collective-permute-start.5 = (s32[2,2]{1,0:T(2,128)S(1)}, s32[2,2]{1,0:T(2,128)S(1)}, u32[]{:S(2)}, u32[]{:S(2)}) collective-permute-start(s32[2,2]{1,0:T(2,128)S(1)} %bitcast.13), channel_id=1, source_target_pairs={{0,9},{1,10},{2,11},{3,12},{4,13},{5,14},{6,15},{7,8},{8,17},{9,18... | collective-permute-start | bytes 56 | tf_op jit(solution)/shard_map/ppermute | solution.py:32
  21.9 18.0 %collective-permute-start.6 = (s32[2,2]{1,0:T(2,128)S(1)}, s32[2,2]{1,0:T(2,128)S(1)}, u32[]{:S(2)}, u32[]{:S(2)}) collective-permute-start(s32[2,2]{1,0:T(2,128)S(1)} %bitcast.12), channel_id=1, source_target_pairs={{0,8},{8,16},{16,24},{24,32},{32,40},{40,48},{48,56},{56,64},{64,7... | collective-permute-start | bytes 56 | tf_op jit(solution)/shard_map/ppermute | solution.py:22
  23.1 14.7 %copy-start.3 = (f32[2,256,512]{2,1,0:T(8,128)S(1)}, f32[2,256,512]{2,1,0:T(8,128)}, u32[]{:S(2)}) copy-start(f32[2,256,512]{2,1,0:T(8,128)} %param.8) | copy-start | bytes 3145732
  26.3 25.9 %collective-permute-start.2 = (bf16[16,2,2,16,512]{4,3,2,1,0:T(8,128)(2,1)}, bf16[16,2,2,16,512]{4,3,2,1,0:T(8,128)(2,1)}, u32[]{:S(2)}, u32[]{:S(2)}) collective-permute-start(bf16[16,2,2,16,512]{4,3,2,1,0:T(8,128)(2,1)} %get-tuple-element.45), channel_id=1, source_target_pairs={{0,1},{1,2},{2,3},{3,4},{4,5},{5,6},{6,7},{7,0},{8,9},{9,10},{10,1... | collective-permute-start | bytes 3145736 | tf_op jit(solution)/shard_map/ppermute | solution.py:22
  38.8 13.3 %collective-permute-start.3 = (f32[2,256,256]{2,1,0:T(8,128)}, f32[2,256,256]{2,1,0:T(8,128)}, u32[]{:S(2)}, u32[]{:S(2)}) collective-permute-start(f32[2,256,256]{2,1,0:T(8,128)} %get-tuple-element.57), channel_id=1, source_target_pairs={{0,1},{1,2},{2,3},{3,4},{4,5},{5,6},{6,7},{7,0},{8,9},{9,10},{10,1... | collective-permute-start | bytes 1572872 | tf_op jit(solution)/shard_map/ppermute | solution.py:22
  39.9 12.3 %collective-permute-start.4 = (f32[2,256,256]{2,1,0:T(8,128)}, f32[2,256,256]{2,1,0:T(8,128)}, u32[]{:S(2)}, u32[]{:S(2)}) collective-permute-start(f32[2,256,256]{2,1,0:T(8,128)} %get-tuple-element.56), channel_id=1, source_target_pairs={{0,7},{1,0},{2,1},{3,2},{4,3},{5,4},{6,5},{7,6},{8,15},{9,8},{10,9... | collective-permute-start | bytes 1572872 | tf_op jit(solution)/shard_map/ppermute | solution.py:22
  50.0 29.1 %copy-start.2 = (s32[4,2]{1,0:T(4,128)}, s32[4,2]{1,0:T(4,128)S(1)}, u32[]{:S(2)}) copy-start(s32[4,2]{1,0:T(4,128)S(1)} %pad_add_fusion.offs) | copy-start | bytes 100
  53.5 5.3 %copy-start.4 = (bf16[16,2,2,16,512]{4,3,2,1,0:T(8,128)(2,1)S(1)}, bf16[16,2,2,16,512]{4,3,2,1,0:T(8,128)(2,1)}, u32[]{:S(2)}) copy-start(bf16[16,2,2,16,512]{4,3,2,1,0:T(8,128)(2,1)} %get-tuple-element.44) | copy-start | bytes 3145732
  56.0 13.7 %collective-permute-start.7 = (f32[2,512,256]{2,1,0:T(8,128)}, f32[2,512,256]{2,1,0:T(8,128)}, u32[]{:S(2)}, u32[]{:S(2)}) collective-permute-start(f32[2,512,256]{2,1,0:T(8,128)} %pad_maximum_fusion.5), channel_id=1, source_target_pairs={{0,1},{1,2},{2,3},{3,4},{4,5},{5,6},{6,7},{7,0},{8,9},{9,10},{10,1... | collective-permute-start | bytes 3145736 | tf_op jit(solution)/shard_map/ppermute | solution.py:22
  58.6 14.5 %collective-permute-start.8 = (f32[2,512,256]{2,1,0:T(8,128)}, f32[2,512,256]{2,1,0:T(8,128)}, u32[]{:S(2)}, u32[]{:S(2)}) collective-permute-start(f32[2,512,256]{2,1,0:T(8,128)} %pad_maximum_fusion.6), channel_id=1, source_target_pairs={{0,7},{1,0},{2,1},{3,2},{4,3},{5,4},{6,5},{7,6},{8,15},{9,8},{10,9... | collective-permute-start | bytes 3145736 | tf_op jit(solution)/shard_map/ppermute | solution.py:22
  61.6 39.9 %all-to-all-start.1 = ((bf16[16,4,2,16,512]{4,3,2,1,0:T(8,128)(2,1)}), bf16[16,4,2,16,512]{4,3,2,1,0:T(8,128)(2,1)}, u32[]{:S(2)}, u32[]{:S(2)}) async-start(bf16[16,4,2,16,512]{4,3,2,1,0:T(8,128)(2,1)} %pad_maximum_fusion.4), calls=%async_computation.1 | async-start | bytes 4194304 | tf_op jit(solution)/shard_map/all_to_all | solution.py:386
  74.5 4.6 %copy-start.1 = (bf16[1024,1024]{1,0:T(8,128)(2,1)S(1)}, bf16[1024,1024]{1,0:T(8,128)(2,1)}, u32[]{:S(2)}) copy-start(bf16[1024,1024]{1,0:T(8,128)(2,1)} %get-tuple-element.23.left) | copy-start | bytes 6291460
  132.7 2.9 %copy-start.5 = (f32[4,32,3,16,128]{4,3,2,1,0:T(8,128)S(1)}, f32[4,32,3,16,128]{4,3,2,1,0:T(8,128)}, u32[]{:S(2)}) copy-start(f32[4,32,3,16,128]{4,3,2,1,0:T(8,128)} %get-tuple-element.30) | copy-start | bytes 9437188
  135.2 14.0 %collective-permute-start.9 = (f16[2,768,256]{2,1,0:T(8,128)(2,1)S(1)}, f16[2,768,256]{2,1,0:T(8,128)(2,1)S(1)}, u32[]{:S(2)}, u32[]{:S(2)}) collective-permute-start(f16[2,768,256]{2,1,0:T(8,128)(2,1)S(1)} %get-tuple-element.40), channel_id=1, source_target_pairs={{0,1},{1,2},{2,3},{3,4},{4,5},{5,6},{6,7},{7,0},{8,9},{9,10},{10,1... | collective-permute-start | bytes 2359304 | tf_op jit(solution)/shard_map/ppermute | solution.py:22
  137.1 39.9 %all-to-all-start.2 = ((f16[128,48,128]{2,1,0:T(8,128)(2,1)}), f16[128,48,128]{2,1,0:T(8,128)(2,1)}, u32[]{:S(2)}, u32[]{:S(2)}) async-start(f16[128,48,128]{2,1,0:T(8,128)(2,1)} %multiply_convert_fusion), calls=%async_computation.2 | async-start | bytes 3145728 | tf_op jit(solution)/shard_map/all_to_all | solution.py:321
  147.9 26.5 %collective-permute-start.10 = (f16[2,768,256]{2,1,0:T(8,128)(2,1)S(1)}, f16[2,768,256]{2,1,0:T(8,128)(2,1)S(1)}, u32[]{:S(2)}, u32[]{:S(2)}) collective-permute-start(f16[2,768,256]{2,1,0:T(8,128)(2,1)S(1)} %get-tuple-element.41), channel_id=1, source_target_pairs={{0,7},{1,0},{2,1},{3,2},{4,3},{5,4},{6,5},{7,6},{8,15},{9,8},{10,9... | collective-permute-start | bytes 2359304 | tf_op jit(solution)/shard_map/ppermute | solution.py:22
  180.1 40.4 %all-to-all-start.3 = ((f16[128,32,128]{2,1,0:T(8,128)(2,1)}), f16[128,32,128]{2,1,0:T(8,128)(2,1)}, u32[]{:S(2)}, u32[]{:S(2)}) async-start(f16[128,32,128]{2,1,0:T(8,128)(2,1)} %broadcast_in_dim.28), calls=%async_computation.3 | async-start | bytes 2097152 | tf_op jit(solution)/shard_map/all_to_all | solution.py:321
  190.9 22.2 %collective-permute-start.11 = (f16[2,256,512]{2,1,0:T(8,128)(2,1)}, f16[2,256,512]{2,1,0:T(8,128)(2,1)}, u32[]{:S(2)}, u32[]{:S(2)}) collective-permute-start(f16[2,256,512]{2,1,0:T(8,128)(2,1)} %get-tuple-element.42), channel_id=1, source_target_pairs={{0,120},{8,0},{16,8},{24,16},{32,24},{40,32},{48,40},{56,48},{64,5... | collective-permute-start | bytes 1572872 | tf_op jit(solution)/shard_map/ppermute | solution.py:22
  196.3 21.8 %collective-permute-start.12 = (f16[2,256,512]{2,1,0:T(8,128)(2,1)}, f16[2,256,512]{2,1,0:T(8,128)(2,1)}, u32[]{:S(2)}, u32[]{:S(2)}) collective-permute-start(f16[2,256,512]{2,1,0:T(8,128)(2,1)} %get-tuple-element.43), channel_id=1, source_target_pairs={{0,8},{8,16},{16,24},{24,32},{32,40},{40,48},{48,56},{56,64},{64,7... | collective-permute-start | bytes 1572872 | tf_op jit(solution)/shard_map/ppermute | solution.py:22

commit v3 on v2

--- a/solution.py
+++ b/solution.py
@@ -2,6 +2,7 @@
 
 import jax
 import jax.numpy as jnp
+import numpy as np
 from jax import lax
 from jax.experimental import pallas as pl
 from jax.experimental.pallas import tpu as pltpu
@@ -33,14 +34,13 @@
 
 
 def dft_tables(size):
-    index = jnp.arange(size, dtype=jnp.int32)
+    index = np.arange(size, dtype=np.int64)
     wrapped = index[:, None] * index[None, :] % size
-    angle = wrapped.astype(jnp.float32) * (2.0 * math.pi / size)
-    norm = 1.0 / math.sqrt(size)
-    return (
-        (jnp.cos(angle) * norm).astype(jnp.bfloat16),
-        (-jnp.sin(angle) * norm).astype(jnp.bfloat16),
-    )
+    angle = wrapped.astype(np.float32) * np.float32(2.0 * math.pi / size)
+    norm = np.float32(1.0 / math.sqrt(size))
+    cos_table = np.cos(angle.astype(np.float64)).astype(np.float32) * norm
+    sin_table = -np.sin(angle.astype(np.float64)).astype(np.float32) * norm
+    return jnp.asarray(cos_table, jnp.bfloat16), jnp.asarray(sin_table, jnp.bfloat16)
 
 
 def narrowed(value, bound):
@@ -60,7 +60,42 @@
     return jnp.where(sub < SUBLANES - shift, rolled[:-1], rolled[1:]).reshape(rows, LANES)
 
 
-def forward_kernel(offs, region, ill, left, right, far, patch, wave, half):
+def build_tables(cos_table, sin_table, left, right):
+    size = cos_table.shape[-1]
+    low, high = slice(0, size), slice(size, 2 * size)
+    for table, sign in ((left, -1), (right, 1)):
+        table[low, low] = cos_table[...]
+        table[high, high] = cos_table[...]
+        table[low, high] = sin_table[...] if sign > 0 else -sin_table[...]
+        table[high, low] = -sin_table[...] if sign > 0 else sin_table[...]
+
+
+def region_copies(pieces, region, sems):
+    upper, lower, middle, west, east, outer_west, outer_east = pieces
+    rows, cols, edge = middle.shape[1], middle.shape[2], west.shape[2]
+    tops = [pl.ds(k * rows, rows) for k in range(3)]
+    center, right = pl.ds(edge, cols), pl.ds(edge + cols, edge)
+    first = pl.ds(0, edge)
+    moves = [
+        (upper, tops[0], center),
+        (middle, tops[1], center),
+        (lower, tops[2], center),
+        (west, tops[1], first),
+        (east, tops[1], right),
+        (outer_west.at[:, pl.ds(0, rows)], tops[0], first),
+        (outer_west.at[:, pl.ds(rows, rows)], tops[2], first),
+        (outer_east.at[:, pl.ds(0, rows)], tops[0], right),
+        (outer_east.at[:, pl.ds(rows, rows)], tops[2], right),
+    ]
+    return [
+        pltpu.make_async_copy(source, region.at[:, place, columns], sems.at[index])
+        for index, (source, place, columns) in enumerate(moves)
+    ]
+
+
+def forward_kernel(offs, *refs):
+    pieces, refs = refs[:7], refs[7:]
+    ill, cos_table, sin_table, far, patch, region, left, right, wave, half, sems = refs
     slot = pl.program_id(0)
     size = ill.shape[-1]
     row = offs[slot, 0]
@@ -70,6 +105,15 @@
     row_base = row - row_shift
     lane = lax.broadcasted_iota(jnp.int32, (CHUNK, LANES), 1)
     blocks = size // LANES
+
+    @pl.when(slot == 0)
+    def _():
+        copies = region_copies(pieces, region, sems)
+        for copy in copies:
+            copy.start()
+        build_tables(cos_table, sin_table, left, right)
+        for copy in copies:
+            copy.wait()
 
     def extract(step, carry):
         at = pl.multiple_of(step * CHUNK, CHUNK)
@@ -121,7 +165,22 @@
 
 
 def backward_kernel(
-    offs, order, far, patch, amp, ill, left, right, accum, sums, corr, back, change, inverse
+    offs,
+    order,
+    far,
+    patch,
+    amp,
+    ill,
+    cos_table,
+    sin_table,
+    accum,
+    sums,
+    corr,
+    back,
+    change,
+    left,
+    right,
+    inverse,
 ):
     slot = pl.program_id(0)
     size = ill.shape[-1]
@@ -138,6 +197,7 @@
 
     @pl.when(slot == 0)
     def _():
+        build_tables(cos_table, sin_table, left, right)
         sums[...] = jnp.zeros_like(sums)
 
         def clear(step, carry):
@@ -249,23 +309,29 @@
     return pl.BlockSpec((1,) + shape, lambda slot, *refs: (slot,) + (0,) * len(shape))
 
 
-def run_forward(offs, region, ill, left, right):
+def run_forward(offs, pieces, ill, cos_table, sin_table):
     slots = offs.shape[0]
     size = ill.shape[-1]
+    rows, cols, edge = pieces[2].shape[1], pieces[2].shape[2], pieces[3].shape[2]
     planes = jax.ShapeDtypeStruct((slots, 2, size, size), jnp.float32)
     return pl.pallas_call(
         forward_kernel,
         grid_spec=pltpu.PrefetchScalarGridSpec(
             num_scalar_prefetch=1,
             grid=(slots,),
-            in_specs=[once(region.shape), once(ill.shape), once(left.shape), once(right.shape)],
+            in_specs=[pl.BlockSpec(memory_space=pl.ANY)] * len(pieces)
+            + [once(ill.shape), once(cos_table.shape), once(sin_table.shape)],
             out_specs=[
                 one_slot((2, size, size)),
                 one_slot((2, size, size)),
             ],
             scratch_shapes=[
+                pltpu.VMEM((2, 3 * rows, cols + 2 * edge), jnp.float32),
+                pltpu.VMEM((2 * size, 2 * size), jnp.bfloat16),
+                pltpu.VMEM((2 * size, 2 * size), jnp.bfloat16),
                 pltpu.VMEM((2 * size, size), jnp.bfloat16),
                 pltpu.VMEM((size, 2 * size), jnp.bfloat16),
+                pltpu.SemaphoreType.DMA((9,)),
             ],
         ),
         out_shape=[planes, planes],
@@ -274,10 +340,10 @@
         ),
         compiler_params=pltpu.CompilerParams(vmem_limit_bytes=48 * 1024 * 1024),
         name="forward",
-    )(offs, region, ill, left, right)
-
-
-def run_backward(offs, order, far, patch, amp, ill, left, right, region_shape):
+    )(offs, *pieces, ill, cos_table, sin_table)
+
+
+def run_backward(offs, order, far, patch, amp, ill, cos_table, sin_table, region_shape):
     slots = offs.shape[0]
     size = ill.shape[-1]
     senders, _, per, height, _ = amp.shape
@@ -294,14 +360,16 @@
                     (senders, 1, per, height, size), lambda slot, *refs: (0, slot, 0, 0, 0)
                 ),
                 once(ill.shape),
-                once(left.shape),
-                once(right.shape),
+                once(cos_table.shape),
+                once(sin_table.shape),
             ],
             out_specs=[whole(region_shape), whole(sums_shape)],
             scratch_shapes=[
                 pltpu.VMEM((2 * size, size), jnp.bfloat16),
                 pltpu.VMEM((size, 2 * size), jnp.bfloat16),
                 pltpu.VMEM((2, size, size), jnp.float32),
+                pltpu.VMEM((2 * size, 2 * size), jnp.bfloat16),
+                pltpu.VMEM((2 * size, 2 * size), jnp.bfloat16),
                 pltpu.SMEM((senders * per,), jnp.int32),
             ],
         ),
@@ -314,7 +382,25 @@
         ),
         compiler_params=pltpu.CompilerParams(vmem_limit_bytes=56 * 1024 * 1024),
         name="backward",
-    )(offs, order, far, patch, amp, ill, left, right)
+    )(offs, order, far, patch, amp, ill, cos_table, sin_table)
+
+
+def unpack_kernel(packed, out):
+    size = out.shape[1]
+    for plane in range(2):
+        out[plane] = packed[:, plane].reshape(size, LANES)
+
+
+def unpacked(packed, size):
+    packed = packed.reshape(size * size // (PIECE * LANES), 2, PIECE, LANES)
+    return pl.pallas_call(
+        unpack_kernel,
+        grid=(size // LANES,),
+        in_specs=[pl.BlockSpec((size // PIECE, 2, PIECE, LANES), lambda at: (at, 0, 0, 0))],
+        out_specs=pl.BlockSpec((2, size, LANES), lambda at: (0, 0, at)),
+        out_shape=jax.ShapeDtypeStruct((2, size, size), jnp.float32),
+        name="unpack",
+    )(packed)
 
 
 def spread_out(value):
@@ -358,54 +444,29 @@
     density_bound = slots * modulus * modulus
     step_bound = math.sqrt(slots * devices) * change_bound
     cos_table, sin_table = dft_tables(size)
-    left = jnp.concatenate(
-        [
-            jnp.concatenate([cos_table, -sin_table], axis=1),
-            jnp.concatenate([sin_table, cos_table], axis=1),
-        ],
-        axis=0,
-    )
-    right = jnp.concatenate(
-        [
-            jnp.concatenate([cos_table, sin_table], axis=1),
-            jnp.concatenate([-sin_table, cos_table], axis=1),
-        ],
-        axis=0,
-    )
     bounds = (change_bound, grad_bound, sum_bound, density_bound, step_bound)
-    upper, lower, moved, west, east, offs, left, right, bounds = lax.optimization_barrier(
-        (upper, lower, moved, west, east, offs, left, right, bounds)
+    upper, lower, moved, west, east, offs, bounds = lax.optimization_barrier(
+        (upper, lower, moved, west, east, offs, bounds)
     )
     change_bound, grad_bound, sum_bound, density_bound, step_bound = bounds
-    outer_west = passed_along(
-        jnp.concatenate([upper[:, :, edge:], lower[:, :, edge:]], axis=1), "col", 1
-    )
-    outer_east = passed_along(
-        jnp.concatenate([upper[:, :, :edge], lower[:, :, :edge]], axis=1), "col", -1
-    )
+    west_edges = jnp.concatenate([upper[:, :, edge:], lower[:, :, edge:]], axis=1)
+    east_edges = jnp.concatenate([upper[:, :, :edge], lower[:, :, :edge]], axis=1)
+    outer_west = passed_along(west_edges, "col", 1)
+    outer_east = passed_along(east_edges, "col", -1)
+    levels = jnp.concatenate([moved, grouped[:, :late]], axis=1)
     arrived = lax.all_to_all(
-        jnp.concatenate([moved, grouped[:, :late]], axis=1),
+        levels,
         "row",
         split_axis=0,
         concat_axis=0,
         tiled=True,
         axis_index_groups=[[(sender + 1) % senders for sender in range(senders)]],
     )
-    region = jnp.concatenate(
-        [
-            jnp.concatenate(
-                [outer_west[:, :tile_rows], upper, outer_east[:, :tile_rows]], axis=2
-            ),
-            jnp.concatenate([west, specimen, east], axis=2),
-            jnp.concatenate(
-                [outer_west[:, tile_rows:], lower, outer_east[:, tile_rows:]], axis=2
-            ),
-        ],
-        axis=1,
-    )
-    far, patch = run_forward(offs, region, illumination, left, right)
+    pieces = (upper, lower, specimen, west, east, outer_west, outer_east)
+    far, patch = run_forward(offs, pieces, illumination, cos_table, sin_table)
+    region_shape = (2, 3 * tile_rows, tile_cols + 2 * edge)
     accum, sums = run_backward(
-        offs, module_row, far, patch, arrived, illumination, left, right, region.shape
+        offs, module_row, far, patch, arrived, illumination, cos_table, sin_table, region_shape
     )
     to_west = narrowed(accum[:, :, :edge], grad_bound)
     to_east = narrowed(accum[:, :, edge + tile_cols :], grad_bound)
@@ -428,10 +489,7 @@
     mine = narrowed(mine, step_bound).reshape(1, 2 * PIECE, LANES)
     copies = jnp.broadcast_to(mine, (devices, 2 * PIECE, LANES))
     result = spread_out(copies)
-    result = widened(result, step_bound).reshape(
-        size // LANES, size // PIECE, 2, PIECE, LANES
-    )
-    illumination_step = result.transpose(2, 1, 3, 0, 4).reshape(2, size, size)
+    illumination_step = unpacked(widened(result, step_bound), size)
     specimen_step = (
         column[:, tile_rows : 2 * tile_rows]
         + widened(from_lower, grad_bound)

time: 226 us -> 232 us (1.027)
  waiting for transfers between devices: 50.2 us -> 79.6 us
  other arithmetic: 47.1 us -> 29.2 us
  local copies, waits for them, and re-layouts: 15.6 us -> 9.59 us
  Pallas kernels: 53.7 us -> 57.2 us
  starting transfers between devices: 55 us -> 52.1 us
    ppermute x1, waiting for transfers between devices: 0.01 us -> 16.2 us  [passed_both(): return lax.ppermute(value, ('row', 'col'), pairs)]
    concatenate x3 -> x1, other arithmetic: 17.4 us -> 2.73 us  [shards(): levels = jnp.concatenate([moved, grouped[:, :late]], axis=1)]
    ppermute x12, waiting for transfers between devices: 50.1 us -> 57.8 us  [passed_along(): return lax.ppermute(value, axis, pairs)]
    all_to_all x3, waiting for transfers between devices: 0.01 us -> 5.57 us  [spread_out(): lax.all_to_all(value, ('row', 'col'), split_axis=0, concat_axis=0, tiled=...]
    convert_element_type x1 -> x0, other arithmetic: 4.39 us -> none  [dft_tables(): (-jnp.sin(angle) * norm).astype(jnp.bfloat16)]
    slice x5 -> x2, local copies, waits for them, and re-layouts: 8.44 us -> 4.38 us  [the longest x1 3.26 us: shards(): levels = jnp.concatenate([moved, grouped[:, :late]], axis=1)]
    neg x1 -> x0, other arithmetic: 4 us -> none  [shards(): -sin_table]
    ppermute x12, starting transfers between devices: 18.3 us -> 22.1 us  [passed_along(): return lax.ppermute(value, axis, pairs)]
  transfers between devices with their start and end apart: 17 -> 17, of which waited for: 5 -> 7; matrix products, arithmetic and copies ran while one was open for 22% -> 11% of each run, Pallas kernels for 10% -> 10%
where the time goes in v3:
time: 232 us; the launch traced here: 231 us
  waiting for transfers between devices  79.6 us (34%)
  Pallas kernels  57.2 us (25%)
  starting transfers between devices  52.1 us (22%)
  other arithmetic  29.2 us (13%)
  local copies, waits for them, and re-layouts  9.59 us (4%)
  between operations  3.63 us (2%)
    ppermute x12, waiting for transfers between devices, passed_along(): return lax.ppermute(value, axis, pairs)  57.8 us
    pallas_call x1, Pallas kernels, run_backward(): pl.pallas_call(backward_kernel, grid_spec=pltpu.PrefetchScalarGridSpec(nu...  30.5 us
    all_to_all x3, starting transfers between devices, spread_out(): lax.all_to_all(value, ('row', 'col'), split_axis=0, concat_axis=0, tiled=...  25.5 us
    pallas_call x1, Pallas kernels, run_forward(): pl.pallas_call(forward_kernel, grid_spec=pltpu.PrefetchScalarGridSpec(num...  22.9 us
    ppermute x12, starting transfers between devices, passed_along(): return lax.ppermute(value, axis, pairs)  22.1 us
    ppermute x1, waiting for transfers between devices, passed_both(): return lax.ppermute(value, ('row', 'col'), pairs)  16.2 us
    convert_element_type x4, other arithmetic, narrowed(): return (value * (HALF_TOP / bound)).astype(jnp.float16)  6.37 us
    all_to_all x3, waiting for transfers between devices, spread_out(): lax.all_to_all(value, ('row', 'col'), split_axis=0, concat_axis=0, tiled=...  5.57 us
  transfers between devices with their start and end apart: 17, of which 7 were waited for; matrix products, arithmetic and copies ran while one was open for 11% of the time, Pallas kernels for 10%

profile of v3, /device:TPU:1, one launch (start us, length us, event | category | flops | bytes accessed | tf_op | source)
XLA Modules:
  0.0 231.4 jit_solution(2171544106739565533)
XLA Ops:
  0.6 2.1 collective-permute-start
  2.7 4.8 %collective-permute-start.1 = (f32[2,256,512]{2,1,0:T(8,128)}, f32[2,256,512]{2,1,0:T(8,128)S(1)}, u32[]{:S(2)}, u32[]{:S(2)}) collective-permute-start(f32[2,256,512]{2,1,0:T(8,128)} %refs_2_.1), channel_id=1, source_target_pairs={{0,120},{8,0},{16,8},{24,16},{32,24},{40,32},{48,40},{56,48},{64,5... | collective-permute-start | bytes 3145736 | tf_op jit(solution)/shard_map/ppermute | solution.py:23
  7.6 3.3 %fusion.8 = (bf16[16,2,2,16,512]{4,3,2,1,0:T(8,128)(2,1)}, bf16[16,2,2,16,512]{4,3,2,1,0:T(8,128)(2,1)}) fusion(bf16[16,4,2,16,512]{4,3,2,1,0:T(8,128)(2,1)} %bitcast.9), kind=kLoop, calls=%fused_computation.33 | loop fusion | bytes 4194304 | tf_op jit(solution)/shard_map/slice | solution.py:456
  10.8 2.1 collective-permute-start.2
  13.0 0.0 copy-done.7
  13.0 0.1 fusion.12
  13.0 0.1 copy.13
  13.1 0.0 collective-permute-start.5
  13.1 0.1 copy.14
  13.2 0.0 collective-permute-start.6
  13.2 0.9 abs_reduce_fusion.1
  14.1 1.1 fusion.11
  15.2 16.2 %collective-permute-done.5 = s32[2,2]{1,0:T(2,128)S(1)} collective-permute-done((s32[2,2]{1,0:T(2,128)S(1)}, s32[2,2]{1,0:T(2,128)S(1)}, u32[]{:S(2)}, u32[]{:S(2)}) %collective-permute-start.5) | collective-permute-done | bytes 48 | tf_op jit(solution)/shard_map/ppermute | solution.py:33
  31.4 0.6 collective-permute-start.3
  32.0 0.0 collective-permute-done.6
  32.0 1.4 collective-permute-start.4
  33.4 1.2 compare_select_fusion.1
  34.7 0.7 iota.14
  35.3 6.4 %all-to-all-start = ((f32[128,1,128]{2,1,0:T(1,128)}), f32[128,1,128]{2,1,0:T(1,128)S(1)}, u32[]{:S(2)}, u32[]{:S(2)}) async-start(f32[128,1,128]{2,1,0:T(1,128)} %iota.14), calls=%async_computation | async-start | bytes 131072 | tf_op jit(solution)/shard_map/all_to_all | solution.py:407
  41.7 2.8 %multiply_reduce_fusion.1 = (f32[]{:T(128)}, f32[]{:T(128)}) fusion(f32[2,512,512]{2,1,0:T(8,128)} %ill.1), kind=kLoop, calls=%fused_computation.5 | loop fusion | flops 2097150 | bytes 2097160 | tf_op jit(solution)/shard_map/reduce_sum | solution.py:435
  45.9 5.6 %all-to-all-done = f32[128,1,128]{2,1,0:T(1,128)S(1)} async-done(((f32[128,1,128]{2,1,0:T(1,128)}), f32[128,1,128]{2,1,0:T(1,128)S(1)}, u32[]{:S(2)}, u32[]{:S(2)}) %all-to-all-start) | async-done | bytes 65568 | tf_op jit(solution)/shard_map/all_to_all | solution.py:407
  51.5 0.9 slice_reduce_fusion
  53.7 0.0 collective-permute-done.3.refs_3_
  53.7 0.0 collective-permute-done.4.refs_4_
  53.7 0.0 collective-permute-done.2
  53.7 0.0 collective-permute-done.refs_0_
  53.7 0.0 collective-permute-done.1.refs_1_
  53.7 1.1 fusion.9
  54.8 1.0 pad_maximum_fusion.2
  55.9 0.8 collective-permute-start.8
  56.6 2.7 %pad_maximum_fusion = bf16[16,4,2,16,512]{4,3,2,1,0:T(8,128)(2,1)} fusion(bf16[16,2,2,16,512]{4,3,2,1,0:T(8,128)(2,1)S(1)} %copy-done.4, bf16[16,2,2,16,512]{4,3,2,1,0:T(8,128)(2,1)} %collective-permute-done.2), kind=kLoop, calls=%fused_computation.3 | loop fusion | flops 1048576 | bytes 4194304 | tf_op jit(solution)/shard_map/concatenate | solution.py:456
  59.4 4.6 %all-to-all-start.1 = ((bf16[16,4,2,16,512]{4,3,2,1,0:T(8,128)(2,1)}), bf16[16,4,2,16,512]{4,3,2,1,0:T(8,128)(2,1)}, u32[]{:S(2)}, u32[]{:S(2)}) async-start(bf16[16,4,2,16,512]{4,3,2,1,0:T(8,128)(2,1)} %pad_maximum_fusion), calls=%async_computation.1 | async-start | bytes 4194304 | tf_op jit(solution)/shard_map/all_to_all | solution.py:457
  63.9 2.2 pad_maximum_fusion.1
  66.2 1.3 collective-permute-start.7
  67.5 3.2 %collective-permute-done.8.refs_6_ = f32[2,512,256]{2,1,0:T(8,128)} collective-permute-done((f32[2,512,256]{2,1,0:T(8,128)}, f32[2,512,256]{2,1,0:T(8,128)}, u32[]{:S(2)}, u32[]{:S(2)}) %collective-permute-start.8) | collective-permute-done | bytes 1048608 | tf_op jit(solution)/shard_map/ppermute | solution.py:23
  70.7 8.8 %collective-permute-done.7.refs_5_ = f32[2,512,256]{2,1,0:T(8,128)} collective-permute-done((f32[2,512,256]{2,1,0:T(8,128)}, f32[2,512,256]{2,1,0:T(8,128)}, u32[]{:S(2)}, u32[]{:S(2)}) %collective-permute-start.7) | collective-permute-done | bytes 1048608 | tf_op jit(solution)/shard_map/ppermute | solution.py:23
  79.5 1.0 copy-done.2
  80.5 1.0 copy-done.3
  81.6 22.9 %forward.1 = (f32[4,2,512,512]{3,2,1,0:T(8,128)}, f32[4,2,512,512]{3,2,1,0:T(8,128)}) custom-call(s32[4,2]{1,0:T(4,128)S(1)} %pad_add_fusion.offs, f32[2,256,512]{2,1,0:T(8,128)S(1)} %collective-permute-done.refs_0_, f32[2,256,512]{2,1,0:T(8,128)S(1)} %collective-permute-done.1.refs_1_, f32[2,256,512]{2,1,0:T(8,128)S(1)} %copy-done, ...), custom_call_target="tpu_custom_call" | custom-call | flops 8589934592 | bytes 30000000 | tf_op jit(solution)/shard_map/forward/pallas_call | solution.py:317
  104.5 0.0 all-to-all-done.1.amp
  104.5 30.5 %backward.1 = (f32[2,768,1024]{2,1,0:T(8,128)}, f32[4,32,3,16,128]{4,3,2,1,0:T(8,128)}) custom-call(s32[4,2]{1,0:T(4,128)} %copy-done.1, s32[32]{0:T(128)} %order.1, f32[4,2,512,512]{3,2,1,0:T(8,128)} %get-tuple-element.21.far, f32[4,2,512,512]{3,2,1,0:T(8,128)} %get-tuple-element.22.patch, bf16[16,4,2,16,512]{4,3,2,1,0:T(8,128)(2,1)} %all-to-all-done.1.amp, ...), custom_call_target="tpu_custom_call" | custom-call | flops 8589934592 | bytes 30000000 | tf_op jit(solution)/shard_map/backward/pallas_call | solution.py:351
  135.0 3.6 %multiply_convert_fusion.2 = (f16[2,768,256]{2,1,0:T(8,128)(2,1)}, f16[2,768,256]{2,1,0:T(8,128)(2,1)}) fusion(f32[2,768,1024]{2,1,0:T(8,128)} %get-tuple-element.24, f32[]{:T(128)S(6)} %div.41), kind=kLoop, calls=%fused_computation.10 | loop fusion | flops 1572864 | bytes 4718596 | tf_op jit(solution)/shard_map/convert_element_type | solution.py:47
  138.6 2.5 %collective-permute-start.9 = (f16[2,768,256]{2,1,0:T(8,128)(2,1)}, f16[2,768,256]{2,1,0:T(8,128)(2,1)}, u32[]{:S(2)}, u32[]{:S(2)}) collective-permute-start(f16[2,768,256]{2,1,0:T(8,128)(2,1)} %get-tuple-element.36), channel_id=1, source_target_pairs={{0,1},{1,2},{2,3},{3,4},{4,5},{5,6},{6,7},{7,0},{8,9},{9,10},{10,1... | collective-permute-start | bytes 2359304 | tf_op jit(solution)/shard_map/ppermute | solution.py:23
  141.1 1.5 multiply_convert_fusion
  142.6 9.6 %all-to-all-start.2 = ((f16[128,48,128]{2,1,0:T(8,128)(2,1)}), f16[128,48,128]{2,1,0:T(8,128)(2,1)}, u32[]{:S(2)}, u32[]{:S(2)}) async-start(f16[128,48,128]{2,1,0:T(8,128)(2,1)} %multiply_convert_fusion), calls=%async_computation.2 | async-start | bytes 3145728 | tf_op jit(solution)/shard_map/all_to_all | solution.py:407
  152.2 1.1 collective-permute-start.10
  153.4 0.0 collective-permute-done.9
  153.4 1.3 convert_multiply_fusion.2
  154.7 24.0 %collective-permute-done.10 = f16[2,768,256]{2,1,0:T(8,128)(2,1)S(1)} collective-permute-done((f16[2,768,256]{2,1,0:T(8,128)(2,1)S(1)}, f16[2,768,256]{2,1,0:T(8,128)(2,1)S(1)}, u32[]{:S(2)}, u32[]{:S(2)}) %collective-permute-start.10) | collective-permute-done | bytes 786464 | tf_op jit(solution)/shard_map/ppermute | solution.py:23
  178.7 0.1 convert_multiply_fusion.1
  178.8 2.5 %maximum_add_fusion = f32[2,768,512]{2,1,0:T(8,128)S(1)} fusion(f32[2,768,256]{2,1,0:T(8,128)S(1)} %convert_multiply_fusion.1, f32[2,768,256]{2,1,0:T(8,128)S(1)} %convert_multiply_fusion.2, f32[2,768,1024]{2,1,0:T(8,128)} %get-tuple-element.24), kind=kLoop, calls=%fused_computation | loop fusion | flops 1572864 | bytes 9437184 | tf_op jit(solution)/shard_map/add | solution.py:480
  181.3 0.0 all-to-all-done.2
  181.3 1.9 multiply_reduce_fusion
  183.2 1.1 broadcast_in_dim.26
  184.3 9.5 %all-to-all-start.3 = ((f16[128,32,128]{2,1,0:T(8,128)(2,1)}), f16[128,32,128]{2,1,0:T(8,128)(2,1)}, u32[]{:S(2)}, u32[]{:S(2)}) async-start(f16[128,32,128]{2,1,0:T(8,128)(2,1)} %broadcast_in_dim.26), calls=%async_computation.3 | async-start | bytes 2097152 | tf_op jit(solution)/shard_map/all_to_all | solution.py:407
  193.9 1.3 fusion.1
  195.2 5.4 %collective-permute-start.11 = (f16[2,256,512]{2,1,0:T(8,128)(2,1)}, f16[2,256,512]{2,1,0:T(8,128)(2,1)}, u32[]{:S(2)}, u32[]{:S(2)}) collective-permute-start(f16[2,256,512]{2,1,0:T(8,128)(2,1)} %get-tuple-element.38), channel_id=1, source_target_pairs={{0,120},{8,0},{16,8},{24,16},{32,24},{40,32},{48,40},{56,48},{64,5... | collective-permute-start | bytes 1572872 | tf_op jit(solution)/shard_map/ppermute | solution.py:23
  200.5 0.0 collective-permute-start.12
  200.6 16.8 %collective-permute-done.11 = f16[2,256,512]{2,1,0:T(8,128)(2,1)} collective-permute-done((f16[2,256,512]{2,1,0:T(8,128)(2,1)}, f16[2,256,512]{2,1,0:T(8,128)(2,1)}, u32[]{:S(2)}, u32[]{:S(2)}) %collective-permute-start.11) | collective-permute-done | bytes 524320 | tf_op jit(solution)/shard_map/ppermute | solution.py:23
  217.4 5.0 %collective-permute-done.12 = f16[2,256,512]{2,1,0:T(8,128)(2,1)} collective-permute-done((f16[2,256,512]{2,1,0:T(8,128)(2,1)}, f16[2,256,512]{2,1,0:T(8,128)(2,1)}, u32[]{:S(2)}, u32[]{:S(2)}) %collective-permute-start.12) | collective-permute-done | bytes 524320 | tf_op jit(solution)/shard_map/ppermute | solution.py:23
  222.3 2.4 %fusion.2 = f32[2,256,512]{2,1,0:T(8,128)} fusion(f32[2,768,512]{2,1,0:T(8,128)S(1)} %maximum_add_fusion, f16[2,256,512]{2,1,0:T(8,128)(2,1)} %collective-permute-done.12, f16[2,256,512]{2,1,0:T(8,128)(2,1)} %collective-permute-done.11, f32[]{:T(128)S(6)} %div.42), kind=kLoop, calls=%fused_computation.16 | loop fusion | flops 1572864 | bytes 3145732 | tf_op jit(solution)/shard_map/add | solution.py:494
  224.7 0.0 all-to-all-done.3
  224.7 2.9 %convert_multiply_fusion = f32[128,32,128]{2,1,0:T(8,128)} fusion(f16[128,32,128]{2,1,0:T(8,128)(2,1)} %all-to-all-done.3, f32[]{:T(128)S(6)} %div.49), kind=kLoop, calls=%fused_computation.4 | loop fusion | flops 1048576 | bytes 3145732 | tf_op jit(solution)/shard_map/mul | solution.py:51
  227.6 3.8 %unpack.1 = f32[2,512,512]{2,1,0:T(8,128)} custom-call(f32[128,2,16,128]{3,2,1,0:T(8,128)} %bitcast.7), custom_call_target="tpu_custom_call" | custom-call | tf_op jit(solution)/shard_map/unpack/pallas_call | solution.py:396
  (18 shorter events, 0.1 us)
Async XLA Ops:
  0.6 53.1 %collective-permute-start = (f32[2,256,512]{2,1,0:T(8,128)}, f32[2,256,512]{2,1,0:T(8,128)S(1)}, u32[]{:S(2)}, u32[]{:S(2)}) collective-permute-start(f32[2,256,512]{2,1,0:T(8,128)} %refs_2_.1), channel_id=1, source_target_pairs={{0,8},{8,16},{16,24},{24,32},{32,40},{40,48},{48,56},{56,64},{64,7... | collective-permute-start | bytes 3145736 | tf_op jit(solution)/shard_map/ppermute | solution.py:23
  2.7 51.0 %collective-permute-start.1 = (f32[2,256,512]{2,1,0:T(8,128)}, f32[2,256,512]{2,1,0:T(8,128)S(1)}, u32[]{:S(2)}, u32[]{:S(2)}) collective-permute-start(f32[2,256,512]{2,1,0:T(8,128)} %refs_2_.1), channel_id=1, source_target_pairs={{0,120},{8,0},{16,8},{24,16},{32,24},{40,32},{48,40},{56,48},{64,5... | collective-permute-start | bytes 3145736 | tf_op jit(solution)/shard_map/ppermute | solution.py:23
  7.5 5.4 %copy-start.7 = (s32[1,1,4,2]{2,3,1,0:T(2,128)S(1)}, s32[1,1,4,2]{2,3,1,0:T(2,128)}, u32[]{:S(2)}) copy-start(s32[1,1,4,2]{2,3,1,0:T(2,128)} %param.9) | copy-start | bytes 100
  7.6 5.7 %copy-start = (f32[2,256,512]{2,1,0:T(8,128)S(1)}, f32[2,256,512]{2,1,0:T(8,128)}, u32[]{:S(2)}) copy-start(f32[2,256,512]{2,1,0:T(8,128)} %refs_2_.1) | copy-start | bytes 3145732
  10.8 42.9 %collective-permute-start.2 = (bf16[16,2,2,16,512]{4,3,2,1,0:T(8,128)(2,1)}, bf16[16,2,2,16,512]{4,3,2,1,0:T(8,128)(2,1)}, u32[]{:S(2)}, u32[]{:S(2)}) collective-permute-start(bf16[16,2,2,16,512]{4,3,2,1,0:T(8,128)(2,1)} %get-tuple-element.41), channel_id=1, source_target_pairs={{0,1},{1,2},{2,3},{3,4},{4,5},{5,6},{6,7},{7,0},{8,9},{9,10},{10,1... | collective-permute-start | bytes 3145736 | tf_op jit(solution)/shard_map/ppermute | solution.py:23
  13.1 18.3 %collective-permute-start.5 = (s32[2,2]{1,0:T(2,128)S(1)}, s32[2,2]{1,0:T(2,128)S(1)}, u32[]{:S(2)}, u32[]{:S(2)}) collective-permute-start(s32[2,2]{1,0:T(2,128)S(1)} %bitcast.11), channel_id=1, source_target_pairs={{0,9},{1,10},{2,11},{3,12},{4,13},{5,14},{6,15},{7,8},{8,17},{9,18... | collective-permute-start | bytes 56 | tf_op jit(solution)/shard_map/ppermute | solution.py:33
  13.2 18.8 %collective-permute-start.6 = (s32[2,2]{1,0:T(2,128)S(1)}, s32[2,2]{1,0:T(2,128)S(1)}, u32[]{:S(2)}, u32[]{:S(2)}) collective-permute-start(s32[2,2]{1,0:T(2,128)S(1)} %bitcast.10), channel_id=1, source_target_pairs={{0,8},{8,16},{16,24},{24,32},{32,40},{40,48},{48,56},{56,64},{64,7... | collective-permute-start | bytes 56 | tf_op jit(solution)/shard_map/ppermute | solution.py:23
  31.4 22.2 %collective-permute-start.3 = (f32[2,256,256]{2,1,0:T(8,128)}, f32[2,256,256]{2,1,0:T(8,128)}, u32[]{:S(2)}, u32[]{:S(2)}) collective-permute-start(f32[2,256,256]{2,1,0:T(8,128)} %get-tuple-element.47), channel_id=1, source_target_pairs={{0,1},{1,2},{2,3},{3,4},{4,5},{5,6},{6,7},{7,0},{8,9},{9,10},{10,1... | collective-permute-start | bytes 1572872 | tf_op jit(solution)/shard_map/ppermute | solution.py:23
  32.0 21.6 %collective-permute-start.4 = (f32[2,256,256]{2,1,0:T(8,128)}, f32[2,256,256]{2,1,0:T(8,128)}, u32[]{:S(2)}, u32[]{:S(2)}) collective-permute-start(f32[2,256,256]{2,1,0:T(8,128)} %get-tuple-element.46), channel_id=1, source_target_pairs={{0,7},{1,0},{2,1},{3,2},{4,3},{5,4},{6,5},{7,6},{8,15},{9,8},{10,9... | collective-permute-start | bytes 1572872 | tf_op jit(solution)/shard_map/ppermute | solution.py:23
  35.3 16.1 %all-to-all-start = ((f32[128,1,128]{2,1,0:T(1,128)}), f32[128,1,128]{2,1,0:T(1,128)S(1)}, u32[]{:S(2)}, u32[]{:S(2)}) async-start(f32[128,1,128]{2,1,0:T(1,128)} %iota.14), calls=%async_computation | async-start | bytes 131072 | tf_op jit(solution)/shard_map/all_to_all | solution.py:407
  45.9 33.6 %copy-start.1 = (s32[4,2]{1,0:T(4,128)}, s32[4,2]{1,0:T(4,128)S(1)}, u32[]{:S(2)}) copy-start(s32[4,2]{1,0:T(4,128)S(1)} %pad_add_fusion.offs) | copy-start | bytes 100
  54.8 1.8 copy-start.4
  55.9 14.8 %collective-permute-start.8 = (f32[2,512,256]{2,1,0:T(8,128)}, f32[2,512,256]{2,1,0:T(8,128)}, u32[]{:S(2)}, u32[]{:S(2)}) collective-permute-start(f32[2,512,256]{2,1,0:T(8,128)} %pad_maximum_fusion.2), channel_id=1, source_target_pairs={{0,7},{1,0},{2,1},{3,2},{4,3},{5,4},{6,5},{7,6},{8,15},{9,8},{10,9... | collective-permute-start | bytes 3145736 | tf_op jit(solution)/shard_map/ppermute | solution.py:23
  59.4 45.1 %all-to-all-start.1 = ((bf16[16,4,2,16,512]{4,3,2,1,0:T(8,128)(2,1)}), bf16[16,4,2,16,512]{4,3,2,1,0:T(8,128)(2,1)}, u32[]{:S(2)}, u32[]{:S(2)}) async-start(bf16[16,4,2,16,512]{4,3,2,1,0:T(8,128)(2,1)} %pad_maximum_fusion), calls=%async_computation.1 | async-start | bytes 4194304 | tf_op jit(solution)/shard_map/all_to_all | solution.py:457
  66.2 13.3 %collective-permute-start.7 = (f32[2,512,256]{2,1,0:T(8,128)}, f32[2,512,256]{2,1,0:T(8,128)}, u32[]{:S(2)}, u32[]{:S(2)}) collective-permute-start(f32[2,512,256]{2,1,0:T(8,128)} %pad_maximum_fusion.1), channel_id=1, source_target_pairs={{0,1},{1,2},{2,3},{3,4},{4,5},{5,6},{6,7},{7,0},{8,9},{9,10},{10,1... | collective-permute-start | bytes 3145736 | tf_op jit(solution)/shard_map/ppermute | solution.py:23
  79.5 1.0 copy-start.2
  80.5 1.0 copy-start.3
  135.0 6.1 %copy-start.5 = (f32[4,32,3,16,128]{4,3,2,1,0:T(8,128)S(1)}, f32[4,32,3,16,128]{4,3,2,1,0:T(8,128)}, u32[]{:S(2)}) copy-start(f32[4,32,3,16,128]{4,3,2,1,0:T(8,128)} %get-tuple-element.26) | copy-start | bytes 9437188
  138.6 14.8 %collective-permute-start.9 = (f16[2,768,256]{2,1,0:T(8,128)(2,1)}, f16[2,768,256]{2,1,0:T(8,128)(2,1)}, u32[]{:S(2)}, u32[]{:S(2)}) collective-permute-start(f16[2,768,256]{2,1,0:T(8,128)(2,1)} %get-tuple-element.36), channel_id=1, source_target_pairs={{0,1},{1,2},{2,3},{3,4},{4,5},{5,6},{6,7},{7,0},{8,9},{9,10},{10,1... | collective-permute-start | bytes 2359304 | tf_op jit(solution)/shard_map/ppermute | solution.py:23
  142.6 9.6 %copy-start.6 = (f16[2,768,256]{2,1,0:T(8,128)(2,1)S(1)}, f16[2,768,256]{2,1,0:T(8,128)(2,1)}, u32[]{:S(2)}) copy-start(f16[2,768,256]{2,1,0:T(8,128)(2,1)} %get-tuple-element.37) | copy-start | bytes 2359300
  142.6 38.7 %all-to-all-start.2 = ((f16[128,48,128]{2,1,0:T(8,128)(2,1)}), f16[128,48,128]{2,1,0:T(8,128)(2,1)}, u32[]{:S(2)}, u32[]{:S(2)}) async-start(f16[128,48,128]{2,1,0:T(8,128)(2,1)} %multiply_convert_fusion), calls=%async_computation.2 | async-start | bytes 3145728 | tf_op jit(solution)/shard_map/all_to_all | solution.py:407
  152.2 26.5 %collective-permute-start.10 = (f16[2,768,256]{2,1,0:T(8,128)(2,1)S(1)}, f16[2,768,256]{2,1,0:T(8,128)(2,1)S(1)}, u32[]{:S(2)}, u32[]{:S(2)}) collective-permute-start(f16[2,768,256]{2,1,0:T(8,128)(2,1)S(1)} %copy-done.6), channel_id=1, source_target_pairs={{0,7},{1,0},{2,1},{3,2},{4,3},{5,4},{6,5},{7,6},{8,15},{9,8},{10,9... | collective-permute-start | bytes 2359304 | tf_op jit(solution)/shard_map/ppermute | solution.py:23
  184.3 40.4 %all-to-all-start.3 = ((f16[128,32,128]{2,1,0:T(8,128)(2,1)}), f16[128,32,128]{2,1,0:T(8,128)(2,1)}, u32[]{:S(2)}, u32[]{:S(2)}) async-start(f16[128,32,128]{2,1,0:T(8,128)(2,1)} %broadcast_in_dim.26), calls=%async_computation.3 | async-start | bytes 2097152 | tf_op jit(solution)/shard_map/all_to_all | solution.py:407
  195.2 22.2 %collective-permute-start.11 = (f16[2,256,512]{2,1,0:T(8,128)(2,1)}, f16[2,256,512]{2,1,0:T(8,128)(2,1)}, u32[]{:S(2)}, u32[]{:S(2)}) collective-permute-start(f16[2,256,512]{2,1,0:T(8,128)(2,1)} %get-tuple-element.38), channel_id=1, source_target_pairs={{0,120},{8,0},{16,8},{24,16},{32,24},{40,32},{48,40},{56,48},{64,5... | collective-permute-start | bytes 1572872 | tf_op jit(solution)/shard_map/ppermute | solution.py:23
  200.5 21.8 %collective-permute-start.12 = (f16[2,256,512]{2,1,0:T(8,128)(2,1)}, f16[2,256,512]{2,1,0:T(8,128)(2,1)}, u32[]{:S(2)}, u32[]{:S(2)}) collective-permute-start(f16[2,256,512]{2,1,0:T(8,128)(2,1)} %get-tuple-element.39), channel_id=1, source_target_pairs={{0,8},{8,16},{16,24},{24,32},{32,40},{40,48},{48,56},{56,64},{64,7... | collective-permute-start | bytes 1572872 | tf_op jit(solution)/shard_map/ppermute | solution.py:23

commit v4 on v3

--- a/solution.py
+++ b/solution.py
@@ -10,7 +10,6 @@
 
 
 LANES = 128
-SUBLANES = 8
 CHUNK = 32
 BLOCK = 256
 PIECE = 16
@@ -40,7 +39,8 @@
     norm = np.float32(1.0 / math.sqrt(size))
     cos_table = np.cos(angle.astype(np.float64)).astype(np.float32) * norm
     sin_table = -np.sin(angle.astype(np.float64)).astype(np.float32) * norm
-    return jnp.asarray(cos_table, jnp.bfloat16), jnp.asarray(sin_table, jnp.bfloat16)
+    tables = (cos_table, sin_table, -sin_table)
+    return tuple(jnp.asarray(table, jnp.bfloat16) for table in tables)
 
 
 def narrowed(value, bound):
@@ -51,79 +51,80 @@
     return value.astype(jnp.float32) * (bound / HALF_TOP)
 
 
-def gather_rows(ref, plane, start, rows, col, shift):
-    tiles = rows // SUBLANES + 1
-    block = ref[plane, pl.ds(start, tiles * SUBLANES), pl.ds(col, LANES)]
-    block = block.reshape(tiles, SUBLANES, LANES)
-    rolled = pltpu.roll(block, (SUBLANES - shift) % SUBLANES, axis=1)
-    sub = lax.broadcasted_iota(jnp.int32, (tiles - 1, SUBLANES, LANES), 1)
-    return jnp.where(sub < SUBLANES - shift, rolled[:-1], rolled[1:]).reshape(rows, LANES)
-
-
-def build_tables(cos_table, sin_table, left, right):
+def table_copies(tables, left, right, sems):
+    cos_table, sin_table, negative = tables
     size = cos_table.shape[-1]
-    low, high = slice(0, size), slice(size, 2 * size)
-    for table, sign in ((left, -1), (right, 1)):
-        table[low, low] = cos_table[...]
-        table[high, high] = cos_table[...]
-        table[low, high] = sin_table[...] if sign > 0 else -sin_table[...]
-        table[high, low] = -sin_table[...] if sign > 0 else sin_table[...]
+    low, high = pl.ds(0, size), pl.ds(size, size)
+    moves = [
+        (cos_table, left, low, low),
+        (cos_table, left, high, high),
+        (negative, left, low, high),
+        (sin_table, left, high, low),
+        (cos_table, right, low, low),
+        (cos_table, right, high, high),
+        (sin_table, right, low, high),
+        (negative, right, high, low),
+    ]
+    return [
+        pltpu.make_async_copy(source, table.at[rows, columns], sems.at[index])
+        for index, (source, table, rows, columns) in enumerate(moves)
+    ]
 
 
 def region_copies(pieces, region, sems):
     upper, lower, middle, west, east, outer_west, outer_east = pieces
     rows, cols, edge = middle.shape[1], middle.shape[2], west.shape[2]
-    tops = [pl.ds(k * rows, rows) for k in range(3)]
-    center, right = pl.ds(edge, cols), pl.ds(edge + cols, edge)
-    first = pl.ds(0, edge)
+    center, right = edge // LANES, (edge + cols) // LANES
     moves = [
-        (upper, tops[0], center),
-        (middle, tops[1], center),
-        (lower, tops[2], center),
-        (west, tops[1], first),
-        (east, tops[1], right),
-        (outer_west.at[:, pl.ds(0, rows)], tops[0], first),
-        (outer_west.at[:, pl.ds(rows, rows)], tops[2], first),
-        (outer_east.at[:, pl.ds(0, rows)], tops[0], right),
-        (outer_east.at[:, pl.ds(rows, rows)], tops[2], right),
+        (upper, 0, 0, center),
+        (middle, 0, 1, center),
+        (lower, 0, 2, center),
+        (west, 0, 1, 0),
+        (east, 0, 1, right),
+        (outer_west, 0, 0, 0),
+        (outer_west, 1, 2, 0),
+        (outer_east, 0, 0, right),
+        (outer_east, 1, 2, right),
     ]
-    return [
-        pltpu.make_async_copy(source, region.at[:, place, columns], sems.at[index])
-        for index, (source, place, columns) in enumerate(moves)
-    ]
+    copies = []
+    for piece, source, target, first in moves:
+        for block in range(piece.shape[2] // LANES):
+            copies.append(
+                pltpu.make_async_copy(
+                    piece.at[:, pl.ds(source * rows, rows), pl.ds(block * LANES, LANES)],
+                    region.at[:, first + block, pl.ds(target * rows, rows)],
+                    sems.at[len(copies)],
+                )
+            )
+    return copies
 
 
 def forward_kernel(offs, *refs):
-    pieces, refs = refs[:7], refs[7:]
-    ill, cos_table, sin_table, far, patch, region, left, right, wave, half, sems = refs
+    pieces, tables, refs = refs[:7], refs[7:10], refs[10:]
+    ill, far, patch, region, left, right, wave, half, region_sems, table_sems = refs
     slot = pl.program_id(0)
     size = ill.shape[-1]
     row = offs[slot, 0]
-    base = slot * LANES
     lane_shift = offs[slot, 1] % LANES
-    row_shift = row % SUBLANES
-    row_base = row - row_shift
     lane = lax.broadcasted_iota(jnp.int32, (CHUNK, LANES), 1)
     blocks = size // LANES
 
     @pl.when(slot == 0)
     def _():
-        copies = region_copies(pieces, region, sems)
-        for copy in copies:
-            copy.start()
-        build_tables(cos_table, sin_table, left, right)
-        for copy in copies:
-            copy.wait()
+        region_moves = region_copies(pieces, region, region_sems)
+        table_moves = table_copies(tables, left, right, table_sems)
+        for move in region_moves + table_moves:
+            move.start()
+        for move in region_moves + table_moves:
+            move.wait()
 
     def extract(step, carry):
         at = pl.multiple_of(step * CHUNK, CHUNK)
-        start = pl.multiple_of(row_base + at, SUBLANES)
         last = [None, None]
         for block in range(blocks + 1):
-            col = pl.multiple_of(base + block * LANES, LANES)
             now = [
                 pltpu.roll(
-                    gather_rows(region, plane, start, CHUNK, col, row_shift),
+                    region[plane, slot + block, pl.ds(row + at, CHUNK), :],
                     (LANES - lane_shift) % LANES,
                     axis=1,
                 )
@@ -148,7 +149,7 @@
             last = now
         return carry
 
-    lax.fori_loop(0, size // CHUNK, extract, 0)
+    lax.fori_loop(0, size // CHUNK, extract, 0, unroll=4)
     for block in range(size // BLOCK):
         to = slice(block * BLOCK, (block + 1) * BLOCK)
         also = slice(size + block * BLOCK, size + (block + 1) * BLOCK)
@@ -173,6 +174,7 @@
     ill,
     cos_table,
     sin_table,
+    negative,
     accum,
     sums,
     corr,
@@ -181,31 +183,33 @@
     left,
     right,
     inverse,
+    table_sems,
 ):
     slot = pl.program_id(0)
     size = ill.shape[-1]
     modules = size // amp.shape[3]
     senders = amp.shape[0]
     row = offs[slot, 0]
-    base = slot * LANES
     lane_shift = offs[slot, 1] % LANES
-    row_shift = row % SUBLANES
-    row_base = row - row_shift
+    tables = (cos_table, sin_table, negative)
     blocks = size // LANES
     height = amp.shape[3]
     per = amp.shape[2]
 
     @pl.when(slot == 0)
     def _():
-        build_tables(cos_table, sin_table, left, right)
+        for move in table_copies(tables, left, right, table_sems):
+            move.start()
         sums[...] = jnp.zeros_like(sums)
 
         def clear(step, carry):
             at = pl.multiple_of(step * CHUNK, CHUNK)
-            accum[:, pl.ds(at, CHUNK), :] = jnp.zeros((2, CHUNK, accum.shape[2]), jnp.float32)
+            accum[:, :, pl.ds(at, CHUNK), :] = jnp.zeros(
+                (2, accum.shape[1], CHUNK, LANES), jnp.float32
+            )
             return carry
 
-        lax.fori_loop(0, accum.shape[1] // CHUNK, clear, 0)
+        lax.fori_loop(0, accum.shape[2] // CHUNK, clear, 0)
 
         def invert(module, carry):
             inverse[order[module]] = module
@@ -221,13 +225,19 @@
         far_imag = far[0, 1, rows, :]
         sender = (module // per + senders - 1) % senders
         level = amp[sender, 0, module % per].astype(jnp.float32)
-        magnitude = jnp.sqrt(far_real * far_real + far_imag * far_imag)
-        factor = level / jnp.maximum(magnitude, 0.25) - 1.0
+        inverse_size = lax.rsqrt(far_real * far_real + far_imag * far_imag)
+        factor = level * jnp.minimum(inverse_size, 4.0) - 1.0
         corr[rows, :] = (factor * far_real).astype(jnp.bfloat16)
         corr[pl.ds(size + at, height), :] = (factor * far_imag).astype(jnp.bfloat16)
         return carry
 
-    lax.fori_loop(0, modules, correct, 0)
+    lax.fori_loop(0, modules, correct, 0, unroll=4)
+
+    @pl.when(slot == 0)
+    def _():
+        for move in table_copies(tables, left, right, table_sems):
+            move.wait()
+
     for block in range(size // BLOCK):
         to = slice(block * BLOCK, (block + 1) * BLOCK)
         also = slice(size + block * BLOCK, size + (block + 1) * BLOCK)
@@ -243,14 +253,10 @@
             )
 
     lane = lax.broadcasted_iota(jnp.int32, (CHUNK, LANES), 1)
-    tiles = CHUNK // SUBLANES
-    sub = lax.broadcasted_iota(jnp.int32, (tiles + 1, SUBLANES, LANES), 1)
-    empty = jnp.zeros((1, SUBLANES, LANES), jnp.float32)
 
     def spread(step, carry):
         at = pl.multiple_of(step * CHUNK, CHUNK)
         rows = pl.ds(at, CHUNK)
-        start = pl.multiple_of(row_base + at, SUBLANES)
         last = [jnp.zeros((CHUNK, LANES), jnp.float32)] * 2
         for block in range(blocks + 1):
             if block < blocks:
@@ -279,20 +285,13 @@
                 now = [pltpu.roll(grad, lane_shift, axis=1) for grad in grads]
             else:
                 now = [jnp.zeros((CHUNK, LANES), jnp.float32)] * 2
-            col = pl.multiple_of(base + block * LANES, LANES)
             for plane in range(2):
                 placed = jnp.where(lane < lane_shift, last[plane], now[plane])
-                placed = pltpu.roll(placed.reshape(tiles, SUBLANES, LANES), row_shift, axis=1)
-                placed = jnp.where(
-                    sub < row_shift,
-                    jnp.concatenate([empty, placed], axis=0),
-                    jnp.concatenate([placed, empty], axis=0),
-                ).reshape(CHUNK + SUBLANES, LANES)
-                accum[plane, pl.ds(start, CHUNK + SUBLANES), pl.ds(col, LANES)] += placed
+                accum[plane, slot + block, pl.ds(row + at, CHUNK), :] += placed
             last = now
         return carry
 
-    lax.fori_loop(0, size // CHUNK, spread, 0)
+    lax.fori_loop(0, size // CHUNK, spread, 0, unroll=4)
 
 
 def whole(shape):
@@ -309,7 +308,7 @@
     return pl.BlockSpec((1,) + shape, lambda slot, *refs: (slot,) + (0,) * len(shape))
 
 
-def run_forward(offs, pieces, ill, cos_table, sin_table):
+def run_forward(offs, pieces, tables, ill):
     slots = offs.shape[0]
     size = ill.shape[-1]
     rows, cols, edge = pieces[2].shape[1], pieces[2].shape[2], pieces[3].shape[2]
@@ -319,31 +318,32 @@
         grid_spec=pltpu.PrefetchScalarGridSpec(
             num_scalar_prefetch=1,
             grid=(slots,),
-            in_specs=[pl.BlockSpec(memory_space=pl.ANY)] * len(pieces)
-            + [once(ill.shape), once(cos_table.shape), once(sin_table.shape)],
+            in_specs=[pl.BlockSpec(memory_space=pltpu.HBM)] * (len(pieces) + len(tables))
+            + [once(ill.shape)],
             out_specs=[
                 one_slot((2, size, size)),
                 one_slot((2, size, size)),
             ],
             scratch_shapes=[
-                pltpu.VMEM((2, 3 * rows, cols + 2 * edge), jnp.float32),
+                pltpu.VMEM((2, (cols + 2 * edge) // LANES, 3 * rows, LANES), jnp.float32),
                 pltpu.VMEM((2 * size, 2 * size), jnp.bfloat16),
                 pltpu.VMEM((2 * size, 2 * size), jnp.bfloat16),
                 pltpu.VMEM((2 * size, size), jnp.bfloat16),
                 pltpu.VMEM((size, 2 * size), jnp.bfloat16),
-                pltpu.SemaphoreType.DMA((9,)),
+                pltpu.SemaphoreType.DMA((24,)),
+                pltpu.SemaphoreType.DMA((8,)),
             ],
         ),
         out_shape=[planes, planes],
         cost_estimate=pl.CostEstimate(
             flops=slots * 16 * size**3, bytes_accessed=30_000_000, transcendentals=0
         ),
-        compiler_params=pltpu.CompilerParams(vmem_limit_bytes=48 * 1024 * 1024),
+        compiler_params=pltpu.CompilerParams(vmem_limit_bytes=67_000_000),
         name="forward",
-    )(offs, *pieces, ill, cos_table, sin_table)
-
-
-def run_backward(offs, order, far, patch, amp, ill, cos_table, sin_table, region_shape):
+    )(offs, *pieces, *tables, ill)
+
+
+def run_backward(offs, order, far, patch, amp, ill, tables, region_shape):
     slots = offs.shape[0]
     size = ill.shape[-1]
     senders, _, per, height, _ = amp.shape
@@ -360,9 +360,8 @@
                     (senders, 1, per, height, size), lambda slot, *refs: (0, slot, 0, 0, 0)
                 ),
                 once(ill.shape),
-                once(cos_table.shape),
-                once(sin_table.shape),
-            ],
+            ]
+            + [pl.BlockSpec(memory_space=pltpu.HBM)] * len(tables),
             out_specs=[whole(region_shape), whole(sums_shape)],
             scratch_shapes=[
                 pltpu.VMEM((2 * size, size), jnp.bfloat16),
@@ -371,6 +370,7 @@
                 pltpu.VMEM((2 * size, 2 * size), jnp.bfloat16),
                 pltpu.VMEM((2 * size, 2 * size), jnp.bfloat16),
                 pltpu.SMEM((senders * per,), jnp.int32),
+                pltpu.SemaphoreType.DMA((8,)),
             ],
         ),
         out_shape=[
@@ -380,9 +380,9 @@
         cost_estimate=pl.CostEstimate(
             flops=slots * 16 * size**3, bytes_accessed=30_000_000, transcendentals=0
         ),
-        compiler_params=pltpu.CompilerParams(vmem_limit_bytes=56 * 1024 * 1024),
+        compiler_params=pltpu.CompilerParams(vmem_limit_bytes=67_000_000),
         name="backward",
-    )(offs, order, far, patch, amp, ill, cos_table, sin_table)
+    )(offs, order, far, patch, amp, ill, *tables)
 
 
 def unpack_kernel(packed, out):
@@ -420,20 +420,28 @@
     grouped = measured.reshape(senders, slots, per, height, size)
     upper = passed_along(specimen, "row", 1)
     lower = passed_along(specimen, "row", -1)
+    early_offs = passed_along(scan_offsets[0, 0, :late], "row", 1)
+    late_offs = passed_both(scan_offsets[0, 0, late:], 1, 1)
+    offs = jnp.concatenate([late_offs, early_offs], axis=0)
     moved = passed_along(grouped[:, late:], "col", 1)
     west = passed_along(specimen[:, :, edge:], "col", 1)
     east = passed_along(specimen[:, :, :edge], "col", -1)
-    early_offs = passed_along(scan_offsets[0, 0, :late], "row", 1)
-    late_offs = passed_both(scan_offsets[0, 0, late:], 1, 1)
-    offs = jnp.concatenate([late_offs, early_offs], axis=0)
+    levels = jnp.concatenate([moved, grouped[:, :late]], axis=1)
     lane = lax.broadcasted_iota(jnp.int32, (devices, 1, LANES), 2)
     peak = jnp.max(jnp.abs(specimen))
     power = jnp.sum(specimen * specimen)
-    peaks = spread_out(jnp.where(lane < LANES // 2, peak, power))
+    stats = jnp.where(lane < LANES // 2, peak, power)
+    peaks = spread_out(stats)
     peak = jnp.maximum(jnp.max(peaks[:, :, : LANES // 2]), 1e-12)
     power = jnp.max(peaks[:, :, LANES // 2 :])
-    ill_power = jnp.sum(illumination * illumination)
-    ill_peak = jnp.maximum(jnp.max(jnp.abs(illumination)), 1e-8)
+    tables = dft_tables(size)
+    upper, lower, west, east, offs, levels, peak, power, probe = (
+        lax.optimization_barrier(
+            (upper, lower, west, east, offs, levels, peak, power, illumination)
+        )
+    )
+    ill_power = jnp.sum(probe * probe)
+    ill_peak = jnp.maximum(jnp.max(jnp.abs(probe)), 1e-8)
     modulus = 1.5 * peak
     energy = jnp.minimum(
         modulus * jnp.sqrt(ill_power), 1.5 * ill_peak * jnp.sqrt(6.0 * power)
@@ -443,17 +451,10 @@
     sum_bound = slots * modulus * change_bound
     density_bound = slots * modulus * modulus
     step_bound = math.sqrt(slots * devices) * change_bound
-    cos_table, sin_table = dft_tables(size)
-    bounds = (change_bound, grad_bound, sum_bound, density_bound, step_bound)
-    upper, lower, moved, west, east, offs, bounds = lax.optimization_barrier(
-        (upper, lower, moved, west, east, offs, bounds)
-    )
-    change_bound, grad_bound, sum_bound, density_bound, step_bound = bounds
     west_edges = jnp.concatenate([upper[:, :, edge:], lower[:, :, edge:]], axis=1)
     east_edges = jnp.concatenate([upper[:, :, :edge], lower[:, :, :edge]], axis=1)
     outer_west = passed_along(west_edges, "col", 1)
     outer_east = passed_along(east_edges, "col", -1)
-    levels = jnp.concatenate([moved, grouped[:, :late]], axis=1)
     arrived = lax.all_to_all(
         levels,
         "row",
@@ -463,13 +464,14 @@
         axis_index_groups=[[(sender + 1) % senders for sender in range(senders)]],
     )
     pieces = (upper, lower, specimen, west, east, outer_west, outer_east)
-    far, patch = run_forward(offs, pieces, illumination, cos_table, sin_table)
-    region_shape = (2, 3 * tile_rows, tile_cols + 2 * edge)
+    far, patch = run_forward(offs, pieces, tables, illumination)
+    region_shape = (2, (tile_cols + 2 * edge) // LANES, 3 * tile_rows, LANES)
     accum, sums = run_backward(
-        offs, module_row, far, patch, arrived, illumination, cos_table, sin_table, region_shape
-    )
-    to_west = narrowed(accum[:, :, :edge], grad_bound)
-    to_east = narrowed(accum[:, :, edge + tile_cols :], grad_bound)
+        offs, module_row, far, patch, arrived, illumination, tables, region_shape
+    )
+    side = edge // LANES
+    to_west = narrowed(accum[:, :side], grad_bound)
+    to_east = narrowed(accum[:, -side:], grad_bound)
     from_east = passed_along(to_west, "col", -1)
     from_west = passed_along(to_east, "col", 1)
     sums = sums.reshape(devices, 3 * PIECE, LANES)
@@ -477,11 +479,11 @@
     bounds = jnp.where(line < 2 * PIECE, sum_bound, density_bound)
     packed = narrowed(sums, bounds)
     parts = spread_out(packed)
-    column = accum[:, :, edge : edge + tile_cols] + jnp.concatenate(
-        [widened(from_west, grad_bound), widened(from_east, grad_bound)], axis=2
-    )
-    to_upper = narrowed(column[:, :tile_rows], grad_bound)
-    to_lower = narrowed(column[:, 2 * tile_rows :], grad_bound)
+    column = accum[:, side:-side] + jnp.concatenate(
+        [widened(from_west, grad_bound), widened(from_east, grad_bound)], axis=1
+    )
+    to_upper = narrowed(column[:, :, :tile_rows], grad_bound)
+    to_lower = narrowed(column[:, :, 2 * tile_rows :], grad_bound)
     from_lower = passed_along(to_upper, "row", -1)
     from_upper = passed_along(to_lower, "row", 1)
     total = jnp.sum(widened(parts, bounds), axis=0)
@@ -490,11 +492,12 @@
     copies = jnp.broadcast_to(mine, (devices, 2 * PIECE, LANES))
     result = spread_out(copies)
     illumination_step = unpacked(widened(result, step_bound), size)
-    specimen_step = (
-        column[:, tile_rows : 2 * tile_rows]
+    middle = (
+        column[:, :, tile_rows : 2 * tile_rows]
         + widened(from_lower, grad_bound)
         + widened(from_upper, grad_bound)
     )
+    specimen_step = middle.swapaxes(1, 2).reshape(2, tile_rows, tile_cols)
     return (specimen_step, illumination_step)
 
 

time: 232 us -> 229 us (0.987)
  Pallas kernels: 57.2 us -> 51 us
  waiting for transfers between devices: 79.6 us -> 85.4 us
  other arithmetic: 29.2 us -> 24.3 us
    pallas_call x1, Pallas kernels: 30.5 us -> 25.7 us  [run_backward(): pl.pallas_call(backward_kernel, grid_spec=pltpu.PrefetchScalarGridSpec(nu...]
    ppermute x1, waiting for transfers between devices: 16.2 us -> 20.4 us  [passed_both(): return lax.ppermute(value, ('row', 'col'), pairs)]
    all_to_all x3, waiting for transfers between devices: 5.57 us -> 9.12 us  [spread_out(): lax.all_to_all(value, ('row', 'col'), split_axis=0, concat_axis=0, tiled=...]
    add x2 -> x1, other arithmetic: 4.86 us -> 2.34 us  [shards(): accum[:, side:-side]]
    transpose x0 -> x1, other arithmetic: none -> 2.38 us  [shards(): specimen_step = middle.swapaxes(1, 2).reshape(2, tile_rows, tile_cols)]
  transfers between devices with their start and end apart: 17 -> 17, of which waited for: 7 -> 7; matrix products, arithmetic and copies ran while one was open for 11% -> 9% of each run, Pallas kernels for 10% -> 9%
where the time goes in v4:
time: 229 us; the launch traced here: 228 us
  waiting for transfers between devices  85.4 us (37%)
  starting transfers between devices  53 us (23%)
  Pallas kernels  51 us (22%)
  other arithmetic  24.3 us (11%)
  local copies, waits for them, and re-layouts  10.6 us (5%)
  between operations  3.52 us (2%)
    ppermute x12, waiting for transfers between devices, passed_along(): return lax.ppermute(value, axis, pairs)  55.9 us
    pallas_call x1, Pallas kernels, run_backward(): pl.pallas_call(backward_kernel, grid_spec=pltpu.PrefetchScalarGridSpec(nu...  25.7 us
    all_to_all x3, starting transfers between devices, spread_out(): lax.all_to_all(value, ('row', 'col'), split_axis=0, concat_axis=0, tiled=...  25.6 us
    ppermute x12, starting transfers between devices, passed_along(): return lax.ppermute(value, axis, pairs)  22.9 us
    pallas_call x1, Pallas kernels, run_forward(): pl.pallas_call(forward_kernel, grid_spec=pltpu.PrefetchScalarGridSpec(num...  21.5 us
    ppermute x1, waiting for transfers between devices, passed_both(): return lax.ppermute(value, ('row', 'col'), pairs)  20.4 us
    all_to_all x3, waiting for transfers between devices, spread_out(): lax.all_to_all(value, ('row', 'col'), split_axis=0, concat_axis=0, tiled=...  9.12 us
    convert_element_type x4, other arithmetic, narrowed(): return (value * (HALF_TOP / bound)).astype(jnp.float16)  5.12 us
  transfers between devices with their start and end apart: 17, of which 7 were waited for; matrix products, arithmetic and copies ran while one was open for 9% of the time, Pallas kernels for 9%

profile of v4, /device:TPU:1, one launch (start us, length us, event | category | flops | bytes accessed | tf_op | source)
XLA Modules:
  0.0 227.8 jit_solution(13031896207376867282)
XLA Ops:
  0.6 0.0 copy-start
  0.7 2.9 %fusion.9 = (bf16[16,2,2,16,512]{4,3,2,1,0:T(8,128)(2,1)}, bf16[16,2,2,16,512]{4,3,2,1,0:T(8,128)(2,1)S(1)}) fusion(bf16[16,4,2,16,512]{4,3,2,1,0:T(8,128)(2,1)} %bitcast.13), kind=kLoop, calls=%fused_computation.34 | loop fusion | bytes 4194304 | tf_op jit(solution)/shard_map/slice | solution.py:426
  3.5 2.7 %collective-permute-start.6 = (bf16[16,2,2,16,512]{4,3,2,1,0:T(8,128)(2,1)}, bf16[16,2,2,16,512]{4,3,2,1,0:T(8,128)(2,1)}, u32[]{:S(2)}, u32[]{:S(2)}) collective-permute-start(bf16[16,2,2,16,512]{4,3,2,1,0:T(8,128)(2,1)} %get-tuple-element.44), channel_id=1, source_target_pairs={{0,1},{1,2},{2,3},{3,4},{4,5},{5,6},{6,7},{7,0},{8,9},{9,10},{10,1... | collective-permute-start | bytes 3145736 | tf_op jit(solution)/shard_map/ppermute | solution.py:22
  6.2 1.2 collective-permute-start
  7.4 4.7 %collective-permute-start.1 = (f32[2,256,512]{2,1,0:T(8,128)S(1)}, f32[2,256,512]{2,1,0:T(8,128)}, u32[]{:S(2)}, u32[]{:S(2)}) collective-permute-start(f32[2,256,512]{2,1,0:T(8,128)S(1)} %copy-done), channel_id=1, source_target_pairs={{0,120},{8,0},{16,8},{24,16},{32,24},{40,32},{48,40},{56,48},{64,5... | collective-permute-start | bytes 3145736 | tf_op jit(solution)/shard_map/ppermute | solution.py:22
  12.1 0.1 fusion.13
  12.2 0.1 copy.20
  12.3 0.0 collective-permute-start.4
  12.3 0.1 copy.21
  12.4 0.0 collective-permute-start.5
  12.4 1.1 fusion.12
  13.5 20.4 %collective-permute-done.4 = s32[2,2]{1,0:T(2,128)S(1)} collective-permute-done((s32[2,2]{1,0:T(2,128)S(1)}, s32[2,2]{1,0:T(2,128)S(1)}, u32[]{:S(2)}, u32[]{:S(2)}) %collective-permute-start.4) | collective-permute-done | bytes 48 | tf_op jit(solution)/shard_map/ppermute | solution.py:32
  33.9 2.5 %collective-permute-start.2 = (f32[2,256,256]{2,1,0:T(8,128)}, f32[2,256,256]{2,1,0:T(8,128)}, u32[]{:S(2)}, u32[]{:S(2)}) collective-permute-start(f32[2,256,256]{2,1,0:T(8,128)} %get-tuple-element.51), channel_id=1, source_target_pairs={{0,1},{1,2},{2,3},{3,4},{4,5},{5,6},{6,7},{7,0},{8,9},{9,10},{10,1... | collective-permute-start | bytes 1572872 | tf_op jit(solution)/shard_map/ppermute | solution.py:22
  36.4 0.0 collective-permute-done.5
  36.4 0.7 collective-permute-start.3
  37.0 0.8 abs_reduce_fusion.1
  37.9 1.2 compare_select_fusion.1
  39.1 0.7 iota.14
  39.7 6.3 %all-to-all-start = ((f32[128,1,128]{2,1,0:T(1,128)}), f32[128,1,128]{2,1,0:T(1,128)S(1)}, u32[]{:S(2)}, u32[]{:S(2)}) async-start(f32[128,1,128]{2,1,0:T(1,128)} %iota.14), calls=%async_computation | async-start | bytes 131072 | tf_op jit(solution)/shard_map/all_to_all | solution.py:407
  46.1 0.6 pad_add_fusion.offs
  46.7 9.1 %all-to-all-done = f32[128,1,128]{2,1,0:T(1,128)S(1)} async-done(((f32[128,1,128]{2,1,0:T(1,128)}), f32[128,1,128]{2,1,0:T(1,128)S(1)}, u32[]{:S(2)}, u32[]{:S(2)}) %all-to-all-start) | async-done | bytes 65568 | tf_op jit(solution)/shard_map/all_to_all | solution.py:407
  55.8 0.8 slice_reduce_fusion
  57.3 0.0 collective-permute-done.6
  57.3 2.7 %pad_maximum_fusion = bf16[16,4,2,16,512]{4,3,2,1,0:T(8,128)(2,1)} fusion(bf16[16,2,2,16,512]{4,3,2,1,0:T(8,128)(2,1)S(1)} %get-tuple-element.45, bf16[16,2,2,16,512]{4,3,2,1,0:T(8,128)(2,1)} %collective-permute-done.6), kind=kLoop, calls=%fused_computation.3 | loop fusion | flops 1048576 | bytes 4194304 | tf_op jit(solution)/shard_map/concatenate | solution.py:429
  60.0 0.0 collective-permute-done.3.refs_4_
  60.0 0.0 collective-permute-done.refs_0_
  60.0 0.0 copy-start.3
  60.0 0.0 collective-permute-done.1.refs_1_
  60.0 1.7 fusion.10
  61.8 1.1 pad_maximum_fusion.2
  62.8 0.8 collective-permute-start.8
  63.6 4.6 %all-to-all-start.1 = ((bf16[16,4,2,16,512]{4,3,2,1,0:T(8,128)(2,1)}), bf16[16,4,2,16,512]{4,3,2,1,0:T(8,128)(2,1)}, u32[]{:S(2)}, u32[]{:S(2)}) async-start(bf16[16,4,2,16,512]{4,3,2,1,0:T(8,128)(2,1)} %pad_maximum_fusion), calls=%async_computation.1 | async-start | bytes 4194304 | tf_op jit(solution)/shard_map/all_to_all | solution.py:458
  68.2 1.1 pad_maximum_fusion.1
  69.2 1.3 collective-permute-start.7
  70.5 1.2 multiply_reduce_fusion.1
  73.6 4.0 %collective-permute-done.8.refs_6_ = f32[2,512,256]{2,1,0:T(8,128)} collective-permute-done((f32[2,512,256]{2,1,0:T(8,128)}, f32[2,512,256]{2,1,0:T(8,128)}, u32[]{:S(2)}, u32[]{:S(2)}) %collective-permute-start.8) | collective-permute-done | bytes 1048608 | tf_op jit(solution)/shard_map/ppermute | solution.py:22
  77.7 4.9 %collective-permute-done.7.refs_5_ = f32[2,512,256]{2,1,0:T(8,128)} collective-permute-done((f32[2,512,256]{2,1,0:T(8,128)}, f32[2,512,256]{2,1,0:T(8,128)}, u32[]{:S(2)}, u32[]{:S(2)}) %collective-permute-start.7) | collective-permute-done | bytes 1048608 | tf_op jit(solution)/shard_map/ppermute | solution.py:22
  82.6 21.5 %forward.1 = (f32[4,2,512,512]{3,2,1,0:T(8,128)}, f32[4,2,512,512]{3,2,1,0:T(8,128)}) custom-call(s32[4,2]{1,0:T(4,128)} %pad_add_fusion.offs, f32[2,256,512]{2,1,0:T(8,128)} %copy-done.3, f32[2,256,512]{2,1,0:T(8,128)} %collective-permute-done.1.refs_1_, f32[2,256,512]{2,1,0:T(8,128)} %refs_2_.1, f32[2,256,256]{2,1,0:T(8,128)} %collective-permute-done.2.refs_3_, ...), custom_call_target="tpu_custom_call" | custom-call | flops 8589934592 | bytes 30000000 | tf_op jit(solution)/shard_map/forward/pallas_call | solution.py:316
  104.0 0.0 all-to-all-done.1.amp
  104.1 25.7 %backward.1 = (f32[2,8,768,128]{3,2,1,0:T(8,128)}, f32[4,32,3,16,128]{4,3,2,1,0:T(8,128)}) custom-call(s32[4,2]{1,0:T(4,128)} %pad_add_fusion.offs, s32[32]{0:T(128)} %order.1, f32[4,2,512,512]{3,2,1,0:T(8,128)} %get-tuple-element.20.far, f32[4,2,512,512]{3,2,1,0:T(8,128)} %get-tuple-element.21.patch, bf16[16,4,2,16,512]{4,3,2,1,0:T(8,128)(2,1)} %all-to-all-done.1.amp, ...), custom_call_target="tpu_custom_call" | custom-call | flops 8589934592 | bytes 30000000 | tf_op jit(solution)/shard_map/backward/pallas_call | solution.py:351
  129.8 2.4 %multiply_convert_fusion.2 = (f16[2,2,768,128]{3,2,1,0:T(8,128)(2,1)S(1)}, f16[2,2,768,128]{3,2,1,0:T(8,128)(2,1)S(1)}) fusion(f32[2,8,768,128]{3,2,1,0:T(8,128)} %get-tuple-element.23, f32[]{:T(128)S(6)} %div.41), kind=kLoop, calls=%fused_computation.10 | loop fusion | flops 1572864 | bytes 4718596 | tf_op jit(solution)/shard_map/convert_element_type | solution.py:47
  132.2 2.5 %collective-permute-start.9 = (f16[2,2,768,128]{3,2,1,0:T(8,128)(2,1)S(1)}, f16[2,2,768,128]{3,2,1,0:T(8,128)(2,1)S(1)}, u32[]{:S(2)}, u32[]{:S(2)}) collective-permute-start(f16[2,2,768,128]{3,2,1,0:T(8,128)(2,1)S(1)} %get-tuple-element.40), channel_id=1, source_target_pairs={{0,1},{1,2},{2,3},{3,4},{4,5},{5,6},{6,7},{7,0},{8,9},{9,10},{10,1... | collective-permute-start | bytes 2359304 | tf_op jit(solution)/shard_map/ppermute | solution.py:22
  134.7 1.5 multiply_convert_fusion
  136.2 9.7 %all-to-all-start.2 = ((f16[128,48,128]{2,1,0:T(8,128)(2,1)}), f16[128,48,128]{2,1,0:T(8,128)(2,1)}, u32[]{:S(2)}, u32[]{:S(2)}) async-start(f16[128,48,128]{2,1,0:T(8,128)(2,1)} %multiply_convert_fusion), calls=%async_computation.2 | async-start | bytes 3145728 | tf_op jit(solution)/shard_map/all_to_all | solution.py:407
  145.9 1.1 collective-permute-start.10
  147.1 0.0 collective-permute-done.9
  147.1 0.1 convert_multiply_fusion.2
  147.2 25.2 %collective-permute-done.10 = f16[2,2,768,128]{3,2,1,0:T(8,128)(2,1)S(1)} collective-permute-done((f16[2,2,768,128]{3,2,1,0:T(8,128)(2,1)S(1)}, f16[2,2,768,128]{3,2,1,0:T(8,128)(2,1)S(1)}, u32[]{:S(2)}, u32[]{:S(2)}) %collective-permute-start.10) | collective-permute-done | bytes 786464 | tf_op jit(solution)/shard_map/ppermute | solution.py:22
  172.4 0.1 convert_multiply_fusion.1
  172.5 2.3 %maximum_add_fusion = f32[2,4,768,128]{3,2,1,0:T(8,128)S(1)} fusion(f32[2,2,768,128]{3,2,1,0:T(8,128)S(1)} %convert_multiply_fusion.1, f32[2,2,768,128]{3,2,1,0:T(8,128)S(1)} %convert_multiply_fusion.2, f32[2,8,768,128]{3,2,1,0:T(8,128)} %get-tuple-element.23), kind=kLoop, calls=%fused_computation | loop fusion | flops 1572864 | bytes 9437184 | tf_op jit(solution)/shard_map/add | solution.py:482
  174.8 1.9 multiply_reduce_fusion
  176.8 1.1 broadcast_in_dim.26
  177.9 9.5 %all-to-all-start.3 = ((f16[128,32,128]{2,1,0:T(8,128)(2,1)}), f16[128,32,128]{2,1,0:T(8,128)(2,1)}, u32[]{:S(2)}, u32[]{:S(2)}) async-start(f16[128,32,128]{2,1,0:T(8,128)(2,1)} %broadcast_in_dim.26), calls=%async_computation.3 | async-start | bytes 2097152 | tf_op jit(solution)/shard_map/all_to_all | solution.py:407
  187.5 1.2 fusion.1
  188.7 5.4 %collective-permute-start.11 = (f16[2,4,256,128]{3,2,1,0:T(8,128)(2,1)}, f16[2,4,256,128]{3,2,1,0:T(8,128)(2,1)}, u32[]{:S(2)}, u32[]{:S(2)}) collective-permute-start(f16[2,4,256,128]{3,2,1,0:T(8,128)(2,1)} %get-tuple-element.42), channel_id=1, source_target_pairs={{0,120},{8,0},{16,8},{24,16},{32,24},{40,32},{48,40},{56,48},{64,5... | collective-permute-start | bytes 1572872 | tf_op jit(solution)/shard_map/ppermute | solution.py:22
  194.1 0.0 collective-permute-start.12
  194.1 16.8 %collective-permute-done.11 = f16[2,4,256,128]{3,2,1,0:T(8,128)(2,1)} collective-permute-done((f16[2,4,256,128]{3,2,1,0:T(8,128)(2,1)}, f16[2,4,256,128]{3,2,1,0:T(8,128)(2,1)}, u32[]{:S(2)}, u32[]{:S(2)}) %collective-permute-start.11) | collective-permute-done | bytes 524320 | tf_op jit(solution)/shard_map/ppermute | solution.py:22
  210.9 5.0 %collective-permute-done.12 = f16[2,4,256,128]{3,2,1,0:T(8,128)(2,1)} collective-permute-done((f16[2,4,256,128]{3,2,1,0:T(8,128)(2,1)}, f16[2,4,256,128]{3,2,1,0:T(8,128)(2,1)}, u32[]{:S(2)}, u32[]{:S(2)}) %collective-permute-start.12) | collective-permute-done | bytes 524320 | tf_op jit(solution)/shard_map/ppermute | solution.py:22
  215.9 2.4 %fusion.3 = f32[2,256,4,128]{3,1,2,0:T(8,128)} fusion(f32[2,4,768,128]{3,2,1,0:T(8,128)S(1)} %maximum_add_fusion, f16[2,4,256,128]{3,2,1,0:T(8,128)(2,1)} %collective-permute-done.12, f16[2,4,256,128]{3,2,1,0:T(8,128)(2,1)} %collective-permute-done.11, f32[]{:T(128)S(6)} %div.42), kind=kLoop, calls=%fused_computation.17 | loop fusion | flops 1572864 | bytes 3145732 | tf_op jit(solution)/shard_map/transpose | solution.py:500
  218.3 1.6 copy.24
  219.8 1.3 copy.25
  221.1 0.0 all-to-all-done.3
  221.1 2.8 %convert_multiply_fusion = f32[128,32,128]{2,1,0:T(8,128)} fusion(f16[128,32,128]{2,1,0:T(8,128)(2,1)} %all-to-all-done.3, f32[]{:T(128)S(6)} %div.49), kind=kLoop, calls=%fused_computation.4 | loop fusion | flops 1048576 | bytes 3145732 | tf_op jit(solution)/shard_map/mul | solution.py:51
  224.0 3.8 %unpack.1 = f32[2,512,512]{2,1,0:T(8,128)} custom-call(f32[128,2,16,128]{3,2,1,0:T(8,128)} %bitcast.10), custom_call_target="tpu_custom_call" | custom-call | tf_op jit(solution)/shard_map/unpack/pallas_call | solution.py:396
  (14 shorter events, 0.1 us)
Async XLA Ops:
  0.6 5.6 %copy-start = (f32[2,256,512]{2,1,0:T(8,128)S(1)}, f32[2,256,512]{2,1,0:T(8,128)}, u32[]{:S(2)}) copy-start(f32[2,256,512]{2,1,0:T(8,128)} %refs_2_.1) | copy-start | bytes 3145732
  0.6 11.5 %copy-start.4 = (s32[1,1,4,2]{2,3,1,0:T(2,128)S(1)}, s32[1,1,4,2]{2,3,1,0:T(2,128)}, u32[]{:S(2)}) copy-start(s32[1,1,4,2]{2,3,1,0:T(2,128)} %param.10) | copy-start | bytes 100
  3.5 53.8 %collective-permute-start.6 = (bf16[16,2,2,16,512]{4,3,2,1,0:T(8,128)(2,1)}, bf16[16,2,2,16,512]{4,3,2,1,0:T(8,128)(2,1)}, u32[]{:S(2)}, u32[]{:S(2)}) collective-permute-start(bf16[16,2,2,16,512]{4,3,2,1,0:T(8,128)(2,1)} %get-tuple-element.44), channel_id=1, source_target_pairs={{0,1},{1,2},{2,3},{3,4},{4,5},{5,6},{6,7},{7,0},{8,9},{9,10},{10,1... | collective-permute-start | bytes 3145736 | tf_op jit(solution)/shard_map/ppermute | solution.py:22
  6.2 53.8 %collective-permute-start = (f32[2,256,512]{2,1,0:T(8,128)S(1)}, f32[2,256,512]{2,1,0:T(8,128)S(1)}, u32[]{:S(2)}, u32[]{:S(2)}) collective-permute-start(f32[2,256,512]{2,1,0:T(8,128)S(1)} %copy-done), channel_id=1, source_target_pairs={{0,8},{8,16},{16,24},{24,32},{32,40},{40,48},{48,56},{56,64},{64,7... | collective-permute-start | bytes 3145736 | tf_op jit(solution)/shard_map/ppermute | solution.py:22
  7.4 52.6 %collective-permute-start.1 = (f32[2,256,512]{2,1,0:T(8,128)S(1)}, f32[2,256,512]{2,1,0:T(8,128)}, u32[]{:S(2)}, u32[]{:S(2)}) collective-permute-start(f32[2,256,512]{2,1,0:T(8,128)S(1)} %copy-done), channel_id=1, source_target_pairs={{0,120},{8,0},{16,8},{24,16},{32,24},{40,32},{48,40},{56,48},{64,5... | collective-permute-start | bytes 3145736 | tf_op jit(solution)/shard_map/ppermute | solution.py:22
  12.3 21.5 %collective-permute-start.4 = (s32[2,2]{1,0:T(2,128)S(1)}, s32[2,2]{1,0:T(2,128)S(1)}, u32[]{:S(2)}, u32[]{:S(2)}) collective-permute-start(s32[2,2]{1,0:T(2,128)S(1)} %bitcast.15), channel_id=1, source_target_pairs={{0,9},{1,10},{2,11},{3,12},{4,13},{5,14},{6,15},{7,8},{8,17},{9,18... | collective-permute-start | bytes 56 | tf_op jit(solution)/shard_map/ppermute | solution.py:32
  12.4 24.0 %collective-permute-start.5 = (s32[2,2]{1,0:T(2,128)S(1)}, s32[2,2]{1,0:T(2,128)S(1)}, u32[]{:S(2)}, u32[]{:S(2)}) collective-permute-start(s32[2,2]{1,0:T(2,128)S(1)} %bitcast.14), channel_id=1, source_target_pairs={{0,8},{8,16},{16,24},{24,32},{32,40},{40,48},{48,56},{56,64},{64,7... | collective-permute-start | bytes 56 | tf_op jit(solution)/shard_map/ppermute | solution.py:22
  33.9 26.2 %collective-permute-start.2 = (f32[2,256,256]{2,1,0:T(8,128)}, f32[2,256,256]{2,1,0:T(8,128)}, u32[]{:S(2)}, u32[]{:S(2)}) collective-permute-start(f32[2,256,256]{2,1,0:T(8,128)} %get-tuple-element.51), channel_id=1, source_target_pairs={{0,1},{1,2},{2,3},{3,4},{4,5},{5,6},{6,7},{7,0},{8,9},{9,10},{10,1... | collective-permute-start | bytes 1572872 | tf_op jit(solution)/shard_map/ppermute | solution.py:22
  36.4 23.6 %collective-permute-start.3 = (f32[2,256,256]{2,1,0:T(8,128)}, f32[2,256,256]{2,1,0:T(8,128)}, u32[]{:S(2)}, u32[]{:S(2)}) collective-permute-start(f32[2,256,256]{2,1,0:T(8,128)} %get-tuple-element.50), channel_id=1, source_target_pairs={{0,7},{1,0},{2,1},{3,2},{4,3},{5,4},{6,5},{7,6},{8,15},{9,8},{10,9... | collective-permute-start | bytes 1572872 | tf_op jit(solution)/shard_map/ppermute | solution.py:22
  39.7 16.0 %all-to-all-start = ((f32[128,1,128]{2,1,0:T(1,128)}), f32[128,1,128]{2,1,0:T(1,128)S(1)}, u32[]{:S(2)}, u32[]{:S(2)}) async-start(f32[128,1,128]{2,1,0:T(1,128)} %iota.14), calls=%async_computation | async-start | bytes 131072 | tf_op jit(solution)/shard_map/all_to_all | solution.py:407
  60.0 3.6 %copy-start.3 = (f32[2,256,512]{2,1,0:T(8,128)}, f32[2,256,512]{2,1,0:T(8,128)S(1)}, u32[]{:S(2)}) copy-start(f32[2,256,512]{2,1,0:T(8,128)S(1)} %collective-permute-done.refs_0_) | copy-start | bytes 3145732
  62.8 14.8 %collective-permute-start.8 = (f32[2,512,256]{2,1,0:T(8,128)}, f32[2,512,256]{2,1,0:T(8,128)}, u32[]{:S(2)}, u32[]{:S(2)}) collective-permute-start(f32[2,512,256]{2,1,0:T(8,128)} %pad_maximum_fusion.2), channel_id=1, source_target_pairs={{0,7},{1,0},{2,1},{3,2},{4,3},{5,4},{6,5},{7,6},{8,15},{9,8},{10,9... | collective-permute-start | bytes 3145736 | tf_op jit(solution)/shard_map/ppermute | solution.py:22
  63.6 40.4 %all-to-all-start.1 = ((bf16[16,4,2,16,512]{4,3,2,1,0:T(8,128)(2,1)}), bf16[16,4,2,16,512]{4,3,2,1,0:T(8,128)(2,1)}, u32[]{:S(2)}, u32[]{:S(2)}) async-start(bf16[16,4,2,16,512]{4,3,2,1,0:T(8,128)(2,1)} %pad_maximum_fusion), calls=%async_computation.1 | async-start | bytes 4194304 | tf_op jit(solution)/shard_map/all_to_all | solution.py:458
  68.2 2.3 %copy-start.2 = (f32[2,512,512]{2,1,0:T(8,128)S(1)}, f32[2,512,512]{2,1,0:T(8,128)}, u32[]{:S(2)}) copy-start(f32[2,512,512]{2,1,0:T(8,128)} %ill.1) | copy-start | bytes 6291460
  69.2 13.3 %collective-permute-start.7 = (f32[2,512,256]{2,1,0:T(8,128)}, f32[2,512,256]{2,1,0:T(8,128)}, u32[]{:S(2)}, u32[]{:S(2)}) collective-permute-start(f32[2,512,256]{2,1,0:T(8,128)} %pad_maximum_fusion.1), channel_id=1, source_target_pairs={{0,1},{1,2},{2,3},{3,4},{4,5},{5,6},{6,7},{7,0},{8,9},{9,10},{10,1... | collective-permute-start | bytes 3145736 | tf_op jit(solution)/shard_map/ppermute | solution.py:22
  129.8 4.9 %copy-start.1 = (f32[4,32,3,16,128]{4,3,2,1,0:T(8,128)S(1)}, f32[4,32,3,16,128]{4,3,2,1,0:T(8,128)}, u32[]{:S(2)}) copy-start(f32[4,32,3,16,128]{4,3,2,1,0:T(8,128)} %get-tuple-element.27) | copy-start | bytes 9437188
  132.2 14.9 %collective-permute-start.9 = (f16[2,2,768,128]{3,2,1,0:T(8,128)(2,1)S(1)}, f16[2,2,768,128]{3,2,1,0:T(8,128)(2,1)S(1)}, u32[]{:S(2)}, u32[]{:S(2)}) collective-permute-start(f16[2,2,768,128]{3,2,1,0:T(8,128)(2,1)S(1)} %get-tuple-element.40), channel_id=1, source_target_pairs={{0,1},{1,2},{2,3},{3,4},{4,5},{5,6},{6,7},{7,0},{8,9},{9,10},{10,1... | collective-permute-start | bytes 2359304 | tf_op jit(solution)/shard_map/ppermute | solution.py:22
  136.2 38.7 %all-to-all-start.2 = ((f16[128,48,128]{2,1,0:T(8,128)(2,1)}), f16[128,48,128]{2,1,0:T(8,128)(2,1)}, u32[]{:S(2)}, u32[]{:S(2)}) async-start(f16[128,48,128]{2,1,0:T(8,128)(2,1)} %multiply_convert_fusion), calls=%async_computation.2 | async-start | bytes 3145728 | tf_op jit(solution)/shard_map/all_to_all | solution.py:407
  145.9 26.5 %collective-permute-start.10 = (f16[2,2,768,128]{3,2,1,0:T(8,128)(2,1)S(1)}, f16[2,2,768,128]{3,2,1,0:T(8,128)(2,1)S(1)}, u32[]{:S(2)}, u32[]{:S(2)}) collective-permute-start(f16[2,2,768,128]{3,2,1,0:T(8,128)(2,1)S(1)} %get-tuple-element.41), channel_id=1, source_target_pairs={{0,7},{1,0},{2,1},{3,2},{4,3},{5,4},{6,5},{7,6},{8,15},{9,8},{10,9... | collective-permute-start | bytes 2359304 | tf_op jit(solution)/shard_map/ppermute | solution.py:22
  177.9 43.2 %all-to-all-start.3 = ((f16[128,32,128]{2,1,0:T(8,128)(2,1)}), f16[128,32,128]{2,1,0:T(8,128)(2,1)}, u32[]{:S(2)}, u32[]{:S(2)}) async-start(f16[128,32,128]{2,1,0:T(8,128)(2,1)} %broadcast_in_dim.26), calls=%async_computation.3 | async-start | bytes 2097152 | tf_op jit(solution)/shard_map/all_to_all | solution.py:407
  188.7 22.2 %collective-permute-start.11 = (f16[2,4,256,128]{3,2,1,0:T(8,128)(2,1)}, f16[2,4,256,128]{3,2,1,0:T(8,128)(2,1)}, u32[]{:S(2)}, u32[]{:S(2)}) collective-permute-start(f16[2,4,256,128]{3,2,1,0:T(8,128)(2,1)} %get-tuple-element.42), channel_id=1, source_target_pairs={{0,120},{8,0},{16,8},{24,16},{32,24},{40,32},{48,40},{56,48},{64,5... | collective-permute-start | bytes 1572872 | tf_op jit(solution)/shard_map/ppermute | solution.py:22
  194.1 21.8 %collective-permute-start.12 = (f16[2,4,256,128]{3,2,1,0:T(8,128)(2,1)}, f16[2,4,256,128]{3,2,1,0:T(8,128)(2,1)}, u32[]{:S(2)}, u32[]{:S(2)}) collective-permute-start(f16[2,4,256,128]{3,2,1,0:T(8,128)(2,1)} %get-tuple-element.43), channel_id=1, source_target_pairs={{0,8},{8,16},{16,24},{24,32},{32,40},{40,48},{48,56},{56,64},{64,7... | collective-permute-start | bytes 1572872 | tf_op jit(solution)/shard_map/ppermute | solution.py:22

commit v5 on v4

--- a/solution.py
+++ b/solution.py
@@ -10,10 +10,10 @@
 
 
 LANES = 128
+SUBLANES = 8
 CHUNK = 32
 BLOCK = 256
 PIECE = 16
-HALF_TOP = 65504.0
 
 
 def passed_along(value, axis, steps):
@@ -43,12 +43,32 @@
     return tuple(jnp.asarray(table, jnp.bfloat16) for table in tables)
 
 
-def narrowed(value, bound):
-    return (value * (HALF_TOP / bound)).astype(jnp.float16)
-
-
-def widened(value, bound):
-    return value.astype(jnp.float32) * (bound / HALF_TOP)
+def exponent(bound):
+    return jnp.ceil(jnp.log2(jnp.maximum(bound, 1e-30))) + 1.0
+
+
+def narrowed(value, power):
+    return (value * jnp.exp2(15.0 - power)).astype(jnp.float16)
+
+
+def widened(value, power):
+    return value.astype(jnp.float32) * jnp.exp2(power - 15.0)
+
+
+def relabelled(value, power):
+    line = lax.broadcasted_iota(jnp.int32, (value.shape[-2], 1), 0)
+    body = value.shape[-2] - SUBLANES
+    return (value * jnp.where(line < body, jnp.exp2(15.0 - power), 1.0)).astype(jnp.float16)
+
+
+def labelled(value, power):
+    label = jnp.broadcast_to(power, value.shape[:-2] + (SUBLANES, value.shape[-1]))
+    return jnp.concatenate([narrowed(value, power), label.astype(jnp.float16)], axis=-2)
+
+
+def opened(value):
+    power = value[(0,) * (value.ndim - 2) + (-1, 0)].astype(jnp.float32)
+    return widened(value[..., :-SUBLANES, :], power), power
 
 
 def table_copies(tables, left, right, sems):
@@ -99,9 +119,16 @@
     return copies
 
 
+def folded(block, combine):
+    parts = [block[at : at + SUBLANES] for at in range(0, block.shape[0], SUBLANES)]
+    while len(parts) > 1:
+        parts = [combine(*pair) for pair in zip(parts[::2], parts[1::2])]
+    return parts[0]
+
+
 def forward_kernel(offs, *refs):
     pieces, tables, refs = refs[:7], refs[7:10], refs[10:]
-    ill, far, patch, region, left, right, wave, half, region_sems, table_sems = refs
+    ill, far, patch, stats, region, left, right, wave, half, region_sems, table_sems = refs
     slot = pl.program_id(0)
     size = ill.shape[-1]
     row = offs[slot, 0]
@@ -115,10 +142,12 @@
         table_moves = table_copies(tables, left, right, table_sems)
         for move in region_moves + table_moves:
             move.start()
-        for move in region_moves + table_moves:
+        stats[...] = jnp.zeros_like(stats)
+        for move in region_moves:
             move.wait()
 
     def extract(step, carry):
+        peak, power = carry
         at = pl.multiple_of(step * CHUNK, CHUNK)
         last = [None, None]
         for block in range(blocks + 1):
@@ -140,16 +169,26 @@
                 patch[0, 1, pl.ds(at, CHUNK), to] = spec_imag
                 ill_real = ill[0, pl.ds(at, CHUNK), to]
                 ill_imag = ill[1, pl.ds(at, CHUNK), to]
-                wave[pl.ds(at, CHUNK), to] = (
-                    ill_real * spec_real - ill_imag * spec_imag
-                ).astype(jnp.bfloat16)
-                wave[pl.ds(size + at, CHUNK), to] = (
-                    ill_real * spec_imag + ill_imag * spec_real
-                ).astype(jnp.bfloat16)
+                wave_real = ill_real * spec_real - ill_imag * spec_imag
+                wave_imag = ill_real * spec_imag + ill_imag * spec_real
+                wave[pl.ds(at, CHUNK), to] = wave_real.astype(jnp.bfloat16)
+                wave[pl.ds(size + at, CHUNK), to] = wave_imag.astype(jnp.bfloat16)
+                most = jnp.maximum(jnp.abs(spec_real), jnp.abs(spec_imag))
+                peak = jnp.maximum(peak, folded(most, jnp.maximum))
+                power = power + folded(wave_real * wave_real + wave_imag * wave_imag, jnp.add)
             last = now
-        return carry
-
-    lax.fori_loop(0, size // CHUNK, extract, 0, unroll=4)
+        return peak, power
+
+    empty = jnp.zeros((SUBLANES, LANES), jnp.float32)
+    peak, power = lax.fori_loop(0, size // CHUNK, extract, (empty, empty), unroll=4)
+    stats[0] = jnp.maximum(stats[0], peak)
+    stats[1] = stats[1] + power
+
+    @pl.when(slot == 0)
+    def _():
+        for move in table_copies(tables, left, right, table_sems):
+            move.wait()
+
     for block in range(size // BLOCK):
         to = slice(block * BLOCK, (block + 1) * BLOCK)
         also = slice(size + block * BLOCK, size + (block + 1) * BLOCK)
@@ -168,6 +207,7 @@
 def backward_kernel(
     offs,
     order,
+    powers,
     far,
     patch,
     amp,
@@ -201,6 +241,12 @@
         for move in table_copies(tables, left, right, table_sems):
             move.start()
         sums[...] = jnp.zeros_like(sums)
+        label_line = lax.broadcasted_iota(jnp.int32, sums.shape[:2] + (SUBLANES, LANES), 2)
+        sums[:, :, 3 * PIECE :, :] = jnp.where(label_line == 0, powers[0], powers[1])
+        height_all = accum.shape[2] - SUBLANES
+        accum[:, :, height_all:, :] = jnp.full(
+            accum.shape[:2] + (SUBLANES, LANES), powers[2], jnp.float32
+        )
 
         def clear(step, carry):
             at = pl.multiple_of(step * CHUNK, CHUNK)
@@ -209,7 +255,7 @@
             )
             return carry
 
-        lax.fori_loop(0, accum.shape[2] // CHUNK, clear, 0)
+        lax.fori_loop(0, height_all // CHUNK, clear, 0)
 
         def invert(module, carry):
             inverse[order[module]] = module
@@ -269,13 +315,13 @@
                 ill_imag = ill[1, rows, to]
                 places = pl.ds(step * (CHUNK // PIECE), CHUNK // PIECE)
                 pieces = (CHUNK // PIECE, PIECE, LANES)
-                sums[block, places, 0] += (spec_real * chg_real + spec_imag * chg_imag).reshape(
+                sums[block, places, :PIECE] += (spec_real * chg_real + spec_imag * chg_imag).reshape(
                     pieces
                 )
-                sums[block, places, 1] += (spec_real * chg_imag - spec_imag * chg_real).reshape(
+                sums[block, places, PIECE : 2 * PIECE] += (spec_real * chg_imag - spec_imag * chg_real).reshape(
                     pieces
                 )
-                sums[block, places, 2] += (spec_real * spec_real + spec_imag * spec_imag).reshape(
+                sums[block, places, 2 * PIECE : 3 * PIECE] += (spec_real * spec_real + spec_imag * spec_imag).reshape(
                     pieces
                 )
                 grads = (
@@ -323,6 +369,7 @@
             out_specs=[
                 one_slot((2, size, size)),
                 one_slot((2, size, size)),
+                whole((2, SUBLANES, LANES)),
             ],
             scratch_shapes=[
                 pltpu.VMEM((2, (cols + 2 * edge) // LANES, 3 * rows, LANES), jnp.float32),
@@ -334,7 +381,7 @@
                 pltpu.SemaphoreType.DMA((8,)),
             ],
         ),
-        out_shape=[planes, planes],
+        out_shape=[planes, planes, jax.ShapeDtypeStruct((2, SUBLANES, LANES), jnp.float32)],
         cost_estimate=pl.CostEstimate(
             flops=slots * 16 * size**3, bytes_accessed=30_000_000, transcendentals=0
         ),
@@ -343,15 +390,15 @@
     )(offs, *pieces, *tables, ill)
 
 
-def run_backward(offs, order, far, patch, amp, ill, tables, region_shape):
+def run_backward(offs, order, powers, far, patch, amp, ill, tables, region_shape):
     slots = offs.shape[0]
     size = ill.shape[-1]
     senders, _, per, height, _ = amp.shape
-    sums_shape = (size // LANES, size // PIECE, 3, PIECE, LANES)
+    sums_shape = (size // LANES, size // PIECE, 3 * PIECE + SUBLANES, LANES)
     return pl.pallas_call(
         backward_kernel,
         grid_spec=pltpu.PrefetchScalarGridSpec(
-            num_scalar_prefetch=2,
+            num_scalar_prefetch=3,
             grid=(slots,),
             in_specs=[
                 one_slot((2, size, size)),
@@ -382,7 +429,7 @@
         ),
         compiler_params=pltpu.CompilerParams(vmem_limit_bytes=67_000_000),
         name="backward",
-    )(offs, order, far, patch, amp, ill, *tables)
+    )(offs, order, powers, far, patch, amp, ill, *tables)
 
 
 def unpack_kernel(packed, out):
@@ -427,30 +474,11 @@
     west = passed_along(specimen[:, :, edge:], "col", 1)
     east = passed_along(specimen[:, :, :edge], "col", -1)
     levels = jnp.concatenate([moved, grouped[:, :late]], axis=1)
-    lane = lax.broadcasted_iota(jnp.int32, (devices, 1, LANES), 2)
-    peak = jnp.max(jnp.abs(specimen))
-    power = jnp.sum(specimen * specimen)
-    stats = jnp.where(lane < LANES // 2, peak, power)
-    peaks = spread_out(stats)
-    peak = jnp.maximum(jnp.max(peaks[:, :, : LANES // 2]), 1e-12)
-    power = jnp.max(peaks[:, :, LANES // 2 :])
     tables = dft_tables(size)
-    upper, lower, west, east, offs, levels, peak, power, probe = (
-        lax.optimization_barrier(
-            (upper, lower, west, east, offs, levels, peak, power, illumination)
-        )
-    )
-    ill_power = jnp.sum(probe * probe)
-    ill_peak = jnp.maximum(jnp.max(jnp.abs(probe)), 1e-8)
-    modulus = 1.5 * peak
-    energy = jnp.minimum(
-        modulus * jnp.sqrt(ill_power), 1.5 * ill_peak * jnp.sqrt(6.0 * power)
-    )
-    change_bound = 9.0 * jnp.maximum(energy, 1e-20)
-    grad_bound = 24.0 * ill_peak * change_bound
-    sum_bound = slots * modulus * change_bound
-    density_bound = slots * modulus * modulus
-    step_bound = math.sqrt(slots * devices) * change_bound
+    upper, lower, west, east, offs, levels, probe = lax.optimization_barrier(
+        (upper, lower, west, east, offs, levels, illumination)
+    )
+    ill_power = exponent(2.0 * jnp.max(jnp.abs(probe)))
     west_edges = jnp.concatenate([upper[:, :, edge:], lower[:, :, edge:]], axis=1)
     east_edges = jnp.concatenate([upper[:, :, :edge], lower[:, :, :edge]], axis=1)
     outer_west = passed_along(west_edges, "col", 1)
@@ -464,38 +492,55 @@
         axis_index_groups=[[(sender + 1) % senders for sender in range(senders)]],
     )
     pieces = (upper, lower, specimen, west, east, outer_west, outer_east)
-    far, patch = run_forward(offs, pieces, tables, illumination)
-    region_shape = (2, (tile_cols + 2 * edge) // LANES, 3 * tile_rows, LANES)
+    far, patch, stats = run_forward(offs, pieces, tables, illumination)
+    patch_power = exponent(1.5 * jnp.max(stats[0]))
+    change_power = exponent(12.0 * jnp.sqrt(jnp.sum(stats[1])))
+    home_power = ill_power + change_power + 1.0
+    region_shape = (2, (tile_cols + 2 * edge) // LANES, 3 * tile_rows + SUBLANES, LANES)
+    powers = jnp.stack([patch_power, change_power, home_power])
     accum, sums = run_backward(
-        offs, module_row, far, patch, arrived, illumination, tables, region_shape
+        offs, module_row, powers, far, patch, arrived, illumination, tables, region_shape
     )
     side = edge // LANES
-    to_west = narrowed(accum[:, :side], grad_bound)
-    to_east = narrowed(accum[:, -side:], grad_bound)
+    to_west = relabelled(accum[:, :side], home_power)
+    to_east = relabelled(accum[:, -side:], home_power)
     from_east = passed_along(to_west, "col", -1)
     from_west = passed_along(to_east, "col", 1)
-    sums = sums.reshape(devices, 3 * PIECE, LANES)
-    line = lax.broadcasted_iota(jnp.int32, (1, 3 * PIECE, 1), 1)
-    bounds = jnp.where(line < 2 * PIECE, sum_bound, density_bound)
-    packed = narrowed(sums, bounds)
+    sums = sums.reshape(devices, 3 * PIECE + SUBLANES, LANES)
+    line = lax.broadcasted_iota(jnp.int32, (1, 3 * PIECE + SUBLANES, 1), 1)
+    scales = jnp.where(
+        line < 2 * PIECE,
+        jnp.exp2(14.0 - patch_power - change_power),
+        jnp.where(line < 3 * PIECE, jnp.exp2(13.0 - 2.0 * patch_power), 1.0),
+    )
+    packed = (sums * scales).astype(jnp.float16)
     parts = spread_out(packed)
-    column = accum[:, side:-side] + jnp.concatenate(
-        [widened(from_west, grad_bound), widened(from_east, grad_bound)], axis=1
-    )
-    to_upper = narrowed(column[:, :, :tile_rows], grad_bound)
-    to_lower = narrowed(column[:, :, 2 * tile_rows :], grad_bound)
+    body = 3 * tile_rows
+    from_west, west_power = opened(from_west)
+    from_east, east_power = opened(from_east)
+    column = accum[:, side:-side, :body] + jnp.concatenate([from_west, from_east], axis=1)
+    column_power = jnp.maximum(jnp.maximum(west_power, east_power), home_power) + 2.0
+    to_upper = labelled(column[:, :, :tile_rows], column_power)
+    to_lower = labelled(column[:, :, 2 * tile_rows : body], column_power)
     from_lower = passed_along(to_upper, "row", -1)
     from_upper = passed_along(to_lower, "row", 1)
-    total = jnp.sum(widened(parts, bounds), axis=0)
+    labels = parts[:, 3 * PIECE :].astype(jnp.float32)
+    patch_powers, change_powers = labels[:, :1, :1], labels[:, 1:2, :1]
+    line = line[:, : 3 * PIECE]
+    powers = jnp.where(
+        line < 2 * PIECE, patch_powers + change_powers + 1.0, 2.0 * patch_powers + 2.0
+    )
+    total = jnp.sum(widened(parts[:, : 3 * PIECE], powers), axis=0)
     mine = total[: 2 * PIECE].reshape(2, PIECE, LANES) / jnp.sqrt(total[2 * PIECE :] + 1e-06)
-    mine = narrowed(mine, step_bound).reshape(1, 2 * PIECE, LANES)
+    step_power = jnp.max(change_powers) + math.ceil(0.5 * math.log2(slots * devices))
+    mine = narrowed(mine, step_power).reshape(1, 2 * PIECE, LANES)
     copies = jnp.broadcast_to(mine, (devices, 2 * PIECE, LANES))
     result = spread_out(copies)
-    illumination_step = unpacked(widened(result, step_bound), size)
+    illumination_step = unpacked(widened(result, step_power), size)
     middle = (
         column[:, :, tile_rows : 2 * tile_rows]
-        + widened(from_lower, grad_bound)
-        + widened(from_upper, grad_bound)
+        + opened(from_lower)[0]
+        + opened(from_upper)[0]
     )
     specimen_step = middle.swapaxes(1, 2).reshape(2, tile_rows, tile_cols)
     return (specimen_step, illumination_step)

time: 229 us -> 219 us (0.956)
  waiting for transfers between devices: 85.4 us -> 78.5 us
  starting transfers between devices: 53 us -> 46.5 us
  between operations: 3.52 us -> 6.93 us
    all_to_all x3 -> x2, waiting for transfers between devices: 9.12 us -> 0.01 us  [spread_out(): lax.all_to_all(value, ('row', 'col'), split_axis=0, concat_axis=0, tiled=...]
    all_to_all x3 -> x2, starting transfers between devices: 25.6 us -> 21.2 us  [spread_out(): lax.all_to_all(value, ('row', 'col'), split_axis=0, concat_axis=0, tiled=...]
    convert_element_type x4 -> x5, other arithmetic: 5.12 us -> 7.23 us  [the longest x1 3.69 us: shards(): packed = (sums * scales).astype(jnp.float16)]
  transfers between devices with their start and end apart: 17 -> 16, of which waited for: 7 -> 9; matrix products, arithmetic and copies ran while one was open for 9% -> 9% of each run, Pallas kernels for 9% -> 9%
where the time goes in v5:
time: 219 us; the launch traced here: 218 us
  waiting for transfers between devices  78.5 us (36%)
  Pallas kernels  50.2 us (23%)
  starting transfers between devices  46.5 us (21%)
  other arithmetic  24.6 us (11%)
  local copies, waits for them, and re-layouts  11.4 us (5%)
  between operations  6.93 us (3%)
    ppermute x12, waiting for transfers between devices, passed_along(): return lax.ppermute(value, axis, pairs)  57.1 us
    pallas_call x1, Pallas kernels, run_backward(): pl.pallas_call(backward_kernel, grid_spec=pltpu.PrefetchScalarGridSpec(nu...  25.9 us
    ppermute x1, waiting for transfers between devices, passed_both(): return lax.ppermute(value, ('row', 'col'), pairs)  21.4 us
    all_to_all x2, starting transfers between devices, spread_out(): lax.all_to_all(value, ('row', 'col'), split_axis=0, concat_axis=0, tiled=...  21.2 us
    ppermute x12, starting transfers between devices, passed_along(): return lax.ppermute(value, axis, pairs)  20.8 us
    pallas_call x1, Pallas kernels, run_forward(): pl.pallas_call(forward_kernel, grid_spec=pltpu.PrefetchScalarGridSpec(num...  20.5 us
    all_to_all x1, starting transfers between devices, shards(): lax.all_to_all(levels, 'row', split_axis=0, concat_axis=0, tiled=True, ax...  4.47 us
  transfers between devices with their start and end apart: 16, of which 9 were waited for; matrix products, arithmetic and copies ran while one was open for 9% of the time, Pallas kernels for 9%

profile of v5, /device:TPU:1, one launch (start us, length us, event | category | flops | bytes accessed | tf_op | source)
XLA Modules:
  0.0 218.2 jit_solution(13039414530871509668)
XLA Ops:
  0.6 0.0 copy-start.1
  0.7 2.9 %fusion.9 = (bf16[16,2,2,16,512]{4,3,2,1,0:T(8,128)(2,1)}, bf16[16,2,2,16,512]{4,3,2,1,0:T(8,128)(2,1)S(1)}) fusion(bf16[16,4,2,16,512]{4,3,2,1,0:T(8,128)(2,1)} %bitcast.25), kind=kLoop, calls=%fused_computation.39 | loop fusion | bytes 4194304 | tf_op jit(solution)/shard_map/slice | solution.py:473
  3.5 2.7 %collective-permute-start.6 = (bf16[16,2,2,16,512]{4,3,2,1,0:T(8,128)(2,1)}, bf16[16,2,2,16,512]{4,3,2,1,0:T(8,128)(2,1)}, u32[]{:S(2)}, u32[]{:S(2)}) collective-permute-start(bf16[16,2,2,16,512]{4,3,2,1,0:T(8,128)(2,1)} %get-tuple-element.41), channel_id=1, source_target_pairs={{0,1},{1,2},{2,3},{3,4},{4,5},{5,6},{6,7},{7,0},{8,9},{9,10},{10,1... | collective-permute-start | bytes 3145736 | tf_op jit(solution)/shard_map/ppermute | solution.py:22
  6.2 1.2 collective-permute-start
  7.4 4.7 %collective-permute-start.1 = (f32[2,256,512]{2,1,0:T(8,128)S(1)}, f32[2,256,512]{2,1,0:T(8,128)}, u32[]{:S(2)}, u32[]{:S(2)}) collective-permute-start(f32[2,256,512]{2,1,0:T(8,128)S(1)} %copy-done.1), channel_id=1, source_target_pairs={{0,120},{8,0},{16,8},{24,16},{32,24},{40,32},{48,40},{56,48},{64,5... | collective-permute-start | bytes 3145736 | tf_op jit(solution)/shard_map/ppermute | solution.py:22
  12.1 0.1 fusion.13
  12.2 0.1 copy.22
  12.3 0.0 collective-permute-start.4
  12.3 0.1 copy.23
  12.4 0.0 collective-permute-start.5
  12.4 0.1 fusion.12
  12.5 21.4 %collective-permute-done.4 = s32[2,2]{1,0:T(2,128)S(1)} collective-permute-done((s32[2,2]{1,0:T(2,128)S(1)}, s32[2,2]{1,0:T(2,128)S(1)}, u32[]{:S(2)}, u32[]{:S(2)}) %collective-permute-start.4) | collective-permute-done | bytes 48 | tf_op jit(solution)/shard_map/ppermute | solution.py:32
  33.9 2.5 %collective-permute-start.2 = (f32[2,256,256]{2,1,0:T(8,128)S(1)}, f32[2,256,256]{2,1,0:T(8,128)S(1)}, u32[]{:S(2)}, u32[]{:S(2)}) collective-permute-start(f32[2,256,256]{2,1,0:T(8,128)S(1)} %get-tuple-element.48), channel_id=1, source_target_pairs={{0,1},{1,2},{2,3},{3,4},{4,5},{5,6},{6,7},{7,0},{8,9},{9,10},{10,1... | collective-permute-start | bytes 1572872 | tf_op jit(solution)/shard_map/ppermute | solution.py:22
  36.4 0.0 collective-permute-done.5
  36.4 0.7 collective-permute-start.3
  37.0 0.5 pad_add_fusion.offs
  37.6 2.7 %pad_maximum_fusion = bf16[16,4,2,16,512]{4,3,2,1,0:T(8,128)(2,1)} fusion(bf16[16,2,2,16,512]{4,3,2,1,0:T(8,128)(2,1)S(1)} %get-tuple-element.42, bf16[16,2,2,16,512]{4,3,2,1,0:T(8,128)(2,1)} %collective-permute-done.6), kind=kLoop, calls=%fused_computation.4 | loop fusion | flops 1048576 | bytes 4194304 | tf_op jit(solution)/shard_map/concatenate | solution.py:476
  40.3 2.2 %collective-permute-done.2.refs_3_ = f32[2,256,256]{2,1,0:T(8,128)S(1)} collective-permute-done((f32[2,256,256]{2,1,0:T(8,128)S(1)}, f32[2,256,256]{2,1,0:T(8,128)S(1)}, u32[]{:S(2)}, u32[]{:S(2)}) %collective-permute-start.2) | collective-permute-done | bytes 524320 | tf_op jit(solution)/shard_map/ppermute | solution.py:22
  42.5 2.8 %collective-permute-done.3.refs_4_ = f32[2,256,256]{2,1,0:T(8,128)S(1)} collective-permute-done((f32[2,256,256]{2,1,0:T(8,128)S(1)}, f32[2,256,256]{2,1,0:T(8,128)S(1)}, u32[]{:S(2)}, u32[]{:S(2)}) %collective-permute-start.3) | collective-permute-done | bytes 524320 | tf_op jit(solution)/shard_map/ppermute | solution.py:22
  45.3 1.9 fusion.10
  47.2 0.1 pad_maximum_fusion.2
  47.3 1.8 collective-permute-start.8
  49.1 1.1 pad_maximum_fusion.1
  50.1 4.5 %all-to-all-start = ((bf16[16,4,2,16,512]{4,3,2,1,0:T(8,128)(2,1)}), bf16[16,4,2,16,512]{4,3,2,1,0:T(8,128)(2,1)}, u32[]{:S(2)}, u32[]{:S(2)}) async-start(bf16[16,4,2,16,512]{4,3,2,1,0:T(8,128)(2,1)} %pad_maximum_fusion), calls=%async_computation | async-start | bytes 4194304 | tf_op jit(solution)/shard_map/all_to_all | solution.py:486
  54.6 0.8 abs_reduce_fusion
  56.2 5.8 %collective-permute-done.8.refs_6_ = f32[2,512,256]{2,1,0:T(8,128)} collective-permute-done((f32[2,512,256]{2,1,0:T(8,128)S(1)}, f32[2,512,256]{2,1,0:T(8,128)}, u32[]{:S(2)}, u32[]{:S(2)}) %collective-permute-start.8) | collective-permute-done | bytes 1048608 | tf_op jit(solution)/shard_map/ppermute | solution.py:22
  62.0 0.3 collective-permute-done.7.refs_5_
  62.2 20.5 %forward.1 = (f32[4,2,512,512]{3,2,1,0:T(8,128)}, f32[4,2,512,512]{3,2,1,0:T(8,128)}, f32[2,8,128]{2,1,0:T(8,128)}) custom-call(s32[4,2]{1,0:T(4,128)} %pad_add_fusion.offs, f32[2,256,512]{2,1,0:T(8,128)} %copy-done.2, f32[2,256,512]{2,1,0:T(8,128)} %collective-permute-done.1.refs_1_, f32[2,256,512]{2,1,0:T(8,128)} %refs_2_.1, f32[2,256,256]{2,1,0:T(8,128)} %copy-done.4, ...), custom_call_target="tpu_custom_call" | custom-call | flops 8589934592 | bytes 30000000 | tf_op jit(solution)/shard_map/forward/pallas_call | solution.py:362
  82.7 1.3 slice_reduce_fusion.2
  85.5 0.6 pad_maximum_fusion.3.powers
  86.1 25.9 %backward.1 = (f32[2,8,776,128]{3,2,1,0:T(8,128)}, f32[4,32,56,128]{3,2,1,0:T(8,128)}) custom-call(s32[4,2]{1,0:T(4,128)} %pad_add_fusion.offs, s32[32]{0:T(128)} %order.1, f32[3]{0:T(128)} %pad_maximum_fusion.3.powers, f32[4,2,512,512]{3,2,1,0:T(8,128)} %get-tuple-element.21.far, f32[4,2,512,512]{3,2,1,0:T(8,128)} %get-tuple-element.22.patch, ...), custom_call_target="tpu_custom_call" | custom-call | flops 8589934592 | bytes 30000000 | tf_op jit(solution)/shard_map/backward/pallas_call | solution.py:398
  112.1 3.7 %fusion = f16[128,56,128]{2,1,0:T(8,128)(2,1)} fusion(f32[4,32,56,128]{3,2,1,0:T(8,128)} %get-tuple-element.25, f32[56]{0:T(128)S(1)} %compare_select_fusion.1), kind=kLoop, calls=%fused_computation.1 | loop fusion | flops 1835008 | bytes 5505248 | tf_op jit(solution)/shard_map/convert_element_type | solution.py:516
  115.8 11.0 %all-to-all-start.1 = ((f16[128,56,128]{2,1,0:T(8,128)(2,1)}), f16[128,56,128]{2,1,0:T(8,128)(2,1)}, u32[]{:S(2)}, u32[]{:S(2)}) async-start(f16[128,56,128]{2,1,0:T(8,128)(2,1)} %fusion), calls=%async_computation.1 | async-start | bytes 3670016 | tf_op jit(solution)/shard_map/all_to_all | solution.py:454
  126.7 2.3 %multiply_convert_fusion.1 = (f16[2,2,776,128]{3,2,1,0:T(8,128)(2,1)S(1)}, f16[2,2,776,128]{3,2,1,0:T(8,128)(2,1)S(1)}) fusion(f32[2,8,776,128]{3,2,1,0:T(8,128)} %get-tuple-element.24, f32[776]{0:T(1024)S(1)} %fusion.8), kind=kLoop, calls=%fused_computation.8 | loop fusion | flops 1589248 | bytes 4770848 | tf_op jit(solution)/shard_map/convert_element_type | solution.py:61
  129.0 1.7 collective-permute-start.9
  130.7 23.7 %collective-permute-done.9 = f16[2,2,776,128]{3,2,1,0:T(8,128)(2,1)S(1)} collective-permute-done((f16[2,2,776,128]{3,2,1,0:T(8,128)(2,1)S(1)}, f16[2,2,776,128]{3,2,1,0:T(8,128)(2,1)S(1)}, u32[]{:S(2)}, u32[]{:S(2)}) %collective-permute-start.9) | collective-permute-done | bytes 794656 | tf_op jit(solution)/shard_map/ppermute | solution.py:22
  154.4 0.5 slice.135
  155.5 1.0 collective-permute-done.10
  156.5 0.5 slice.137
  157.7 0.1 convert_multiply_fusion.2
  157.8 0.1 convert_multiply_fusion.1
  157.9 2.3 %maximum_add_fusion = f32[2,4,768,128]{3,2,1,0:T(8,128)S(1)} fusion(f32[2,2,768,128]{3,2,1,0:T(8,128)S(1)} %convert_multiply_fusion.1, f32[2,2,768,128]{3,2,1,0:T(8,128)S(1)} %convert_multiply_fusion.2, f32[2,8,776,128]{3,2,1,0:T(8,128)} %get-tuple-element.24), kind=kLoop, calls=%fused_computation.2 | loop fusion | flops 1572864 | bytes 9437184 | tf_op jit(solution)/shard_map/add | solution.py:521
  160.3 0.0 all-to-all-done.1
  160.3 1.0 slice_convert_fusion
  161.3 1.4 slice_reduce_fusion
  162.7 0.1 multiply_exponential_fusion
  162.8 2.1 multiply_reduce_fusion
  165.6 1.1 broadcast_in_dim.73
  166.7 10.3 %all-to-all-start.2 = ((f16[128,32,128]{2,1,0:T(8,128)(2,1)}), f16[128,32,128]{2,1,0:T(8,128)(2,1)}, u32[]{:S(2)}, u32[]{:S(2)}) async-start(f16[128,32,128]{2,1,0:T(8,128)(2,1)} %broadcast_in_dim.73), calls=%async_computation.2 | async-start | bytes 2097152 | tf_op jit(solution)/shard_map/all_to_all | solution.py:454
  177.0 0.3 fusion.2
  177.3 0.1 concatenate.26
  177.4 5.5 %collective-permute-start.11 = (f16[2,4,264,128]{3,2,1,0:T(8,128)(2,1)S(1)}, f16[2,4,264,128]{3,2,1,0:T(8,128)(2,1)S(1)}, u32[]{:S(2)}, u32[]{:S(2)}) collective-permute-start(f16[2,4,264,128]{3,2,1,0:T(8,128)(2,1)S(1)} %concatenate.26), channel_id=1, source_target_pairs={{0,120},{8,0},{16,8},{24,16},{32,24},{40,32},{48,40},{56,48},{64,5... | collective-permute-start | bytes 1622024 | tf_op jit(solution)/shard_map/ppermute | solution.py:22
  182.9 0.1 concatenate.27
  183.0 0.1 collective-permute-start.12
  183.1 17.7 %collective-permute-done.11 = f16[2,4,264,128]{3,2,1,0:T(8,128)(2,1)S(1)} collective-permute-done((f16[2,4,264,128]{3,2,1,0:T(8,128)(2,1)S(1)}, f16[2,4,264,128]{3,2,1,0:T(8,128)(2,1)S(1)}, u32[]{:S(2)}, u32[]{:S(2)}) %collective-permute-start.11) | collective-permute-done | bytes 540704 | tf_op jit(solution)/shard_map/ppermute | solution.py:22
  200.7 0.5 slice.141
  201.9 3.7 %collective-permute-done.12 = f16[2,4,264,128]{3,2,1,0:T(8,128)(2,1)S(1)} collective-permute-done((f16[2,4,264,128]{3,2,1,0:T(8,128)(2,1)S(1)}, f16[2,4,264,128]{3,2,1,0:T(8,128)(2,1)S(1)}, u32[]{:S(2)}, u32[]{:S(2)}) %collective-permute-start.12) | collective-permute-done | bytes 540704 | tf_op jit(solution)/shard_map/ppermute | solution.py:22
  205.7 0.5 slice.144
  206.9 1.2 fusion.4
  208.1 1.6 copy.24
  209.6 1.3 copy.25
  211.6 0.0 all-to-all-done.2
  211.6 2.9 %convert_multiply_fusion = f32[128,32,128]{2,1,0:T(8,128)} fusion(f16[128,32,128]{2,1,0:T(8,128)(2,1)} %all-to-all-done.2, f32[]{:T(128)S(6)} %exp2.125), kind=kLoop, calls=%fused_computation.5 | loop fusion | flops 1048576 | bytes 3145732 | tf_op jit(solution)/shard_map/mul | solution.py:55
  214.4 3.8 %unpack.1 = f32[2,512,512]{2,1,0:T(8,128)} custom-call(f32[128,2,16,128]{3,2,1,0:T(8,128)} %bitcast.23), custom_call_target="tpu_custom_call" | custom-call | tf_op jit(solution)/shard_map/unpack/pallas_call | solution.py:443
  (23 shorter events, 0.1 us)
Async XLA Ops:
  0.6 5.6 %copy-start.1 = (f32[2,256,512]{2,1,0:T(8,128)S(1)}, f32[2,256,512]{2,1,0:T(8,128)}, u32[]{:S(2)}) copy-start(f32[2,256,512]{2,1,0:T(8,128)} %refs_2_.1) | copy-start | bytes 3145732
  0.6 11.5 %copy-start.3 = (s32[1,1,4,2]{2,3,1,0:T(2,128)S(1)}, s32[1,1,4,2]{2,3,1,0:T(2,128)}, u32[]{:S(2)}) copy-start(s32[1,1,4,2]{2,3,1,0:T(2,128)} %param.10) | copy-start | bytes 100
  3.5 34.1 %collective-permute-start.6 = (bf16[16,2,2,16,512]{4,3,2,1,0:T(8,128)(2,1)}, bf16[16,2,2,16,512]{4,3,2,1,0:T(8,128)(2,1)}, u32[]{:S(2)}, u32[]{:S(2)}) collective-permute-start(bf16[16,2,2,16,512]{4,3,2,1,0:T(8,128)(2,1)} %get-tuple-element.41), channel_id=1, source_target_pairs={{0,1},{1,2},{2,3},{3,4},{4,5},{5,6},{6,7},{7,0},{8,9},{9,10},{10,1... | collective-permute-start | bytes 3145736 | tf_op jit(solution)/shard_map/ppermute | solution.py:22
  6.2 39.1 %collective-permute-start = (f32[2,256,512]{2,1,0:T(8,128)S(1)}, f32[2,256,512]{2,1,0:T(8,128)S(1)}, u32[]{:S(2)}, u32[]{:S(2)}) collective-permute-start(f32[2,256,512]{2,1,0:T(8,128)S(1)} %copy-done.1), channel_id=1, source_target_pairs={{0,8},{8,16},{16,24},{24,32},{32,40},{40,48},{48,56},{56,64},{64,7... | collective-permute-start | bytes 3145736 | tf_op jit(solution)/shard_map/ppermute | solution.py:22
  7.4 37.9 %collective-permute-start.1 = (f32[2,256,512]{2,1,0:T(8,128)S(1)}, f32[2,256,512]{2,1,0:T(8,128)}, u32[]{:S(2)}, u32[]{:S(2)}) collective-permute-start(f32[2,256,512]{2,1,0:T(8,128)S(1)} %copy-done.1), channel_id=1, source_target_pairs={{0,120},{8,0},{16,8},{24,16},{32,24},{40,32},{48,40},{56,48},{64,5... | collective-permute-start | bytes 3145736 | tf_op jit(solution)/shard_map/ppermute | solution.py:22
  12.3 21.5 %collective-permute-start.4 = (s32[2,2]{1,0:T(2,128)S(1)}, s32[2,2]{1,0:T(2,128)S(1)}, u32[]{:S(2)}, u32[]{:S(2)}) collective-permute-start(s32[2,2]{1,0:T(2,128)S(1)} %bitcast.27), channel_id=1, source_target_pairs={{0,9},{1,10},{2,11},{3,12},{4,13},{5,14},{6,15},{7,8},{8,17},{9,18... | collective-permute-start | bytes 56 | tf_op jit(solution)/shard_map/ppermute | solution.py:32
  12.4 24.0 %collective-permute-start.5 = (s32[2,2]{1,0:T(2,128)S(1)}, s32[2,2]{1,0:T(2,128)S(1)}, u32[]{:S(2)}, u32[]{:S(2)}) collective-permute-start(s32[2,2]{1,0:T(2,128)S(1)} %bitcast.26), channel_id=1, source_target_pairs={{0,8},{8,16},{16,24},{24,32},{32,40},{40,48},{48,56},{56,64},{64,7... | collective-permute-start | bytes 56 | tf_op jit(solution)/shard_map/ppermute | solution.py:22
  33.9 8.6 %collective-permute-start.2 = (f32[2,256,256]{2,1,0:T(8,128)S(1)}, f32[2,256,256]{2,1,0:T(8,128)S(1)}, u32[]{:S(2)}, u32[]{:S(2)}) collective-permute-start(f32[2,256,256]{2,1,0:T(8,128)S(1)} %get-tuple-element.48), channel_id=1, source_target_pairs={{0,1},{1,2},{2,3},{3,4},{4,5},{5,6},{6,7},{7,0},{8,9},{9,10},{10,1... | collective-permute-start | bytes 1572872 | tf_op jit(solution)/shard_map/ppermute | solution.py:22
  36.4 8.9 %collective-permute-start.3 = (f32[2,256,256]{2,1,0:T(8,128)S(1)}, f32[2,256,256]{2,1,0:T(8,128)S(1)}, u32[]{:S(2)}, u32[]{:S(2)}) collective-permute-start(f32[2,256,256]{2,1,0:T(8,128)S(1)} %get-tuple-element.47), channel_id=1, source_target_pairs={{0,7},{1,0},{2,1},{3,2},{4,3},{5,4},{6,5},{7,6},{8,15},{9,8},{10,9... | collective-permute-start | bytes 1572872 | tf_op jit(solution)/shard_map/ppermute | solution.py:22
  42.5 4.7 %copy-start.4 = (f32[2,256,256]{2,1,0:T(8,128)}, f32[2,256,256]{2,1,0:T(8,128)S(1)}, u32[]{:S(2)}) copy-start(f32[2,256,256]{2,1,0:T(8,128)S(1)} %collective-permute-done.2.refs_3_) | copy-start | bytes 1572868
  45.3 2.0 copy-start.5
  45.3 2.0 copy-start.2
  47.3 14.6 %collective-permute-start.8 = (f32[2,512,256]{2,1,0:T(8,128)S(1)}, f32[2,512,256]{2,1,0:T(8,128)}, u32[]{:S(2)}, u32[]{:S(2)}) collective-permute-start(f32[2,512,256]{2,1,0:T(8,128)S(1)} %pad_maximum_fusion.2), channel_id=1, source_target_pairs={{0,7},{1,0},{2,1},{3,2},{4,3},{5,4},{6,5},{7,6},{8,15},{9,8},{10,9... | collective-permute-start | bytes 3145736 | tf_op jit(solution)/shard_map/ppermute | solution.py:22
  50.1 4.5 %copy-start = (f32[2,512,512]{2,1,0:T(8,128)S(1)}, f32[2,512,512]{2,1,0:T(8,128)}, u32[]{:S(2)}) copy-start(f32[2,512,512]{2,1,0:T(8,128)} %ill.1) | copy-start | bytes 6291460
  50.1 12.1 %collective-permute-start.7 = (f32[2,512,256]{2,1,0:T(8,128)}, f32[2,512,256]{2,1,0:T(8,128)}, u32[]{:S(2)}, u32[]{:S(2)}) collective-permute-start(f32[2,512,256]{2,1,0:T(8,128)} %pad_maximum_fusion.1), channel_id=1, source_target_pairs={{0,1},{1,2},{2,3},{3,4},{4,5},{5,6},{6,7},{7,0},{8,9},{9,10},{10,1... | collective-permute-start | bytes 3145736 | tf_op jit(solution)/shard_map/ppermute | solution.py:22
  50.1 36.0 %all-to-all-start = ((bf16[16,4,2,16,512]{4,3,2,1,0:T(8,128)(2,1)}), bf16[16,4,2,16,512]{4,3,2,1,0:T(8,128)(2,1)}, u32[]{:S(2)}, u32[]{:S(2)}) async-start(bf16[16,4,2,16,512]{4,3,2,1,0:T(8,128)(2,1)} %pad_maximum_fusion), calls=%async_computation | async-start | bytes 4194304 | tf_op jit(solution)/shard_map/all_to_all | solution.py:486
  115.8 44.5 %all-to-all-start.1 = ((f16[128,56,128]{2,1,0:T(8,128)(2,1)}), f16[128,56,128]{2,1,0:T(8,128)(2,1)}, u32[]{:S(2)}, u32[]{:S(2)}) async-start(f16[128,56,128]{2,1,0:T(8,128)(2,1)} %fusion), calls=%async_computation.1 | async-start | bytes 3670016 | tf_op jit(solution)/shard_map/all_to_all | solution.py:454
  129.0 25.4 %collective-permute-start.9 = (f16[2,2,776,128]{3,2,1,0:T(8,128)(2,1)S(1)}, f16[2,2,776,128]{3,2,1,0:T(8,128)(2,1)S(1)}, u32[]{:S(2)}, u32[]{:S(2)}) collective-permute-start(f16[2,2,776,128]{3,2,1,0:T(8,128)(2,1)S(1)} %get-tuple-element.37), channel_id=1, source_target_pairs={{0,1},{1,2},{2,3},{3,4},{4,5},{5,6},{6,7},{7,0},{8,9},{9,10},{10,1... | collective-permute-start | bytes 2383880 | tf_op jit(solution)/shard_map/ppermute | solution.py:22
  130.7 25.8 %collective-permute-start.10 = (f16[2,2,776,128]{3,2,1,0:T(8,128)(2,1)S(1)}, f16[2,2,776,128]{3,2,1,0:T(8,128)(2,1)S(1)}, u32[]{:S(2)}, u32[]{:S(2)}) collective-permute-start(f16[2,2,776,128]{3,2,1,0:T(8,128)(2,1)S(1)} %get-tuple-element.38), channel_id=1, source_target_pairs={{0,7},{1,0},{2,1},{3,2},{4,3},{5,4},{6,5},{7,6},{8,15},{9,8},{10,9... | collective-permute-start | bytes 2383880 | tf_op jit(solution)/shard_map/ppermute | solution.py:22
  166.7 44.8 %all-to-all-start.2 = ((f16[128,32,128]{2,1,0:T(8,128)(2,1)}), f16[128,32,128]{2,1,0:T(8,128)(2,1)}, u32[]{:S(2)}, u32[]{:S(2)}) async-start(f16[128,32,128]{2,1,0:T(8,128)(2,1)} %broadcast_in_dim.73), calls=%async_computation.2 | async-start | bytes 2097152 | tf_op jit(solution)/shard_map/all_to_all | solution.py:454
  177.4 23.3 %collective-permute-start.11 = (f16[2,4,264,128]{3,2,1,0:T(8,128)(2,1)S(1)}, f16[2,4,264,128]{3,2,1,0:T(8,128)(2,1)S(1)}, u32[]{:S(2)}, u32[]{:S(2)}) collective-permute-start(f16[2,4,264,128]{3,2,1,0:T(8,128)(2,1)S(1)} %concatenate.26), channel_id=1, source_target_pairs={{0,120},{8,0},{16,8},{24,16},{32,24},{40,32},{48,40},{56,48},{64,5... | collective-permute-start | bytes 1622024 | tf_op jit(solution)/shard_map/ppermute | solution.py:22
  183.0 22.7 %collective-permute-start.12 = (f16[2,4,264,128]{3,2,1,0:T(8,128)(2,1)S(1)}, f16[2,4,264,128]{3,2,1,0:T(8,128)(2,1)S(1)}, u32[]{:S(2)}, u32[]{:S(2)}) collective-permute-start(f16[2,4,264,128]{3,2,1,0:T(8,128)(2,1)S(1)} %concatenate.27), channel_id=1, source_target_pairs={{0,8},{8,16},{16,24},{24,32},{32,40},{40,48},{48,56},{56,64},{64,7... | collective-permute-start | bytes 1622024 | tf_op jit(solution)/shard_map/ppermute | solution.py:22

commit v6 on v5

--- a/solution.py
+++ b/solution.py
@@ -92,27 +92,29 @@
 
 
 def region_copies(pieces, region, sems):
-    upper, lower, middle, west, east, outer_west, outer_east = pieces
+    middle, west, east = pieces[:3]
     rows, cols, edge = middle.shape[1], middle.shape[2], west.shape[2]
     center, right = edge // LANES, (edge + cols) // LANES
-    moves = [
-        (upper, 0, 0, center),
-        (middle, 0, 1, center),
-        (lower, 0, 2, center),
-        (west, 0, 1, 0),
-        (east, 0, 1, right),
-        (outer_west, 0, 0, 0),
-        (outer_west, 1, 2, 0),
-        (outer_east, 0, 0, right),
-        (outer_east, 1, 2, right),
-    ]
+    both = pl.ds(0, 2)
+    moves = [(middle, both, 0, 1, center), (west, both, 0, 1, 0), (east, both, 0, 1, right)]
+    for plane in range(2):
+        upper, lower, outer_west, outer_east = pieces[3 + 4 * plane : 7 + 4 * plane]
+        one = pl.ds(plane, 1)
+        moves += [
+            (upper, one, 0, 0, center),
+            (lower, one, 0, 2, center),
+            (outer_west, one, 0, 0, 0),
+            (outer_west, one, 1, 2, 0),
+            (outer_east, one, 0, 0, right),
+            (outer_east, one, 1, 2, right),
+        ]
     copies = []
-    for piece, source, target, first in moves:
+    for piece, planes, source, target, first in moves:
         for block in range(piece.shape[2] // LANES):
             copies.append(
                 pltpu.make_async_copy(
                     piece.at[:, pl.ds(source * rows, rows), pl.ds(block * LANES, LANES)],
-                    region.at[:, first + block, pl.ds(target * rows, rows)],
+                    region.at[planes, first + block, pl.ds(target * rows, rows)],
                     sems.at[len(copies)],
                 )
             )
@@ -127,7 +129,7 @@
 
 
 def forward_kernel(offs, *refs):
-    pieces, tables, refs = refs[:7], refs[7:10], refs[10:]
+    pieces, tables, refs = refs[:11], refs[11:14], refs[14:]
     ill, far, patch, stats, region, left, right, wave, half, region_sems, table_sems = refs
     slot = pl.program_id(0)
     size = ill.shape[-1]
@@ -357,7 +359,7 @@
 def run_forward(offs, pieces, tables, ill):
     slots = offs.shape[0]
     size = ill.shape[-1]
-    rows, cols, edge = pieces[2].shape[1], pieces[2].shape[2], pieces[3].shape[2]
+    rows, cols, edge = pieces[0].shape[1], pieces[0].shape[2], pieces[1].shape[2]
     planes = jax.ShapeDtypeStruct((slots, 2, size, size), jnp.float32)
     return pl.pallas_call(
         forward_kernel,
@@ -377,7 +379,7 @@
                 pltpu.VMEM((2 * size, 2 * size), jnp.bfloat16),
                 pltpu.VMEM((2 * size, size), jnp.bfloat16),
                 pltpu.VMEM((size, 2 * size), jnp.bfloat16),
-                pltpu.SemaphoreType.DMA((24,)),
+                pltpu.SemaphoreType.DMA((40,)),
                 pltpu.SemaphoreType.DMA((8,)),
             ],
         ),
@@ -432,24 +434,6 @@
     )(offs, order, powers, far, patch, amp, ill, *tables)
 
 
-def unpack_kernel(packed, out):
-    size = out.shape[1]
-    for plane in range(2):
-        out[plane] = packed[:, plane].reshape(size, LANES)
-
-
-def unpacked(packed, size):
-    packed = packed.reshape(size * size // (PIECE * LANES), 2, PIECE, LANES)
-    return pl.pallas_call(
-        unpack_kernel,
-        grid=(size // LANES,),
-        in_specs=[pl.BlockSpec((size // PIECE, 2, PIECE, LANES), lambda at: (at, 0, 0, 0))],
-        out_specs=pl.BlockSpec((2, size, LANES), lambda at: (0, 0, at)),
-        out_shape=jax.ShapeDtypeStruct((2, size, size), jnp.float32),
-        name="unpack",
-    )(packed)
-
-
 def spread_out(value):
     return lax.all_to_all(value, ("row", "col"), split_axis=0, concat_axis=0, tiled=True)
 
@@ -465,8 +449,10 @@
     late = slots // 2
     edge = tile_cols // 2
     grouped = measured.reshape(senders, slots, per, height, size)
-    upper = passed_along(specimen, "row", 1)
-    lower = passed_along(specimen, "row", -1)
+    uppers, lowers = [], []
+    for plane in range(2):
+        uppers.append(passed_along(specimen[plane : plane + 1], "row", 1))
+        lowers.append(passed_along(specimen[plane : plane + 1], "row", -1))
     early_offs = passed_along(scan_offsets[0, 0, :late], "row", 1)
     late_offs = passed_both(scan_offsets[0, 0, late:], 1, 1)
     offs = jnp.concatenate([late_offs, early_offs], axis=0)
@@ -475,14 +461,20 @@
     east = passed_along(specimen[:, :, :edge], "col", -1)
     levels = jnp.concatenate([moved, grouped[:, :late]], axis=1)
     tables = dft_tables(size)
-    upper, lower, west, east, offs, levels, probe = lax.optimization_barrier(
-        (upper, lower, west, east, offs, levels, illumination)
-    )
+    outers = []
+    for plane in range(2):
+        upper, lower = uppers[plane], lowers[plane]
+        west_edges = jnp.concatenate([upper[:, :, edge:], lower[:, :, edge:]], axis=1)
+        east_edges = jnp.concatenate([upper[:, :, :edge], lower[:, :, :edge]], axis=1)
+        if plane == 0:
+            uppers[1], lowers[1], _, _ = lax.optimization_barrier(
+                (uppers[1], lowers[1], west_edges, east_edges)
+            )
+        outer_west = passed_along(west_edges, "col", 1)
+        outer_east = passed_along(east_edges, "col", -1)
+        outers.append((upper, lower, outer_west, outer_east))
+    levels, probe, _ = lax.optimization_barrier((levels, illumination, uppers[0]))
     ill_power = exponent(2.0 * jnp.max(jnp.abs(probe)))
-    west_edges = jnp.concatenate([upper[:, :, edge:], lower[:, :, edge:]], axis=1)
-    east_edges = jnp.concatenate([upper[:, :, :edge], lower[:, :, :edge]], axis=1)
-    outer_west = passed_along(west_edges, "col", 1)
-    outer_east = passed_along(east_edges, "col", -1)
     arrived = lax.all_to_all(
         levels,
         "row",
@@ -491,7 +483,7 @@
         tiled=True,
         axis_index_groups=[[(sender + 1) % senders for sender in range(senders)]],
     )
-    pieces = (upper, lower, specimen, west, east, outer_west, outer_east)
+    pieces = (specimen, west, east) + outers[0] + outers[1]
     far, patch, stats = run_forward(offs, pieces, tables, illumination)
     patch_power = exponent(1.5 * jnp.max(stats[0]))
     change_power = exponent(12.0 * jnp.sqrt(jnp.sum(stats[1])))
@@ -536,7 +528,9 @@
     mine = narrowed(mine, step_power).reshape(1, 2 * PIECE, LANES)
     copies = jnp.broadcast_to(mine, (devices, 2 * PIECE, LANES))
     result = spread_out(copies)
-    illumination_step = unpacked(widened(result, step_power), size)
+    result = result.reshape(size // LANES, size // PIECE, 2, PIECE, LANES)
+    result = result.transpose(2, 1, 3, 0, 4).reshape(2, size, size)
+    illumination_step = widened(result, step_power)
     middle = (
         column[:, :, tile_rows : 2 * tile_rows]
         + opened(from_lower)[0]

time: 219 us -> 211 us (0.963)
  waiting for transfers between devices: 78.5 us -> 60.4 us
  local copies, waits for them, and re-layouts: 11.4 us -> 18 us
  starting transfers between devices: 46.5 us -> 52.1 us
  Pallas kernels: 50.2 us -> 47.5 us
    ppermute x1, waiting for transfers between devices: 21.4 us -> 0.01 us  [passed_both(): return lax.ppermute(value, ('row', 'col'), pairs)]
    ppermute x12 -> x16, starting transfers between devices: 20.8 us -> 30.2 us  [passed_along(): return lax.ppermute(value, axis, pairs)]
    pallas_call x1 -> x0, Pallas kernels: 3.77 us -> none  [unpacked(): pl.pallas_call(unpack_kernel, grid=(size // LANES,), in_specs=[pl.BlockSp...]
    all_to_all x2, starting transfers between devices: 21.2 us -> 17.6 us  [spread_out(): lax.all_to_all(value, ('row', 'col'), split_axis=0, concat_axis=0, tiled=...]
    slice x0 -> x2, local copies, waits for them, and re-layouts: none -> 3.32 us  [the longest x1 2.25 us: shards(): uppers.append(passed_along(specimen[plane:plane + 1], 'row', 1))]
    mul x0 -> x2, local copies, waits for them, and re-layouts: none -> 3.2 us  [widened(): return value.astype(jnp.float32) * jnp.exp2(power - 15.0)]
    ppermute x12 -> x16, waiting for transfers between devices: 57.1 us -> 59.3 us  [passed_along(): return lax.ppermute(value, axis, pairs)]
  transfers between devices with their start and end apart: 16 -> 20, of which waited for: 9 -> 10; matrix products, arithmetic and copies ran while one was open for 9% -> 13% of each run, Pallas kernels for 9% -> 10%
where the time goes in v6:
time: 211 us
  waiting for transfers between devices  60.4 us (29%)
  starting transfers between devices  52.1 us (25%)
  Pallas kernels  47.5 us (23%)
  other arithmetic  25.8 us (12%)
  local copies, waits for them, and re-layouts  18 us (9%)
  between operations  6.79 us (3%)
    ppermute x16, waiting for transfers between devices, passed_along(): return lax.ppermute(value, axis, pairs)  59.3 us
    ppermute x16, starting transfers between devices, passed_along(): return lax.ppermute(value, axis, pairs)  30.2 us
    pallas_call x1, Pallas kernels, run_backward(): pl.pallas_call(backward_kernel, grid_spec=pltpu.PrefetchScalarGridSpec(nu...  25.9 us
    pallas_call x1, Pallas kernels, run_forward(): pl.pallas_call(forward_kernel, grid_spec=pltpu.PrefetchScalarGridSpec(num...  21.6 us
    all_to_all x2, starting transfers between devices, spread_out(): lax.all_to_all(value, ('row', 'col'), split_axis=0, concat_axis=0, tiled=...  17.6 us
    all_to_all x1, starting transfers between devices, shards(): lax.all_to_all(levels, 'row', split_axis=0, concat_axis=0, tiled=True, ax...  4.34 us
  transfers between devices with their start and end apart: 20, of which 10 were waited for; matrix products, arithmetic and copies ran while one was open for 13% of the time, Pallas kernels for 10%

profile of v6, /device:TPU:1, one launch (start us, length us, event | category | flops | bytes accessed | tf_op | source)
XLA Modules:
  0.0 210.7 jit_solution(5965033078983093641)
XLA Ops:
  0.6 2.3 %fusion.10 = (f32[1,256,512]{2,1,0:T(8,128)}, f32[1,256,512]{2,1,0:T(8,128)}) fusion(f32[2,256,512]{2,1,0:T(8,128)} %refs_0_.1), kind=kLoop, calls=%fused_computation.42 | loop fusion | bytes 2097152 | tf_op jit(solution)/shard_map/slice | solution.py:454
  2.9 2.0 collective-permute-start.4
  4.9 4.7 %collective-permute-start.5 = (f32[1,256,512]{2,1,0:T(8,128)}, f32[1,256,512]{2,1,0:T(8,128)}, u32[]{:S(2)}, u32[]{:S(2)}) collective-permute-start(f32[1,256,512]{2,1,0:T(8,128)} %get-tuple-element.40), channel_id=1, source_target_pairs={{0,120},{8,0},{16,8},{24,16},{32,24},{40,32},{48,40},{56,48},{64,5... | collective-permute-start | bytes 1572872 | tf_op jit(solution)/shard_map/ppermute | solution.py:22
  9.7 4.8 %collective-permute-start.9 = (f32[1,256,512]{2,1,0:T(8,128)}, f32[1,256,512]{2,1,0:T(8,128)}, u32[]{:S(2)}, u32[]{:S(2)}) collective-permute-start(f32[1,256,512]{2,1,0:T(8,128)} %get-tuple-element.39), channel_id=1, source_target_pairs={{0,120},{8,0},{16,8},{24,16},{32,24},{40,32},{48,40},{56,48},{64,5... | collective-permute-start | bytes 1572872 | tf_op jit(solution)/shard_map/ppermute | solution.py:22
  14.6 1.8 fusion.9
  16.5 0.9 fusion.11
  17.4 4.2 %collective-permute-done.4.refs_3_ = f32[1,256,512]{2,1,0:T(8,128)} collective-permute-done((f32[1,256,512]{2,1,0:T(8,128)}, f32[1,256,512]{2,1,0:T(8,128)}, u32[]{:S(2)}, u32[]{:S(2)}) %collective-permute-start.4) | collective-permute-done | bytes 524320 | tf_op jit(solution)/shard_map/ppermute | solution.py:22
  21.6 3.3 %collective-permute-start.12 = (bf16[16,2,2,16,512]{4,3,2,1,0:T(8,128)(2,1)S(1)}, bf16[16,2,2,16,512]{4,3,2,1,0:T(8,128)(2,1)S(1)}, u32[]{:S(2)}, u32[]{:S(2)}) collective-permute-start(bf16[16,2,2,16,512]{4,3,2,1,0:T(8,128)(2,1)S(1)} %get-tuple-element.37), channel_id=1, source_target_pairs={{0,1},{1,2},{2,3},{3,4},{4,5},{5,6},{6,7},{7,0},{8,9},{9,10},{10,1... | collective-permute-start | bytes 3145736 | tf_op jit(solution)/shard_map/ppermute | solution.py:22
  24.9 1.1 fusion.14
  26.0 1.1 fusion.15
  27.1 0.9 pad_maximum_fusion.1
  27.9 0.8 pad_maximum_fusion.2
  28.8 4.1 %collective-permute-done.8.refs_7_ = f32[1,256,512]{2,1,0:T(8,128)} collective-permute-done((f32[1,256,512]{2,1,0:T(8,128)}, f32[1,256,512]{2,1,0:T(8,128)}, u32[]{:S(2)}, u32[]{:S(2)}) %collective-permute-start.8) | collective-permute-done | bytes 524320 | tf_op jit(solution)/shard_map/ppermute | solution.py:22
  32.8 1.3 collective-permute-start.3
  34.1 1.3 fusion.12
  35.4 0.8 pad_maximum_fusion.4
  36.2 0.8 pad_maximum_fusion.3
  37.0 1.2 collective-permute-start.6
  38.2 0.3 collective-permute-done.1
  38.6 2.4 %collective-permute-start.7 = (f32[1,512,256]{2,1,0:T(8,128)}, f32[1,512,256]{2,1,0:T(8,128)}, u32[]{:S(2)}, u32[]{:S(2)}) collective-permute-start(f32[1,512,256]{2,1,0:T(8,128)} %pad_maximum_fusion.2), channel_id=1, source_target_pairs={{0,7},{1,0},{2,1},{3,2},{4,3},{5,4},{6,5},{7,6},{8,15},{9,8},{10,9... | collective-permute-start | bytes 1572872 | tf_op jit(solution)/shard_map/ppermute | solution.py:22
  41.0 1.3 collective-permute-done.2.refs_1_
  42.3 2.5 %collective-permute-start.11 = (f32[1,512,256]{2,1,0:T(8,128)}, f32[1,512,256]{2,1,0:T(8,128)}, u32[]{:S(2)}, u32[]{:S(2)}) collective-permute-start(f32[1,512,256]{2,1,0:T(8,128)} %pad_maximum_fusion.4), channel_id=1, source_target_pairs={{0,7},{1,0},{2,1},{3,2},{4,3},{5,4},{6,5},{7,6},{8,15},{9,8},{10,9... | collective-permute-start | bytes 1572872 | tf_op jit(solution)/shard_map/ppermute | solution.py:22
  44.8 0.8 collective-permute-start.10
  45.5 1.5 pad_maximum_fusion
  47.0 4.3 %all-to-all-start = ((bf16[16,4,2,16,512]{4,3,2,1,0:T(8,128)(2,1)}), bf16[16,4,2,16,512]{4,3,2,1,0:T(8,128)(2,1)}, u32[]{:S(2)}, u32[]{:S(2)}) async-start(bf16[16,4,2,16,512]{4,3,2,1,0:T(8,128)(2,1)} %pad_maximum_fusion), calls=%async_computation | async-start | bytes 4194304 | tf_op jit(solution)/shard_map/all_to_all | solution.py:478
  51.4 0.5 pad_add_fusion.offs
  51.9 3.3 %collective-permute-done.11.refs_10_ = f32[1,512,256]{2,1,0:T(8,128)} collective-permute-done((f32[1,512,256]{2,1,0:T(8,128)}, f32[1,512,256]{2,1,0:T(8,128)}, u32[]{:S(2)}, u32[]{:S(2)}) %collective-permute-start.11) | collective-permute-done | bytes 524320 | tf_op jit(solution)/shard_map/ppermute | solution.py:22
  55.3 21.6 %forward.1 = (f32[4,2,512,512]{3,2,1,0:T(8,128)}, f32[4,2,512,512]{3,2,1,0:T(8,128)}, f32[2,8,128]{2,1,0:T(8,128)}) custom-call(s32[4,2]{1,0:T(4,128)} %pad_add_fusion.offs, f32[2,256,512]{2,1,0:T(8,128)} %refs_0_.1, f32[2,256,256]{2,1,0:T(8,128)} %copy-done.2, f32[2,256,256]{2,1,0:T(8,128)} %collective-permute-done.3.refs_2_, ...), custom_call_target="tpu_custom_call" | custom-call | flops 8589934592 | bytes 30000000 | tf_op jit(solution)/shard_map/forward/pallas_call | solution.py:364
  76.8 1.3 slice_reduce_fusion.2
  79.5 2.4 %abs_reduce_fusion = f32[]{:T(128)} fusion(f32[2,512,512]{2,1,0:T(8,128)} %ill.1), kind=kLoop, calls=%fused_computation.6 | loop fusion | flops 1048575 | bytes 2097156 | tf_op jit(solution)/shard_map/reduce_max | solution.py:477
  82.6 0.6 pad_maximum_fusion.5.powers
  83.2 1.1 all-to-all-done.amp
  84.3 25.9 %backward.1 = (f32[2,8,776,128]{3,2,1,0:T(8,128)}, f32[4,32,56,128]{3,2,1,0:T(8,128)}) custom-call(s32[4,2]{1,0:T(4,128)} %pad_add_fusion.offs, s32[32]{0:T(128)} %order.1, f32[3]{0:T(128)} %pad_maximum_fusion.5.powers, f32[4,2,512,512]{3,2,1,0:T(8,128)} %get-tuple-element.15.far, f32[4,2,512,512]{3,2,1,0:T(8,128)} %get-tuple-element.16.patch, ...), custom_call_target="tpu_custom_call" | custom-call | flops 8589934592 | bytes 30000000 | tf_op jit(solution)/shard_map/backward/pallas_call | solution.py:400
  110.3 3.7 %fusion = f16[128,56,128]{2,1,0:T(8,128)(2,1)} fusion(f32[4,32,56,128]{3,2,1,0:T(8,128)} %get-tuple-element.19, f32[56]{0:T(128)S(1)} %compare_select_fusion.1), kind=kLoop, calls=%fused_computation.1 | loop fusion | flops 1835008 | bytes 5505248 | tf_op jit(solution)/shard_map/convert_element_type | solution.py:508
  113.9 7.4 %all-to-all-start.1 = ((f16[128,56,128]{2,1,0:T(8,128)(2,1)}), f16[128,56,128]{2,1,0:T(8,128)(2,1)}, u32[]{:S(2)}, u32[]{:S(2)}) async-start(f16[128,56,128]{2,1,0:T(8,128)(2,1)} %fusion), calls=%async_computation.1 | async-start | bytes 3670016 | tf_op jit(solution)/shard_map/all_to_all | solution.py:438
  121.4 2.3 %multiply_convert_fusion.1 = (f16[2,2,776,128]{3,2,1,0:T(8,128)(2,1)S(1)}, f16[2,2,776,128]{3,2,1,0:T(8,128)(2,1)S(1)}) fusion(f32[2,8,776,128]{3,2,1,0:T(8,128)} %get-tuple-element.18, f32[776]{0:T(1024)S(1)} %fusion.8), kind=kLoop, calls=%fused_computation.8 | loop fusion | flops 1589248 | bytes 4770848 | tf_op jit(solution)/shard_map/convert_element_type | solution.py:61
  123.7 1.6 collective-permute-start.13
  125.3 23.8 %collective-permute-done.13 = f16[2,2,776,128]{3,2,1,0:T(8,128)(2,1)S(1)} collective-permute-done((f16[2,2,776,128]{3,2,1,0:T(8,128)(2,1)S(1)}, f16[2,2,776,128]{3,2,1,0:T(8,128)(2,1)S(1)}, u32[]{:S(2)}, u32[]{:S(2)}) %collective-permute-start.13) | collective-permute-done | bytes 794656 | tf_op jit(solution)/shard_map/ppermute | solution.py:22
  149.1 0.5 slice.165
  150.1 0.9 collective-permute-done.14
  151.1 0.5 slice.167
  152.3 0.1 convert_multiply_fusion.2
  152.4 0.1 convert_multiply_fusion.1
  152.5 2.3 %maximum_add_fusion = f32[2,4,768,128]{3,2,1,0:T(8,128)S(1)} fusion(f32[2,2,768,128]{3,2,1,0:T(8,128)S(1)} %convert_multiply_fusion.1, f32[2,2,768,128]{3,2,1,0:T(8,128)S(1)} %convert_multiply_fusion.2, f32[2,8,776,128]{3,2,1,0:T(8,128)} %get-tuple-element.18), kind=kLoop, calls=%fused_computation.2 | loop fusion | flops 1572864 | bytes 9437184 | tf_op jit(solution)/shard_map/add | solution.py:513
  154.9 1.0 slice_convert_fusion
  155.8 1.4 slice_reduce_fusion
  157.3 0.1 multiply_exponential_fusion
  157.4 2.1 %multiply_reduce_fusion = f32[48,128]{1,0:T(8,128)S(1)} fusion(f16[128,56,128]{2,1,0:T(8,128)(2,1)} %all-to-all-done.1, f32[128,48]{1,0:T(8,128)S(1)} %multiply_exponential_fusion), kind=kLoop, calls=%fused_computation.3 | loop fusion | flops 2353152 | bytes 1622016 | tf_op jit(solution)/shard_map/reduce_sum | solution.py:525
  160.1 1.1 broadcast_in_dim.73
  161.2 10.2 %all-to-all-start.2 = ((f16[128,32,128]{2,1,0:T(8,128)(2,1)}), f16[128,32,128]{2,1,0:T(8,128)(2,1)}, u32[]{:S(2)}, u32[]{:S(2)}) async-start(f16[128,32,128]{2,1,0:T(8,128)(2,1)} %broadcast_in_dim.73), calls=%async_computation.2 | async-start | bytes 2097152 | tf_op jit(solution)/shard_map/all_to_all | solution.py:438
  171.4 0.3 fusion.2
  171.7 0.1 concatenate.34
  171.8 5.5 %collective-permute-start.15 = (f16[2,4,264,128]{3,2,1,0:T(8,128)(2,1)S(1)}, f16[2,4,264,128]{3,2,1,0:T(8,128)(2,1)S(1)}, u32[]{:S(2)}, u32[]{:S(2)}) collective-permute-start(f16[2,4,264,128]{3,2,1,0:T(8,128)(2,1)S(1)} %concatenate.34), channel_id=1, source_target_pairs={{0,120},{8,0},{16,8},{24,16},{32,24},{40,32},{48,40},{56,48},{64,5... | collective-permute-start | bytes 1622024 | tf_op jit(solution)/shard_map/ppermute | solution.py:22
  177.3 0.1 concatenate.35
  177.5 17.7 %collective-permute-done.15 = f16[2,4,264,128]{3,2,1,0:T(8,128)(2,1)S(1)} collective-permute-done((f16[2,4,264,128]{3,2,1,0:T(8,128)(2,1)S(1)}, f16[2,4,264,128]{3,2,1,0:T(8,128)(2,1)S(1)}, u32[]{:S(2)}, u32[]{:S(2)}) %collective-permute-start.15) | collective-permute-done | bytes 540704 | tf_op jit(solution)/shard_map/ppermute | solution.py:22
  195.1 0.5 slice.171
  196.4 3.7 %collective-permute-done.16 = f16[2,4,264,128]{3,2,1,0:T(8,128)(2,1)S(1)} collective-permute-done((f16[2,4,264,128]{3,2,1,0:T(8,128)(2,1)S(1)}, f16[2,4,264,128]{3,2,1,0:T(8,128)(2,1)S(1)}, u32[]{:S(2)}, u32[]{:S(2)}) %collective-permute-start.16) | collective-permute-done | bytes 540704 | tf_op jit(solution)/shard_map/ppermute | solution.py:22
  200.1 0.5 slice.174
  201.3 1.2 fusion.4
  202.5 1.6 copy.31
  204.0 1.3 copy.33
  206.0 1.5 convert_multiply_fusion
  207.5 1.4 copy.32
  208.8 1.8 mul.123
  (31 shorter events, 0.4 us)
Async XLA Ops:
  0.6 13.8 %copy-start.1 = (s32[1,1,4,2]{2,3,1,0:T(2,128)S(1)}, s32[1,1,4,2]{2,3,1,0:T(2,128)}, u32[]{:S(2)}) copy-start(s32[1,1,4,2]{2,3,1,0:T(2,128)} %param.10) | copy-start | bytes 100
  2.9 18.7 %collective-permute-start.4 = (f32[1,256,512]{2,1,0:T(8,128)}, f32[1,256,512]{2,1,0:T(8,128)}, u32[]{:S(2)}, u32[]{:S(2)}) collective-permute-start(f32[1,256,512]{2,1,0:T(8,128)} %get-tuple-element.40), channel_id=1, source_target_pairs={{0,8},{8,16},{16,24},{24,32},{32,40},{40,48},{48,56},{56,64},{64,7... | collective-permute-start | bytes 1572872 | tf_op jit(solution)/shard_map/ppermute | solution.py:22
  4.9 21.0 %collective-permute-start.5 = (f32[1,256,512]{2,1,0:T(8,128)}, f32[1,256,512]{2,1,0:T(8,128)}, u32[]{:S(2)}, u32[]{:S(2)}) collective-permute-start(f32[1,256,512]{2,1,0:T(8,128)} %get-tuple-element.40), channel_id=1, source_target_pairs={{0,120},{8,0},{16,8},{24,16},{32,24},{40,32},{48,40},{56,48},{64,5... | collective-permute-start | bytes 1572872 | tf_op jit(solution)/shard_map/ppermute | solution.py:22
  9.7 23.2 %collective-permute-start.8 = (f32[1,256,512]{2,1,0:T(8,128)}, f32[1,256,512]{2,1,0:T(8,128)}, u32[]{:S(2)}, u32[]{:S(2)}) collective-permute-start(f32[1,256,512]{2,1,0:T(8,128)} %get-tuple-element.39), channel_id=1, source_target_pairs={{0,8},{8,16},{16,24},{24,32},{32,40},{40,48},{48,56},{56,64},{64,7... | collective-permute-start | bytes 1572872 | tf_op jit(solution)/shard_map/ppermute | solution.py:22
  9.7 23.2 %collective-permute-start.9 = (f32[1,256,512]{2,1,0:T(8,128)}, f32[1,256,512]{2,1,0:T(8,128)}, u32[]{:S(2)}, u32[]{:S(2)}) collective-permute-start(f32[1,256,512]{2,1,0:T(8,128)} %get-tuple-element.39), channel_id=1, source_target_pairs={{0,120},{8,0},{16,8},{24,16},{32,24},{40,32},{48,40},{56,48},{64,5... | collective-permute-start | bytes 1572872 | tf_op jit(solution)/shard_map/ppermute | solution.py:22
  14.6 22.4 %collective-permute-start = (s32[2,2]{1,0:T(2,128)S(1)}, s32[2,2]{1,0:T(2,128)S(1)}, u32[]{:S(2)}, u32[]{:S(2)}) collective-permute-start(s32[2,2]{1,0:T(2,128)S(1)} %bitcast.28), channel_id=1, source_target_pairs={{0,9},{1,10},{2,11},{3,12},{4,13},{5,14},{6,15},{7,8},{8,17},{9,18... | collective-permute-start | bytes 56 | tf_op jit(solution)/shard_map/ppermute | solution.py:32
  14.6 1.9 copy-start
  21.6 23.2 %collective-permute-start.12 = (bf16[16,2,2,16,512]{4,3,2,1,0:T(8,128)(2,1)S(1)}, bf16[16,2,2,16,512]{4,3,2,1,0:T(8,128)(2,1)S(1)}, u32[]{:S(2)}, u32[]{:S(2)}) collective-permute-start(bf16[16,2,2,16,512]{4,3,2,1,0:T(8,128)(2,1)S(1)} %get-tuple-element.37), channel_id=1, source_target_pairs={{0,1},{1,2},{2,3},{3,4},{4,5},{5,6},{6,7},{7,0},{8,9},{9,10},{10,1... | collective-permute-start | bytes 3145736 | tf_op jit(solution)/shard_map/ppermute | solution.py:22
  26.0 16.3 %collective-permute-start.2 = (f32[2,256,256]{2,1,0:T(8,128)S(1)}, f32[2,256,256]{2,1,0:T(8,128)S(1)}, u32[]{:S(2)}, u32[]{:S(2)}) collective-permute-start(f32[2,256,256]{2,1,0:T(8,128)S(1)} %get-tuple-element.42), channel_id=1, source_target_pairs={{0,1},{1,2},{2,3},{3,4},{4,5},{5,6},{6,7},{7,0},{8,9},{9,10},{10,1... | collective-permute-start | bytes 1572872 | tf_op jit(solution)/shard_map/ppermute | solution.py:22
  32.8 5.7 %collective-permute-start.1 = (s32[2,2]{1,0:T(2,128)S(1)}, s32[2,2]{1,0:T(2,128)S(1)}, u32[]{:S(2)}, u32[]{:S(2)}) collective-permute-start(s32[2,2]{1,0:T(2,128)S(1)} %bitcast.29), channel_id=1, source_target_pairs={{0,8},{8,16},{16,24},{24,32},{32,40},{40,48},{48,56},{56,64},{64,7... | collective-permute-start | bytes 56 | tf_op jit(solution)/shard_map/ppermute | solution.py:22
  32.8 19.1 %collective-permute-start.3 = (f32[2,256,256]{2,1,0:T(8,128)}, f32[2,256,256]{2,1,0:T(8,128)}, u32[]{:S(2)}, u32[]{:S(2)}) collective-permute-start(f32[2,256,256]{2,1,0:T(8,128)} %get-tuple-element.41), channel_id=1, source_target_pairs={{0,7},{1,0},{2,1},{3,2},{4,3},{5,4},{6,5},{7,6},{8,15},{9,8},{10,9... | collective-permute-start | bytes 1572872 | tf_op jit(solution)/shard_map/ppermute | solution.py:22
  37.0 18.2 %collective-permute-start.6 = (f32[1,512,256]{2,1,0:T(8,128)}, f32[1,512,256]{2,1,0:T(8,128)}, u32[]{:S(2)}, u32[]{:S(2)}) collective-permute-start(f32[1,512,256]{2,1,0:T(8,128)} %pad_maximum_fusion.1), channel_id=1, source_target_pairs={{0,1},{1,2},{2,3},{3,4},{4,5},{5,6},{6,7},{7,0},{8,9},{9,10},{10,1... | collective-permute-start | bytes 1572872 | tf_op jit(solution)/shard_map/ppermute | solution.py:22
  38.6 16.7 %collective-permute-start.7 = (f32[1,512,256]{2,1,0:T(8,128)}, f32[1,512,256]{2,1,0:T(8,128)}, u32[]{:S(2)}, u32[]{:S(2)}) collective-permute-start(f32[1,512,256]{2,1,0:T(8,128)} %pad_maximum_fusion.2), channel_id=1, source_target_pairs={{0,7},{1,0},{2,1},{3,2},{4,3},{5,4},{6,5},{7,6},{8,15},{9,8},{10,9... | collective-permute-start | bytes 1572872 | tf_op jit(solution)/shard_map/ppermute | solution.py:22
  42.3 2.5 %copy-start.2 = (f32[2,256,256]{2,1,0:T(8,128)}, f32[2,256,256]{2,1,0:T(8,128)S(1)}, u32[]{:S(2)}) copy-start(f32[2,256,256]{2,1,0:T(8,128)S(1)} %collective-permute-done.2.refs_1_) | copy-start | bytes 1572868
  42.3 13.0 %collective-permute-start.11 = (f32[1,512,256]{2,1,0:T(8,128)}, f32[1,512,256]{2,1,0:T(8,128)}, u32[]{:S(2)}, u32[]{:S(2)}) collective-permute-start(f32[1,512,256]{2,1,0:T(8,128)} %pad_maximum_fusion.4), channel_id=1, source_target_pairs={{0,7},{1,0},{2,1},{3,2},{4,3},{5,4},{6,5},{7,6},{8,15},{9,8},{10,9... | collective-permute-start | bytes 1572872 | tf_op jit(solution)/shard_map/ppermute | solution.py:22
  44.8 10.5 %collective-permute-start.10 = (f32[1,512,256]{2,1,0:T(8,128)}, f32[1,512,256]{2,1,0:T(8,128)}, u32[]{:S(2)}, u32[]{:S(2)}) collective-permute-start(f32[1,512,256]{2,1,0:T(8,128)} %pad_maximum_fusion.3), channel_id=1, source_target_pairs={{0,1},{1,2},{2,3},{3,4},{4,5},{5,6},{6,7},{7,0},{8,9},{9,10},{10,1... | collective-permute-start | bytes 1572872 | tf_op jit(solution)/shard_map/ppermute | solution.py:22
  47.0 37.3 %all-to-all-start = ((bf16[16,4,2,16,512]{4,3,2,1,0:T(8,128)(2,1)}), bf16[16,4,2,16,512]{4,3,2,1,0:T(8,128)(2,1)}, u32[]{:S(2)}, u32[]{:S(2)}) async-start(bf16[16,4,2,16,512]{4,3,2,1,0:T(8,128)(2,1)} %pad_maximum_fusion), calls=%async_computation | async-start | bytes 4194304 | tf_op jit(solution)/shard_map/all_to_all | solution.py:478
  113.9 40.9 %all-to-all-start.1 = ((f16[128,56,128]{2,1,0:T(8,128)(2,1)}), f16[128,56,128]{2,1,0:T(8,128)(2,1)}, u32[]{:S(2)}, u32[]{:S(2)}) async-start(f16[128,56,128]{2,1,0:T(8,128)(2,1)} %fusion), calls=%async_computation.1 | async-start | bytes 3670016 | tf_op jit(solution)/shard_map/all_to_all | solution.py:438
  123.7 25.4 %collective-permute-start.13 = (f16[2,2,776,128]{3,2,1,0:T(8,128)(2,1)S(1)}, f16[2,2,776,128]{3,2,1,0:T(8,128)(2,1)S(1)}, u32[]{:S(2)}, u32[]{:S(2)}) collective-permute-start(f16[2,2,776,128]{3,2,1,0:T(8,128)(2,1)S(1)} %get-tuple-element.33), channel_id=1, source_target_pairs={{0,1},{1,2},{2,3},{3,4},{4,5},{5,6},{6,7},{7,0},{8,9},{9,10},{10,1... | collective-permute-start | bytes 2383880 | tf_op jit(solution)/shard_map/ppermute | solution.py:22
  125.3 25.8 %collective-permute-start.14 = (f16[2,2,776,128]{3,2,1,0:T(8,128)(2,1)S(1)}, f16[2,2,776,128]{3,2,1,0:T(8,128)(2,1)S(1)}, u32[]{:S(2)}, u32[]{:S(2)}) collective-permute-start(f16[2,2,776,128]{3,2,1,0:T(8,128)(2,1)S(1)} %get-tuple-element.34), channel_id=1, source_target_pairs={{0,7},{1,0},{2,1},{3,2},{4,3},{5,4},{6,5},{7,6},{8,15},{9,8},{10,9... | collective-permute-start | bytes 2383880 | tf_op jit(solution)/shard_map/ppermute | solution.py:22
  161.2 44.7 %all-to-all-start.2 = ((f16[128,32,128]{2,1,0:T(8,128)(2,1)}), f16[128,32,128]{2,1,0:T(8,128)(2,1)}, u32[]{:S(2)}, u32[]{:S(2)}) async-start(f16[128,32,128]{2,1,0:T(8,128)(2,1)} %broadcast_in_dim.73), calls=%async_computation.2 | async-start | bytes 2097152 | tf_op jit(solution)/shard_map/all_to_all | solution.py:438
  171.8 23.3 %collective-permute-start.15 = (f16[2,4,264,128]{3,2,1,0:T(8,128)(2,1)S(1)}, f16[2,4,264,128]{3,2,1,0:T(8,128)(2,1)S(1)}, u32[]{:S(2)}, u32[]{:S(2)}) collective-permute-start(f16[2,4,264,128]{3,2,1,0:T(8,128)(2,1)S(1)} %concatenate.34), channel_id=1, source_target_pairs={{0,120},{8,0},{16,8},{24,16},{32,24},{40,32},{48,40},{56,48},{64,5... | collective-permute-start | bytes 1622024 | tf_op jit(solution)/shard_map/ppermute | solution.py:22
  177.4 22.7 %collective-permute-start.16 = (f16[2,4,264,128]{3,2,1,0:T(8,128)(2,1)S(1)}, f16[2,4,264,128]{3,2,1,0:T(8,128)(2,1)S(1)}, u32[]{:S(2)}, u32[]{:S(2)}) collective-permute-start(f16[2,4,264,128]{3,2,1,0:T(8,128)(2,1)S(1)} %concatenate.35), channel_id=1, source_target_pairs={{0,8},{8,16},{16,24},{24,32},{32,40},{40,48},{48,56},{56,64},{64,7... | collective-permute-start | bytes 1622024 | tf_op jit(solution)/shard_map/ppermute | solution.py:22

commit v7 on v6

--- a/solution.py
+++ b/solution.py
@@ -182,7 +182,7 @@
         return peak, power
 
     empty = jnp.zeros((SUBLANES, LANES), jnp.float32)
-    peak, power = lax.fori_loop(0, size // CHUNK, extract, (empty, empty), unroll=4)
+    peak, power = lax.fori_loop(0, size // CHUNK, extract, (empty, empty), unroll=8)
     stats[0] = jnp.maximum(stats[0], peak)
     stats[1] = stats[1] + power
 
@@ -279,7 +279,7 @@
         corr[pl.ds(size + at, height), :] = (factor * far_imag).astype(jnp.bfloat16)
         return carry
 
-    lax.fori_loop(0, modules, correct, 0, unroll=4)
+    lax.fori_loop(0, modules, correct, 0, unroll=8)
 
     @pl.when(slot == 0)
     def _():
@@ -339,7 +339,7 @@
             last = now
         return carry
 
-    lax.fori_loop(0, size // CHUNK, spread, 0, unroll=4)
+    lax.fori_loop(0, size // CHUNK, spread, 0, unroll=8)
 
 
 def whole(shape):
@@ -434,6 +434,26 @@
     )(offs, order, powers, far, patch, amp, ill, *tables)
 
 
+def unpack_kernel(packed, out):
+    size = out.shape[1]
+    per = size // PIECE
+    for column in range(size // LANES):
+        for plane in range(2):
+            part = packed[column * per : (column + 1) * per, plane * PIECE : (plane + 1) * PIECE]
+            out[plane, :, column * LANES : (column + 1) * LANES] = part.reshape(size, LANES)
+
+
+def unpacked(packed, size):
+    return pl.pallas_call(
+        unpack_kernel,
+        in_specs=[pl.BlockSpec(memory_space=pltpu.VMEM)],
+        out_specs=pl.BlockSpec(memory_space=pltpu.VMEM),
+        out_shape=jax.ShapeDtypeStruct((2, size, size), jnp.float32),
+        compiler_params=pltpu.CompilerParams(vmem_limit_bytes=16 * 1024 * 1024),
+        name="unpack",
+    )(packed)
+
+
 def spread_out(value):
     return lax.all_to_all(value, ("row", "col"), split_axis=0, concat_axis=0, tiled=True)
 
@@ -475,6 +495,7 @@
         outers.append((upper, lower, outer_west, outer_east))
     levels, probe, _ = lax.optimization_barrier((levels, illumination, uppers[0]))
     ill_power = exponent(2.0 * jnp.max(jnp.abs(probe)))
+    levels, ill_power = lax.optimization_barrier((levels, ill_power))
     arrived = lax.all_to_all(
         levels,
         "row",
@@ -528,9 +549,7 @@
     mine = narrowed(mine, step_power).reshape(1, 2 * PIECE, LANES)
     copies = jnp.broadcast_to(mine, (devices, 2 * PIECE, LANES))
     result = spread_out(copies)
-    result = result.reshape(size // LANES, size // PIECE, 2, PIECE, LANES)
-    result = result.transpose(2, 1, 3, 0, 4).reshape(2, size, size)
-    illumination_step = widened(result, step_power)
+    illumination_step = unpacked(widened(result, step_power), size)
     middle = (
         column[:, :, tile_rows : 2 * tile_rows]
         + opened(from_lower)[0]

time: 211 us -> 216 us (1.024)
  starting transfers between devices: 52.1 us -> 56 us
  waiting for transfers between devices: 60.4 us -> 64 us
  other arithmetic: 25.8 us -> 22.9 us
    ppermute x16, waiting for transfers between devices: 59.3 us -> 64 us  [passed_along(): return lax.ppermute(value, axis, pairs)]
    mul x2 -> x0, local copies, waits for them, and re-layouts: 3.2 us -> none  [widened(): return value.astype(jnp.float32) * jnp.exp2(power - 15.0)]
    all_to_all x2, starting transfers between devices: 17.6 us -> 20.7 us  [spread_out(): lax.all_to_all(value, ('row', 'col'), split_axis=0, concat_axis=0, tiled=...]
    unnamed x7 -> x21, local copies, waits for them, and re-layouts: 1.32 us -> 3.77 us
  transfers between devices with their start and end apart: 20 -> 20, of which waited for: 10 -> 8; matrix products, arithmetic and copies ran while one was open for 13% -> 11% of each run, Pallas kernels for 10% -> 10%
where the time goes in v7:
time: 216 us
  waiting for transfers between devices  64 us (30%)
  starting transfers between devices  56 us (26%)
  Pallas kernels  48.4 us (22%)
  other arithmetic  22.9 us (11%)
  local copies, waits for them, and re-layouts  17 us (8%)
  between operations  7.29 us (3%)
    ppermute x16, waiting for transfers between devices, passed_along(): return lax.ppermute(value, axis, pairs)  64 us
    ppermute x16, starting transfers between devices, passed_along(): return lax.ppermute(value, axis, pairs)  30.3 us
    pallas_call x1, Pallas kernels, run_backward(): pl.pallas_call(backward_kernel, grid_spec=pltpu.PrefetchScalarGridSpec(nu...  25.7 us
    pallas_call x1, Pallas kernels, run_forward(): pl.pallas_call(forward_kernel, grid_spec=pltpu.PrefetchScalarGridSpec(num...  21 us
    all_to_all x2, starting transfers between devices, spread_out(): lax.all_to_all(value, ('row', 'col'), split_axis=0, concat_axis=0, tiled=...  20.7 us
    all_to_all x1, starting transfers between devices, shards(): lax.all_to_all(levels, 'row', split_axis=0, concat_axis=0, tiled=True, ax...  5.03 us
  transfers between devices with their start and end apart: 20, of which 8 were waited for; matrix products, arithmetic and copies ran while one was open for 11% of the time, Pallas kernels for 10%

profile of v7, /device:TPU:1, one launch (start us, length us, event | category | flops | bytes accessed | tf_op | source)
XLA Modules:
  0.0 215.6 jit_solution(17545427645315171881)
XLA Ops:
  0.6 2.4 %fusion.10 = (f32[1,256,512]{2,1,0:T(8,128)}, f32[1,256,512]{2,1,0:T(8,128)}) fusion(f32[2,256,512]{2,1,0:T(8,128)} %refs_0_.1), kind=kLoop, calls=%fused_computation.42 | loop fusion | bytes 2097152 | tf_op jit(solution)/shard_map/slice | solution.py:474
  3.0 2.0 collective-permute-start.4
  5.1 4.7 %collective-permute-start.5 = (f32[1,256,512]{2,1,0:T(8,128)}, f32[1,256,512]{2,1,0:T(8,128)}, u32[]{:S(2)}, u32[]{:S(2)}) collective-permute-start(f32[1,256,512]{2,1,0:T(8,128)} %get-tuple-element.42), channel_id=1, source_target_pairs={{0,120},{8,0},{16,8},{24,16},{32,24},{40,32},{48,40},{56,48},{64,5... | collective-permute-start | bytes 1572872 | tf_op jit(solution)/shard_map/ppermute | solution.py:22
  9.8 4.8 %collective-permute-start.9 = (f32[1,256,512]{2,1,0:T(8,128)}, f32[1,256,512]{2,1,0:T(8,128)}, u32[]{:S(2)}, u32[]{:S(2)}) collective-permute-start(f32[1,256,512]{2,1,0:T(8,128)} %get-tuple-element.41), channel_id=1, source_target_pairs={{0,120},{8,0},{16,8},{24,16},{32,24},{40,32},{48,40},{56,48},{64,5... | collective-permute-start | bytes 1572872 | tf_op jit(solution)/shard_map/ppermute | solution.py:22
  14.6 0.2 fusion.9
  14.8 2.7 %collective-permute-start.12 = (bf16[16,2,2,16,512]{4,3,2,1,0:T(8,128)(2,1)S(1)}, bf16[16,2,2,16,512]{4,3,2,1,0:T(8,128)(2,1)S(1)}, u32[]{:S(2)}, u32[]{:S(2)}) collective-permute-start(bf16[16,2,2,16,512]{4,3,2,1,0:T(8,128)(2,1)S(1)} %get-tuple-element.39), channel_id=1, source_target_pairs={{0,1},{1,2},{2,3},{3,4},{4,5},{5,6},{6,7},{7,0},{8,9},{9,10},{10,1... | collective-permute-start | bytes 3145736 | tf_op jit(solution)/shard_map/ppermute | solution.py:22
  17.5 1.1 fusion.11
  18.7 0.1 copy.22
  18.9 2.9 %collective-permute-done.4.refs_3_ = f32[1,256,512]{2,1,0:T(8,128)} collective-permute-done((f32[1,256,512]{2,1,0:T(8,128)}, f32[1,256,512]{2,1,0:T(8,128)}, u32[]{:S(2)}, u32[]{:S(2)}) %collective-permute-start.4) | collective-permute-done | bytes 524320 | tf_op jit(solution)/shard_map/ppermute | solution.py:22
  21.7 1.1 fusion.14
  22.8 1.3 collective-permute-start.1
  24.1 1.1 fusion.15
  25.2 0.8 pad_maximum_fusion.1
  26.0 0.8 pad_maximum_fusion.2
  26.8 6.2 %collective-permute-done.8.refs_7_ = f32[1,256,512]{2,1,0:T(8,128)} collective-permute-done((f32[1,256,512]{2,1,0:T(8,128)}, f32[1,256,512]{2,1,0:T(8,128)}, u32[]{:S(2)}, u32[]{:S(2)}) %collective-permute-start.8) | collective-permute-done | bytes 524320 | tf_op jit(solution)/shard_map/ppermute | solution.py:22
  33.0 2.5 %collective-permute-start.2 = (f32[2,256,256]{2,1,0:T(8,128)}, f32[2,256,256]{2,1,0:T(8,128)}, u32[]{:S(2)}, u32[]{:S(2)}) collective-permute-start(f32[2,256,256]{2,1,0:T(8,128)} %get-tuple-element.44), channel_id=1, source_target_pairs={{0,1},{1,2},{2,3},{3,4},{4,5},{5,6},{6,7},{7,0},{8,9},{9,10},{10,1... | collective-permute-start | bytes 1572872 | tf_op jit(solution)/shard_map/ppermute | solution.py:22
  35.4 2.1 fusion.12
  37.5 1.7 collective-permute-start.6
  39.3 1.5 pad_maximum_fusion
  40.8 0.8 copy-done.1
  41.6 0.9 abs_reduce_fusion
  43.3 5.0 %all-to-all-start = ((bf16[16,4,2,16,512]{4,3,2,1,0:T(8,128)(2,1)}), bf16[16,4,2,16,512]{4,3,2,1,0:T(8,128)(2,1)}, u32[]{:S(2)}, u32[]{:S(2)}) async-start(bf16[16,4,2,16,512]{4,3,2,1,0:T(8,128)(2,1)} %pad_maximum_fusion), calls=%async_computation | async-start | bytes 4194304 | tf_op jit(solution)/shard_map/all_to_all | solution.py:499
  48.4 1.0 collective-permute-start.11
  49.4 0.8 collective-permute-start.10
  50.2 1.6 collective-permute-start.7
  51.8 0.6 pad_add_fusion.offs
  52.4 5.0 %collective-permute-done.11.refs_10_ = f32[1,512,256]{2,1,0:T(8,128)S(1)} collective-permute-done((f32[1,512,256]{2,1,0:T(8,128)S(1)}, f32[1,512,256]{2,1,0:T(8,128)S(1)}, u32[]{:S(2)}, u32[]{:S(2)}) %collective-permute-start.11) | collective-permute-done | bytes 524320 | tf_op jit(solution)/shard_map/ppermute | solution.py:22
  57.5 0.8 copy-done.8
  58.3 0.8 copy-done.9
  59.0 4.0 %collective-permute-done.7.refs_6_ = f32[1,512,256]{2,1,0:T(8,128)} collective-permute-done((f32[1,512,256]{2,1,0:T(8,128)S(1)}, f32[1,512,256]{2,1,0:T(8,128)}, u32[]{:S(2)}, u32[]{:S(2)}) %collective-permute-start.7) | collective-permute-done | bytes 524320 | tf_op jit(solution)/shard_map/ppermute | solution.py:22
  63.1 21.0 %forward.1 = (f32[4,2,512,512]{3,2,1,0:T(8,128)}, f32[4,2,512,512]{3,2,1,0:T(8,128)}, f32[2,8,128]{2,1,0:T(8,128)}) custom-call(s32[4,2]{1,0:T(4,128)} %pad_add_fusion.offs, f32[2,256,512]{2,1,0:T(8,128)} %refs_0_.1, f32[2,256,256]{2,1,0:T(8,128)} %collective-permute-done.2.refs_1_, f32[2,256,256]{2,1,0:T(8,128)} %collective-permute-done.3.refs_2_, ...), custom_call_target="tpu_custom_call" | custom-call | flops 8589934592 | bytes 30000000 | tf_op jit(solution)/shard_map/forward/pallas_call | solution.py:364
  84.1 1.3 slice_reduce_fusion.2
  86.9 0.7 pad_maximum_fusion.5.powers
  87.6 25.7 %backward.1 = (f32[2,8,776,128]{3,2,1,0:T(8,128)}, f32[4,32,56,128]{3,2,1,0:T(8,128)}) custom-call(s32[4,2]{1,0:T(4,128)} %pad_add_fusion.offs, s32[32]{0:T(128)} %order.1, f32[3]{0:T(128)} %pad_maximum_fusion.5.powers, f32[4,2,512,512]{3,2,1,0:T(8,128)} %get-tuple-element.19.far, f32[4,2,512,512]{3,2,1,0:T(8,128)} %get-tuple-element.20.patch, ...), custom_call_target="tpu_custom_call" | custom-call | flops 8589934592 | bytes 30000000 | tf_op jit(solution)/shard_map/backward/pallas_call | solution.py:400
  113.3 3.7 %fusion = f16[128,56,128]{2,1,0:T(8,128)(2,1)} fusion(f32[4,32,56,128]{3,2,1,0:T(8,128)} %get-tuple-element.23, f32[56]{0:T(128)S(1)} %compare_select_fusion.1), kind=kLoop, calls=%fused_computation.1 | loop fusion | flops 1835008 | bytes 5505248 | tf_op jit(solution)/shard_map/convert_element_type | solution.py:529
  117.0 10.3 %all-to-all-start.1 = ((f16[128,56,128]{2,1,0:T(8,128)(2,1)}), f16[128,56,128]{2,1,0:T(8,128)(2,1)}, u32[]{:S(2)}, u32[]{:S(2)}) async-start(f16[128,56,128]{2,1,0:T(8,128)(2,1)} %fusion), calls=%async_computation.1 | async-start | bytes 3670016 | tf_op jit(solution)/shard_map/all_to_all | solution.py:458
  127.4 2.3 %multiply_convert_fusion.1 = (f16[2,2,776,128]{3,2,1,0:T(8,128)(2,1)S(1)}, f16[2,2,776,128]{3,2,1,0:T(8,128)(2,1)S(1)}) fusion(f32[2,8,776,128]{3,2,1,0:T(8,128)} %get-tuple-element.22, f32[776]{0:T(1024)S(1)} %fusion.8), kind=kLoop, calls=%fused_computation.8 | loop fusion | flops 1589248 | bytes 4770848 | tf_op jit(solution)/shard_map/convert_element_type | solution.py:61
  129.7 1.6 collective-permute-start.13
  131.3 23.7 %collective-permute-done.13 = f16[2,2,776,128]{3,2,1,0:T(8,128)(2,1)S(1)} collective-permute-done((f16[2,2,776,128]{3,2,1,0:T(8,128)(2,1)S(1)}, f16[2,2,776,128]{3,2,1,0:T(8,128)(2,1)S(1)}, u32[]{:S(2)}, u32[]{:S(2)}) %collective-permute-start.13) | collective-permute-done | bytes 794656 | tf_op jit(solution)/shard_map/ppermute | solution.py:22
  155.1 0.6 slice.165
  156.3 0.8 collective-permute-done.14
  157.1 0.6 slice.167
  158.4 0.1 convert_multiply_fusion.2
  158.5 0.1 convert_multiply_fusion.1
  158.7 2.3 %maximum_add_fusion = f32[2,4,768,128]{3,2,1,0:T(8,128)S(1)} fusion(f32[2,2,768,128]{3,2,1,0:T(8,128)S(1)} %convert_multiply_fusion.1, f32[2,2,768,128]{3,2,1,0:T(8,128)S(1)} %convert_multiply_fusion.2, f32[2,8,776,128]{3,2,1,0:T(8,128)} %get-tuple-element.22), kind=kLoop, calls=%fused_computation.2 | loop fusion | flops 1572864 | bytes 9437184 | tf_op jit(solution)/shard_map/add | solution.py:534
  161.0 1.0 slice_convert_fusion
  162.0 1.5 slice_reduce_fusion
  163.5 0.1 multiply_exponential_fusion
  163.6 2.1 multiply_reduce_fusion
  166.4 1.1 broadcast_in_dim.73
  167.5 10.3 %all-to-all-start.2 = ((f16[128,32,128]{2,1,0:T(8,128)(2,1)}), f16[128,32,128]{2,1,0:T(8,128)(2,1)}, u32[]{:S(2)}, u32[]{:S(2)}) async-start(f16[128,32,128]{2,1,0:T(8,128)(2,1)} %broadcast_in_dim.73), calls=%async_computation.2 | async-start | bytes 2097152 | tf_op jit(solution)/shard_map/all_to_all | solution.py:458
  177.9 0.3 fusion.2
  178.2 0.1 concatenate.34
  178.3 5.5 %collective-permute-start.15 = (f16[2,4,264,128]{3,2,1,0:T(8,128)(2,1)S(1)}, f16[2,4,264,128]{3,2,1,0:T(8,128)(2,1)S(1)}, u32[]{:S(2)}, u32[]{:S(2)}) collective-permute-start(f16[2,4,264,128]{3,2,1,0:T(8,128)(2,1)S(1)} %concatenate.34), channel_id=1, source_target_pairs={{0,120},{8,0},{16,8},{24,16},{32,24},{40,32},{48,40},{56,48},{64,5... | collective-permute-start | bytes 1622024 | tf_op jit(solution)/shard_map/ppermute | solution.py:22
  183.7 0.1 concatenate.35
  183.9 17.7 %collective-permute-done.15 = f16[2,4,264,128]{3,2,1,0:T(8,128)(2,1)S(1)} collective-permute-done((f16[2,4,264,128]{3,2,1,0:T(8,128)(2,1)S(1)}, f16[2,4,264,128]{3,2,1,0:T(8,128)(2,1)S(1)}, u32[]{:S(2)}, u32[]{:S(2)}) %collective-permute-start.15) | collective-permute-done | bytes 540704 | tf_op jit(solution)/shard_map/ppermute | solution.py:22
  201.6 0.5 slice.171
  202.8 3.7 %collective-permute-done.16 = f16[2,4,264,128]{3,2,1,0:T(8,128)(2,1)S(1)} collective-permute-done((f16[2,4,264,128]{3,2,1,0:T(8,128)(2,1)S(1)}, f16[2,4,264,128]{3,2,1,0:T(8,128)(2,1)S(1)}, u32[]{:S(2)}, u32[]{:S(2)}) %collective-permute-start.16) | collective-permute-done | bytes 540704 | tf_op jit(solution)/shard_map/ppermute | solution.py:22
  206.6 0.5 slice.174
  207.8 1.2 fusion.4
  209.0 1.6 copy.24
  210.5 1.3 copy.25
  212.5 1.5 convert_multiply_fusion.packed
  214.0 1.6 unpack.1
  (44 shorter events, 0.4 us)
Async XLA Ops:
  0.6 14.0 %copy-start.2 = (bf16[64,2,16,512]{3,2,1,0:T(8,128)(2,1)S(1)}, bf16[64,2,16,512]{3,2,1,0:T(8,128)(2,1)}, u32[]{:S(2)}) copy-start(bf16[64,2,16,512]{3,2,1,0:T(8,128)(2,1)} %param.8) | copy-start | bytes 6291460
  3.0 18.7 %collective-permute-start.4 = (f32[1,256,512]{2,1,0:T(8,128)}, f32[1,256,512]{2,1,0:T(8,128)}, u32[]{:S(2)}, u32[]{:S(2)}) collective-permute-start(f32[1,256,512]{2,1,0:T(8,128)} %get-tuple-element.42), channel_id=1, source_target_pairs={{0,8},{8,16},{16,24},{24,32},{32,40},{40,48},{48,56},{56,64},{64,7... | collective-permute-start | bytes 1572872 | tf_op jit(solution)/shard_map/ppermute | solution.py:22
  5.1 17.8 %collective-permute-start.5 = (f32[1,256,512]{2,1,0:T(8,128)}, f32[1,256,512]{2,1,0:T(8,128)}, u32[]{:S(2)}, u32[]{:S(2)}) collective-permute-start(f32[1,256,512]{2,1,0:T(8,128)} %get-tuple-element.42), channel_id=1, source_target_pairs={{0,120},{8,0},{16,8},{24,16},{32,24},{40,32},{48,40},{56,48},{64,5... | collective-permute-start | bytes 1572872 | tf_op jit(solution)/shard_map/ppermute | solution.py:22
  9.8 23.2 %collective-permute-start.8 = (f32[1,256,512]{2,1,0:T(8,128)}, f32[1,256,512]{2,1,0:T(8,128)}, u32[]{:S(2)}, u32[]{:S(2)}) collective-permute-start(f32[1,256,512]{2,1,0:T(8,128)} %get-tuple-element.41), channel_id=1, source_target_pairs={{0,8},{8,16},{16,24},{24,32},{32,40},{40,48},{48,56},{56,64},{64,7... | collective-permute-start | bytes 1572872 | tf_op jit(solution)/shard_map/ppermute | solution.py:22
  9.8 25.6 %collective-permute-start.9 = (f32[1,256,512]{2,1,0:T(8,128)}, f32[1,256,512]{2,1,0:T(8,128)}, u32[]{:S(2)}, u32[]{:S(2)}) collective-permute-start(f32[1,256,512]{2,1,0:T(8,128)} %get-tuple-element.41), channel_id=1, source_target_pairs={{0,120},{8,0},{16,8},{24,16},{32,24},{40,32},{48,40},{56,48},{64,5... | collective-permute-start | bytes 1572872 | tf_op jit(solution)/shard_map/ppermute | solution.py:22
  14.6 3.0 %copy-start = (f32[2,256,512]{2,1,0:T(8,128)S(1)}, f32[2,256,512]{2,1,0:T(8,128)}, u32[]{:S(2)}) copy-start(f32[2,256,512]{2,1,0:T(8,128)} %refs_0_.1) | copy-start | bytes 3145732
  14.8 3.8 %copy-start.7 = (s32[1,1,4,2]{2,3,1,0:T(2,128)S(1)}, s32[1,1,4,2]{2,3,1,0:T(2,128)}, u32[]{:S(2)}) copy-start(s32[1,1,4,2]{2,3,1,0:T(2,128)} %param.10) | copy-start | bytes 100
  14.8 22.7 %collective-permute-start.12 = (bf16[16,2,2,16,512]{4,3,2,1,0:T(8,128)(2,1)S(1)}, bf16[16,2,2,16,512]{4,3,2,1,0:T(8,128)(2,1)S(1)}, u32[]{:S(2)}, u32[]{:S(2)}) collective-permute-start(bf16[16,2,2,16,512]{4,3,2,1,0:T(8,128)(2,1)S(1)} %get-tuple-element.39), channel_id=1, source_target_pairs={{0,1},{1,2},{2,3},{3,4},{4,5},{5,6},{6,7},{7,0},{8,9},{9,10},{10,1... | collective-permute-start | bytes 3145736 | tf_op jit(solution)/shard_map/ppermute | solution.py:22
  21.7 26.7 %collective-permute-start = (s32[2,2]{1,0:T(2,128)S(1)}, s32[2,2]{1,0:T(2,128)S(1)}, u32[]{:S(2)}, u32[]{:S(2)}) collective-permute-start(s32[2,2]{1,0:T(2,128)S(1)} %bitcast.25), channel_id=1, source_target_pairs={{0,9},{1,10},{2,11},{3,12},{4,13},{5,14},{6,15},{7,8},{8,17},{9,18... | collective-permute-start | bytes 56 | tf_op jit(solution)/shard_map/ppermute | solution.py:32
  22.8 26.6 %collective-permute-start.1 = (s32[2,2]{1,0:T(2,128)S(1)}, s32[2,2]{1,0:T(2,128)S(1)}, u32[]{:S(2)}, u32[]{:S(2)}) collective-permute-start(s32[2,2]{1,0:T(2,128)S(1)} %bitcast.24), channel_id=1, source_target_pairs={{0,8},{8,16},{16,24},{24,32},{32,40},{40,48},{48,56},{56,64},{64,7... | collective-permute-start | bytes 56 | tf_op jit(solution)/shard_map/ppermute | solution.py:22
  33.0 17.2 %collective-permute-start.2 = (f32[2,256,256]{2,1,0:T(8,128)}, f32[2,256,256]{2,1,0:T(8,128)}, u32[]{:S(2)}, u32[]{:S(2)}) collective-permute-start(f32[2,256,256]{2,1,0:T(8,128)} %get-tuple-element.44), channel_id=1, source_target_pairs={{0,1},{1,2},{2,3},{3,4},{4,5},{5,6},{6,7},{7,0},{8,9},{9,10},{10,1... | collective-permute-start | bytes 1572872 | tf_op jit(solution)/shard_map/ppermute | solution.py:22
  35.4 17.0 %collective-permute-start.3 = (f32[2,256,256]{2,1,0:T(8,128)}, f32[2,256,256]{2,1,0:T(8,128)}, u32[]{:S(2)}, u32[]{:S(2)}) collective-permute-start(f32[2,256,256]{2,1,0:T(8,128)} %get-tuple-element.43), channel_id=1, source_target_pairs={{0,7},{1,0},{2,1},{3,2},{4,3},{5,4},{6,5},{7,6},{8,15},{9,8},{10,9... | collective-permute-start | bytes 1572872 | tf_op jit(solution)/shard_map/ppermute | solution.py:22
  37.5 20.7 %collective-permute-start.6 = (f32[1,512,256]{2,1,0:T(8,128)}, f32[1,512,256]{2,1,0:T(8,128)}, u32[]{:S(2)}, u32[]{:S(2)}) collective-permute-start(f32[1,512,256]{2,1,0:T(8,128)} %pad_maximum_fusion.1), channel_id=1, source_target_pairs={{0,1},{1,2},{2,3},{3,4},{4,5},{5,6},{6,7},{7,0},{8,9},{9,10},{10,1... | collective-permute-start | bytes 1572872 | tf_op jit(solution)/shard_map/ppermute | solution.py:22
  39.3 2.3 %copy-start.1 = (f32[2,512,512]{2,1,0:T(8,128)S(1)}, f32[2,512,512]{2,1,0:T(8,128)}, u32[]{:S(2)}) copy-start(f32[2,512,512]{2,1,0:T(8,128)} %ill.1) | copy-start | bytes 6291460
  43.2 5.1 %copy-start.4 = (f32[1,256,256]{2,1,0:T(8,128)S(1)}, f32[1,256,256]{2,1,0:T(8,128)}, u32[]{:S(2)}) copy-start(f32[1,256,256]{2,1,0:T(8,128)} %get-tuple-element.45) | copy-start | bytes 786436
  43.2 5.1 %copy-start.5 = (f32[1,256,256]{2,1,0:T(8,128)S(1)}, f32[1,256,256]{2,1,0:T(8,128)}, u32[]{:S(2)}) copy-start(f32[1,256,256]{2,1,0:T(8,128)} %get-tuple-element.56) | copy-start | bytes 786436
  43.2 5.1 %copy-start.3 = (f32[1,256,256]{2,1,0:T(8,128)S(1)}, f32[1,256,256]{2,1,0:T(8,128)}, u32[]{:S(2)}) copy-start(f32[1,256,256]{2,1,0:T(8,128)} %get-tuple-element.55) | copy-start | bytes 786436
  43.3 44.3 %all-to-all-start = ((bf16[16,4,2,16,512]{4,3,2,1,0:T(8,128)(2,1)}), bf16[16,4,2,16,512]{4,3,2,1,0:T(8,128)(2,1)}, u32[]{:S(2)}, u32[]{:S(2)}) async-start(bf16[16,4,2,16,512]{4,3,2,1,0:T(8,128)(2,1)} %pad_maximum_fusion), calls=%async_computation | async-start | bytes 4194304 | tf_op jit(solution)/shard_map/all_to_all | solution.py:499
  48.3 1.9 copy-start.6
  48.4 9.0 %collective-permute-start.11 = (f32[1,512,256]{2,1,0:T(8,128)S(1)}, f32[1,512,256]{2,1,0:T(8,128)S(1)}, u32[]{:S(2)}, u32[]{:S(2)}) collective-permute-start(f32[1,512,256]{2,1,0:T(8,128)S(1)} %pad_maximum_fusion.4), channel_id=1, source_target_pairs={{0,7},{1,0},{2,1},{3,2},{4,3},{5,4},{6,5},{7,6},{8,15},{9,8},{10,9... | collective-permute-start | bytes 1572872 | tf_op jit(solution)/shard_map/ppermute | solution.py:22
  49.4 8.0 %collective-permute-start.10 = (f32[1,512,256]{2,1,0:T(8,128)S(1)}, f32[1,512,256]{2,1,0:T(8,128)S(1)}, u32[]{:S(2)}, u32[]{:S(2)}) collective-permute-start(f32[1,512,256]{2,1,0:T(8,128)S(1)} %pad_maximum_fusion.3), channel_id=1, source_target_pairs={{0,1},{1,2},{2,3},{3,4},{4,5},{5,6},{6,7},{7,0},{8,9},{9,10},{10,1... | collective-permute-start | bytes 1572872 | tf_op jit(solution)/shard_map/ppermute | solution.py:22
  50.2 12.9 %collective-permute-start.7 = (f32[1,512,256]{2,1,0:T(8,128)S(1)}, f32[1,512,256]{2,1,0:T(8,128)}, u32[]{:S(2)}, u32[]{:S(2)}) collective-permute-start(f32[1,512,256]{2,1,0:T(8,128)S(1)} %copy-done.6), channel_id=1, source_target_pairs={{0,7},{1,0},{2,1},{3,2},{4,3},{5,4},{6,5},{7,6},{8,15},{9,8},{10,9... | collective-permute-start | bytes 1572872 | tf_op jit(solution)/shard_map/ppermute | solution.py:22
  57.4 0.8 copy-start.8
  58.3 0.8 copy-start.9
  117.0 44.0 %all-to-all-start.1 = ((f16[128,56,128]{2,1,0:T(8,128)(2,1)}), f16[128,56,128]{2,1,0:T(8,128)(2,1)}, u32[]{:S(2)}, u32[]{:S(2)}) async-start(f16[128,56,128]{2,1,0:T(8,128)(2,1)} %fusion), calls=%async_computation.1 | async-start | bytes 3670016 | tf_op jit(solution)/shard_map/all_to_all | solution.py:458
  129.7 25.4 %collective-permute-start.13 = (f16[2,2,776,128]{3,2,1,0:T(8,128)(2,1)S(1)}, f16[2,2,776,128]{3,2,1,0:T(8,128)(2,1)S(1)}, u32[]{:S(2)}, u32[]{:S(2)}) collective-permute-start(f16[2,2,776,128]{3,2,1,0:T(8,128)(2,1)S(1)} %get-tuple-element.35), channel_id=1, source_target_pairs={{0,1},{1,2},{2,3},{3,4},{4,5},{5,6},{6,7},{7,0},{8,9},{9,10},{10,1... | collective-permute-start | bytes 2383880 | tf_op jit(solution)/shard_map/ppermute | solution.py:22
  131.3 25.8 %collective-permute-start.14 = (f16[2,2,776,128]{3,2,1,0:T(8,128)(2,1)S(1)}, f16[2,2,776,128]{3,2,1,0:T(8,128)(2,1)S(1)}, u32[]{:S(2)}, u32[]{:S(2)}) collective-permute-start(f16[2,2,776,128]{3,2,1,0:T(8,128)(2,1)S(1)} %get-tuple-element.36), channel_id=1, source_target_pairs={{0,7},{1,0},{2,1},{3,2},{4,3},{5,4},{6,5},{7,6},{8,15},{9,8},{10,9... | collective-permute-start | bytes 2383880 | tf_op jit(solution)/shard_map/ppermute | solution.py:22
  167.5 44.9 %all-to-all-start.2 = ((f16[128,32,128]{2,1,0:T(8,128)(2,1)}), f16[128,32,128]{2,1,0:T(8,128)(2,1)}, u32[]{:S(2)}, u32[]{:S(2)}) async-start(f16[128,32,128]{2,1,0:T(8,128)(2,1)} %broadcast_in_dim.73), calls=%async_computation.2 | async-start | bytes 2097152 | tf_op jit(solution)/shard_map/all_to_all | solution.py:458
  178.3 23.3 %collective-permute-start.15 = (f16[2,4,264,128]{3,2,1,0:T(8,128)(2,1)S(1)}, f16[2,4,264,128]{3,2,1,0:T(8,128)(2,1)S(1)}, u32[]{:S(2)}, u32[]{:S(2)}) collective-permute-start(f16[2,4,264,128]{3,2,1,0:T(8,128)(2,1)S(1)} %concatenate.34), channel_id=1, source_target_pairs={{0,120},{8,0},{16,8},{24,16},{32,24},{40,32},{48,40},{56,48},{64,5... | collective-permute-start | bytes 1622024 | tf_op jit(solution)/shard_map/ppermute | solution.py:22
  183.9 22.7 %collective-permute-start.16 = (f16[2,4,264,128]{3,2,1,0:T(8,128)(2,1)S(1)}, f16[2,4,264,128]{3,2,1,0:T(8,128)(2,1)S(1)}, u32[]{:S(2)}, u32[]{:S(2)}) collective-permute-start(f16[2,4,264,128]{3,2,1,0:T(8,128)(2,1)S(1)} %concatenate.35), channel_id=1, source_target_pairs={{0,8},{8,16},{16,24},{24,32},{32,40},{40,48},{48,56},{56,64},{64,7... | collective-permute-start | bytes 1622024 | tf_op jit(solution)/shard_map/ppermute | solution.py:22

commit v8 on v4

--- a/solution.py
+++ b/solution.py
@@ -72,27 +72,29 @@
 
 
 def region_copies(pieces, region, sems):
-    upper, lower, middle, west, east, outer_west, outer_east = pieces
+    middle, west, east = pieces[:3]
     rows, cols, edge = middle.shape[1], middle.shape[2], west.shape[2]
     center, right = edge // LANES, (edge + cols) // LANES
-    moves = [
-        (upper, 0, 0, center),
-        (middle, 0, 1, center),
-        (lower, 0, 2, center),
-        (west, 0, 1, 0),
-        (east, 0, 1, right),
-        (outer_west, 0, 0, 0),
-        (outer_west, 1, 2, 0),
-        (outer_east, 0, 0, right),
-        (outer_east, 1, 2, right),
-    ]
+    both = pl.ds(0, 2)
+    moves = [(middle, both, 0, 1, center), (west, both, 0, 1, 0), (east, both, 0, 1, right)]
+    for plane in range(2):
+        upper, lower, outer_west, outer_east = pieces[3 + 4 * plane : 7 + 4 * plane]
+        one = pl.ds(plane, 1)
+        moves += [
+            (upper, one, 0, 0, center),
+            (lower, one, 0, 2, center),
+            (outer_west, one, 0, 0, 0),
+            (outer_west, one, 1, 2, 0),
+            (outer_east, one, 0, 0, right),
+            (outer_east, one, 1, 2, right),
+        ]
     copies = []
-    for piece, source, target, first in moves:
+    for piece, planes, source, target, first in moves:
         for block in range(piece.shape[2] // LANES):
             copies.append(
                 pltpu.make_async_copy(
                     piece.at[:, pl.ds(source * rows, rows), pl.ds(block * LANES, LANES)],
-                    region.at[:, first + block, pl.ds(target * rows, rows)],
+                    region.at[planes, first + block, pl.ds(target * rows, rows)],
                     sems.at[len(copies)],
                 )
             )
@@ -100,7 +102,7 @@
 
 
 def forward_kernel(offs, *refs):
-    pieces, tables, refs = refs[:7], refs[7:10], refs[10:]
+    pieces, tables, refs = refs[:11], refs[11:14], refs[14:]
     ill, far, patch, region, left, right, wave, half, region_sems, table_sems = refs
     slot = pl.program_id(0)
     size = ill.shape[-1]
@@ -113,10 +115,12 @@
     def _():
         region_moves = region_copies(pieces, region, region_sems)
         table_moves = table_copies(tables, left, right, table_sems)
-        for move in region_moves + table_moves:
+        for move in region_moves:
             move.start()
-        for move in region_moves + table_moves:
+        for move in region_moves:
             move.wait()
+        for move in table_moves:
+            move.start()
 
     def extract(step, carry):
         at = pl.multiple_of(step * CHUNK, CHUNK)
@@ -149,7 +153,13 @@
             last = now
         return carry
 
-    lax.fori_loop(0, size // CHUNK, extract, 0, unroll=4)
+    lax.fori_loop(0, size // CHUNK, extract, 0, unroll=8)
+
+    @pl.when(slot == 0)
+    def _():
+        for move in table_copies(tables, left, right, table_sems):
+            move.wait()
+
     for block in range(size // BLOCK):
         to = slice(block * BLOCK, (block + 1) * BLOCK)
         also = slice(size + block * BLOCK, size + (block + 1) * BLOCK)
@@ -231,7 +241,7 @@
         corr[pl.ds(size + at, height), :] = (factor * far_imag).astype(jnp.bfloat16)
         return carry
 
-    lax.fori_loop(0, modules, correct, 0, unroll=4)
+    lax.fori_loop(0, modules, correct, 0, unroll=8)
 
     @pl.when(slot == 0)
     def _():
@@ -291,7 +301,7 @@
             last = now
         return carry
 
-    lax.fori_loop(0, size // CHUNK, spread, 0, unroll=4)
+    lax.fori_loop(0, size // CHUNK, spread, 0, unroll=8)
 
 
 def whole(shape):
@@ -311,7 +321,7 @@
 def run_forward(offs, pieces, tables, ill):
     slots = offs.shape[0]
     size = ill.shape[-1]
-    rows, cols, edge = pieces[2].shape[1], pieces[2].shape[2], pieces[3].shape[2]
+    rows, cols, edge = pieces[0].shape[1], pieces[0].shape[2], pieces[1].shape[2]
     planes = jax.ShapeDtypeStruct((slots, 2, size, size), jnp.float32)
     return pl.pallas_call(
         forward_kernel,
@@ -330,7 +340,7 @@
                 pltpu.VMEM((2 * size, 2 * size), jnp.bfloat16),
                 pltpu.VMEM((2 * size, size), jnp.bfloat16),
                 pltpu.VMEM((size, 2 * size), jnp.bfloat16),
-                pltpu.SemaphoreType.DMA((24,)),
+                pltpu.SemaphoreType.DMA((40,)),
                 pltpu.SemaphoreType.DMA((8,)),
             ],
         ),
@@ -387,18 +397,20 @@
 
 def unpack_kernel(packed, out):
     size = out.shape[1]
-    for plane in range(2):
-        out[plane] = packed[:, plane].reshape(size, LANES)
+    per = size // PIECE
+    for column in range(size // LANES):
+        for plane in range(2):
+            part = packed[column * per : (column + 1) * per, plane * PIECE : (plane + 1) * PIECE]
+            out[plane, :, column * LANES : (column + 1) * LANES] = part.reshape(size, LANES)
 
 
 def unpacked(packed, size):
-    packed = packed.reshape(size * size // (PIECE * LANES), 2, PIECE, LANES)
     return pl.pallas_call(
         unpack_kernel,
-        grid=(size // LANES,),
-        in_specs=[pl.BlockSpec((size // PIECE, 2, PIECE, LANES), lambda at: (at, 0, 0, 0))],
-        out_specs=pl.BlockSpec((2, size, LANES), lambda at: (0, 0, at)),
+        in_specs=[pl.BlockSpec(memory_space=pltpu.VMEM)],
+        out_specs=pl.BlockSpec(memory_space=pltpu.VMEM),
         out_shape=jax.ShapeDtypeStruct((2, size, size), jnp.float32),
+        compiler_params=pltpu.CompilerParams(vmem_limit_bytes=16 * 1024 * 1024),
         name="unpack",
     )(packed)
 
@@ -418,8 +430,10 @@
     late = slots // 2
     edge = tile_cols // 2
     grouped = measured.reshape(senders, slots, per, height, size)
-    upper = passed_along(specimen, "row", 1)
-    lower = passed_along(specimen, "row", -1)
+    uppers, lowers = [], []
+    for plane in range(2):
+        uppers.append(passed_along(specimen[plane : plane + 1], "row", 1))
+        lowers.append(passed_along(specimen[plane : plane + 1], "row", -1))
     early_offs = passed_along(scan_offsets[0, 0, :late], "row", 1)
     late_offs = passed_both(scan_offsets[0, 0, late:], 1, 1)
     offs = jnp.concatenate([late_offs, early_offs], axis=0)
@@ -427,21 +441,30 @@
     west = passed_along(specimen[:, :, edge:], "col", 1)
     east = passed_along(specimen[:, :, :edge], "col", -1)
     levels = jnp.concatenate([moved, grouped[:, :late]], axis=1)
+    tables = dft_tables(size)
     lane = lax.broadcasted_iota(jnp.int32, (devices, 1, LANES), 2)
-    peak = jnp.max(jnp.abs(specimen))
-    power = jnp.sum(specimen * specimen)
-    stats = jnp.where(lane < LANES // 2, peak, power)
+    stats = jnp.where(
+        lane < LANES // 2, jnp.max(jnp.abs(specimen)), jnp.sum(specimen * specimen)
+    )
     peaks = spread_out(stats)
     peak = jnp.maximum(jnp.max(peaks[:, :, : LANES // 2]), 1e-12)
     power = jnp.max(peaks[:, :, LANES // 2 :])
-    tables = dft_tables(size)
-    upper, lower, west, east, offs, levels, peak, power, probe = (
-        lax.optimization_barrier(
-            (upper, lower, west, east, offs, levels, peak, power, illumination)
-        )
-    )
+    outers = []
+    for plane in range(2):
+        upper, lower = uppers[plane], lowers[plane]
+        west_edges = jnp.concatenate([upper[:, :, edge:], lower[:, :, edge:]], axis=1)
+        east_edges = jnp.concatenate([upper[:, :, :edge], lower[:, :, :edge]], axis=1)
+        if plane == 0:
+            uppers[1], lowers[1], _, _ = lax.optimization_barrier(
+                (uppers[1], lowers[1], west_edges, east_edges)
+            )
+        outer_west = passed_along(west_edges, "col", 1)
+        outer_east = passed_along(east_edges, "col", -1)
+        outers.append((upper, lower, outer_west, outer_east))
+    levels, probe, _ = lax.optimization_barrier((levels, illumination, uppers[0]))
     ill_power = jnp.sum(probe * probe)
     ill_peak = jnp.maximum(jnp.max(jnp.abs(probe)), 1e-8)
+    levels, ill_power, ill_peak = lax.optimization_barrier((levels, ill_power, ill_peak))
     modulus = 1.5 * peak
     energy = jnp.minimum(
         modulus * jnp.sqrt(ill_power), 1.5 * ill_peak * jnp.sqrt(6.0 * power)
@@ -451,10 +474,6 @@
     sum_bound = slots * modulus * change_bound
     density_bound = slots * modulus * modulus
     step_bound = math.sqrt(slots * devices) * change_bound
-    west_edges = jnp.concatenate([upper[:, :, edge:], lower[:, :, edge:]], axis=1)
-    east_edges = jnp.concatenate([upper[:, :, :edge], lower[:, :, :edge]], axis=1)
-    outer_west = passed_along(west_edges, "col", 1)
-    outer_east = passed_along(east_edges, "col", -1)
     arrived = lax.all_to_all(
         levels,
         "row",
@@ -463,7 +482,7 @@
         tiled=True,
         axis_index_groups=[[(sender + 1) % senders for sender in range(senders)]],
     )
-    pieces = (upper, lower, specimen, west, east, outer_west, outer_east)
+    pieces = (specimen, west, east) + outers[0] + outers[1]
     far, patch = run_forward(offs, pieces, tables, illumination)
     region_shape = (2, (tile_cols + 2 * edge) // LANES, 3 * tile_rows, LANES)
     accum, sums = run_backward(

time: 229 us -> 205 us (0.90)
  waiting for transfers between devices: 85.4 us -> 57.3 us
  starting transfers between devices: 53 us -> 60 us
  local copies, waits for them, and re-layouts: 10.6 us -> 14.3 us
  other arithmetic: 24.3 us -> 20.7 us
  Pallas kernels: 51 us -> 48.5 us
    ppermute x1, waiting for transfers between devices: 20.4 us -> 0.01 us  [passed_both(): return lax.ppermute(value, ('row', 'col'), pairs)]
    all_to_all x3, waiting for transfers between devices: 9.12 us -> 0.01 us  [spread_out(): lax.all_to_all(value, ('row', 'col'), split_axis=0, concat_axis=0, tiled=...]
    ppermute x12 -> x16, starting transfers between devices: 22.9 us -> 27.6 us  [passed_along(): return lax.ppermute(value, axis, pairs)]
    slice x0 -> x2, local copies, waits for them, and re-layouts: none -> 3.45 us  [the longest x1 2.38 us: shards(): uppers.append(passed_along(specimen[plane:plane + 1], 'row', 1))]
    all_to_all x3, starting transfers between devices: 25.6 us -> 22.6 us  [spread_out(): lax.all_to_all(value, ('row', 'col'), split_axis=0, concat_axis=0, tiled=...]
    all_to_all x1, starting transfers between devices: 4.56 us -> 7.27 us  [shards(): lax.all_to_all(levels, 'row', split_axis=0, concat_axis=0, tiled=True, ax...]
    ppermute x1, starting transfers between devices: 0.01 us -> 2.54 us  [passed_both(): return lax.ppermute(value, ('row', 'col'), pairs)]
    ppermute x12 -> x16, waiting for transfers between devices: 55.9 us -> 57.2 us  [passed_along(): return lax.ppermute(value, axis, pairs)]
  transfers between devices with their start and end apart: 17 -> 21, of which waited for: 7 -> 5; matrix products, arithmetic and copies ran while one was open for 9% -> 12% of each run, Pallas kernels for 9% -> 10%
where the time goes in v8:
time: 205 us; the launch traced here: 204 us
  starting transfers between devices  60 us (29%)
  waiting for transfers between devices  57.3 us (28%)
  Pallas kernels  48.5 us (24%)
  other arithmetic  20.7 us (10%)
  local copies, waits for them, and re-layouts  14.3 us (7%)
  between operations  3.72 us (2%)
    ppermute x16, waiting for transfers between devices, passed_along(): return lax.ppermute(value, axis, pairs)  57.2 us
    ppermute x16, starting transfers between devices, passed_along(): return lax.ppermute(value, axis, pairs)  27.6 us
    pallas_call x1, Pallas kernels, run_backward(): pl.pallas_call(backward_kernel, grid_spec=pltpu.PrefetchScalarGridSpec(nu...  25.5 us
    all_to_all x3, starting transfers between devices, spread_out(): lax.all_to_all(value, ('row', 'col'), split_axis=0, concat_axis=0, tiled=...  22.6 us
    pallas_call x1, Pallas kernels, run_forward(): pl.pallas_call(forward_kernel, grid_spec=pltpu.PrefetchScalarGridSpec(num...  21.4 us
    all_to_all x1, starting transfers between devices, shards(): lax.all_to_all(levels, 'row', split_axis=0, concat_axis=0, tiled=True, ax...  7.27 us
    convert_element_type x4, other arithmetic, narrowed(): return (value * (HALF_TOP / bound)).astype(jnp.float16)  5.15 us
  transfers between devices with their start and end apart: 21, of which 5 were waited for; matrix products, arithmetic and copies ran while one was open for 12% of the time, Pallas kernels for 10%

profile of v8, /device:TPU:1, one launch (start us, length us, event | category | flops | bytes accessed | tf_op | source)
XLA Modules:
  0.0 204.5 jit_solution(11437901392016908056)
XLA Ops:
  0.6 2.4 %fusion.10 = (f32[1,256,512]{2,1,0:T(8,128)}, f32[1,256,512]{2,1,0:T(8,128)}) fusion(f32[2,256,512]{2,1,0:T(8,128)} %refs_0_.1), kind=kLoop, calls=%fused_computation.37 | loop fusion | bytes 2097152 | tf_op jit(solution)/shard_map/slice | solution.py:435
  3.0 2.0 collective-permute-start.4
  5.1 4.7 %collective-permute-start.5 = (f32[1,256,512]{2,1,0:T(8,128)}, f32[1,256,512]{2,1,0:T(8,128)}, u32[]{:S(2)}, u32[]{:S(2)}) collective-permute-start(f32[1,256,512]{2,1,0:T(8,128)} %get-tuple-element.43), channel_id=1, source_target_pairs={{0,120},{8,0},{16,8},{24,16},{32,24},{40,32},{48,40},{56,48},{64,5... | collective-permute-start | bytes 1572872 | tf_op jit(solution)/shard_map/ppermute | solution.py:22
  9.8 0.0 collective-permute-start.8
  9.8 4.8 %collective-permute-start.9 = (f32[1,256,512]{2,1,0:T(8,128)}, f32[1,256,512]{2,1,0:T(8,128)}, u32[]{:S(2)}, u32[]{:S(2)}) collective-permute-start(f32[1,256,512]{2,1,0:T(8,128)} %get-tuple-element.42), channel_id=1, source_target_pairs={{0,120},{8,0},{16,8},{24,16},{32,24},{40,32},{48,40},{56,48},{64,5... | collective-permute-start | bytes 1572872 | tf_op jit(solution)/shard_map/ppermute | solution.py:22
  14.6 1.2 fusion.9
  15.8 2.7 %collective-permute-start.12 = (bf16[16,2,2,16,512]{4,3,2,1,0:T(8,128)(2,1)}, bf16[16,2,2,16,512]{4,3,2,1,0:T(8,128)(2,1)S(1)}, u32[]{:S(2)}, u32[]{:S(2)}) collective-permute-start(bf16[16,2,2,16,512]{4,3,2,1,0:T(8,128)(2,1)} %get-tuple-element.40), channel_id=1, source_target_pairs={{0,1},{1,2},{2,3},{3,4},{4,5},{5,6},{6,7},{7,0},{8,9},{9,10},{10,1... | collective-permute-start | bytes 3145736 | tf_op jit(solution)/shard_map/ppermute | solution.py:22
  18.5 0.9 abs_reduce_fusion.1
  19.3 1.2 compare_select_fusion.1
  20.6 0.7 iota.14
  21.3 4.0 %all-to-all-start.1 = ((f32[128,1,128]{2,1,0:T(1,128)}), f32[128,1,128]{2,1,0:T(1,128)S(1)}, u32[]{:S(2)}, u32[]{:S(2)}) async-start(f32[128,1,128]{2,1,0:T(1,128)} %iota.14), calls=%async_computation.1 | async-start | bytes 131072 | tf_op jit(solution)/shard_map/all_to_all | solution.py:419
  25.3 0.1 fusion.16
  25.4 0.1 copy.20
  25.5 0.1 copy.21
  25.6 1.1 fusion.11
  26.7 2.5 %collective-permute-start = (s32[2,2]{1,0:T(2,128)S(1)}, s32[2,2]{1,0:T(2,128)S(1)}, u32[]{:S(2)}, u32[]{:S(2)}) collective-permute-start(s32[2,2]{1,0:T(2,128)S(1)} %bitcast.13), channel_id=1, source_target_pairs={{0,9},{1,10},{2,11},{3,12},{4,13},{5,14},{6,15},{7,8},{8,17},{9,18... | collective-permute-start | bytes 56 | tf_op jit(solution)/shard_map/ppermute | solution.py:32
  29.2 1.1 fusion.14
  30.3 1.3 collective-permute-start.1
  31.6 1.1 fusion.15
  32.6 0.8 pad_maximum_fusion.1
  33.4 0.0 collective-permute-done.12
  33.4 0.6 collective-permute-start.2
  34.0 1.5 pad_maximum_fusion
  35.5 0.8 copy-done.3
  36.4 1.2 abs_reduce_fusion
  38.2 0.0 all-to-all-done.1
  38.2 7.3 %all-to-all-start = ((bf16[16,4,2,16,512]{4,3,2,1,0:T(8,128)(2,1)}), bf16[16,4,2,16,512]{4,3,2,1,0:T(8,128)(2,1)}, u32[]{:S(2)}, u32[]{:S(2)}) async-start(bf16[16,4,2,16,512]{4,3,2,1,0:T(8,128)(2,1)} %pad_maximum_fusion), calls=%async_computation | async-start | bytes 4194304 | tf_op jit(solution)/shard_map/all_to_all | solution.py:477
  45.5 0.0 collective-permute-done.8.refs_7_
  45.6 0.5 collective-permute-start.3
  46.1 1.2 collective-permute-start.6
  47.3 1.3 fusion.12
  48.7 0.0 collective-permute-done
  48.7 0.1 collective-permute-start.11
  48.8 1.7 collective-permute-start.10
  50.5 1.3 collective-permute-start.7
  51.8 0.6 pad_add_fusion.offs
  52.4 0.9 slice_reduce_fusion
  55.3 0.0 copy-start.7
  55.4 4.8 %collective-permute-done.11.refs_10_ = f32[1,512,256]{2,1,0:T(8,128)} collective-permute-done((f32[1,512,256]{2,1,0:T(8,128)S(1)}, f32[1,512,256]{2,1,0:T(8,128)}, u32[]{:S(2)}, u32[]{:S(2)}) %collective-permute-start.11) | collective-permute-done | bytes 524320 | tf_op jit(solution)/shard_map/ppermute | solution.py:22
  60.2 5.6 %collective-permute-done.7.refs_6_ = f32[1,512,256]{2,1,0:T(8,128)} collective-permute-done((f32[1,512,256]{2,1,0:T(8,128)S(1)}, f32[1,512,256]{2,1,0:T(8,128)}, u32[]{:S(2)}, u32[]{:S(2)}) %collective-permute-start.7) | collective-permute-done | bytes 524320 | tf_op jit(solution)/shard_map/ppermute | solution.py:22
  65.8 21.4 %forward.1 = (f32[4,2,512,512]{3,2,1,0:T(8,128)}, f32[4,2,512,512]{3,2,1,0:T(8,128)}) custom-call(s32[4,2]{1,0:T(4,128)} %pad_add_fusion.offs, f32[2,256,512]{2,1,0:T(8,128)} %refs_0_.1, f32[2,256,256]{2,1,0:T(8,128)} %collective-permute-done.2.refs_1_, f32[2,256,256]{2,1,0:T(8,128)} %copy-done.7, f32[1,256,512]{2,1,0:T(8,128)} %collective-permute-done.4.refs_3_, ...), custom_call_target="tpu_custom_call" | custom-call | flops 8589934592 | bytes 30000000 | tf_op jit(solution)/shard_map/forward/pallas_call | solution.py:326
  87.2 25.5 %backward.1 = (f32[2,8,768,128]{3,2,1,0:T(8,128)}, f32[4,32,3,16,128]{4,3,2,1,0:T(8,128)}) custom-call(s32[4,2]{1,0:T(4,128)} %pad_add_fusion.offs, s32[32]{0:T(128)} %order.1, f32[4,2,512,512]{3,2,1,0:T(8,128)} %get-tuple-element.15.far, f32[4,2,512,512]{3,2,1,0:T(8,128)} %get-tuple-element.16.patch, bf16[16,4,2,16,512]{4,3,2,1,0:T(8,128)(2,1)} %all-to-all-done.amp, ...), custom_call_target="tpu_custom_call" | custom-call | flops 8589934592 | bytes 30000000 | tf_op jit(solution)/shard_map/backward/pallas_call | solution.py:361
  112.7 2.4 %multiply_convert_fusion.2 = (f16[2,2,768,128]{3,2,1,0:T(8,128)(2,1)S(1)}, f16[2,2,768,128]{3,2,1,0:T(8,128)(2,1)S(1)}) fusion(f32[2,8,768,128]{3,2,1,0:T(8,128)} %get-tuple-element.20, f32[]{:T(128)S(6)} %div.41), kind=kLoop, calls=%fused_computation.10 | loop fusion | flops 1572864 | bytes 4718596 | tf_op jit(solution)/shard_map/convert_element_type | solution.py:47
  115.1 0.0 collective-permute-start.13
  115.1 0.4 copy-done.1
  115.6 1.5 multiply_convert_fusion
  117.1 9.0 %all-to-all-start.2 = ((f16[128,48,128]{2,1,0:T(8,128)(2,1)}), f16[128,48,128]{2,1,0:T(8,128)(2,1)}, u32[]{:S(2)}, u32[]{:S(2)}) async-start(f16[128,48,128]{2,1,0:T(8,128)(2,1)} %multiply_convert_fusion), calls=%async_computation.2 | async-start | bytes 3145728 | tf_op jit(solution)/shard_map/all_to_all | solution.py:419
  126.1 1.3 collective-permute-start.14
  127.5 0.1 convert_multiply_fusion.2
  127.6 25.0 %collective-permute-done.14 = f16[2,2,768,128]{3,2,1,0:T(8,128)(2,1)S(1)} collective-permute-done((f16[2,2,768,128]{3,2,1,0:T(8,128)(2,1)S(1)}, f16[2,2,768,128]{3,2,1,0:T(8,128)(2,1)S(1)}, u32[]{:S(2)}, u32[]{:S(2)}) %collective-permute-start.14) | collective-permute-done | bytes 786464 | tf_op jit(solution)/shard_map/ppermute | solution.py:22
  152.6 0.1 convert_multiply_fusion.1
  152.7 2.3 %maximum_add_fusion = f32[2,4,768,128]{3,2,1,0:T(8,128)S(1)} fusion(f32[2,2,768,128]{3,2,1,0:T(8,128)S(1)} %convert_multiply_fusion.1, f32[2,2,768,128]{3,2,1,0:T(8,128)S(1)} %convert_multiply_fusion.2, f32[2,8,768,128]{3,2,1,0:T(8,128)} %get-tuple-element.20), kind=kLoop, calls=%fused_computation | loop fusion | flops 1572864 | bytes 9437184 | tf_op jit(solution)/shard_map/add | solution.py:501
  155.1 1.9 multiply_reduce_fusion
  157.0 1.1 broadcast_in_dim.26
  158.1 9.5 %all-to-all-start.3 = ((f16[128,32,128]{2,1,0:T(8,128)(2,1)}), f16[128,32,128]{2,1,0:T(8,128)(2,1)}, u32[]{:S(2)}, u32[]{:S(2)}) async-start(f16[128,32,128]{2,1,0:T(8,128)(2,1)} %broadcast_in_dim.26), calls=%async_computation.3 | async-start | bytes 2097152 | tf_op jit(solution)/shard_map/all_to_all | solution.py:419
  167.7 1.3 fusion.1
  169.0 5.4 %collective-permute-start.15 = (f16[2,4,256,128]{3,2,1,0:T(8,128)(2,1)}, f16[2,4,256,128]{3,2,1,0:T(8,128)(2,1)}, u32[]{:S(2)}, u32[]{:S(2)}) collective-permute-start(f16[2,4,256,128]{3,2,1,0:T(8,128)(2,1)} %get-tuple-element.38), channel_id=1, source_target_pairs={{0,120},{8,0},{16,8},{24,16},{32,24},{40,32},{48,40},{56,48},{64,5... | collective-permute-start | bytes 1572872 | tf_op jit(solution)/shard_map/ppermute | solution.py:22
  174.3 16.8 %collective-permute-done.15 = f16[2,4,256,128]{3,2,1,0:T(8,128)(2,1)} collective-permute-done((f16[2,4,256,128]{3,2,1,0:T(8,128)(2,1)}, f16[2,4,256,128]{3,2,1,0:T(8,128)(2,1)}, u32[]{:S(2)}, u32[]{:S(2)}) %collective-permute-start.15) | collective-permute-done | bytes 524320 | tf_op jit(solution)/shard_map/ppermute | solution.py:22
  191.2 5.0 %collective-permute-done.16 = f16[2,4,256,128]{3,2,1,0:T(8,128)(2,1)} collective-permute-done((f16[2,4,256,128]{3,2,1,0:T(8,128)(2,1)}, f16[2,4,256,128]{3,2,1,0:T(8,128)(2,1)}, u32[]{:S(2)}, u32[]{:S(2)}) %collective-permute-start.16) | collective-permute-done | bytes 524320 | tf_op jit(solution)/shard_map/ppermute | solution.py:22
  196.1 2.4 %fusion.3 = f32[2,256,4,128]{3,1,2,0:T(8,128)} fusion(f32[2,4,768,128]{3,2,1,0:T(8,128)S(1)} %maximum_add_fusion, f16[2,4,256,128]{3,2,1,0:T(8,128)(2,1)} %collective-permute-done.16, f16[2,4,256,128]{3,2,1,0:T(8,128)(2,1)} %collective-permute-done.15, f32[]{:T(128)S(6)} %div.42), kind=kLoop, calls=%fused_computation.17 | loop fusion | flops 1572864 | bytes 3145732 | tf_op jit(solution)/shard_map/transpose | solution.py:519
  198.5 1.6 copy.24
  200.1 1.3 copy.25
  201.4 1.5 convert_multiply_fusion.packed
  202.9 1.6 unpack.1
  (33 shorter events, 0.2 us)
Async XLA Ops:
  0.6 14.0 %copy-start.2 = (bf16[64,2,16,512]{3,2,1,0:T(8,128)(2,1)S(1)}, bf16[64,2,16,512]{3,2,1,0:T(8,128)(2,1)}, u32[]{:S(2)}) copy-start(bf16[64,2,16,512]{3,2,1,0:T(8,128)(2,1)} %param.8) | copy-start | bytes 6291460
  3.0 23.7 %collective-permute-start.4 = (f32[1,256,512]{2,1,0:T(8,128)}, f32[1,256,512]{2,1,0:T(8,128)}, u32[]{:S(2)}, u32[]{:S(2)}) collective-permute-start(f32[1,256,512]{2,1,0:T(8,128)} %get-tuple-element.43), channel_id=1, source_target_pairs={{0,8},{8,16},{16,24},{24,32},{32,40},{40,48},{48,56},{56,64},{64,7... | collective-permute-start | bytes 1572872 | tf_op jit(solution)/shard_map/ppermute | solution.py:22
  5.1 25.2 %collective-permute-start.5 = (f32[1,256,512]{2,1,0:T(8,128)}, f32[1,256,512]{2,1,0:T(8,128)}, u32[]{:S(2)}, u32[]{:S(2)}) collective-permute-start(f32[1,256,512]{2,1,0:T(8,128)} %get-tuple-element.43), channel_id=1, source_target_pairs={{0,120},{8,0},{16,8},{24,16},{32,24},{40,32},{48,40},{56,48},{64,5... | collective-permute-start | bytes 1572872 | tf_op jit(solution)/shard_map/ppermute | solution.py:22
  9.8 35.7 %collective-permute-start.8 = (f32[1,256,512]{2,1,0:T(8,128)}, f32[1,256,512]{2,1,0:T(8,128)}, u32[]{:S(2)}, u32[]{:S(2)}) collective-permute-start(f32[1,256,512]{2,1,0:T(8,128)} %get-tuple-element.42), channel_id=1, source_target_pairs={{0,8},{8,16},{16,24},{24,32},{32,40},{40,48},{48,56},{56,64},{64,7... | collective-permute-start | bytes 1572872 | tf_op jit(solution)/shard_map/ppermute | solution.py:22
  9.8 36.3 %collective-permute-start.9 = (f32[1,256,512]{2,1,0:T(8,128)}, f32[1,256,512]{2,1,0:T(8,128)}, u32[]{:S(2)}, u32[]{:S(2)}) collective-permute-start(f32[1,256,512]{2,1,0:T(8,128)} %get-tuple-element.42), channel_id=1, source_target_pairs={{0,120},{8,0},{16,8},{24,16},{32,24},{40,32},{48,40},{56,48},{64,5... | collective-permute-start | bytes 1572872 | tf_op jit(solution)/shard_map/ppermute | solution.py:22
  14.6 3.9 %copy-start = (f32[2,256,512]{2,1,0:T(8,128)S(1)}, f32[2,256,512]{2,1,0:T(8,128)}, u32[]{:S(2)}) copy-start(f32[2,256,512]{2,1,0:T(8,128)} %refs_0_.1) | copy-start | bytes 3145732
  14.6 10.7 %copy-start.6 = (s32[1,1,4,2]{2,3,1,0:T(2,128)S(1)}, s32[1,1,4,2]{2,3,1,0:T(2,128)}, u32[]{:S(2)}) copy-start(s32[1,1,4,2]{2,3,1,0:T(2,128)} %param.10) | copy-start | bytes 100
  15.8 17.7 %collective-permute-start.12 = (bf16[16,2,2,16,512]{4,3,2,1,0:T(8,128)(2,1)}, bf16[16,2,2,16,512]{4,3,2,1,0:T(8,128)(2,1)S(1)}, u32[]{:S(2)}, u32[]{:S(2)}) collective-permute-start(bf16[16,2,2,16,512]{4,3,2,1,0:T(8,128)(2,1)} %get-tuple-element.40), channel_id=1, source_target_pairs={{0,1},{1,2},{2,3},{3,4},{4,5},{5,6},{6,7},{7,0},{8,9},{9,10},{10,1... | collective-permute-start | bytes 3145736 | tf_op jit(solution)/shard_map/ppermute | solution.py:22
  21.3 17.0 %all-to-all-start.1 = ((f32[128,1,128]{2,1,0:T(1,128)}), f32[128,1,128]{2,1,0:T(1,128)S(1)}, u32[]{:S(2)}, u32[]{:S(2)}) async-start(f32[128,1,128]{2,1,0:T(1,128)} %iota.14), calls=%async_computation.1 | async-start | bytes 131072 | tf_op jit(solution)/shard_map/all_to_all | solution.py:419
  26.7 22.0 %collective-permute-start = (s32[2,2]{1,0:T(2,128)S(1)}, s32[2,2]{1,0:T(2,128)S(1)}, u32[]{:S(2)}, u32[]{:S(2)}) collective-permute-start(s32[2,2]{1,0:T(2,128)S(1)} %bitcast.13), channel_id=1, source_target_pairs={{0,9},{1,10},{2,11},{3,12},{4,13},{5,14},{6,15},{7,8},{8,17},{9,18... | collective-permute-start | bytes 56 | tf_op jit(solution)/shard_map/ppermute | solution.py:32
  30.3 18.5 %collective-permute-start.1 = (s32[2,2]{1,0:T(2,128)S(1)}, s32[2,2]{1,0:T(2,128)S(1)}, u32[]{:S(2)}, u32[]{:S(2)}) collective-permute-start(s32[2,2]{1,0:T(2,128)S(1)} %bitcast.12), channel_id=1, source_target_pairs={{0,8},{8,16},{16,24},{24,32},{32,40},{40,48},{48,56},{56,64},{64,7... | collective-permute-start | bytes 56 | tf_op jit(solution)/shard_map/ppermute | solution.py:22
  33.4 17.0 %collective-permute-start.2 = (f32[2,256,256]{2,1,0:T(8,128)}, f32[2,256,256]{2,1,0:T(8,128)}, u32[]{:S(2)}, u32[]{:S(2)}) collective-permute-start(f32[2,256,256]{2,1,0:T(8,128)} %get-tuple-element.45), channel_id=1, source_target_pairs={{0,1},{1,2},{2,3},{3,4},{4,5},{5,6},{6,7},{7,0},{8,9},{9,10},{10,1... | collective-permute-start | bytes 1572872 | tf_op jit(solution)/shard_map/ppermute | solution.py:22
  34.0 2.3 %copy-start.3 = (f32[2,512,512]{2,1,0:T(8,128)S(1)}, f32[2,512,512]{2,1,0:T(8,128)}, u32[]{:S(2)}) copy-start(f32[2,512,512]{2,1,0:T(8,128)} %ill.1) | copy-start | bytes 6291460
  38.2 7.3 %copy-start.5 = (f32[2,256,256]{2,1,0:T(8,128)S(1)}, f32[2,256,256]{2,1,0:T(8,128)}, u32[]{:S(2)}) copy-start(f32[2,256,256]{2,1,0:T(8,128)} %get-tuple-element.44) | copy-start | bytes 1572868
  38.2 7.9 %copy-start.4 = (f32[1,512,256]{2,1,0:T(8,128)S(1)}, f32[1,512,256]{2,1,0:T(8,128)}, u32[]{:S(2)}) copy-start(f32[1,512,256]{2,1,0:T(8,128)} %pad_maximum_fusion.1) | copy-start | bytes 1572868
  38.2 49.0 %all-to-all-start = ((bf16[16,4,2,16,512]{4,3,2,1,0:T(8,128)(2,1)}), bf16[16,4,2,16,512]{4,3,2,1,0:T(8,128)(2,1)}, u32[]{:S(2)}, u32[]{:S(2)}) async-start(bf16[16,4,2,16,512]{4,3,2,1,0:T(8,128)(2,1)} %pad_maximum_fusion), calls=%async_computation | async-start | bytes 4194304 | tf_op jit(solution)/shard_map/all_to_all | solution.py:477
  45.6 9.8 %collective-permute-start.3 = (f32[2,256,256]{2,1,0:T(8,128)S(1)}, f32[2,256,256]{2,1,0:T(8,128)S(1)}, u32[]{:S(2)}, u32[]{:S(2)}) collective-permute-start(f32[2,256,256]{2,1,0:T(8,128)S(1)} %copy-done.5), channel_id=1, source_target_pairs={{0,7},{1,0},{2,1},{3,2},{4,3},{5,4},{6,5},{7,6},{8,15},{9,8},{10,9... | collective-permute-start | bytes 1572872 | tf_op jit(solution)/shard_map/ppermute | solution.py:22
  46.1 14.1 %collective-permute-start.6 = (f32[1,512,256]{2,1,0:T(8,128)S(1)}, f32[1,512,256]{2,1,0:T(8,128)}, u32[]{:S(2)}, u32[]{:S(2)}) collective-permute-start(f32[1,512,256]{2,1,0:T(8,128)S(1)} %copy-done.4), channel_id=1, source_target_pairs={{0,1},{1,2},{2,3},{3,4},{4,5},{5,6},{6,7},{7,0},{8,9},{9,10},{10,1... | collective-permute-start | bytes 1572872 | tf_op jit(solution)/shard_map/ppermute | solution.py:22
  48.7 11.5 %collective-permute-start.11 = (f32[1,512,256]{2,1,0:T(8,128)S(1)}, f32[1,512,256]{2,1,0:T(8,128)}, u32[]{:S(2)}, u32[]{:S(2)}) collective-permute-start(f32[1,512,256]{2,1,0:T(8,128)S(1)} %pad_maximum_fusion.4), channel_id=1, source_target_pairs={{0,7},{1,0},{2,1},{3,2},{4,3},{5,4},{6,5},{7,6},{8,15},{9,8},{10,9... | collective-permute-start | bytes 1572872 | tf_op jit(solution)/shard_map/ppermute | solution.py:22
  48.8 11.4 %collective-permute-start.10 = (f32[1,512,256]{2,1,0:T(8,128)S(1)}, f32[1,512,256]{2,1,0:T(8,128)}, u32[]{:S(2)}, u32[]{:S(2)}) collective-permute-start(f32[1,512,256]{2,1,0:T(8,128)S(1)} %pad_maximum_fusion.3), channel_id=1, source_target_pairs={{0,1},{1,2},{2,3},{3,4},{4,5},{5,6},{6,7},{7,0},{8,9},{9,10},{10,1... | collective-permute-start | bytes 1572872 | tf_op jit(solution)/shard_map/ppermute | solution.py:22
  50.5 15.3 %collective-permute-start.7 = (f32[1,512,256]{2,1,0:T(8,128)S(1)}, f32[1,512,256]{2,1,0:T(8,128)}, u32[]{:S(2)}, u32[]{:S(2)}) collective-permute-start(f32[1,512,256]{2,1,0:T(8,128)S(1)} %pad_maximum_fusion.2), channel_id=1, source_target_pairs={{0,7},{1,0},{2,1},{3,2},{4,3},{5,4},{6,5},{7,6},{8,15},{9,8},{10,9... | collective-permute-start | bytes 1572872 | tf_op jit(solution)/shard_map/ppermute | solution.py:22
  55.3 4.9 %copy-start.7 = (f32[2,256,256]{2,1,0:T(8,128)}, f32[2,256,256]{2,1,0:T(8,128)S(1)}, u32[]{:S(2)}) copy-start(f32[2,256,256]{2,1,0:T(8,128)S(1)} %collective-permute-done.3.refs_2_) | copy-start | bytes 1572868
  112.7 2.8 %copy-start.1 = (f32[4,32,3,16,128]{4,3,2,1,0:T(8,128)S(1)}, f32[4,32,3,16,128]{4,3,2,1,0:T(8,128)}, u32[]{:S(2)}) copy-start(f32[4,32,3,16,128]{4,3,2,1,0:T(8,128)} %get-tuple-element.23) | copy-start | bytes 9437188
  115.1 12.4 %collective-permute-start.13 = (f16[2,2,768,128]{3,2,1,0:T(8,128)(2,1)S(1)}, f16[2,2,768,128]{3,2,1,0:T(8,128)(2,1)S(1)}, u32[]{:S(2)}, u32[]{:S(2)}) collective-permute-start(f16[2,2,768,128]{3,2,1,0:T(8,128)(2,1)S(1)} %get-tuple-element.36), channel_id=1, source_target_pairs={{0,1},{1,2},{2,3},{3,4},{4,5},{5,6},{6,7},{7,0},{8,9},{9,10},{10,1... | collective-permute-start | bytes 2359304 | tf_op jit(solution)/shard_map/ppermute | solution.py:22
  117.1 38.0 %all-to-all-start.2 = ((f16[128,48,128]{2,1,0:T(8,128)(2,1)}), f16[128,48,128]{2,1,0:T(8,128)(2,1)}, u32[]{:S(2)}, u32[]{:S(2)}) async-start(f16[128,48,128]{2,1,0:T(8,128)(2,1)} %multiply_convert_fusion), calls=%async_computation.2 | async-start | bytes 3145728 | tf_op jit(solution)/shard_map/all_to_all | solution.py:419
  126.1 26.5 %collective-permute-start.14 = (f16[2,2,768,128]{3,2,1,0:T(8,128)(2,1)S(1)}, f16[2,2,768,128]{3,2,1,0:T(8,128)(2,1)S(1)}, u32[]{:S(2)}, u32[]{:S(2)}) collective-permute-start(f16[2,2,768,128]{3,2,1,0:T(8,128)(2,1)S(1)} %get-tuple-element.37), channel_id=1, source_target_pairs={{0,7},{1,0},{2,1},{3,2},{4,3},{5,4},{6,5},{7,6},{8,15},{9,8},{10,9... | collective-permute-start | bytes 2359304 | tf_op jit(solution)/shard_map/ppermute | solution.py:22
  158.1 43.2 %all-to-all-start.3 = ((f16[128,32,128]{2,1,0:T(8,128)(2,1)}), f16[128,32,128]{2,1,0:T(8,128)(2,1)}, u32[]{:S(2)}, u32[]{:S(2)}) async-start(f16[128,32,128]{2,1,0:T(8,128)(2,1)} %broadcast_in_dim.26), calls=%async_computation.3 | async-start | bytes 2097152 | tf_op jit(solution)/shard_map/all_to_all | solution.py:419
  169.0 22.2 %collective-permute-start.15 = (f16[2,4,256,128]{3,2,1,0:T(8,128)(2,1)}, f16[2,4,256,128]{3,2,1,0:T(8,128)(2,1)}, u32[]{:S(2)}, u32[]{:S(2)}) collective-permute-start(f16[2,4,256,128]{3,2,1,0:T(8,128)(2,1)} %get-tuple-element.38), channel_id=1, source_target_pairs={{0,120},{8,0},{16,8},{24,16},{32,24},{40,32},{48,40},{56,48},{64,5... | collective-permute-start | bytes 1572872 | tf_op jit(solution)/shard_map/ppermute | solution.py:22
  174.3 21.8 %collective-permute-start.16 = (f16[2,4,256,128]{3,2,1,0:T(8,128)(2,1)}, f16[2,4,256,128]{3,2,1,0:T(8,128)(2,1)}, u32[]{:S(2)}, u32[]{:S(2)}) collective-permute-start(f16[2,4,256,128]{3,2,1,0:T(8,128)(2,1)} %get-tuple-element.39), channel_id=1, source_target_pairs={{0,8},{8,16},{16,24},{24,32},{32,40},{40,48},{48,56},{56,64},{64,7... | collective-permute-start | bytes 1572872 | tf_op jit(solution)/shard_map/ppermute | solution.py:22

commit v9 on v8

--- a/solution.py
+++ b/solution.py
@@ -72,29 +72,20 @@
 
 
 def region_copies(pieces, region, sems):
-    middle, west, east = pieces[:3]
+    middle, west, _ = pieces[:3]
     rows, cols, edge = middle.shape[1], middle.shape[2], west.shape[2]
     center, right = edge // LANES, (edge + cols) // LANES
-    both = pl.ds(0, 2)
-    moves = [(middle, both, 0, 1, center), (west, both, 0, 1, 0), (east, both, 0, 1, right)]
-    for plane in range(2):
-        upper, lower, outer_west, outer_east = pieces[3 + 4 * plane : 7 + 4 * plane]
-        one = pl.ds(plane, 1)
-        moves += [
-            (upper, one, 0, 0, center),
-            (lower, one, 0, 2, center),
-            (outer_west, one, 0, 0, 0),
-            (outer_west, one, 1, 2, 0),
-            (outer_east, one, 0, 0, right),
-            (outer_east, one, 1, 2, right),
-        ]
+    half = center + edge // LANES
+    places = [(1, center), (1, 0), (1, right)]
+    places += [(0, half), (2, half), (0, center), (2, center)]
+    places += [(0, 0), (2, 0), (0, right), (2, right)]
     copies = []
-    for piece, planes, source, target, first in moves:
+    for piece, (target, first) in zip(pieces, places):
         for block in range(piece.shape[2] // LANES):
             copies.append(
                 pltpu.make_async_copy(
-                    piece.at[:, pl.ds(source * rows, rows), pl.ds(block * LANES, LANES)],
-                    region.at[planes, first + block, pl.ds(target * rows, rows)],
+                    piece.at[:, :, pl.ds(block * LANES, LANES)],
+                    region.at[:, first + block, pl.ds(target * rows, rows)],
                     sems.at[len(copies)],
                 )
             )
@@ -340,7 +331,7 @@
                 pltpu.VMEM((2 * size, 2 * size), jnp.bfloat16),
                 pltpu.VMEM((2 * size, size), jnp.bfloat16),
                 pltpu.VMEM((size, 2 * size), jnp.bfloat16),
-                pltpu.SemaphoreType.DMA((40,)),
+                pltpu.SemaphoreType.DMA((24,)),
                 pltpu.SemaphoreType.DMA((8,)),
             ],
         ),
@@ -430,16 +421,17 @@
     late = slots // 2
     edge = tile_cols // 2
     grouped = measured.reshape(senders, slots, per, height, size)
-    uppers, lowers = [], []
-    for plane in range(2):
-        uppers.append(passed_along(specimen[plane : plane + 1], "row", 1))
-        lowers.append(passed_along(specimen[plane : plane + 1], "row", -1))
+    halves = {"left": specimen[:, :, :edge], "right": specimen[:, :, edge:]}
+    rows = []
+    for name in ("right", "left"):
+        rows.append(passed_along(halves[name], "row", 1))
+        rows.append(passed_along(halves[name], "row", -1))
     early_offs = passed_along(scan_offsets[0, 0, :late], "row", 1)
     late_offs = passed_both(scan_offsets[0, 0, late:], 1, 1)
     offs = jnp.concatenate([late_offs, early_offs], axis=0)
     moved = passed_along(grouped[:, late:], "col", 1)
-    west = passed_along(specimen[:, :, edge:], "col", 1)
-    east = passed_along(specimen[:, :, :edge], "col", -1)
+    west = passed_along(halves["right"], "col", 1)
+    east = passed_along(halves["left"], "col", -1)
     levels = jnp.concatenate([moved, grouped[:, :late]], axis=1)
     tables = dft_tables(size)
     lane = lax.broadcasted_iota(jnp.int32, (devices, 1, LANES), 2)
@@ -447,33 +439,10 @@
         lane < LANES // 2, jnp.max(jnp.abs(specimen)), jnp.sum(specimen * specimen)
     )
     peaks = spread_out(stats)
-    peak = jnp.maximum(jnp.max(peaks[:, :, : LANES // 2]), 1e-12)
-    power = jnp.max(peaks[:, :, LANES // 2 :])
     outers = []
-    for plane in range(2):
-        upper, lower = uppers[plane], lowers[plane]
-        west_edges = jnp.concatenate([upper[:, :, edge:], lower[:, :, edge:]], axis=1)
-        east_edges = jnp.concatenate([upper[:, :, :edge], lower[:, :, :edge]], axis=1)
-        if plane == 0:
-            uppers[1], lowers[1], _, _ = lax.optimization_barrier(
-                (uppers[1], lowers[1], west_edges, east_edges)
-            )
-        outer_west = passed_along(west_edges, "col", 1)
-        outer_east = passed_along(east_edges, "col", -1)
-        outers.append((upper, lower, outer_west, outer_east))
-    levels, probe, _ = lax.optimization_barrier((levels, illumination, uppers[0]))
-    ill_power = jnp.sum(probe * probe)
-    ill_peak = jnp.maximum(jnp.max(jnp.abs(probe)), 1e-8)
-    levels, ill_power, ill_peak = lax.optimization_barrier((levels, ill_power, ill_peak))
-    modulus = 1.5 * peak
-    energy = jnp.minimum(
-        modulus * jnp.sqrt(ill_power), 1.5 * ill_peak * jnp.sqrt(6.0 * power)
-    )
-    change_bound = 9.0 * jnp.maximum(energy, 1e-20)
-    grad_bound = 24.0 * ill_peak * change_bound
-    sum_bound = slots * modulus * change_bound
-    density_bound = slots * modulus * modulus
-    step_bound = math.sqrt(slots * devices) * change_bound
+    for index, (steps, name) in enumerate(((1, "west"), (1, "west"), (-1, "east"), (-1, "east"))):
+        outers.append(passed_along(rows[index], "col", steps))
+    levels, _ = lax.optimization_barrier((levels, tuple(rows)))
     arrived = lax.all_to_all(
         levels,
         "row",
@@ -482,8 +451,25 @@
         tiled=True,
         axis_index_groups=[[(sender + 1) % senders for sender in range(senders)]],
     )
-    pieces = (specimen, west, east) + outers[0] + outers[1]
+    pieces = (specimen, west, east, *rows, *outers)
     far, patch = run_forward(offs, pieces, tables, illumination)
+    far, probe, peaks = lax.optimization_barrier((far, illumination, peaks))
+    peak = jnp.maximum(jnp.max(peaks[:, :, : LANES // 2]), 1e-12)
+    power = jnp.max(peaks[:, :, LANES // 2 :])
+    ill_power = jnp.sum(probe * probe)
+    ill_peak = jnp.maximum(jnp.max(jnp.abs(probe)), 1e-8)
+    modulus = 1.5 * peak
+    energy = jnp.minimum(
+        modulus * jnp.sqrt(ill_power), 1.5 * ill_peak * jnp.sqrt(6.0 * power)
+    )
+    change_bound = 9.0 * jnp.maximum(energy, 1e-20)
+    grad_bound = 24.0 * ill_peak * change_bound
+    sum_bound = slots * modulus * change_bound
+    density_bound = slots * modulus * modulus
+    step_bound = math.sqrt(slots * devices) * change_bound
+    bounds = (grad_bound, sum_bound, density_bound, step_bound)
+    far, bounds = lax.optimization_barrier((far, bounds))
+    grad_bound, sum_bound, density_bound, step_bound = bounds
     region_shape = (2, (tile_cols + 2 * edge) // LANES, 3 * tile_rows, LANES)
     accum, sums = run_backward(
         offs, module_row, far, patch, arrived, illumination, tables, region_shape

time: 205 us -> 237 us (1.16)
  waiting for transfers between devices: 57.3 us -> 85.1 us
  starting transfers between devices: 60 us -> 68 us
  local copies, waits for them, and re-layouts: 14.3 us -> 10 us
    ppermute x16, waiting for transfers between devices: 57.2 us -> 78.1 us  [passed_along(): return lax.ppermute(value, axis, pairs)]
    all_to_all x3, starting transfers between devices: 22.6 us -> 32 us  [spread_out(): lax.all_to_all(value, ('row', 'col'), split_axis=0, concat_axis=0, tiled=...]
    all_to_all x3, waiting for transfers between devices: 0.01 us -> 6.98 us  [spread_out(): lax.all_to_all(value, ('row', 'col'), split_axis=0, concat_axis=0, tiled=...]
    slice x5 -> x1, local copies, waits for them, and re-layouts: 6.88 us -> 0.09 us  [shards(): halves = {'left': specimen[:, :, :edge], 'right': specimen[:, :, edge:]}]
    reduce_sum x0 -> x1, other arithmetic: none -> 2.83 us  [shards(): ill_power = jnp.sum(probe * probe)]
    all_to_all x1, starting transfers between devices: 7.27 us -> 4.57 us  [shards(): lax.all_to_all(levels, 'row', split_axis=0, concat_axis=0, tiled=True, ax...]
  transfers between devices with their start and end apart: 21 -> 21, of which waited for: 5 -> 8; matrix products, arithmetic and copies ran while one was open for 12% -> 8% of each run, Pallas kernels for 10% -> 9%
where the time goes in v9:
time: 237 us; the launch traced here: 236 us
  waiting for transfers between devices  85.1 us (36%)
  starting transfers between devices  68 us (29%)
  Pallas kernels  48.2 us (20%)
  other arithmetic  21.4 us (9%)
  local copies, waits for them, and re-layouts  10 us (4%)
  between operations  3.6 us (2%)
    ppermute x16, waiting for transfers between devices, passed_along(): return lax.ppermute(value, axis, pairs)  78.1 us
    all_to_all x3, starting transfers between devices, spread_out(): lax.all_to_all(value, ('row', 'col'), split_axis=0, concat_axis=0, tiled=...  32 us
    ppermute x16, starting transfers between devices, passed_along(): return lax.ppermute(value, axis, pairs)  29.1 us
    pallas_call x1, Pallas kernels, run_backward(): pl.pallas_call(backward_kernel, grid_spec=pltpu.PrefetchScalarGridSpec(nu...  25.5 us
    pallas_call x1, Pallas kernels, run_forward(): pl.pallas_call(forward_kernel, grid_spec=pltpu.PrefetchScalarGridSpec(num...  21.2 us
    all_to_all x3, waiting for transfers between devices, spread_out(): lax.all_to_all(value, ('row', 'col'), split_axis=0, concat_axis=0, tiled=...  6.98 us
    convert_element_type x4, other arithmetic, narrowed(): return (value * (HALF_TOP / bound)).astype(jnp.float16)  5.13 us
  transfers between devices with their start and end apart: 21, of which 8 were waited for; matrix products, arithmetic and copies ran while one was open for 8% of the time, Pallas kernels for 9%

profile of v9, /device:TPU:1, one launch (start us, length us, event | category | flops | bytes accessed | tf_op | source)
XLA Modules:
  0.0 236.3 jit_solution(7690617378258999184)
XLA Ops:
  0.6 0.0 copy-start
  0.6 1.8 fusion.9
  2.5 2.7 %collective-permute-start.12 = (bf16[16,2,2,16,512]{4,3,2,1,0:T(8,128)(2,1)S(1)}, bf16[16,2,2,16,512]{4,3,2,1,0:T(8,128)(2,1)S(1)}, u32[]{:S(2)}, u32[]{:S(2)}) collective-permute-start(bf16[16,2,2,16,512]{4,3,2,1,0:T(8,128)(2,1)S(1)} %get-tuple-element.44), channel_id=1, source_target_pairs={{0,1},{1,2},{2,3},{3,4},{4,5},{5,6},{6,7},{7,0},{8,9},{9,10},{10,1... | collective-permute-start | bytes 3145736 | tf_op jit(solution)/shard_map/ppermute | solution.py:22
  5.2 0.1 fusion.10
  5.3 1.3 collective-permute-start.4
  6.6 4.8 %collective-permute-start.5 = (f32[2,256,256]{2,1,0:T(8,128)S(1)}, f32[2,256,256]{2,1,0:T(8,128)}, u32[]{:S(2)}, u32[]{:S(2)}) collective-permute-start(f32[2,256,256]{2,1,0:T(8,128)S(1)} %get-tuple-element.47), channel_id=1, source_target_pairs={{0,120},{8,0},{16,8},{24,16},{32,24},{40,32},{48,40},{56,48},{64,5... | collective-permute-start | bytes 1572872 | tf_op jit(solution)/shard_map/ppermute | solution.py:22
  11.4 0.0 collective-permute-start.6
  11.4 4.8 %collective-permute-start.7 = (f32[2,256,256]{2,1,0:T(8,128)S(1)}, f32[2,256,256]{2,1,0:T(8,128)}, u32[]{:S(2)}, u32[]{:S(2)}) collective-permute-start(f32[2,256,256]{2,1,0:T(8,128)S(1)} %get-tuple-element.46), channel_id=1, source_target_pairs={{0,120},{8,0},{16,8},{24,16},{32,24},{40,32},{48,40},{56,48},{64,5... | collective-permute-start | bytes 1572872 | tf_op jit(solution)/shard_map/ppermute | solution.py:22
  16.2 0.8 collective-permute-done.12
  16.9 2.5 %collective-permute-start.2 = (f32[2,256,256]{2,1,0:T(8,128)S(1)}, f32[2,256,256]{2,1,0:T(8,128)}, u32[]{:S(2)}, u32[]{:S(2)}) collective-permute-start(f32[2,256,256]{2,1,0:T(8,128)S(1)} %get-tuple-element.47), channel_id=1, source_target_pairs={{0,1},{1,2},{2,3},{3,4},{4,5},{5,6},{6,7},{7,0},{8,9},{9,10},{10,1... | collective-permute-start | bytes 1572872 | tf_op jit(solution)/shard_map/ppermute | solution.py:22
  19.4 0.9 abs_reduce_fusion.1
  20.3 1.3 compare_select_fusion.1
  21.6 0.7 iota.14
  22.2 9.8 %all-to-all-start = ((f32[128,1,128]{2,1,0:T(1,128)}), f32[128,1,128]{2,1,0:T(1,128)S(1)}, u32[]{:S(2)}, u32[]{:S(2)}) async-start(f32[128,1,128]{2,1,0:T(1,128)} %iota.14), calls=%async_computation | async-start | bytes 131072 | tf_op jit(solution)/shard_map/all_to_all | solution.py:410
  32.1 1.5 pad_maximum_fusion
  33.6 0.0 collective-permute-done.4.refs_3_
  33.6 1.1 collective-permute-start.3
  34.6 0.0 collective-permute-done.5.refs_4_
  34.6 7.0 %all-to-all-done = f32[128,1,128]{2,1,0:T(1,128)S(1)} async-done(((f32[128,1,128]{2,1,0:T(1,128)}), f32[128,1,128]{2,1,0:T(1,128)S(1)}, u32[]{:S(2)}, u32[]{:S(2)}) %all-to-all-start) | async-done | bytes 65568 | tf_op jit(solution)/shard_map/all_to_all | solution.py:410
  41.6 4.6 %all-to-all-start.1 = ((bf16[16,4,2,16,512]{4,3,2,1,0:T(8,128)(2,1)}), bf16[16,4,2,16,512]{4,3,2,1,0:T(8,128)(2,1)}, u32[]{:S(2)}, u32[]{:S(2)}) async-start(bf16[16,4,2,16,512]{4,3,2,1,0:T(8,128)(2,1)} %pad_maximum_fusion), calls=%async_computation.1 | async-start | bytes 4194304 | tf_op jit(solution)/shard_map/all_to_all | solution.py:446
  46.2 0.1 fusion.11
  46.3 0.1 copy.21
  46.4 0.2 collective-permute-start.1
  46.5 0.1 copy.20
  46.6 2.3 collective-permute-start
  48.9 0.0 collective-permute-start.8
  48.9 24.7 %collective-permute-done.1 = s32[2,2]{1,0:T(2,128)S(1)} collective-permute-done((s32[2,2]{1,0:T(2,128)S(1)}, s32[2,2]{1,0:T(2,128)S(1)}, u32[]{:S(2)}, u32[]{:S(2)}) %collective-permute-start.1) | collective-permute-done | bytes 48 | tf_op jit(solution)/shard_map/ppermute | solution.py:22
  73.6 0.6 collective-permute-start.9
  74.3 0.0 collective-permute-done
  74.3 0.4 collective-permute-start.10
  74.6 2.5 %collective-permute-start.11 = (f32[2,256,256]{2,1,0:T(8,128)}, f32[2,256,256]{2,1,0:T(8,128)}, u32[]{:S(2)}, u32[]{:S(2)}) collective-permute-start(f32[2,256,256]{2,1,0:T(8,128)} %collective-permute-done.7.refs_6_), channel_id=1, source_target_pairs={{0,7},{1,0},{2,1},{3,2},{4,3},{5,4},{6,5},{7,6},{8,15},{9,8},{10,9... | collective-permute-start | bytes 1572872 | tf_op jit(solution)/shard_map/ppermute | solution.py:22
  77.1 0.6 pad_add_fusion.offs
  77.7 0.8 copy-done.5
  78.5 0.8 copy-done.6
  79.3 1.4 collective-permute-done.9.refs_8_
  80.7 0.8 copy-done.7
  81.5 1.9 collective-permute-done.10.refs_9_
  83.4 0.8 copy-done.8
  84.2 4.6 %collective-permute-done.11.refs_10_ = f32[2,256,256]{2,1,0:T(8,128)} collective-permute-done((f32[2,256,256]{2,1,0:T(8,128)}, f32[2,256,256]{2,1,0:T(8,128)}, u32[]{:S(2)}, u32[]{:S(2)}) %collective-permute-start.11) | collective-permute-done | bytes 524320 | tf_op jit(solution)/shard_map/ppermute | solution.py:22
  88.8 21.2 %forward.1 = (f32[4,2,512,512]{3,2,1,0:T(8,128)}, f32[4,2,512,512]{3,2,1,0:T(8,128)}) custom-call(s32[4,2]{1,0:T(4,128)} %pad_add_fusion.offs, f32[2,256,512]{2,1,0:T(8,128)} %refs_0_.1, f32[2,256,256]{2,1,0:T(8,128)} %collective-permute-done.2.refs_1_, f32[2,256,256]{2,1,0:T(8,128)} %copy-done.5, f32[2,256,256]{2,1,0:T(8,128)} %collective-permute-done.4.refs_3_, ...), custom_call_target="tpu_custom_call" | custom-call | flops 8589934592 | bytes 30000000 | tf_op jit(solution)/shard_map/forward/pallas_call | solution.py:317
  110.0 2.8 %multiply_reduce_fusion.1 = (f32[]{:T(128)}, f32[]{:T(128)}) fusion(f32[2,512,512]{2,1,0:T(8,128)} %ill.1), kind=kLoop, calls=%fused_computation.5 | loop fusion | flops 2097150 | bytes 2097160 | tf_op jit(solution)/shard_map/reduce_sum | solution.py:459
  114.2 0.8 slice_reduce_fusion
  116.4 25.5 %backward.1 = (f32[2,8,768,128]{3,2,1,0:T(8,128)}, f32[4,32,3,16,128]{4,3,2,1,0:T(8,128)}) custom-call(s32[4,2]{1,0:T(4,128)} %pad_add_fusion.offs, s32[32]{0:T(128)} %order.1, f32[4,2,512,512]{3,2,1,0:T(8,128)} %get-tuple-element.19.far, f32[4,2,512,512]{3,2,1,0:T(8,128)} %get-tuple-element.20.patch, bf16[16,4,2,16,512]{4,3,2,1,0:T(8,128)(2,1)} %all-to-all-done.1.amp, ...), custom_call_target="tpu_custom_call" | custom-call | flops 8589934592 | bytes 30000000 | tf_op jit(solution)/shard_map/backward/pallas_call | solution.py:352
  141.9 2.4 multiply_convert_fusion.2
  144.2 1.3 collective-permute-start.14
  145.5 1.5 multiply_convert_fusion
  147.0 11.0 %all-to-all-start.2 = ((f16[128,48,128]{2,1,0:T(8,128)(2,1)}), f16[128,48,128]{2,1,0:T(8,128)(2,1)}, u32[]{:S(2)}, u32[]{:S(2)}) async-start(f16[128,48,128]{2,1,0:T(8,128)(2,1)} %multiply_convert_fusion), calls=%async_computation.2 | async-start | bytes 3145728 | tf_op jit(solution)/shard_map/all_to_all | solution.py:410
  158.1 1.6 collective-permute-start.13
  159.8 0.1 convert_multiply_fusion.1
  159.9 23.0 %collective-permute-done.13 = f16[2,2,768,128]{3,2,1,0:T(8,128)(2,1)S(1)} collective-permute-done((f16[2,2,768,128]{3,2,1,0:T(8,128)(2,1)S(1)}, f16[2,2,768,128]{3,2,1,0:T(8,128)(2,1)S(1)}, u32[]{:S(2)}, u32[]{:S(2)}) %collective-permute-start.13) | collective-permute-done | bytes 786464 | tf_op jit(solution)/shard_map/ppermute | solution.py:22
  182.9 0.1 convert_multiply_fusion.2
  183.0 2.3 maximum_add_fusion
  185.3 1.9 multiply_reduce_fusion
  187.3 1.1 broadcast_in_dim.26
  188.4 11.1 %all-to-all-start.3 = ((f16[128,32,128]{2,1,0:T(8,128)(2,1)}), f16[128,32,128]{2,1,0:T(8,128)(2,1)}, u32[]{:S(2)}, u32[]{:S(2)}) async-start(f16[128,32,128]{2,1,0:T(8,128)(2,1)} %broadcast_in_dim.26), calls=%async_computation.3 | async-start | bytes 2097152 | tf_op jit(solution)/shard_map/all_to_all | solution.py:410
  199.5 1.2 fusion.1
  200.8 1.4 collective-permute-start.16
  202.1 4.0 %collective-permute-start.15 = (f16[2,4,256,128]{3,2,1,0:T(8,128)(2,1)}, f16[2,4,256,128]{3,2,1,0:T(8,128)(2,1)}, u32[]{:S(2)}, u32[]{:S(2)}) collective-permute-start(f16[2,4,256,128]{3,2,1,0:T(8,128)(2,1)} %get-tuple-element.42), channel_id=1, source_target_pairs={{0,120},{8,0},{16,8},{24,16},{32,24},{40,32},{48,40},{56,48},{64,5... | collective-permute-start | bytes 1572872 | tf_op jit(solution)/shard_map/ppermute | solution.py:22
  206.2 21.8 %collective-permute-done.16 = f16[2,4,256,128]{3,2,1,0:T(8,128)(2,1)} collective-permute-done((f16[2,4,256,128]{3,2,1,0:T(8,128)(2,1)}, f16[2,4,256,128]{3,2,1,0:T(8,128)(2,1)}, u32[]{:S(2)}, u32[]{:S(2)}) %collective-permute-start.16) | collective-permute-done | bytes 524320 | tf_op jit(solution)/shard_map/ppermute | solution.py:22
  228.0 2.4 %fusion.3 = f32[2,256,4,128]{3,1,2,0:T(8,128)} fusion(f32[2,4,768,128]{3,2,1,0:T(8,128)S(1)} %maximum_add_fusion, f16[2,4,256,128]{3,2,1,0:T(8,128)(2,1)} %collective-permute-done.16, f16[2,4,256,128]{3,2,1,0:T(8,128)(2,1)} %collective-permute-done.15, f32[]{:T(128)S(6)} %div.42), kind=kLoop, calls=%fused_computation.17 | loop fusion | flops 1572864 | bytes 3145732 | tf_op jit(solution)/shard_map/transpose | solution.py:505
  230.3 1.6 copy.24
  231.9 1.3 copy.25
  233.2 1.5 convert_multiply_fusion.packed
  234.7 1.6 unpack.1
  (27 shorter events, 0.1 us)
Async XLA Ops:
  0.6 4.5 %copy-start = (f32[2,256,512]{2,1,0:T(8,128)S(1)}, f32[2,256,512]{2,1,0:T(8,128)}, u32[]{:S(2)}) copy-start(f32[2,256,512]{2,1,0:T(8,128)} %refs_0_.1) | copy-start | bytes 3145732
  2.5 14.4 %collective-permute-start.12 = (bf16[16,2,2,16,512]{4,3,2,1,0:T(8,128)(2,1)S(1)}, bf16[16,2,2,16,512]{4,3,2,1,0:T(8,128)(2,1)S(1)}, u32[]{:S(2)}, u32[]{:S(2)}) collective-permute-start(bf16[16,2,2,16,512]{4,3,2,1,0:T(8,128)(2,1)S(1)} %get-tuple-element.44), channel_id=1, source_target_pairs={{0,1},{1,2},{2,3},{3,4},{4,5},{5,6},{6,7},{7,0},{8,9},{9,10},{10,1... | collective-permute-start | bytes 3145736 | tf_op jit(solution)/shard_map/ppermute | solution.py:22
  5.3 28.3 %collective-permute-start.4 = (f32[2,256,256]{2,1,0:T(8,128)S(1)}, f32[2,256,256]{2,1,0:T(8,128)}, u32[]{:S(2)}, u32[]{:S(2)}) collective-permute-start(f32[2,256,256]{2,1,0:T(8,128)S(1)} %get-tuple-element.47), channel_id=1, source_target_pairs={{0,8},{8,16},{16,24},{24,32},{32,40},{40,48},{48,56},{56,64},{64,7... | collective-permute-start | bytes 1572872 | tf_op jit(solution)/shard_map/ppermute | solution.py:22
  6.6 28.1 %collective-permute-start.5 = (f32[2,256,256]{2,1,0:T(8,128)S(1)}, f32[2,256,256]{2,1,0:T(8,128)}, u32[]{:S(2)}, u32[]{:S(2)}) collective-permute-start(f32[2,256,256]{2,1,0:T(8,128)S(1)} %get-tuple-element.47), channel_id=1, source_target_pairs={{0,120},{8,0},{16,8},{24,16},{32,24},{40,32},{48,40},{56,48},{64,5... | collective-permute-start | bytes 1572872 | tf_op jit(solution)/shard_map/ppermute | solution.py:22
  11.4 23.3 %collective-permute-start.6 = (f32[2,256,256]{2,1,0:T(8,128)S(1)}, f32[2,256,256]{2,1,0:T(8,128)}, u32[]{:S(2)}, u32[]{:S(2)}) collective-permute-start(f32[2,256,256]{2,1,0:T(8,128)S(1)} %get-tuple-element.46), channel_id=1, source_target_pairs={{0,8},{8,16},{16,24},{24,32},{32,40},{40,48},{48,56},{56,64},{64,7... | collective-permute-start | bytes 1572872 | tf_op jit(solution)/shard_map/ppermute | solution.py:22
  11.4 23.3 %collective-permute-start.7 = (f32[2,256,256]{2,1,0:T(8,128)S(1)}, f32[2,256,256]{2,1,0:T(8,128)}, u32[]{:S(2)}, u32[]{:S(2)}) collective-permute-start(f32[2,256,256]{2,1,0:T(8,128)S(1)} %get-tuple-element.46), channel_id=1, source_target_pairs={{0,120},{8,0},{16,8},{24,16},{32,24},{40,32},{48,40},{56,48},{64,5... | collective-permute-start | bytes 1572872 | tf_op jit(solution)/shard_map/ppermute | solution.py:22
  16.9 57.7 %collective-permute-start.2 = (f32[2,256,256]{2,1,0:T(8,128)S(1)}, f32[2,256,256]{2,1,0:T(8,128)}, u32[]{:S(2)}, u32[]{:S(2)}) collective-permute-start(f32[2,256,256]{2,1,0:T(8,128)S(1)} %get-tuple-element.47), channel_id=1, source_target_pairs={{0,1},{1,2},{2,3},{3,4},{4,5},{5,6},{6,7},{7,0},{8,9},{9,10},{10,1... | collective-permute-start | bytes 1572872 | tf_op jit(solution)/shard_map/ppermute | solution.py:22
  22.2 19.4 %all-to-all-start = ((f32[128,1,128]{2,1,0:T(1,128)}), f32[128,1,128]{2,1,0:T(1,128)S(1)}, u32[]{:S(2)}, u32[]{:S(2)}) async-start(f32[128,1,128]{2,1,0:T(1,128)} %iota.14), calls=%async_computation | async-start | bytes 131072 | tf_op jit(solution)/shard_map/all_to_all | solution.py:410
  33.6 12.6 %copy-start.4 = (s32[1,1,4,2]{2,3,1,0:T(2,128)S(1)}, s32[1,1,4,2]{2,3,1,0:T(2,128)}, u32[]{:S(2)}) copy-start(s32[1,1,4,2]{2,3,1,0:T(2,128)} %param.10) | copy-start | bytes 100
  33.6 44.2 %collective-permute-start.3 = (f32[2,256,256]{2,1,0:T(8,128)S(1)}, f32[2,256,256]{2,1,0:T(8,128)S(1)}, u32[]{:S(2)}, u32[]{:S(2)}) collective-permute-start(f32[2,256,256]{2,1,0:T(8,128)S(1)} %get-tuple-element.46), channel_id=1, source_target_pairs={{0,7},{1,0},{2,1},{3,2},{4,3},{5,4},{6,5},{7,6},{8,15},{9,8},{10,9... | collective-permute-start | bytes 1572872 | tf_op jit(solution)/shard_map/ppermute | solution.py:22
  41.6 4.7 %copy-start.2 = (f32[128,1,128]{2,1,0:T(1,128)}, f32[128,1,128]{2,1,0:T(1,128)S(1)}, u32[]{:S(2)}) copy-start(f32[128,1,128]{2,1,0:T(1,128)S(1)} %all-to-all-done) | copy-start | bytes 196612
  41.6 74.8 %all-to-all-start.1 = ((bf16[16,4,2,16,512]{4,3,2,1,0:T(8,128)(2,1)}), bf16[16,4,2,16,512]{4,3,2,1,0:T(8,128)(2,1)}, u32[]{:S(2)}, u32[]{:S(2)}) async-start(bf16[16,4,2,16,512]{4,3,2,1,0:T(8,128)(2,1)} %pad_maximum_fusion), calls=%async_computation.1 | async-start | bytes 4194304 | tf_op jit(solution)/shard_map/all_to_all | solution.py:446
  46.4 27.3 %collective-permute-start.1 = (s32[2,2]{1,0:T(2,128)S(1)}, s32[2,2]{1,0:T(2,128)S(1)}, u32[]{:S(2)}, u32[]{:S(2)}) collective-permute-start(s32[2,2]{1,0:T(2,128)S(1)} %bitcast.13), channel_id=1, source_target_pairs={{0,8},{8,16},{16,24},{24,32},{32,40},{40,48},{48,56},{56,64},{64,7... | collective-permute-start | bytes 56 | tf_op jit(solution)/shard_map/ppermute | solution.py:22
  46.6 27.6 %collective-permute-start = (s32[2,2]{1,0:T(2,128)S(1)}, s32[2,2]{1,0:T(2,128)S(1)}, u32[]{:S(2)}, u32[]{:S(2)}) collective-permute-start(s32[2,2]{1,0:T(2,128)S(1)} %bitcast.12), channel_id=1, source_target_pairs={{0,9},{1,10},{2,11},{3,12},{4,13},{5,14},{6,15},{7,8},{8,17},{9,18... | collective-permute-start | bytes 56 | tf_op jit(solution)/shard_map/ppermute | solution.py:32
  48.9 29.6 %collective-permute-start.8 = (f32[2,256,256]{2,1,0:T(8,128)}, f32[2,256,256]{2,1,0:T(8,128)S(1)}, u32[]{:S(2)}, u32[]{:S(2)}) collective-permute-start(f32[2,256,256]{2,1,0:T(8,128)} %collective-permute-done.4.refs_3_), channel_id=1, source_target_pairs={{0,1},{1,2},{2,3},{3,4},{4,5},{5,6},{6,7},{7,0},{8,9},{9,10},{10,1... | collective-permute-start | bytes 1572872 | tf_op jit(solution)/shard_map/ppermute | solution.py:22
  73.6 7.1 %collective-permute-start.9 = (f32[2,256,256]{2,1,0:T(8,128)}, f32[2,256,256]{2,1,0:T(8,128)S(1)}, u32[]{:S(2)}, u32[]{:S(2)}) collective-permute-start(f32[2,256,256]{2,1,0:T(8,128)} %collective-permute-done.5.refs_4_), channel_id=1, source_target_pairs={{0,1},{1,2},{2,3},{3,4},{4,5},{5,6},{6,7},{7,0},{8,9},{9,10},{10,1... | collective-permute-start | bytes 1572872 | tf_op jit(solution)/shard_map/ppermute | solution.py:22
  74.3 9.1 %collective-permute-start.10 = (f32[2,256,256]{2,1,0:T(8,128)}, f32[2,256,256]{2,1,0:T(8,128)S(1)}, u32[]{:S(2)}, u32[]{:S(2)}) collective-permute-start(f32[2,256,256]{2,1,0:T(8,128)} %collective-permute-done.6.refs_5_), channel_id=1, source_target_pairs={{0,7},{1,0},{2,1},{3,2},{4,3},{5,4},{6,5},{7,6},{8,15},{9,8},{10,9... | collective-permute-start | bytes 1572872 | tf_op jit(solution)/shard_map/ppermute | solution.py:22
  74.6 14.2 %collective-permute-start.11 = (f32[2,256,256]{2,1,0:T(8,128)}, f32[2,256,256]{2,1,0:T(8,128)}, u32[]{:S(2)}, u32[]{:S(2)}) collective-permute-start(f32[2,256,256]{2,1,0:T(8,128)} %collective-permute-done.7.refs_6_), channel_id=1, source_target_pairs={{0,7},{1,0},{2,1},{3,2},{4,3},{5,4},{6,5},{7,6},{8,15},{9,8},{10,9... | collective-permute-start | bytes 1572872 | tf_op jit(solution)/shard_map/ppermute | solution.py:22
  77.7 0.8 copy-start.5
  78.5 0.8 copy-start.6
  80.7 0.8 copy-start.7
  83.4 0.8 copy-start.8
  110.0 4.2 %copy-start.3 = (f32[128,1,128]{2,1,0:T(1,128)S(1)}, f32[128,1,128]{2,1,0:T(1,128)}, u32[]{:S(2)}) copy-start(f32[128,1,128]{2,1,0:T(1,128)} %copy-done.2) | copy-start | bytes 196612
  141.9 3.6 %copy-start.1 = (f32[4,32,3,16,128]{4,3,2,1,0:T(8,128)S(1)}, f32[4,32,3,16,128]{4,3,2,1,0:T(8,128)}, u32[]{:S(2)}) copy-start(f32[4,32,3,16,128]{4,3,2,1,0:T(8,128)} %get-tuple-element.24) | copy-start | bytes 9437188
  144.2 15.5 %collective-permute-start.14 = (f16[2,2,768,128]{3,2,1,0:T(8,128)(2,1)S(1)}, f16[2,2,768,128]{3,2,1,0:T(8,128)(2,1)S(1)}, u32[]{:S(2)}, u32[]{:S(2)}) collective-permute-start(f16[2,2,768,128]{3,2,1,0:T(8,128)(2,1)S(1)} %get-tuple-element.41), channel_id=1, source_target_pairs={{0,7},{1,0},{2,1},{3,2},{4,3},{5,4},{6,5},{7,6},{8,15},{9,8},{10,9... | collective-permute-start | bytes 2359304 | tf_op jit(solution)/shard_map/ppermute | solution.py:22
  147.0 38.3 %all-to-all-start.2 = ((f16[128,48,128]{2,1,0:T(8,128)(2,1)}), f16[128,48,128]{2,1,0:T(8,128)(2,1)}, u32[]{:S(2)}, u32[]{:S(2)}) async-start(f16[128,48,128]{2,1,0:T(8,128)(2,1)} %multiply_convert_fusion), calls=%async_computation.2 | async-start | bytes 3145728 | tf_op jit(solution)/shard_map/all_to_all | solution.py:410
  158.1 24.8 %collective-permute-start.13 = (f16[2,2,768,128]{3,2,1,0:T(8,128)(2,1)S(1)}, f16[2,2,768,128]{3,2,1,0:T(8,128)(2,1)S(1)}, u32[]{:S(2)}, u32[]{:S(2)}) collective-permute-start(f16[2,2,768,128]{3,2,1,0:T(8,128)(2,1)S(1)} %get-tuple-element.40), channel_id=1, source_target_pairs={{0,1},{1,2},{2,3},{3,4},{4,5},{5,6},{6,7},{7,0},{8,9},{9,10},{10,1... | collective-permute-start | bytes 2359304 | tf_op jit(solution)/shard_map/ppermute | solution.py:22
  188.4 44.8 %all-to-all-start.3 = ((f16[128,32,128]{2,1,0:T(8,128)(2,1)}), f16[128,32,128]{2,1,0:T(8,128)(2,1)}, u32[]{:S(2)}, u32[]{:S(2)}) async-start(f16[128,32,128]{2,1,0:T(8,128)(2,1)} %broadcast_in_dim.26), calls=%async_computation.3 | async-start | bytes 2097152 | tf_op jit(solution)/shard_map/all_to_all | solution.py:410
  200.8 27.2 %collective-permute-start.16 = (f16[2,4,256,128]{3,2,1,0:T(8,128)(2,1)}, f16[2,4,256,128]{3,2,1,0:T(8,128)(2,1)}, u32[]{:S(2)}, u32[]{:S(2)}) collective-permute-start(f16[2,4,256,128]{3,2,1,0:T(8,128)(2,1)} %get-tuple-element.43), channel_id=1, source_target_pairs={{0,8},{8,16},{16,24},{24,32},{32,40},{40,48},{48,56},{56,64},{64,7... | collective-permute-start | bytes 1572872 | tf_op jit(solution)/shard_map/ppermute | solution.py:22
  202.1 25.8 %collective-permute-start.15 = (f16[2,4,256,128]{3,2,1,0:T(8,128)(2,1)}, f16[2,4,256,128]{3,2,1,0:T(8,128)(2,1)}, u32[]{:S(2)}, u32[]{:S(2)}) collective-permute-start(f16[2,4,256,128]{3,2,1,0:T(8,128)(2,1)} %get-tuple-element.42), channel_id=1, source_target_pairs={{0,120},{8,0},{16,8},{24,16},{32,24},{40,32},{48,40},{56,48},{64,5... | collective-permute-start | bytes 1572872 | tf_op jit(solution)/shard_map/ppermute | solution.py:22

commit v10 on v9

--- a/solution.py
+++ b/solution.py
@@ -421,7 +421,9 @@
     late = slots // 2
     edge = tile_cols // 2
     grouped = measured.reshape(senders, slots, per, height, size)
-    halves = {"left": specimen[:, :, :edge], "right": specimen[:, :, edge:]}
+    right_half = specimen[:, :, edge:]
+    again, _ = lax.optimization_barrier((specimen, right_half))
+    halves = {"left": again[:, :, :edge], "right": right_half}
     rows = []
     for name in ("right", "left"):
         rows.append(passed_along(halves[name], "row", 1))
@@ -442,7 +444,9 @@
     outers = []
     for index, (steps, name) in enumerate(((1, "west"), (1, "west"), (-1, "east"), (-1, "east"))):
         outers.append(passed_along(rows[index], "col", steps))
-    levels, _ = lax.optimization_barrier((levels, tuple(rows)))
+    levels, probe, _ = lax.optimization_barrier((levels, illumination, tuple(rows)))
+    ill_power = jnp.sum(probe * probe)
+    ill_peak = jnp.maximum(jnp.max(jnp.abs(probe)), 1e-8)
     arrived = lax.all_to_all(
         levels,
         "row",
@@ -451,13 +455,8 @@
         tiled=True,
         axis_index_groups=[[(sender + 1) % senders for sender in range(senders)]],
     )
-    pieces = (specimen, west, east, *rows, *outers)
-    far, patch = run_forward(offs, pieces, tables, illumination)
-    far, probe, peaks = lax.optimization_barrier((far, illumination, peaks))
     peak = jnp.maximum(jnp.max(peaks[:, :, : LANES // 2]), 1e-12)
     power = jnp.max(peaks[:, :, LANES // 2 :])
-    ill_power = jnp.sum(probe * probe)
-    ill_peak = jnp.maximum(jnp.max(jnp.abs(probe)), 1e-8)
     modulus = 1.5 * peak
     energy = jnp.minimum(
         modulus * jnp.sqrt(ill_power), 1.5 * ill_peak * jnp.sqrt(6.0 * power)
@@ -468,8 +467,10 @@
     density_bound = slots * modulus * modulus
     step_bound = math.sqrt(slots * devices) * change_bound
     bounds = (grad_bound, sum_bound, density_bound, step_bound)
-    far, bounds = lax.optimization_barrier((far, bounds))
+    offs, bounds = lax.optimization_barrier((offs, bounds))
     grad_bound, sum_bound, density_bound, step_bound = bounds
+    pieces = (specimen, west, east, *rows, *outers)
+    far, patch = run_forward(offs, pieces, tables, illumination)
     region_shape = (2, (tile_cols + 2 * edge) // LANES, 3 * tile_rows, LANES)
     accum, sums = run_backward(
         offs, module_row, far, patch, arrived, illumination, tables, region_shape

time: 237 us -> 230 us (0.970)
  starting transfers between devices: 68 us -> 57.5 us
  waiting for transfers between devices: 85.1 us -> 91.9 us
    ppermute x1, waiting for transfers between devices: 0.01 us -> 23.9 us  [passed_both(): return lax.ppermute(value, ('row', 'col'), pairs)]
    ppermute x16, waiting for transfers between devices: 78.1 us -> 63.8 us  [passed_along(): return lax.ppermute(value, axis, pairs)]
    all_to_all x3, starting transfers between devices: 32 us -> 23.5 us  [spread_out(): lax.all_to_all(value, ('row', 'col'), split_axis=0, concat_axis=0, tiled=...]
    unnamed x19 -> x11, local copies, waits for them, and re-layouts: 4.5 us -> 1.33 us
    all_to_all x3, waiting for transfers between devices: 6.98 us -> 4.16 us  [spread_out(): lax.all_to_all(value, ('row', 'col'), split_axis=0, concat_axis=0, tiled=...]
  transfers between devices with their start and end apart: 21 -> 21, of which waited for: 8 -> 8; matrix products, arithmetic and copies ran while one was open for 8% -> 9% of each run, Pallas kernels for 9% -> 9%
where the time goes in v10:
time: 230 us; the launch traced here: 229 us
  waiting for transfers between devices  91.9 us (40%)
  starting transfers between devices  57.5 us (25%)
  Pallas kernels  48.3 us (21%)
  other arithmetic  19.9 us (9%)
  local copies, waits for them, and re-layouts  8.39 us (4%)
  between operations  3.43 us (1%)
    ppermute x16, waiting for transfers between devices, passed_along(): return lax.ppermute(value, axis, pairs)  63.8 us
    ppermute x16, starting transfers between devices, passed_along(): return lax.ppermute(value, axis, pairs)  28.2 us
    pallas_call x1, Pallas kernels, run_backward(): pl.pallas_call(backward_kernel, grid_spec=pltpu.PrefetchScalarGridSpec(nu...  25.4 us
    ppermute x1, waiting for transfers between devices, passed_both(): return lax.ppermute(value, ('row', 'col'), pairs)  23.9 us
    all_to_all x3, starting transfers between devices, spread_out(): lax.all_to_all(value, ('row', 'col'), split_axis=0, concat_axis=0, tiled=...  23.5 us
    pallas_call x1, Pallas kernels, run_forward(): pl.pallas_call(forward_kernel, grid_spec=pltpu.PrefetchScalarGridSpec(num...  21.2 us
    all_to_all x1, starting transfers between devices, shards(): lax.all_to_all(levels, 'row', split_axis=0, concat_axis=0, tiled=True, ax...  5.83 us
    convert_element_type x4, other arithmetic, narrowed(): return (value * (HALF_TOP / bound)).astype(jnp.float16)  5.15 us
  transfers between devices with their start and end apart: 21, of which 8 were waited for; matrix products, arithmetic and copies ran while one was open for 9% of the time, Pallas kernels for 9%

profile of v10, /device:TPU:1, one launch (start us, length us, event | category | flops | bytes accessed | tf_op | source)
XLA Modules:
  0.0 229.4 jit_solution(9013121511990579372)
XLA Ops:
  0.6 0.0 copy-start
  0.6 1.8 fusion.9
  2.5 2.7 %collective-permute-start.2 = (bf16[16,2,2,16,512]{4,3,2,1,0:T(8,128)(2,1)S(1)}, bf16[16,2,2,16,512]{4,3,2,1,0:T(8,128)(2,1)S(1)}, u32[]{:S(2)}, u32[]{:S(2)}) collective-permute-start(bf16[16,2,2,16,512]{4,3,2,1,0:T(8,128)(2,1)S(1)} %get-tuple-element.42), channel_id=1, source_target_pairs={{0,1},{1,2},{2,3},{3,4},{4,5},{5,6},{6,7},{7,0},{8,9},{9,10},{10,1... | collective-permute-start | bytes 3145736 | tf_op jit(solution)/shard_map/ppermute | solution.py:22
  5.2 0.8 slice.52
  6.0 0.8 slice.53
  6.8 1.2 collective-permute-start.5
  8.0 4.7 %collective-permute-start.6 = (f32[2,256,256]{2,1,0:T(8,128)}, f32[2,256,256]{2,1,0:T(8,128)}, u32[]{:S(2)}, u32[]{:S(2)}) collective-permute-start(f32[2,256,256]{2,1,0:T(8,128)} %slice.53), channel_id=1, source_target_pairs={{0,120},{8,0},{16,8},{24,16},{32,24},{40,32},{48,40},{56,48},{64,5... | collective-permute-start | bytes 1572872 | tf_op jit(solution)/shard_map/ppermute | solution.py:22
  12.8 0.0 collective-permute-start.3
  12.8 4.8 %collective-permute-start.4 = (f32[2,256,256]{2,1,0:T(8,128)}, f32[2,256,256]{2,1,0:T(8,128)}, u32[]{:S(2)}, u32[]{:S(2)}) collective-permute-start(f32[2,256,256]{2,1,0:T(8,128)} %slice.52), channel_id=1, source_target_pairs={{0,120},{8,0},{16,8},{24,16},{32,24},{40,32},{48,40},{56,48},{64,5... | collective-permute-start | bytes 1572872 | tf_op jit(solution)/shard_map/ppermute | solution.py:22
  17.6 0.9 abs_reduce_fusion.1
  18.5 1.3 compare_select_fusion.1
  19.9 0.7 iota.14
  20.5 3.9 %all-to-all-start = ((f32[128,1,128]{2,1,0:T(1,128)}), f32[128,1,128]{2,1,0:T(1,128)S(1)}, u32[]{:S(2)}, u32[]{:S(2)}) async-start(f32[128,1,128]{2,1,0:T(1,128)} %iota.14), calls=%async_computation | async-start | bytes 131072 | tf_op jit(solution)/shard_map/all_to_all | solution.py:410
  24.4 1.5 pad_maximum_fusion
  25.9 0.0 collective-permute-done.5.refs_5_
  25.9 0.0 collective-permute-done.6.refs_6_
  25.9 10.1 %collective-permute-done.3.refs_3_ = f32[2,256,256]{2,1,0:T(8,128)} collective-permute-done((f32[2,256,256]{2,1,0:T(8,128)}, f32[2,256,256]{2,1,0:T(8,128)}, u32[]{:S(2)}, u32[]{:S(2)}) %collective-permute-start.3) | collective-permute-done | bytes 524320 | tf_op jit(solution)/shard_map/ppermute | solution.py:22
  36.0 4.2 %all-to-all-done = f32[128,1,128]{2,1,0:T(1,128)S(1)} async-done(((f32[128,1,128]{2,1,0:T(1,128)}), f32[128,1,128]{2,1,0:T(1,128)S(1)}, u32[]{:S(2)}, u32[]{:S(2)}) %all-to-all-start) | async-done | bytes 65568 | tf_op jit(solution)/shard_map/all_to_all | solution.py:410
  40.2 5.8 %all-to-all-start.1 = ((bf16[16,4,2,16,512]{4,3,2,1,0:T(8,128)(2,1)}), bf16[16,4,2,16,512]{4,3,2,1,0:T(8,128)(2,1)}, u32[]{:S(2)}, u32[]{:S(2)}) async-start(bf16[16,4,2,16,512]{4,3,2,1,0:T(8,128)(2,1)} %pad_maximum_fusion), calls=%async_computation.1 | async-start | bytes 4194304 | tf_op jit(solution)/shard_map/all_to_all | solution.py:450
  46.0 1.2 collective-permute-start.8
  47.2 0.5 collective-permute-start.7
  47.7 0.1 fusion.10
  47.8 0.1 copy.20
  47.9 0.0 collective-permute-start
  47.9 0.1 copy.21
  48.0 1.2 collective-permute-start.1
  49.2 1.0 collective-permute-start.11
  50.1 23.9 %collective-permute-done = s32[2,2]{1,0:T(2,128)S(1)} collective-permute-done((s32[2,2]{1,0:T(2,128)S(1)}, s32[2,2]{1,0:T(2,128)S(1)}, u32[]{:S(2)}, u32[]{:S(2)}) %collective-permute-start) | collective-permute-done | bytes 48 | tf_op jit(solution)/shard_map/ppermute | solution.py:32
  74.0 0.8 collective-permute-start.12
  74.8 0.9 collective-permute-start.10
  75.8 0.0 collective-permute-done.8.refs_2_
  75.8 0.1 collective-permute-start.9
  75.8 0.6 pad_add_fusion.offs
  76.5 0.8 slice_reduce_fusion
  78.5 1.2 multiply_reduce_fusion.1
  81.0 2.2 collective-permute-done.12.refs_10_
  83.2 0.0 collective-permute-done.10.refs_8_
  83.2 4.6 %collective-permute-done.9.refs_7_ = f32[2,256,256]{2,1,0:T(8,128)} collective-permute-done((f32[2,256,256]{2,1,0:T(8,128)}, f32[2,256,256]{2,1,0:T(8,128)}, u32[]{:S(2)}, u32[]{:S(2)}) %collective-permute-start.9) | collective-permute-done | bytes 524320 | tf_op jit(solution)/shard_map/ppermute | solution.py:22
  87.8 21.2 %forward.1 = (f32[4,2,512,512]{3,2,1,0:T(8,128)}, f32[4,2,512,512]{3,2,1,0:T(8,128)}) custom-call(s32[4,2]{1,0:T(4,128)} %pad_add_fusion.offs, f32[2,256,512]{2,1,0:T(8,128)} %refs_0_.1, f32[2,256,256]{2,1,0:T(8,128)} %collective-permute-done.7.refs_1_, f32[2,256,256]{2,1,0:T(8,128)} %copy-done.4, f32[2,256,256]{2,1,0:T(8,128)} %collective-permute-done.3.refs_3_, ...), custom_call_target="tpu_custom_call" | custom-call | flops 8589934592 | bytes 30000000 | tf_op jit(solution)/shard_map/forward/pallas_call | solution.py:317
  109.0 0.0 all-to-all-done.1.amp
  109.0 25.4 %backward.1 = (f32[2,8,768,128]{3,2,1,0:T(8,128)}, f32[4,32,3,16,128]{4,3,2,1,0:T(8,128)}) custom-call(s32[4,2]{1,0:T(4,128)} %pad_add_fusion.offs, s32[32]{0:T(128)} %order.1, f32[4,2,512,512]{3,2,1,0:T(8,128)} %get-tuple-element.17.far, f32[4,2,512,512]{3,2,1,0:T(8,128)} %get-tuple-element.18.patch, bf16[16,4,2,16,512]{4,3,2,1,0:T(8,128)(2,1)} %all-to-all-done.1.amp, ...), custom_call_target="tpu_custom_call" | custom-call | flops 8589934592 | bytes 30000000 | tf_op jit(solution)/shard_map/backward/pallas_call | solution.py:352
  134.5 2.4 %multiply_convert_fusion.2 = (f16[2,2,768,128]{3,2,1,0:T(8,128)(2,1)S(1)}, f16[2,2,768,128]{3,2,1,0:T(8,128)(2,1)S(1)}) fusion(f32[2,8,768,128]{3,2,1,0:T(8,128)} %get-tuple-element.20, f32[]{:T(128)S(6)} %div.41), kind=kLoop, calls=%fused_computation.10 | loop fusion | flops 1572864 | bytes 4718596 | tf_op jit(solution)/shard_map/convert_element_type | solution.py:47
  136.8 2.5 %collective-permute-start.13 = (f16[2,2,768,128]{3,2,1,0:T(8,128)(2,1)S(1)}, f16[2,2,768,128]{3,2,1,0:T(8,128)(2,1)S(1)}, u32[]{:S(2)}, u32[]{:S(2)}) collective-permute-start(f16[2,2,768,128]{3,2,1,0:T(8,128)(2,1)S(1)} %get-tuple-element.38), channel_id=1, source_target_pairs={{0,1},{1,2},{2,3},{3,4},{4,5},{5,6},{6,7},{7,0},{8,9},{9,10},{10,1... | collective-permute-start | bytes 2359304 | tf_op jit(solution)/shard_map/ppermute | solution.py:22
  139.4 1.5 multiply_convert_fusion
  140.9 10.1 %all-to-all-start.2 = ((f16[128,48,128]{2,1,0:T(8,128)(2,1)}), f16[128,48,128]{2,1,0:T(8,128)(2,1)}, u32[]{:S(2)}, u32[]{:S(2)}) async-start(f16[128,48,128]{2,1,0:T(8,128)(2,1)} %multiply_convert_fusion), calls=%async_computation.2 | async-start | bytes 3145728 | tf_op jit(solution)/shard_map/all_to_all | solution.py:410
  151.0 1.1 collective-permute-start.14
  152.2 0.1 convert_multiply_fusion.2
  152.3 25.2 %collective-permute-done.14 = f16[2,2,768,128]{3,2,1,0:T(8,128)(2,1)S(1)} collective-permute-done((f16[2,2,768,128]{3,2,1,0:T(8,128)(2,1)S(1)}, f16[2,2,768,128]{3,2,1,0:T(8,128)(2,1)S(1)}, u32[]{:S(2)}, u32[]{:S(2)}) %collective-permute-start.14) | collective-permute-done | bytes 786464 | tf_op jit(solution)/shard_map/ppermute | solution.py:22
  177.5 0.1 convert_multiply_fusion.1
  177.6 2.3 %maximum_add_fusion = f32[2,4,768,128]{3,2,1,0:T(8,128)S(1)} fusion(f32[2,2,768,128]{3,2,1,0:T(8,128)S(1)} %convert_multiply_fusion.1, f32[2,2,768,128]{3,2,1,0:T(8,128)S(1)} %convert_multiply_fusion.2, f32[2,8,768,128]{3,2,1,0:T(8,128)} %get-tuple-element.20), kind=kLoop, calls=%fused_computation | loop fusion | flops 1572864 | bytes 9437184 | tf_op jit(solution)/shard_map/add | solution.py:488
  180.0 0.0 all-to-all-done.2
  180.0 1.9 multiply_reduce_fusion
  181.9 1.1 broadcast_in_dim.26
  183.0 9.5 %all-to-all-start.3 = ((f16[128,32,128]{2,1,0:T(8,128)(2,1)}), f16[128,32,128]{2,1,0:T(8,128)(2,1)}, u32[]{:S(2)}, u32[]{:S(2)}) async-start(f16[128,32,128]{2,1,0:T(8,128)(2,1)} %broadcast_in_dim.26), calls=%async_computation.3 | async-start | bytes 2097152 | tf_op jit(solution)/shard_map/all_to_all | solution.py:410
  192.6 1.3 fusion.1
  193.8 5.4 %collective-permute-start.15 = (f16[2,4,256,128]{3,2,1,0:T(8,128)(2,1)}, f16[2,4,256,128]{3,2,1,0:T(8,128)(2,1)}, u32[]{:S(2)}, u32[]{:S(2)}) collective-permute-start(f16[2,4,256,128]{3,2,1,0:T(8,128)(2,1)} %get-tuple-element.40), channel_id=1, source_target_pairs={{0,120},{8,0},{16,8},{24,16},{32,24},{40,32},{48,40},{56,48},{64,5... | collective-permute-start | bytes 1572872 | tf_op jit(solution)/shard_map/ppermute | solution.py:22
  199.2 0.0 collective-permute-start.16
  199.2 16.8 %collective-permute-done.15 = f16[2,4,256,128]{3,2,1,0:T(8,128)(2,1)} collective-permute-done((f16[2,4,256,128]{3,2,1,0:T(8,128)(2,1)}, f16[2,4,256,128]{3,2,1,0:T(8,128)(2,1)}, u32[]{:S(2)}, u32[]{:S(2)}) %collective-permute-start.15) | collective-permute-done | bytes 524320 | tf_op jit(solution)/shard_map/ppermute | solution.py:22
  216.1 5.0 %collective-permute-done.16 = f16[2,4,256,128]{3,2,1,0:T(8,128)(2,1)} collective-permute-done((f16[2,4,256,128]{3,2,1,0:T(8,128)(2,1)}, f16[2,4,256,128]{3,2,1,0:T(8,128)(2,1)}, u32[]{:S(2)}, u32[]{:S(2)}) %collective-permute-start.16) | collective-permute-done | bytes 524320 | tf_op jit(solution)/shard_map/ppermute | solution.py:22
  221.0 2.4 %fusion.3 = f32[2,256,4,128]{3,1,2,0:T(8,128)} fusion(f32[2,4,768,128]{3,2,1,0:T(8,128)S(1)} %maximum_add_fusion, f16[2,4,256,128]{3,2,1,0:T(8,128)(2,1)} %collective-permute-done.16, f16[2,4,256,128]{3,2,1,0:T(8,128)(2,1)} %collective-permute-done.15, f32[]{:T(128)S(6)} %div.42), kind=kLoop, calls=%fused_computation.17 | loop fusion | flops 1572864 | bytes 3145732 | tf_op jit(solution)/shard_map/transpose | solution.py:506
  223.4 1.6 copy.24
  224.9 1.3 copy.25
  226.3 1.5 convert_multiply_fusion.packed
  227.8 1.6 unpack.1
  (20 shorter events, 0.1 us)
Async XLA Ops:
  0.6 4.5 %copy-start = (f32[2,256,512]{2,1,0:T(8,128)S(1)}, f32[2,256,512]{2,1,0:T(8,128)}, u32[]{:S(2)}) copy-start(f32[2,256,512]{2,1,0:T(8,128)} %refs_0_.1) | copy-start | bytes 3145732
  2.5 22.0 %collective-permute-start.2 = (bf16[16,2,2,16,512]{4,3,2,1,0:T(8,128)(2,1)S(1)}, bf16[16,2,2,16,512]{4,3,2,1,0:T(8,128)(2,1)S(1)}, u32[]{:S(2)}, u32[]{:S(2)}) collective-permute-start(bf16[16,2,2,16,512]{4,3,2,1,0:T(8,128)(2,1)S(1)} %get-tuple-element.42), channel_id=1, source_target_pairs={{0,1},{1,2},{2,3},{3,4},{4,5},{5,6},{6,7},{7,0},{8,9},{9,10},{10,1... | collective-permute-start | bytes 3145736 | tf_op jit(solution)/shard_map/ppermute | solution.py:22
  6.8 19.1 %collective-permute-start.5 = (f32[2,256,256]{2,1,0:T(8,128)}, f32[2,256,256]{2,1,0:T(8,128)}, u32[]{:S(2)}, u32[]{:S(2)}) collective-permute-start(f32[2,256,256]{2,1,0:T(8,128)} %slice.53), channel_id=1, source_target_pairs={{0,8},{8,16},{16,24},{24,32},{32,40},{40,48},{48,56},{56,64},{64,7... | collective-permute-start | bytes 1572872 | tf_op jit(solution)/shard_map/ppermute | solution.py:22
  8.0 17.9 %collective-permute-start.6 = (f32[2,256,256]{2,1,0:T(8,128)}, f32[2,256,256]{2,1,0:T(8,128)}, u32[]{:S(2)}, u32[]{:S(2)}) collective-permute-start(f32[2,256,256]{2,1,0:T(8,128)} %slice.53), channel_id=1, source_target_pairs={{0,120},{8,0},{16,8},{24,16},{32,24},{40,32},{48,40},{56,48},{64,5... | collective-permute-start | bytes 1572872 | tf_op jit(solution)/shard_map/ppermute | solution.py:22
  12.8 23.2 %collective-permute-start.3 = (f32[2,256,256]{2,1,0:T(8,128)}, f32[2,256,256]{2,1,0:T(8,128)}, u32[]{:S(2)}, u32[]{:S(2)}) collective-permute-start(f32[2,256,256]{2,1,0:T(8,128)} %slice.52), channel_id=1, source_target_pairs={{0,8},{8,16},{16,24},{24,32},{32,40},{40,48},{48,56},{56,64},{64,7... | collective-permute-start | bytes 1572872 | tf_op jit(solution)/shard_map/ppermute | solution.py:22
  12.8 23.2 %collective-permute-start.4 = (f32[2,256,256]{2,1,0:T(8,128)}, f32[2,256,256]{2,1,0:T(8,128)}, u32[]{:S(2)}, u32[]{:S(2)}) collective-permute-start(f32[2,256,256]{2,1,0:T(8,128)} %slice.52), channel_id=1, source_target_pairs={{0,120},{8,0},{16,8},{24,16},{32,24},{40,32},{48,40},{56,48},{64,5... | collective-permute-start | bytes 1572872 | tf_op jit(solution)/shard_map/ppermute | solution.py:22
  20.5 19.7 %all-to-all-start = ((f32[128,1,128]{2,1,0:T(1,128)}), f32[128,1,128]{2,1,0:T(1,128)S(1)}, u32[]{:S(2)}, u32[]{:S(2)}) async-start(f32[128,1,128]{2,1,0:T(1,128)} %iota.14), calls=%async_computation | async-start | bytes 131072 | tf_op jit(solution)/shard_map/all_to_all | solution.py:410
  25.9 21.8 %copy-start.3 = (s32[1,1,4,2]{2,3,1,0:T(2,128)S(1)}, s32[1,1,4,2]{2,3,1,0:T(2,128)}, u32[]{:S(2)}) copy-start(s32[1,1,4,2]{2,3,1,0:T(2,128)} %param.10) | copy-start | bytes 100
  25.9 52.6 %copy-start.2 = (f32[2,512,512]{2,1,0:T(8,128)S(1)}, f32[2,512,512]{2,1,0:T(8,128)}, u32[]{:S(2)}) copy-start(f32[2,512,512]{2,1,0:T(8,128)} %ill.1) | copy-start | bytes 6291460
  40.2 68.8 %all-to-all-start.1 = ((bf16[16,4,2,16,512]{4,3,2,1,0:T(8,128)(2,1)}), bf16[16,4,2,16,512]{4,3,2,1,0:T(8,128)(2,1)}, u32[]{:S(2)}, u32[]{:S(2)}) async-start(bf16[16,4,2,16,512]{4,3,2,1,0:T(8,128)(2,1)} %pad_maximum_fusion), calls=%async_computation.1 | async-start | bytes 4194304 | tf_op jit(solution)/shard_map/all_to_all | solution.py:450
  46.0 29.8 %collective-permute-start.8 = (f32[2,256,256]{2,1,0:T(8,128)}, f32[2,256,256]{2,1,0:T(8,128)S(1)}, u32[]{:S(2)}, u32[]{:S(2)}) collective-permute-start(f32[2,256,256]{2,1,0:T(8,128)} %slice.53), channel_id=1, source_target_pairs={{0,7},{1,0},{2,1},{3,2},{4,3},{5,4},{6,5},{7,6},{8,15},{9,8},{10,9... | collective-permute-start | bytes 1572872 | tf_op jit(solution)/shard_map/ppermute | solution.py:22
  47.2 33.8 %collective-permute-start.7 = (f32[2,256,256]{2,1,0:T(8,128)}, f32[2,256,256]{2,1,0:T(8,128)}, u32[]{:S(2)}, u32[]{:S(2)}) collective-permute-start(f32[2,256,256]{2,1,0:T(8,128)} %slice.52), channel_id=1, source_target_pairs={{0,1},{1,2},{2,3},{3,4},{4,5},{5,6},{6,7},{7,0},{8,9},{9,10},{10,1... | collective-permute-start | bytes 1572872 | tf_op jit(solution)/shard_map/ppermute | solution.py:22
  47.9 26.1 %collective-permute-start = (s32[2,2]{1,0:T(2,128)S(1)}, s32[2,2]{1,0:T(2,128)S(1)}, u32[]{:S(2)}, u32[]{:S(2)}) collective-permute-start(s32[2,2]{1,0:T(2,128)S(1)} %bitcast.13), channel_id=1, source_target_pairs={{0,9},{1,10},{2,11},{3,12},{4,13},{5,14},{6,15},{7,8},{8,17},{9,18... | collective-permute-start | bytes 56 | tf_op jit(solution)/shard_map/ppermute | solution.py:32
  48.0 26.8 %collective-permute-start.1 = (s32[2,2]{1,0:T(2,128)S(1)}, s32[2,2]{1,0:T(2,128)S(1)}, u32[]{:S(2)}, u32[]{:S(2)}) collective-permute-start(s32[2,2]{1,0:T(2,128)S(1)} %bitcast.12), channel_id=1, source_target_pairs={{0,8},{8,16},{16,24},{24,32},{32,40},{40,48},{48,56},{56,64},{64,7... | collective-permute-start | bytes 56 | tf_op jit(solution)/shard_map/ppermute | solution.py:22
  49.2 31.8 %collective-permute-start.11 = (f32[2,256,256]{2,1,0:T(8,128)}, f32[2,256,256]{2,1,0:T(8,128)}, u32[]{:S(2)}, u32[]{:S(2)}) collective-permute-start(f32[2,256,256]{2,1,0:T(8,128)} %collective-permute-done.5.refs_5_), channel_id=1, source_target_pairs={{0,7},{1,0},{2,1},{3,2},{4,3},{5,4},{6,5},{7,6},{8,15},{9,8},{10,9... | collective-permute-start | bytes 1572872 | tf_op jit(solution)/shard_map/ppermute | solution.py:22
  74.0 9.2 %collective-permute-start.12 = (f32[2,256,256]{2,1,0:T(8,128)}, f32[2,256,256]{2,1,0:T(8,128)}, u32[]{:S(2)}, u32[]{:S(2)}) collective-permute-start(f32[2,256,256]{2,1,0:T(8,128)} %collective-permute-done.6.refs_6_), channel_id=1, source_target_pairs={{0,7},{1,0},{2,1},{3,2},{4,3},{5,4},{6,5},{7,6},{8,15},{9,8},{10,9... | collective-permute-start | bytes 1572872 | tf_op jit(solution)/shard_map/ppermute | solution.py:22
  74.8 8.4 %collective-permute-start.10 = (f32[2,256,256]{2,1,0:T(8,128)}, f32[2,256,256]{2,1,0:T(8,128)}, u32[]{:S(2)}, u32[]{:S(2)}) collective-permute-start(f32[2,256,256]{2,1,0:T(8,128)} %collective-permute-done.4.refs_4_), channel_id=1, source_target_pairs={{0,1},{1,2},{2,3},{3,4},{4,5},{5,6},{6,7},{7,0},{8,9},{9,10},{10,1... | collective-permute-start | bytes 1572872 | tf_op jit(solution)/shard_map/ppermute | solution.py:22
  75.8 5.2 %copy-start.4 = (f32[2,256,256]{2,1,0:T(8,128)}, f32[2,256,256]{2,1,0:T(8,128)S(1)}, u32[]{:S(2)}) copy-start(f32[2,256,256]{2,1,0:T(8,128)S(1)} %collective-permute-done.8.refs_2_) | copy-start | bytes 1572868
  75.8 12.1 %collective-permute-start.9 = (f32[2,256,256]{2,1,0:T(8,128)}, f32[2,256,256]{2,1,0:T(8,128)}, u32[]{:S(2)}, u32[]{:S(2)}) collective-permute-start(f32[2,256,256]{2,1,0:T(8,128)} %collective-permute-done.3.refs_3_), channel_id=1, source_target_pairs={{0,1},{1,2},{2,3},{3,4},{4,5},{5,6},{6,7},{7,0},{8,9},{9,10},{10,1... | collective-permute-start | bytes 1572872 | tf_op jit(solution)/shard_map/ppermute | solution.py:22
  134.5 4.9 %copy-start.1 = (f32[4,32,3,16,128]{4,3,2,1,0:T(8,128)S(1)}, f32[4,32,3,16,128]{4,3,2,1,0:T(8,128)}, u32[]{:S(2)}) copy-start(f32[4,32,3,16,128]{4,3,2,1,0:T(8,128)} %get-tuple-element.22) | copy-start | bytes 9437188
  136.8 15.3 %collective-permute-start.13 = (f16[2,2,768,128]{3,2,1,0:T(8,128)(2,1)S(1)}, f16[2,2,768,128]{3,2,1,0:T(8,128)(2,1)S(1)}, u32[]{:S(2)}, u32[]{:S(2)}) collective-permute-start(f16[2,2,768,128]{3,2,1,0:T(8,128)(2,1)S(1)} %get-tuple-element.38), channel_id=1, source_target_pairs={{0,1},{1,2},{2,3},{3,4},{4,5},{5,6},{6,7},{7,0},{8,9},{9,10},{10,1... | collective-permute-start | bytes 2359304 | tf_op jit(solution)/shard_map/ppermute | solution.py:22
  140.9 39.1 %all-to-all-start.2 = ((f16[128,48,128]{2,1,0:T(8,128)(2,1)}), f16[128,48,128]{2,1,0:T(8,128)(2,1)}, u32[]{:S(2)}, u32[]{:S(2)}) async-start(f16[128,48,128]{2,1,0:T(8,128)(2,1)} %multiply_convert_fusion), calls=%async_computation.2 | async-start | bytes 3145728 | tf_op jit(solution)/shard_map/all_to_all | solution.py:410
  151.0 26.5 %collective-permute-start.14 = (f16[2,2,768,128]{3,2,1,0:T(8,128)(2,1)S(1)}, f16[2,2,768,128]{3,2,1,0:T(8,128)(2,1)S(1)}, u32[]{:S(2)}, u32[]{:S(2)}) collective-permute-start(f16[2,2,768,128]{3,2,1,0:T(8,128)(2,1)S(1)} %get-tuple-element.39), channel_id=1, source_target_pairs={{0,7},{1,0},{2,1},{3,2},{4,3},{5,4},{6,5},{7,6},{8,15},{9,8},{10,9... | collective-permute-start | bytes 2359304 | tf_op jit(solution)/shard_map/ppermute | solution.py:22
  183.0 43.2 %all-to-all-start.3 = ((f16[128,32,128]{2,1,0:T(8,128)(2,1)}), f16[128,32,128]{2,1,0:T(8,128)(2,1)}, u32[]{:S(2)}, u32[]{:S(2)}) async-start(f16[128,32,128]{2,1,0:T(8,128)(2,1)} %broadcast_in_dim.26), calls=%async_computation.3 | async-start | bytes 2097152 | tf_op jit(solution)/shard_map/all_to_all | solution.py:410
  193.8 22.2 %collective-permute-start.15 = (f16[2,4,256,128]{3,2,1,0:T(8,128)(2,1)}, f16[2,4,256,128]{3,2,1,0:T(8,128)(2,1)}, u32[]{:S(2)}, u32[]{:S(2)}) collective-permute-start(f16[2,4,256,128]{3,2,1,0:T(8,128)(2,1)} %get-tuple-element.40), channel_id=1, source_target_pairs={{0,120},{8,0},{16,8},{24,16},{32,24},{40,32},{48,40},{56,48},{64,5... | collective-permute-start | bytes 1572872 | tf_op jit(solution)/shard_map/ppermute | solution.py:22
  199.2 21.8 %collective-permute-start.16 = (f16[2,4,256,128]{3,2,1,0:T(8,128)(2,1)}, f16[2,4,256,128]{3,2,1,0:T(8,128)(2,1)}, u32[]{:S(2)}, u32[]{:S(2)}) collective-permute-start(f16[2,4,256,128]{3,2,1,0:T(8,128)(2,1)} %get-tuple-element.41), channel_id=1, source_target_pairs={{0,8},{8,16},{16,24},{24,32},{32,40},{40,48},{48,56},{56,64},{64,7... | collective-permute-start | bytes 1572872 | tf_op jit(solution)/shard_map/ppermute | solution.py:22

commit v11 on v10

--- a/solution.py
+++ b/solution.py
@@ -20,16 +20,6 @@
     count = lax.axis_size(axis)
     pairs = [(source, (source + steps) % count) for source in range(count)]
     return lax.ppermute(value, axis, pairs)
-
-
-def passed_both(value, row_steps, col_steps):
-    rows, cols = lax.axis_size("row"), lax.axis_size("col")
-    pairs = [
-        (row * cols + col, (row + row_steps) % rows * cols + (col + col_steps) % cols)
-        for row in range(rows)
-        for col in range(cols)
-    ]
-    return lax.ppermute(value, ("row", "col"), pairs)
 
 
 def dft_tables(size):
@@ -428,19 +418,18 @@
     for name in ("right", "left"):
         rows.append(passed_along(halves[name], "row", 1))
         rows.append(passed_along(halves[name], "row", -1))
-    early_offs = passed_along(scan_offsets[0, 0, :late], "row", 1)
-    late_offs = passed_both(scan_offsets[0, 0, late:], 1, 1)
-    offs = jnp.concatenate([late_offs, early_offs], axis=0)
     moved = passed_along(grouped[:, late:], "col", 1)
     west = passed_along(halves["right"], "col", 1)
     east = passed_along(halves["left"], "col", -1)
     levels = jnp.concatenate([moved, grouped[:, :late]], axis=1)
     tables = dft_tables(size)
-    lane = lax.broadcasted_iota(jnp.int32, (devices, 1, LANES), 2)
-    stats = jnp.where(
-        lane < LANES // 2, jnp.max(jnp.abs(specimen)), jnp.sum(specimen * specimen)
-    )
-    peaks = spread_out(stats)
+    lane = lax.broadcasted_iota(jnp.int32, (1, 1, LANES), 2)
+    count = 2 * slots
+    own_offs = scan_offsets[0, 0].reshape(1, 1, count).astype(jnp.float32)
+    stats = jnp.pad(own_offs, ((0, 0), (0, 0), (0, LANES - count)))
+    stats = jnp.where(lane == count, jnp.max(jnp.abs(specimen)), stats)
+    stats = jnp.where(lane == count + 1, jnp.sum(specimen * specimen), stats)
+    peaks = spread_out(jnp.broadcast_to(stats, (devices, 1, LANES)))
     outers = []
     for index, (steps, name) in enumerate(((1, "west"), (1, "west"), (-1, "east"), (-1, "east"))):
         outers.append(passed_along(rows[index], "col", steps))
@@ -455,8 +444,18 @@
         tiled=True,
         axis_index_groups=[[(sender + 1) % senders for sender in range(senders)]],
     )
-    peak = jnp.maximum(jnp.max(peaks[:, :, : LANES // 2]), 1e-12)
-    power = jnp.max(peaks[:, :, LANES // 2 :])
+    most = jnp.max(peaks, axis=0)
+    peak = jnp.maximum(most[0, count], 1e-12)
+    power = most[0, count + 1]
+    cols = lax.axis_size("col")
+    col_index = lax.axis_index("col")
+    above = (lax.axis_index("row") + senders - 1) % senders * cols
+    near = lax.dynamic_slice(peaks, (above + col_index, 0, 0), (1, 1, LANES))
+    far_off = above + (col_index + cols - 1) % cols
+    far_off = lax.dynamic_slice(peaks, (far_off, 0, 0), (1, 1, LANES))
+    offs = jnp.concatenate(
+        [far_off[0, 0, 2 * late : count], near[0, 0, : 2 * late]]
+    ).astype(jnp.int32).reshape(slots, 2)
     modulus = 1.5 * peak
     energy = jnp.minimum(
         modulus * jnp.sqrt(ill_power), 1.5 * ill_peak * jnp.sqrt(6.0 * power)

time: 230 us -> 208 us (0.904)
  waiting for transfers between devices: 91.9 us -> 71.9 us
  starting transfers between devices: 57.5 us -> 54.6 us
    ppermute x1 -> x0, waiting for transfers between devices: 23.9 us -> none  [passed_both(): return lax.ppermute(value, ('row', 'col'), pairs)]
    ppermute x16 -> x15, waiting for transfers between devices: 63.8 us -> 67.7 us  [passed_along(): return lax.ppermute(value, axis, pairs)]
    ppermute x16 -> x15, starting transfers between devices: 28.2 us -> 25.7 us  [passed_along(): return lax.ppermute(value, axis, pairs)]
  transfers between devices with their start and end apart: 21 -> 19, of which waited for: 8 -> 8; matrix products, arithmetic and copies ran while one was open for 9% -> 9% of each run, Pallas kernels for 9% -> 10%
where the time goes in v11:
time: 208 us
  waiting for transfers between devices  71.9 us (35%)
  starting transfers between devices  54.6 us (26%)
  Pallas kernels  48.2 us (23%)
  other arithmetic  19 us (9%)
  local copies, waits for them, and re-layouts  10.4 us (5%)
  between operations  3.44 us (2%)
    ppermute x15, waiting for transfers between devices, passed_along(): return lax.ppermute(value, axis, pairs)  67.7 us
    ppermute x15, starting transfers between devices, passed_along(): return lax.ppermute(value, axis, pairs)  25.7 us
    pallas_call x1, Pallas kernels, run_backward(): pl.pallas_call(backward_kernel, grid_spec=pltpu.PrefetchScalarGridSpec(nu...  25.5 us
    all_to_all x3, starting transfers between devices, spread_out(): lax.all_to_all(value, ('row', 'col'), split_axis=0, concat_axis=0, tiled=...  23.1 us
    pallas_call x1, Pallas kernels, run_forward(): pl.pallas_call(forward_kernel, grid_spec=pltpu.PrefetchScalarGridSpec(num...  21.2 us
    all_to_all x1, starting transfers between devices, shards(): lax.all_to_all(levels, 'row', split_axis=0, concat_axis=0, tiled=True, ax...  5.83 us
    convert_element_type x4, other arithmetic, narrowed(): return (value * (HALF_TOP / bound)).astype(jnp.float16)  5.16 us
  transfers between devices with their start and end apart: 19, of which 8 were waited for; matrix products, arithmetic and copies ran while one was open for 9% of the time, Pallas kernels for 10%

profile of v11, /device:TPU:1, one launch (start us, length us, event | category | flops | bytes accessed | tf_op | source)
XLA Modules:
  0.0 207.6 jit_solution(11490371267041368068)
XLA Ops:
  0.6 0.0 copy-start
  0.6 2.9 %fusion.10 = (bf16[16,2,2,16,512]{4,3,2,1,0:T(8,128)(2,1)}, bf16[16,2,2,16,512]{4,3,2,1,0:T(8,128)(2,1)S(1)}) fusion(bf16[16,4,2,16,512]{4,3,2,1,0:T(8,128)(2,1)} %bitcast.14), kind=kLoop, calls=%fused_computation.36 | loop fusion | bytes 4194304 | tf_op jit(solution)/shard_map/slice | solution.py:421
  3.5 2.7 %collective-permute-start = (bf16[16,2,2,16,512]{4,3,2,1,0:T(8,128)(2,1)}, bf16[16,2,2,16,512]{4,3,2,1,0:T(8,128)(2,1)S(1)}, u32[]{:S(2)}, u32[]{:S(2)}) collective-permute-start(bf16[16,2,2,16,512]{4,3,2,1,0:T(8,128)(2,1)} %get-tuple-element.36), channel_id=1, source_target_pairs={{0,1},{1,2},{2,3},{3,4},{4,5},{5,6},{6,7},{7,0},{8,9},{9,10},{10,1... | collective-permute-start | bytes 3145736 | tf_op jit(solution)/shard_map/ppermute | solution.py:22
  6.2 0.8 slice.52
  7.0 0.8 slice.53
  7.9 1.2 collective-permute-start.3
  9.1 4.7 %collective-permute-start.4 = (f32[2,256,256]{2,1,0:T(8,128)}, f32[2,256,256]{2,1,0:T(8,128)}, u32[]{:S(2)}, u32[]{:S(2)}) collective-permute-start(f32[2,256,256]{2,1,0:T(8,128)} %slice.53), channel_id=1, source_target_pairs={{0,120},{8,0},{16,8},{24,16},{32,24},{40,32},{48,40},{56,48},{64,5... | collective-permute-start | bytes 1572872 | tf_op jit(solution)/shard_map/ppermute | solution.py:22
  13.8 0.0 collective-permute-start.1
  13.8 4.8 %collective-permute-start.2 = (f32[2,256,256]{2,1,0:T(8,128)}, f32[2,256,256]{2,1,0:T(8,128)}, u32[]{:S(2)}, u32[]{:S(2)}) collective-permute-start(f32[2,256,256]{2,1,0:T(8,128)} %slice.52), channel_id=1, source_target_pairs={{0,120},{8,0},{16,8},{24,16},{32,24},{40,32},{48,40},{56,48},{64,5... | collective-permute-start | bytes 1572872 | tf_op jit(solution)/shard_map/ppermute | solution.py:22
  18.6 0.1 copy.11
  18.7 0.1 convert_element_type.59
  18.8 0.9 multiply_reduce_fusion.2
  19.7 1.2 fusion.7
  20.9 0.7 broadcast_in_dim.31
  21.5 3.9 %all-to-all-start = ((f32[128,1,128]{2,1,0:T(1,128)}), f32[128,1,128]{2,1,0:T(1,128)S(1)}, u32[]{:S(2)}, u32[]{:S(2)}) async-start(f32[128,1,128]{2,1,0:T(1,128)} %broadcast_in_dim.31), calls=%async_computation | async-start | bytes 131072 | tf_op jit(solution)/shard_map/all_to_all | solution.py:400
  25.4 1.5 pad_maximum_fusion
  26.9 0.0 collective-permute-done.3.refs_5_
  26.9 0.0 collective-permute-done.4.refs_6_
  26.9 10.1 %collective-permute-done.1.refs_3_ = f32[2,256,256]{2,1,0:T(8,128)} collective-permute-done((f32[2,256,256]{2,1,0:T(8,128)}, f32[2,256,256]{2,1,0:T(8,128)}, u32[]{:S(2)}, u32[]{:S(2)}) %collective-permute-start.1) | collective-permute-done | bytes 524320 | tf_op jit(solution)/shard_map/ppermute | solution.py:22
  37.0 0.0 collective-permute-done.2.refs_4_
  37.0 4.2 %all-to-all-done = f32[128,1,128]{2,1,0:T(1,128)S(1)} async-done(((f32[128,1,128]{2,1,0:T(1,128)}), f32[128,1,128]{2,1,0:T(1,128)S(1)}, u32[]{:S(2)}, u32[]{:S(2)}) %all-to-all-start) | async-done | bytes 65568 | tf_op jit(solution)/shard_map/all_to_all | solution.py:400
  41.2 5.8 %all-to-all-start.1 = ((bf16[16,4,2,16,512]{4,3,2,1,0:T(8,128)(2,1)}), bf16[16,4,2,16,512]{4,3,2,1,0:T(8,128)(2,1)}, u32[]{:S(2)}, u32[]{:S(2)}) async-start(bf16[16,4,2,16,512]{4,3,2,1,0:T(8,128)(2,1)} %pad_maximum_fusion), calls=%async_computation.1 | async-start | bytes 4194304 | tf_op jit(solution)/shard_map/all_to_all | solution.py:439
  47.0 1.2 collective-permute-start.6
  48.2 0.5 collective-permute-start.5
  48.8 0.1 slice_reduce_fusion
  48.9 0.1 concatenate.14
  48.9 0.1 concatenate.15
  49.0 0.2 reduce_max.31
  49.2 0.0 collective-permute-start.10
  49.2 2.5 %collective-permute-start.9 = (f32[2,256,256]{2,1,0:T(8,128)}, f32[2,256,256]{2,1,0:T(8,128)}, u32[]{:S(2)}, u32[]{:S(2)}) collective-permute-start(f32[2,256,256]{2,1,0:T(8,128)} %collective-permute-done.3.refs_5_), channel_id=1, source_target_pairs={{0,7},{1,0},{2,1},{3,2},{4,3},{5,4},{6,5},{7,6},{8,15},{9,8},{10,9... | collective-permute-start | bytes 1572872 | tf_op jit(solution)/shard_map/ppermute | solution.py:22
  51.7 0.0 collective-permute-start.7
  51.7 4.6 %collective-permute-done.6.refs_2_ = f32[2,256,256]{2,1,0:T(8,128)S(1)} collective-permute-done((f32[2,256,256]{2,1,0:T(8,128)}, f32[2,256,256]{2,1,0:T(8,128)S(1)}, u32[]{:S(2)}, u32[]{:S(2)}) %collective-permute-start.6) | collective-permute-done | bytes 524320 | tf_op jit(solution)/shard_map/ppermute | solution.py:22
  56.2 0.8 fusion.11
  58.3 0.6 maximum_convert_fusion.offs
  58.9 1.2 multiply_reduce_fusion.1
  61.3 0.5 collective-permute-done.10.refs_10_
  61.9 5.6 %collective-permute-done.9.refs_9_ = f32[2,256,256]{2,1,0:T(8,128)} collective-permute-done((f32[2,256,256]{2,1,0:T(8,128)}, f32[2,256,256]{2,1,0:T(8,128)}, u32[]{:S(2)}, u32[]{:S(2)}) %collective-permute-start.9) | collective-permute-done | bytes 524320 | tf_op jit(solution)/shard_map/ppermute | solution.py:22
  67.5 0.0 collective-permute-done.7.refs_7_
  67.5 0.0 collective-permute-done.8.refs_8_
  67.5 21.2 %forward.1 = (f32[4,2,512,512]{3,2,1,0:T(8,128)}, f32[4,2,512,512]{3,2,1,0:T(8,128)}) custom-call(s32[4,2]{1,0:T(4,128)} %maximum_convert_fusion.offs, f32[2,256,512]{2,1,0:T(8,128)} %refs_0_.1, f32[2,256,256]{2,1,0:T(8,128)} %collective-permute-done.5.refs_1_, f32[2,256,256]{2,1,0:T(8,128)} %copy-done.4, f32[2,256,256]{2,1,0:T(8,128)} %collective-permute-done.1.refs_3_, ...), custom_call_target="tpu_custom_call" | custom-call | flops 8589934592 | bytes 30000000 | tf_op jit(solution)/shard_map/forward/pallas_call | solution.py:307
  88.7 25.5 %backward.1 = (f32[2,8,768,128]{3,2,1,0:T(8,128)}, f32[4,32,3,16,128]{4,3,2,1,0:T(8,128)}) custom-call(s32[4,2]{1,0:T(4,128)} %maximum_convert_fusion.offs, s32[32]{0:T(128)} %order.1, f32[4,2,512,512]{3,2,1,0:T(8,128)} %get-tuple-element.17.far, f32[4,2,512,512]{3,2,1,0:T(8,128)} %get-tuple-element.18.patch, ...), custom_call_target="tpu_custom_call" | custom-call | flops 8589934592 | bytes 30000000 | tf_op jit(solution)/shard_map/backward/pallas_call | solution.py:342
  114.1 2.4 %multiply_convert_fusion.2 = (f16[2,2,768,128]{3,2,1,0:T(8,128)(2,1)S(1)}, f16[2,2,768,128]{3,2,1,0:T(8,128)(2,1)S(1)}) fusion(f32[2,8,768,128]{3,2,1,0:T(8,128)} %get-tuple-element.20, f32[]{:T(128)S(6)} %div.41), kind=kLoop, calls=%fused_computation.10 | loop fusion | flops 1572864 | bytes 4718596 | tf_op jit(solution)/shard_map/convert_element_type | solution.py:37
  116.5 1.5 collective-permute-start.11
  118.0 1.5 multiply_convert_fusion
  119.5 9.7 %all-to-all-start.2 = ((f16[128,48,128]{2,1,0:T(8,128)(2,1)}), f16[128,48,128]{2,1,0:T(8,128)(2,1)}, u32[]{:S(2)}, u32[]{:S(2)}) async-start(f16[128,48,128]{2,1,0:T(8,128)(2,1)} %multiply_convert_fusion), calls=%async_computation.2 | async-start | bytes 3145728 | tf_op jit(solution)/shard_map/all_to_all | solution.py:400
  129.1 1.1 collective-permute-start.12
  130.4 0.0 collective-permute-done.11
  130.4 0.1 convert_multiply_fusion.2
  130.5 25.2 %collective-permute-done.12 = f16[2,2,768,128]{3,2,1,0:T(8,128)(2,1)S(1)} collective-permute-done((f16[2,2,768,128]{3,2,1,0:T(8,128)(2,1)S(1)}, f16[2,2,768,128]{3,2,1,0:T(8,128)(2,1)S(1)}, u32[]{:S(2)}, u32[]{:S(2)}) %collective-permute-start.12) | collective-permute-done | bytes 786464 | tf_op jit(solution)/shard_map/ppermute | solution.py:22
  155.7 0.1 convert_multiply_fusion.1
  155.8 2.3 %maximum_add_fusion = f32[2,4,768,128]{3,2,1,0:T(8,128)S(1)} fusion(f32[2,2,768,128]{3,2,1,0:T(8,128)S(1)} %convert_multiply_fusion.1, f32[2,2,768,128]{3,2,1,0:T(8,128)S(1)} %convert_multiply_fusion.2, f32[2,8,768,128]{3,2,1,0:T(8,128)} %get-tuple-element.20), kind=kLoop, calls=%fused_computation | loop fusion | flops 1572864 | bytes 9437184 | tf_op jit(solution)/shard_map/add | solution.py:487
  158.1 0.0 all-to-all-done.2
  158.1 1.9 multiply_reduce_fusion
  160.1 1.1 broadcast_in_dim.34
  161.2 9.5 %all-to-all-start.3 = ((f16[128,32,128]{2,1,0:T(8,128)(2,1)}), f16[128,32,128]{2,1,0:T(8,128)(2,1)}, u32[]{:S(2)}, u32[]{:S(2)}) async-start(f16[128,32,128]{2,1,0:T(8,128)(2,1)} %broadcast_in_dim.34), calls=%async_computation.3 | async-start | bytes 2097152 | tf_op jit(solution)/shard_map/all_to_all | solution.py:400
  170.8 1.3 fusion.1
  172.0 5.4 %collective-permute-start.13 = (f16[2,4,256,128]{3,2,1,0:T(8,128)(2,1)}, f16[2,4,256,128]{3,2,1,0:T(8,128)(2,1)}, u32[]{:S(2)}, u32[]{:S(2)}) collective-permute-start(f16[2,4,256,128]{3,2,1,0:T(8,128)(2,1)} %get-tuple-element.34), channel_id=1, source_target_pairs={{0,120},{8,0},{16,8},{24,16},{32,24},{40,32},{48,40},{56,48},{64,5... | collective-permute-start | bytes 1572872 | tf_op jit(solution)/shard_map/ppermute | solution.py:22
  177.4 16.8 %collective-permute-done.13 = f16[2,4,256,128]{3,2,1,0:T(8,128)(2,1)} collective-permute-done((f16[2,4,256,128]{3,2,1,0:T(8,128)(2,1)}, f16[2,4,256,128]{3,2,1,0:T(8,128)(2,1)}, u32[]{:S(2)}, u32[]{:S(2)}) %collective-permute-start.13) | collective-permute-done | bytes 524320 | tf_op jit(solution)/shard_map/ppermute | solution.py:22
  194.2 5.0 %collective-permute-done.14 = f16[2,4,256,128]{3,2,1,0:T(8,128)(2,1)} collective-permute-done((f16[2,4,256,128]{3,2,1,0:T(8,128)(2,1)}, f16[2,4,256,128]{3,2,1,0:T(8,128)(2,1)}, u32[]{:S(2)}, u32[]{:S(2)}) %collective-permute-start.14) | collective-permute-done | bytes 524320 | tf_op jit(solution)/shard_map/ppermute | solution.py:22
  199.2 2.4 %fusion.3 = f32[2,256,4,128]{3,1,2,0:T(8,128)} fusion(f32[2,4,768,128]{3,2,1,0:T(8,128)S(1)} %maximum_add_fusion, f16[2,4,256,128]{3,2,1,0:T(8,128)(2,1)} %collective-permute-done.14, f16[2,4,256,128]{3,2,1,0:T(8,128)(2,1)} %collective-permute-done.13, f32[]{:T(128)S(6)} %div.42), kind=kLoop, calls=%fused_computation.17 | loop fusion | flops 1572864 | bytes 3145732 | tf_op jit(solution)/shard_map/transpose | solution.py:505
  201.6 1.6 copy.12
  203.1 1.3 copy.13
  204.4 1.5 convert_multiply_fusion.packed
  205.9 1.6 unpack.1
  (21 shorter events, 0.1 us)
Async XLA Ops:
  0.6 5.5 %copy-start = (f32[2,256,512]{2,1,0:T(8,128)S(1)}, f32[2,256,512]{2,1,0:T(8,128)}, u32[]{:S(2)}) copy-start(f32[2,256,512]{2,1,0:T(8,128)} %refs_0_.1) | copy-start | bytes 3145732
  3.5 15.1 %copy-start.3 = (s32[1,1,4,2]{2,3,1,0:T(2,128)S(1)}, s32[1,1,4,2]{2,3,1,0:T(2,128)}, u32[]{:S(2)}) copy-start(s32[1,1,4,2]{2,3,1,0:T(2,128)} %param.10) | copy-start | bytes 100
  3.5 21.9 %collective-permute-start = (bf16[16,2,2,16,512]{4,3,2,1,0:T(8,128)(2,1)}, bf16[16,2,2,16,512]{4,3,2,1,0:T(8,128)(2,1)S(1)}, u32[]{:S(2)}, u32[]{:S(2)}) collective-permute-start(bf16[16,2,2,16,512]{4,3,2,1,0:T(8,128)(2,1)} %get-tuple-element.36), channel_id=1, source_target_pairs={{0,1},{1,2},{2,3},{3,4},{4,5},{5,6},{6,7},{7,0},{8,9},{9,10},{10,1... | collective-permute-start | bytes 3145736 | tf_op jit(solution)/shard_map/ppermute | solution.py:22
  7.9 19.1 %collective-permute-start.3 = (f32[2,256,256]{2,1,0:T(8,128)}, f32[2,256,256]{2,1,0:T(8,128)}, u32[]{:S(2)}, u32[]{:S(2)}) collective-permute-start(f32[2,256,256]{2,1,0:T(8,128)} %slice.53), channel_id=1, source_target_pairs={{0,8},{8,16},{16,24},{24,32},{32,40},{40,48},{48,56},{56,64},{64,7... | collective-permute-start | bytes 1572872 | tf_op jit(solution)/shard_map/ppermute | solution.py:22
  9.1 17.9 %collective-permute-start.4 = (f32[2,256,256]{2,1,0:T(8,128)}, f32[2,256,256]{2,1,0:T(8,128)}, u32[]{:S(2)}, u32[]{:S(2)}) collective-permute-start(f32[2,256,256]{2,1,0:T(8,128)} %slice.53), channel_id=1, source_target_pairs={{0,120},{8,0},{16,8},{24,16},{32,24},{40,32},{48,40},{56,48},{64,5... | collective-permute-start | bytes 1572872 | tf_op jit(solution)/shard_map/ppermute | solution.py:22
  13.8 23.2 %collective-permute-start.1 = (f32[2,256,256]{2,1,0:T(8,128)}, f32[2,256,256]{2,1,0:T(8,128)}, u32[]{:S(2)}, u32[]{:S(2)}) collective-permute-start(f32[2,256,256]{2,1,0:T(8,128)} %slice.52), channel_id=1, source_target_pairs={{0,8},{8,16},{16,24},{24,32},{32,40},{40,48},{48,56},{56,64},{64,7... | collective-permute-start | bytes 1572872 | tf_op jit(solution)/shard_map/ppermute | solution.py:22
  13.8 23.2 %collective-permute-start.2 = (f32[2,256,256]{2,1,0:T(8,128)}, f32[2,256,256]{2,1,0:T(8,128)}, u32[]{:S(2)}, u32[]{:S(2)}) collective-permute-start(f32[2,256,256]{2,1,0:T(8,128)} %slice.52), channel_id=1, source_target_pairs={{0,120},{8,0},{16,8},{24,16},{32,24},{40,32},{48,40},{56,48},{64,5... | collective-permute-start | bytes 1572872 | tf_op jit(solution)/shard_map/ppermute | solution.py:22
  21.5 19.7 %all-to-all-start = ((f32[128,1,128]{2,1,0:T(1,128)}), f32[128,1,128]{2,1,0:T(1,128)S(1)}, u32[]{:S(2)}, u32[]{:S(2)}) async-start(f32[128,1,128]{2,1,0:T(1,128)} %broadcast_in_dim.31), calls=%async_computation | async-start | bytes 131072 | tf_op jit(solution)/shard_map/all_to_all | solution.py:400
  26.9 31.9 %copy-start.2 = (f32[2,512,512]{2,1,0:T(8,128)S(1)}, f32[2,512,512]{2,1,0:T(8,128)}, u32[]{:S(2)}) copy-start(f32[2,512,512]{2,1,0:T(8,128)} %ill.1) | copy-start | bytes 6291460
  41.2 47.5 %all-to-all-start.1 = ((bf16[16,4,2,16,512]{4,3,2,1,0:T(8,128)(2,1)}), bf16[16,4,2,16,512]{4,3,2,1,0:T(8,128)(2,1)}, u32[]{:S(2)}, u32[]{:S(2)}) async-start(bf16[16,4,2,16,512]{4,3,2,1,0:T(8,128)(2,1)} %pad_maximum_fusion), calls=%async_computation.1 | async-start | bytes 4194304 | tf_op jit(solution)/shard_map/all_to_all | solution.py:439
  47.0 9.2 %collective-permute-start.6 = (f32[2,256,256]{2,1,0:T(8,128)}, f32[2,256,256]{2,1,0:T(8,128)S(1)}, u32[]{:S(2)}, u32[]{:S(2)}) collective-permute-start(f32[2,256,256]{2,1,0:T(8,128)} %slice.53), channel_id=1, source_target_pairs={{0,7},{1,0},{2,1},{3,2},{4,3},{5,4},{6,5},{7,6},{8,15},{9,8},{10,9... | collective-permute-start | bytes 1572872 | tf_op jit(solution)/shard_map/ppermute | solution.py:22
  48.2 13.1 %collective-permute-start.5 = (f32[2,256,256]{2,1,0:T(8,128)}, f32[2,256,256]{2,1,0:T(8,128)}, u32[]{:S(2)}, u32[]{:S(2)}) collective-permute-start(f32[2,256,256]{2,1,0:T(8,128)} %slice.52), channel_id=1, source_target_pairs={{0,1},{1,2},{2,3},{3,4},{4,5},{5,6},{6,7},{7,0},{8,9},{9,10},{10,1... | collective-permute-start | bytes 1572872 | tf_op jit(solution)/shard_map/ppermute | solution.py:22
  49.2 12.7 %collective-permute-start.10 = (f32[2,256,256]{2,1,0:T(8,128)}, f32[2,256,256]{2,1,0:T(8,128)}, u32[]{:S(2)}, u32[]{:S(2)}) collective-permute-start(f32[2,256,256]{2,1,0:T(8,128)} %collective-permute-done.4.refs_6_), channel_id=1, source_target_pairs={{0,7},{1,0},{2,1},{3,2},{4,3},{5,4},{6,5},{7,6},{8,15},{9,8},{10,9... | collective-permute-start | bytes 1572872 | tf_op jit(solution)/shard_map/ppermute | solution.py:22
  49.2 18.3 %collective-permute-start.9 = (f32[2,256,256]{2,1,0:T(8,128)}, f32[2,256,256]{2,1,0:T(8,128)}, u32[]{:S(2)}, u32[]{:S(2)}) collective-permute-start(f32[2,256,256]{2,1,0:T(8,128)} %collective-permute-done.3.refs_5_), channel_id=1, source_target_pairs={{0,7},{1,0},{2,1},{3,2},{4,3},{5,4},{6,5},{7,6},{8,15},{9,8},{10,9... | collective-permute-start | bytes 1572872 | tf_op jit(solution)/shard_map/ppermute | solution.py:22
  51.7 15.8 %collective-permute-start.7 = (f32[2,256,256]{2,1,0:T(8,128)}, f32[2,256,256]{2,1,0:T(8,128)}, u32[]{:S(2)}, u32[]{:S(2)}) collective-permute-start(f32[2,256,256]{2,1,0:T(8,128)} %collective-permute-done.1.refs_3_), channel_id=1, source_target_pairs={{0,1},{1,2},{2,3},{3,4},{4,5},{5,6},{6,7},{7,0},{8,9},{9,10},{10,1... | collective-permute-start | bytes 1572872 | tf_op jit(solution)/shard_map/ppermute | solution.py:22
  56.2 5.0 %copy-start.4 = (f32[2,256,256]{2,1,0:T(8,128)}, f32[2,256,256]{2,1,0:T(8,128)S(1)}, u32[]{:S(2)}) copy-start(f32[2,256,256]{2,1,0:T(8,128)S(1)} %collective-permute-done.6.refs_2_) | copy-start | bytes 1572868
  56.2 11.2 %collective-permute-start.8 = (f32[2,256,256]{2,1,0:T(8,128)}, f32[2,256,256]{2,1,0:T(8,128)}, u32[]{:S(2)}, u32[]{:S(2)}) collective-permute-start(f32[2,256,256]{2,1,0:T(8,128)} %collective-permute-done.2.refs_4_), channel_id=1, source_target_pairs={{0,1},{1,2},{2,3},{3,4},{4,5},{5,6},{6,7},{7,0},{8,9},{9,10},{10,1... | collective-permute-start | bytes 1572872 | tf_op jit(solution)/shard_map/ppermute | solution.py:22
  114.1 3.8 %copy-start.1 = (f32[4,32,3,16,128]{4,3,2,1,0:T(8,128)S(1)}, f32[4,32,3,16,128]{4,3,2,1,0:T(8,128)}, u32[]{:S(2)}) copy-start(f32[4,32,3,16,128]{4,3,2,1,0:T(8,128)} %get-tuple-element.22) | copy-start | bytes 9437188
  116.5 13.9 %collective-permute-start.11 = (f16[2,2,768,128]{3,2,1,0:T(8,128)(2,1)S(1)}, f16[2,2,768,128]{3,2,1,0:T(8,128)(2,1)S(1)}, u32[]{:S(2)}, u32[]{:S(2)}) collective-permute-start(f16[2,2,768,128]{3,2,1,0:T(8,128)(2,1)S(1)} %get-tuple-element.32), channel_id=1, source_target_pairs={{0,1},{1,2},{2,3},{3,4},{4,5},{5,6},{6,7},{7,0},{8,9},{9,10},{10,1... | collective-permute-start | bytes 2359304 | tf_op jit(solution)/shard_map/ppermute | solution.py:22
  119.5 38.6 %all-to-all-start.2 = ((f16[128,48,128]{2,1,0:T(8,128)(2,1)}), f16[128,48,128]{2,1,0:T(8,128)(2,1)}, u32[]{:S(2)}, u32[]{:S(2)}) async-start(f16[128,48,128]{2,1,0:T(8,128)(2,1)} %multiply_convert_fusion), calls=%async_computation.2 | async-start | bytes 3145728 | tf_op jit(solution)/shard_map/all_to_all | solution.py:400
  129.1 26.5 %collective-permute-start.12 = (f16[2,2,768,128]{3,2,1,0:T(8,128)(2,1)S(1)}, f16[2,2,768,128]{3,2,1,0:T(8,128)(2,1)S(1)}, u32[]{:S(2)}, u32[]{:S(2)}) collective-permute-start(f16[2,2,768,128]{3,2,1,0:T(8,128)(2,1)S(1)} %get-tuple-element.33), channel_id=1, source_target_pairs={{0,7},{1,0},{2,1},{3,2},{4,3},{5,4},{6,5},{7,6},{8,15},{9,8},{10,9... | collective-permute-start | bytes 2359304 | tf_op jit(solution)/shard_map/ppermute | solution.py:22
  161.2 43.2 %all-to-all-start.3 = ((f16[128,32,128]{2,1,0:T(8,128)(2,1)}), f16[128,32,128]{2,1,0:T(8,128)(2,1)}, u32[]{:S(2)}, u32[]{:S(2)}) async-start(f16[128,32,128]{2,1,0:T(8,128)(2,1)} %broadcast_in_dim.34), calls=%async_computation.3 | async-start | bytes 2097152 | tf_op jit(solution)/shard_map/all_to_all | solution.py:400
  172.0 22.2 %collective-permute-start.13 = (f16[2,4,256,128]{3,2,1,0:T(8,128)(2,1)}, f16[2,4,256,128]{3,2,1,0:T(8,128)(2,1)}, u32[]{:S(2)}, u32[]{:S(2)}) collective-permute-start(f16[2,4,256,128]{3,2,1,0:T(8,128)(2,1)} %get-tuple-element.34), channel_id=1, source_target_pairs={{0,120},{8,0},{16,8},{24,16},{32,24},{40,32},{48,40},{56,48},{64,5... | collective-permute-start | bytes 1572872 | tf_op jit(solution)/shard_map/ppermute | solution.py:22
  177.4 21.8 %collective-permute-start.14 = (f16[2,4,256,128]{3,2,1,0:T(8,128)(2,1)}, f16[2,4,256,128]{3,2,1,0:T(8,128)(2,1)}, u32[]{:S(2)}, u32[]{:S(2)}) collective-permute-start(f16[2,4,256,128]{3,2,1,0:T(8,128)(2,1)} %get-tuple-element.35), channel_id=1, source_target_pairs={{0,8},{8,16},{16,24},{24,32},{32,40},{40,48},{48,56},{56,64},{64,7... | collective-permute-start | bytes 1572872 | tf_op jit(solution)/shard_map/ppermute | solution.py:22
